TPU v7x, 32 devices: a whole 2x2x4 slice. The times are simulated.
32 devices in a mesh: dp: 4 (over x, core), ctx: 8 (over z, y).
Axes of the slice: x: 2, y: 2, z: 4, core: 2. Of those that a mesh axis runs over, the one named last changes fastest.
Arguments:
- patches: bfloat16 [4, 2304, 1024], P('dp', 'ctx'), may hold values from -6 to 6
- enc_pos: bfloat16 [2304, 1024], P('ctx'), may hold values from -6 to 6
- w_embed: bfloat16 [1024, 1024], replicated, may hold values from -0.1875 to 0.1875
- enc_gain: bfloat16 [1024], replicated, may hold values from 0.25 to 1.75
- w_qkv: bfloat16 [1024, 1536], replicated, may hold values from -0.3125 to 0.3125
- w_out: bfloat16 [512, 1024], replicated, may hold values from -0.25 to 0.25
- enc_out_gain: bfloat16 [1024], replicated, may hold values from 0.25 to 1.75
- w_dec_embed: bfloat16 [1024, 512], replicated, may hold values from -0.1875 to 0.1875
- mask_token: bfloat16 [512], replicated, may hold values from -4 to 4
- dec_pos: bfloat16 [2304, 512], P('ctx'), may hold values from -6 to 6
- dec_attn_gain: bfloat16 [512], replicated, may hold values from 0.25 to 1.75
- decoder_query_key_value_weight: bfloat16 [512, 768], replicated, may hold values from -0.4375 to 0.4375
- w_dec_out: bfloat16 [256, 512], replicated, may hold values from -0.375 to 0.375
- decoder_feed_gain: bfloat16 [512], replicated, may hold values from 0.25 to 1.75
- w_up: bfloat16 [512, 2048], replicated, may hold values from -0.25 to 0.25
- w_down: bfloat16 [2048, 512], replicated, may hold values from -0.125 to 0.125
- head_gain: bfloat16 [512], replicated, may hold values from 0.25 to 1.75
- w_head: bfloat16 [512, 1024], replicated, may hold values from -0.25 to 0.25
- visible_rows: int32 [4, 2304], P('dp', 'ctx'), may hold values from -1 to 287, as said below
- visible_count: int32 [4, 8], P('dp', 'ctx'), may hold values from 0 to 288, as said below
- owner_slot: int32 [4, 2304], P('dp', 'ctx'), may hold values from 0 to 2303, as said below
Outputs:
- reconstruction: bfloat16 [4, 2304, 1024], P('dp', 'ctx')
- grad_head: float32 [512, 1024], replicated
- grad_dec_out: float32 [256, 512], replicated
- loss: float32 [], replicated
Inputs may be any that keep to these rules, and one draw needn't show every extreme that they name: `visible_rows`: slots from visible_count onward hold -1; the first visible_count slots hold distinct local indices in increasing order. `visible_count`: the counts of one gather sum to 768; in every gather one device has exactly 288. `owner_slot`: A permutation of each gather's patches; exactly 36 patches of device c go to device d, into rows c * 36 to (c + 1) * 36 - 1 of its local rows.
All inputs are finite; a program needn't handle non-finite values.
Results may differ from a plain program's by a relative error of at most 0.019.
Values may be sent and summed in bfloat16 or wider, within the bound.
No kernel may reach another device: no remote copies, remote signals or barrier semaphores. Data moves between devices by JAX's collectives and lax.ppermute only.
A program may use at most 128 MiB of HBM per device.

v0:
```python
import jax
import jax.numpy as jnp
from jax import lax
from jax.sharding import PartitionSpec as P

EH = 8
DH = 8


def layer_norm(x, gain):
    row_mean = jnp.mean(x, axis=-1, keepdims=True)
    centered_input = x - row_mean
    var = jnp.mean(centered_input * centered_input, axis=-1, keepdims=True)
    return centered_input * lax.rsqrt(var + 1e-06) * gain.astype(jnp.float32)


def norm_backward(z, gain, upstream):
    row_mean = jnp.mean(z, axis=-1, keepdims=True)
    centered_input = z - row_mean
    inverse_scale = lax.rsqrt(
        jnp.mean(centered_input * centered_input, axis=-1, keepdims=True) + 1e-06
    )
    normalized_input = centered_input * inverse_scale
    input_gradient = upstream * gain.astype(jnp.float32)
    return inverse_scale * (
        input_gradient
        - jnp.mean(input_gradient, axis=-1, keepdims=True)
        - normalized_input * jnp.mean(input_gradient * normalized_input, axis=-1, keepdims=True)
    )


def attend(queries, keys, values, key_valid, heads):
    rows = queries.shape[0]
    width = queries.shape[1]
    size = width // heads
    q_heads = queries.reshape(rows, heads, size).transpose(1, 0, 2)
    k_heads = keys.reshape(-1, heads, size).transpose(1, 0, 2)
    v_heads = values.reshape(-1, heads, size).transpose(1, 0, 2)

    def one_head(items):
        q_one, k_one, v_one = items
        score = jnp.dot(q_one, k_one.T, preferred_element_type=jnp.float32) * size ** (-0.5)
        if key_valid is not None:
            score = jnp.where(key_valid[None, :], score, -jnp.inf)
        top = jnp.max(score, axis=1, keepdims=True)
        weight = jnp.exp(score - top)
        weight = (weight / jnp.sum(weight, axis=1, keepdims=True)).astype(jnp.bfloat16)
        return jnp.dot(weight, v_one, preferred_element_type=jnp.float32).astype(jnp.bfloat16)

    out = lax.map(one_head, (q_heads, k_heads, v_heads))
    return out.transpose(1, 0, 2).reshape(rows, width)


def on_device(
    patches,
    enc_pos,
    w_embed,
    enc_gain,
    w_qkv,
    w_out,
    enc_out_gain,
    w_dec_embed,
    mask_token,
    dec_pos,
    dec_attn_gain,
    decoder_query_key_value_weight,
    w_dec_out,
    decoder_feed_gain,
    w_up,
    w_down,
    head_gain,
    w_head,
    visible_rows,
    visible_count,
    owner_slot,
):
    groups = lax.axis_size("ctx")
    here = lax.axis_index("ctx")
    device_local_rows = patches.shape[1]
    slots = visible_rows.shape[1]
    share = slots // 3
    enc_width = w_out.shape[0]
    dec_width = w_dec_embed.shape[1]
    dec_attn_width = w_dec_out.shape[0]
    block = device_local_rows // groups
    source = patches[0]
    slot_rows = visible_rows[0]
    count = visible_count[0, 0]
    slot_index = jnp.arange(slots, dtype=jnp.int32)
    live = slot_index < count
    safe_rows = jnp.clip(slot_rows, 0, device_local_rows - 1)
    start = (
        jnp.dot(source[safe_rows], w_embed, preferred_element_type=jnp.float32)
        + enc_pos[safe_rows].astype(jnp.float32)
    ).astype(jnp.bfloat16)
    counts = lax.all_gather(visible_count, "ctx", axis=1, tiled=True)[0]
    key_valid = (slot_index[None, :] < counts[:, None]).reshape(-1)
    normed = layer_norm(start.astype(jnp.float32), enc_gain).astype(jnp.bfloat16)
    qkv = jnp.dot(normed, w_qkv, preferred_element_type=jnp.float32).astype(jnp.bfloat16)
    keys, values = (
        lax.all_gather(qkv[:, enc_width : 2 * enc_width], "ctx", axis=0, tiled=True),
        lax.all_gather(qkv[:, 2 * enc_width :], "ctx", axis=0, tiled=True),
    )
    attended = attend(qkv[:, :enc_width], keys, values, key_valid, EH)
    encoded = start.astype(jnp.float32) + jnp.dot(
        attended, w_out, preferred_element_type=jnp.float32
    )
    dec_normed = layer_norm(encoded, enc_out_gain).astype(jnp.bfloat16)
    dec_tok = jnp.dot(dec_normed, w_dec_embed, preferred_element_type=jnp.float32).astype(
        jnp.bfloat16
    )
    place = jnp.where(live, slot_rows, device_local_rows)
    filled = jnp.broadcast_to(
        mask_token.astype(jnp.float32)[None, :], (device_local_rows, dec_width)
    )
    filled = filled.at[place].set(dec_tok.astype(jnp.float32), mode="drop")
    decoder_in = (filled + dec_pos.astype(jnp.float32)).astype(jnp.bfloat16)
    masked = (
        jnp.ones((device_local_rows,), jnp.bfloat16)
        .at[place]
        .set(jnp.zeros((slots,), jnp.bfloat16), mode="drop")
    )
    owners = owner_slot[0]
    position = owners // device_local_rows * block + owners % device_local_rows - here * block
    send_tok = jnp.zeros_like(decoder_in).at[position].set(decoder_in)
    send_target = jnp.zeros_like(source).at[position].set(source)
    send_flag = jnp.zeros_like(masked).at[position].set(masked)
    y_own, target, flag = (
        lax.all_to_all(send_tok, "ctx", split_axis=0, concat_axis=0, tiled=True),
        lax.all_to_all(send_target, "ctx", split_axis=0, concat_axis=0, tiled=True),
        lax.all_to_all(send_flag, "ctx", split_axis=0, concat_axis=0, tiled=True),
    )
    attn_in = layer_norm(y_own.astype(jnp.float32), dec_attn_gain).astype(jnp.bfloat16)
    dec_qkv = jnp.dot(
        attn_in, decoder_query_key_value_weight, preferred_element_type=jnp.float32
    ).astype(jnp.bfloat16)
    dec_keys, dec_values = (
        lax.all_gather(dec_qkv[:, dec_attn_width : 2 * dec_attn_width], "ctx", axis=0, tiled=True),
        lax.all_gather(dec_qkv[:, 2 * dec_attn_width :], "ctx", axis=0, tiled=True),
    )
    dec_att = attend(dec_qkv[:, :dec_attn_width], dec_keys, dec_values, None, DH)
    y_mid = y_own.astype(jnp.float32) + jnp.dot(
        dec_att, w_dec_out, preferred_element_type=jnp.float32
    )
    first = layer_norm(y_mid, decoder_feed_gain).astype(jnp.bfloat16)
    pre_act = jnp.dot(first, w_up, preferred_element_type=jnp.float32)
    act = jax.nn.gelu(pre_act).astype(jnp.bfloat16)
    z = y_mid + jnp.dot(act, w_down, preferred_element_type=jnp.float32)
    zn = layer_norm(z, head_gain).astype(jnp.bfloat16)
    pred = jnp.dot(zn, w_head, preferred_element_type=jnp.float32)
    err = (pred - target.astype(jnp.float32)) * flag.astype(jnp.float32)[:, None]
    pixels = w_head.shape[1]
    loss_part = jnp.sum(err * err) / pixels
    dpred = (err * (2.0 / pixels)).astype(jnp.bfloat16)
    head_part = jnp.dot(zn.T, dpred, preferred_element_type=jnp.float32)
    upstream = jnp.dot(dpred, w_head.T, preferred_element_type=jnp.float32)
    dz = norm_backward(z, head_gain, upstream).astype(jnp.bfloat16)
    back_act = jnp.dot(dz, w_down.T, preferred_element_type=jnp.float32)
    gelu_back = jax.vjp(jax.nn.gelu, pre_act)[1]
    pre_grad = gelu_back(back_act)[0].astype(jnp.bfloat16)
    back_first = jnp.dot(pre_grad, w_up.T, preferred_element_type=jnp.float32)
    mid_grad = (
        dz.astype(jnp.float32) + norm_backward(y_mid, decoder_feed_gain, back_first)
    ).astype(jnp.bfloat16)
    out_part = jnp.dot(dec_att.T, mid_grad, preferred_element_type=jnp.float32)
    partial_sums = (
        lax.psum(head_part.astype(jnp.bfloat16), "ctx").astype(jnp.float32),
        lax.psum(out_part.astype(jnp.bfloat16), "ctx").astype(jnp.float32),
        lax.psum(loss_part.astype(jnp.bfloat16), "ctx").astype(jnp.float32),
    )
    grad_head, grad_dec_out, loss_total = (
        lax.psum(partial_sums[0].astype(jnp.bfloat16), "dp").astype(jnp.float32),
        lax.psum(partial_sums[1].astype(jnp.bfloat16), "dp").astype(jnp.float32),
        lax.psum(partial_sums[2].astype(jnp.bfloat16), "dp").astype(jnp.float32),
    )
    masked_total = lax.axis_size("dp") * (groups * device_local_rows - share * groups)
    return (pred.astype(jnp.bfloat16)[None], grad_head, grad_dec_out, loss_total / masked_total)


def solution(mesh):
    in_specs = (
        P("dp", "ctx", None),
        P("ctx", None),
        P(),
        P(),
        P(),
        P(),
        P(),
        P(),
        P(),
        P("ctx", None),
        P(),
        P(),
        P(),
        P(),
        P(),
        P(),
        P(),
        P(),
        P("dp", "ctx"),
        P("dp", "ctx"),
        P("dp", "ctx"),
    )
    out_specs = (P("dp", "ctx", None), P(), P(), P())
    return jax.shard_map(
        on_device, mesh=mesh, in_specs=in_specs, out_specs=out_specs, check_vma=False
    )
```

profile of v0, /device:TPU:0, one launch (start us, length us, event | category | flops | bytes accessed | tf_op | source)
XLA Modules:
  0.0 471.7 jit_solution(4662674791598275151)
XLA Ops:
  9.4 4.4 gather_fusion
  13.9 4.4 gather_fusion.1
  18.3 2.8 convert_reduce_fusion
  25.7 13.2 %all-reduce = s32[8]{0:T(128)S(1)} all-reduce(s32[8]{0:T(128)S(1)} %bitcast_dynamic-update-slice_fusion), channel_id=1, replica_groups=mesh['dp'=4,'ctx'=8] {'ctx'}, use_global_device_ids=true, to_apply=%add | all-reduce | flops 8 | bytes 64
  40.4 38.2 %all-gather.5.cloned.1.call-done = bf16[2304,512]{1,0:T(8,128)(2,1)} async-done(((bf16[288,512]{1,0:T(8,128)(2,1)}), bf16[2304,512]{1,0:T(8,128)(2,1)}) %all-gather.5.cloned.1.call-update) | async-done | bytes 2359312 | tf_op jit(solution)/shard_map/all_gather | solution.py:101
  78.6 4.4 copy.44
  83.0 48.5 %all-gather.7.cloned.1.call-done = bf16[2304,512]{1,0:T(8,128)(2,1)} async-done(((bf16[288,512]{1,0:T(8,128)(2,1)}), bf16[2304,512]{1,0:T(8,128)(2,1)}) %all-gather.7.cloned.1.call-update) | async-done | bytes 2359312 | tf_op jit(solution)/shard_map/all_gather | solution.py:102
  131.4 4.4 copy.45
  135.8 32.3 %while.22 = (s32[]{:T(128)}, bf16[8,288,64]{1,2,0:T(8,128)(2,1)S(1)}, bf16[8,288,64]{1,2,0:T(8,128)(2,1)}, bf16[8,2304,64]{1,2,0:T(8,128)(2,1)}, bf16[8,2304,64]{1,2,0:T(8,128)(2,1)}, /*index=5*/s32[8]{0:T(128)S(1)}, s32[]{:T(128)}) while((s32[]{:T(128)}, bf16[8,288,64]{1,2,0:T(8,128)(2,1)S(1)}, bf16[8,288,64]{1,2,0:T(8,128)(2,1)}, ...), condition=%wide.region_5.6_spmd.clone, body=%wide.region_2.5_spmd.clone.sunk | while | flops 175197888 | bytes 8669677 | solution.py:50
  138.1 1.7 fusion.135
  140.0 1.7 fusion.133
  142.2 1.7 fusion.135
  146.2 1.7 fusion.135
  150.3 1.7 fusion.135
  152.1 1.7 fusion.133
  154.3 1.7 fusion.135
  158.3 1.7 fusion.135
  162.4 1.7 fusion.135
  164.2 1.7 fusion.133
  166.4 1.7 fusion.135
  168.1 2.1 fusion.98
  172.7 3.9 scatter_fusion
  176.6 2.3 scatter_custom_fusion.1
  179.7 3.4 all-to-all-start
  183.2 9.9 %all-to-all-done = bf16[8,36,512]{2,1,0:T(8,128)(2,1)S(1)} async-done(((bf16[8,36,512]{2,1,0:T(8,128)(2,1)}), bf16[8,36,512]{2,1,0:T(8,128)(2,1)S(1)}, u32[]{:S(2)}, u32[]{:S(2)}) %all-to-all-start) | async-done | bytes 294944 | tf_op jit(solution)/shard_map/all_to_all | solution.py:129
  194.5 1.8 convolution_convert_fusion.2
  197.6 2.4 scatter_custom_fusion.3
  200.0 2.5 scatter_custom_fusion.4
  203.2 3.6 all-to-all-start.2
  206.8 3.1 scatter_custom_fusion.2
  209.9 2.0 all_to_all.20
  213.2 4.8 %all-to-all-start.1 = ((bf16[8,36,1024]{2,1,0:T(8,128)(2,1)}), bf16[8,36,1024]{2,1,0:T(8,128)(2,1)}, u32[]{:S(2)}, u32[]{:S(2)}) async-start(bf16[8,36,1024]{2,1,0:T(8,128)(2,1)} %all_to_all.20), calls=%async_computation.1 | async-start | bytes 1310720 | tf_op jit(solution)/shard_map/all_to_all | solution.py:130
  218.1 25.7 %all-to-all-done.1 = bf16[8,36,1024]{2,1,0:T(8,128)(2,1)} async-done(((bf16[8,36,1024]{2,1,0:T(8,128)(2,1)}), bf16[8,36,1024]{2,1,0:T(8,128)(2,1)}, u32[]{:S(2)}, u32[]{:S(2)}) %all-to-all-start.1) | async-done | bytes 589856 | tf_op jit(solution)/shard_map/all_to_all | solution.py:130
  243.9 2.2 reshape.291
  246.9 2.4 copy.50
  249.2 35.9 %all-gather.11.cloned.1.call-done = bf16[2304,256]{1,0:T(8,128)(2,1)} async-done(((bf16[288,256]{1,0:T(8,128)(2,1)}), bf16[2304,256]{1,0:T(8,128)(2,1)}) %all-gather.11.cloned.1.call-update) | async-done | bytes 1179664 | tf_op jit(solution)/shard_map/all_gather | solution.py:139
  285.2 2.4 copy.51
  287.5 29.5 %while.21 = (s32[]{:T(128)}, bf16[8,288,32]{1,2,0:T(8,128)(2,1)S(1)}, bf16[8,288,32]{1,2,0:T(8,128)(2,1)}, bf16[8,2304,32]{1,2,0:T(8,128)(2,1)}, bf16[8,2304,32]{1,2,0:T(8,128)(2,1)}, /*index=5*/s32[]{:T(128)}) while((s32[]{:T(128)}, bf16[8,288,32]{1,2,0:T(8,128)(2,1)S(1)}, bf16[8,288,32]{1,2,0:T(8,128)(2,1)}, ...), condition=%wide.region_15.16_spmd, body=%wide.region_12.15_spmd.sunk | while | flops 89588160 | bytes 8316357 | solution.py:50
  317.1 1.7 fusion.99
  323.0 2.0 multiply_reduce_fusion
  325.6 1.8 convolution_convert_fusion.1
  327.7 6.4 %fusion.92 = (f32[288]{0:T(512)S(1)}, f32[288]{0:T(512)S(1)}, f32[288,512]{1,0:T(8,128)}) fusion(f32[288]{0:T(512)S(1)} %add_rsqrt_fusion.2, f32[288,512]{1,0:T(8,128)} %copy-done.1, f32[288]{0:T(512)S(1)} %broadcast_multiply_fusion.6, f32[512]{0:T(512)S(1)} %convert_element_type.166, bf16[512,2048]{1,0:T(8,128)(2,1)} %param.39, ...), kind=kOutput, calls=%fused_computation.163 | convolution fusion | flops 1220640256 | bytes 8034816 | tf_op jit(solution)/shard_map/dot_general | solution.py:161
  334.1 2.5 convolution_convert_fusion.4
  336.6 82.6 %all-reduce.6.cloned.1.call-done = (bf16[512,1024]{1,0:T(8,128)(2,1)}, bf16[256,512]{1,0:T(8,128)(2,1)}) async-done(((bf16[512,1024]{1,0:T(8,128)(2,1)}, bf16[256,512]{1,0:T(8,128)(2,1)}), (bf16[512,1024]{1,0:T(8,128)(2,1)}, bf16[256,512]{1,0:T(8,128)(2,1)})) %all-reduce.6.cloned.1.call-update) | async-done | bytes 1310736 | tf_op jit(solution)/shard_map/psum | solution.py:167
  419.9 20.0 %psum.46 = bf16[]{:T(256)} all-reduce(bf16[]{:T(256)S(6)} %div.103), channel_id=1, replica_groups=mesh['dp'=4,'ctx'=8] {'ctx'}, use_global_device_ids=true, to_apply=%region_32.33 | all-reduce | flops 1 | bytes 4 | tf_op jit(solution)/shard_map/psum | solution.py:169
  440.0 6.3 %psum.47 = bf16[]{:T(256)} all-reduce(bf16[]{:T(256)} %psum.46), channel_id=1, replica_groups=mesh['dp'=4,'ctx'=8] {'dp'}, use_global_device_ids=true, to_apply=%region_33.34 | all-reduce | flops 1 | bytes 4 | tf_op jit(solution)/shard_map/psum | solution.py:174
  446.9 13.2 %all-reduce.8.cloned.1.call-done = (bf16[512,1024]{1,0:T(8,128)(2,1)}, bf16[256,512]{1,0:T(8,128)(2,1)}) async-done(((bf16[512,1024]{1,0:T(8,128)(2,1)}, bf16[256,512]{1,0:T(8,128)(2,1)}), (bf16[512,1024]{1,0:T(8,128)(2,1)}, bf16[256,512]{1,0:T(8,128)(2,1)})) %all-reduce.8.cloned.1.call-update) | async-done | bytes 1310736 | tf_op jit(solution)/shard_map/psum | solution.py:172
  460.1 2.8 convert_element_type.178
  (161 shorter events, 65.5 us)
Async XLA Ops:
  7.2 14.3 %copy-start = (bf16[1024,1536]{1,0:T(8,128)(2,1)S(1)}, bf16[1024,1536]{1,0:T(8,128)(2,1)}, u32[]{:S(2)}) copy-start(bf16[1024,1536]{1,0:T(8,128)(2,1)} %param.29) | copy-start | bytes 9437188
  7.2 71.4 %all-gather.5.cloned.1.call-start = ((), (), s32[]{:S(2)}) async-start(), calls=%async_computation.3 | async-start | bytes 2654208 | tf_op jit(solution)/shard_map/all_gather | solution.py:101
  18.3 3.1 copy-start.12
  21.1 1.6 copy-start.5
  22.7 1.7 copy-start.20
  22.7 17.1 %copy-start.13 = (bf16[1024]{0:T(1024)(128)(2,1)S(1)}, bf16[1024]{0:T(1024)(128)(2,1)}, u32[]{:S(2)}) copy-start(bf16[1024]{0:T(1024)(128)(2,1)} %param.31) | copy-start | bytes 6148
  22.7 17.1 %copy-start.14 = (s32[1,288]{1,0:T(1,128)S(1)}, s32[1,288]{1,0:T(1,128)}, u32[]{:S(2)}) copy-start(s32[1,288]{1,0:T(1,128)} %param.45) | copy-start | bytes 3460
  23.6 107.8 %all-gather.7.cloned.1.call-start = ((), (), s32[]{:S(2)}) async-start(), calls=%async_computation.4 | async-start | bytes 2654208 | tf_op jit(solution)/shard_map/all_gather | solution.py:102
  83.0 52.9 %copy-start.9 = (bf16[8,288,64]{1,2,0:T(8,128)(2,1)S(1)}, bf16[8,288,64]{1,2,0:T(8,128)(2,1)}, u32[]{:S(2)}) copy-start(bf16[8,288,64]{1,2,0:T(8,128)(2,1)} %custom-call.5) | copy-start | bytes 884740
  168.1 2.4 copy-start.7
  170.2 1.7 copy-start.15
  170.2 2.5 copy-start.11
  176.6 6.6 %copy-start.16 = (bf16[512]{0:T(512)(128)(2,1)S(1)}, bf16[512]{0:T(512)(128)(2,1)}, u32[]{:S(2)}) copy-start(bf16[512]{0:T(512)(128)(2,1)} %param.35) | copy-start | bytes 3076
  179.7 13.4 %all-to-all-start = ((bf16[8,36,512]{2,1,0:T(8,128)(2,1)}), bf16[8,36,512]{2,1,0:T(8,128)(2,1)S(1)}, u32[]{:S(2)}, u32[]{:S(2)}) async-start(bf16[8,36,512]{2,1,0:T(8,128)(2,1)} %all_to_all.18), calls=%async_computation | async-start | bytes 655360 | tf_op jit(solution)/shard_map/all_to_all | solution.py:129
  183.1 63.7 %all-gather.9.cloned.1.call-start = ((), (), s32[]{:S(2)}) async-start(), calls=%async_computation.5 | async-start | bytes 1327104 | tf_op jit(solution)/shard_map/all_gather | solution.py:138
  196.3 21.7 %copy-start.17 = (bf16[512]{0:T(512)(128)(2,1)S(1)}, bf16[512]{0:T(512)(128)(2,1)}, u32[]{:S(2)}) copy-start(bf16[512]{0:T(512)(128)(2,1)} %param.38) | copy-start | bytes 3076
  196.3 21.7 %copy-start.18 = (bf16[512]{0:T(512)(128)(2,1)S(1)}, bf16[512]{0:T(512)(128)(2,1)}, u32[]{:S(2)}) copy-start(bf16[512]{0:T(512)(128)(2,1)} %param.41) | copy-start | bytes 3076
  197.0 88.1 %all-gather.11.cloned.1.call-start = ((), (), s32[]{:S(2)}) async-start(), calls=%async_computation.6 | async-start | bytes 1327104 | tf_op jit(solution)/shard_map/all_gather | solution.py:139
  203.2 10.0 %all-to-all-start.2 = ((bf16[8,36,1]{1,2,0:T(2,128)(2,1)}), bf16[8,36,1]{1,2,0:T(2,128)(2,1)S(1)}, u32[]{:S(2)}, u32[]{:S(2)}) async-start(bf16[8,36,1]{1,2,0:T(2,128)(2,1)} %all_to_all.24), calls=%async_computation.2 | async-start | bytes 8192 | tf_op jit(solution)/shard_map/all_to_all | solution.py:131
  213.2 30.7 %all-to-all-start.1 = ((bf16[8,36,1024]{2,1,0:T(8,128)(2,1)}), bf16[8,36,1024]{2,1,0:T(8,128)(2,1)}, u32[]{:S(2)}, u32[]{:S(2)}) async-start(bf16[8,36,1024]{2,1,0:T(8,128)(2,1)} %all_to_all.20), calls=%async_computation.1 | async-start | bytes 1310720 | tf_op jit(solution)/shard_map/all_to_all | solution.py:130
  217.9 201.3 %all-reduce.6.cloned.1.call-start = ((), (), s32[]{:S(2)}) async-start(), calls=%async_computation.7 | async-start | bytes 2621440 | tf_op jit(solution)/shard_map/psum | solution.py:167
  317.0 2.8 copy-start.8
  317.0 1.9 copy-start.6
  318.7 1.1 copy-start.1
  319.0 1.6 copy-start.19
  320.6 1.4 copy-start.4
  320.6 2.1 copy-start.2
  320.6 2.4 copy-start.3
  336.6 123.5 %all-reduce.8.cloned.1.call-start = ((), (), s32[]{:S(2)}) async-start(), calls=%async_computation.8 | async-start | bytes 2621440 | tf_op jit(solution)/shard_map/psum | solution.py:172
  460.1 2.8 copy-start.10
Sparse Core Ops, SparseCore 0:
  23.8 54.7 all-gather.4
  80.8 50.5 all-gather.6
  197.2 46.4 all-gather.8
  245.7 39.3 all-gather.10
  336.7 82.5 all-reduce.5
  421.8 38.2 all-reduce.7
where the time goes:
time: 474 us; the launch traced here: 472 us
  waiting for transfers between devices  256 us (54%)
  matrix products  77.6 us (16%)
  local copies, waits for them, and re-layouts  49.2 us (10%)
  blocking collectives  39.5 us (8%)
  other arithmetic  18.8 us (4%)
  between operations  17.8 us (4%)
  starting transfers between devices  12.2 us (3%)
    psum x1, waiting for transfers between devices, on_device(): lax.psum(head_part.astype(jnp.bfloat16), 'ctx').astype(jnp.float32)  82.6 us
    all_gather x1, waiting for transfers between devices, on_device(): lax.all_gather(qkv[:, 2 * enc_width:], 'ctx', axis=0, tiled=True)  48.5 us
    all_gather x1, waiting for transfers between devices, on_device(): lax.all_gather(qkv[:, enc_width:2 * enc_width], 'ctx', axis=0, tiled=True)  38.2 us
    all_gather x1, waiting for transfers between devices, on_device(): lax.all_gather(dec_qkv[:, 2 * dec_attn_width:], 'ctx', axis=0, tiled=True)  35.9 us
    dot_general x16, matrix products, one_head(): jnp.dot(weight, v_one, preferred_element_type=jnp.float32)  25.9 us
    dot_general x16, matrix products, one_head(): jnp.dot(q_one, k_one.T, preferred_element_type=jnp.float32) * size ** (-0.5)  25.8 us
    all_to_all x1, waiting for transfers between devices, on_device(): lax.all_to_all(send_target, 'ctx', split_axis=0, concat_axis=0, tiled=True)  25.7 us
    psum x1, blocking collectives, on_device(): lax.psum(loss_part.astype(jnp.bfloat16), 'ctx').astype(jnp.float32)  20 us
  transfers between devices with their start and end apart: 9, of which 8 were waited for; matrix products, arithmetic and copies ran while one was open for 4% of the time, Pallas kernels for 0%

commit v1 on v0

v1 whole, which is shorter than its diff:
```python
import functools
import math

import jax
import jax.numpy as jnp
from jax import lax
from jax.experimental import pallas as pl
from jax.experimental.pallas import tpu as pltpu
from jax.sharding import PartitionSpec as P

HEADS = 8
BF = jnp.bfloat16
F32 = jnp.float32
LOG2E = math.log2(math.e)
VMEM_LIMIT = 56 << 20


def layer_norm(x, gain):
    row_mean = jnp.mean(x, axis=-1, keepdims=True)
    centered_input = x - row_mean
    var = jnp.mean(centered_input * centered_input, axis=-1, keepdims=True)
    return centered_input * lax.rsqrt(var + 1e-06) * gain.astype(F32)


def norm_backward(z, gain, upstream):
    row_mean = jnp.mean(z, axis=-1, keepdims=True)
    centered_input = z - row_mean
    inverse_scale = lax.rsqrt(
        jnp.mean(centered_input * centered_input, axis=-1, keepdims=True) + 1e-06
    )
    normalized_input = centered_input * inverse_scale
    input_gradient = upstream * gain.astype(F32)
    return inverse_scale * (
        input_gradient
        - jnp.mean(input_gradient, axis=-1, keepdims=True)
        - normalized_input * jnp.mean(input_gradient * normalized_input, axis=-1, keepdims=True)
    )


def dot(a, b):
    return jnp.dot(a, b, preferred_element_type=F32)


def dot_t(a, b):
    return lax.dot_general(a, b, (((1,), (1,)), ((), ())), preferred_element_type=F32)


def swap_halves(x):
    half = x.shape[1] // 2
    return jnp.concatenate([x[:, half:], x[:, :half]], axis=1)


def slot_of_row(slots_row):
    size = slots_row.shape[1]
    row = lax.broadcasted_iota(jnp.int32, (size, size), 0)
    return jnp.where(row == slots_row, 1.0, 0.0)


def embed_kernel(
    patch_ref, pos_ref, w_embed_ref, gain_ref, w_qkv_ref, slots_ref,
    send_ref, tok_ref, normed_ref, qkv_ref,
):
    rows, width = patch_ref.shape
    half = rows // 2
    att = w_qkv_ref.shape[1] // 3
    size = att // HEADS
    tile = 256

    @pl.loop(0, width // tile)
    def _(step):
        cols = pl.ds(pl.multiple_of(step * tile, tile), tile)
        tok_ref[:, cols] = (
            dot(patch_ref[...], w_embed_ref[:, cols]) + pos_ref[:, cols].astype(F32)
        ).astype(BF)

    normed_ref[...] = layer_norm(tok_ref[...].astype(F32), gain_ref[...]).astype(BF)
    pick = slot_of_row(slots_ref[...]).astype(BF)

    @pl.loop(0, 3 * att // tile)
    def _(step):
        cols = pl.ds(pl.multiple_of(step * tile, tile), tile)
        part = dot(normed_ref[...], w_qkv_ref[:, cols]).astype(BF)
        qkv_ref[:, cols] = lax.dot_general(
            pick, part, (((0,), (0,)), ((), ())), preferred_element_type=F32
        ).astype(BF)

    count = jnp.sum(jnp.where(slots_ref[...] >= 0, 1.0, 0.0), axis=1, keepdims=True)
    high = jnp.floor(count * (1.0 / 16))
    lane = lax.broadcasted_iota(jnp.int32, (16, 128), 1)
    info = jnp.where(lane < 64, high, count - 16.0 * high).astype(BF)
    for head in range(HEADS):
        at = head * size
        q = qkv_ref[:, at : at + size]
        k = qkv_ref[:, att + at : att + at + size]
        v = qkv_ref[:, 2 * att + at : 2 * att + at + size]
        send_ref[head, :half, :] = jnp.concatenate([q[:half], q[half:]], axis=1)
        send_ref[head, half : half + rows, :] = jnp.concatenate([k, v], axis=1)
        send_ref[head, half + rows :, :] = info


def enc_attend_kernel(
    first_ref, q_ref, kv_ref, out_ref, q_buf, kv_buf, o_buf, *, q_at, kv_at, rows, cap_q, cap_k
):
    half = rows // 2
    sources = kv_ref.shape[0]
    lane16 = lax.broadcasted_iota(jnp.int32, (16, 128), 1)
    lane_h = lax.broadcasted_iota(jnp.int32, (half, 128), 1)

    def count_of(source):
        info = kv_ref[source, kv_at + rows : kv_at + rows + 16, :].astype(F32)
        high = jnp.max(jnp.where(lane16 < 64, info, 0.0)).astype(jnp.int32)
        low = jnp.max(jnp.where(lane16 >= 64, info, 0.0)).astype(jnp.int32)
        return high * 16 + low

    q_buf[...] = jnp.zeros_like(q_buf)
    o_buf[...] = jnp.zeros_like(o_buf)
    kv_buf[:, :128] = jnp.zeros((kv_buf.shape[0], 128), BF)
    kv_buf[:, 128:] = jnp.ones((kv_buf.shape[0], 128), BF)

    key = lax.broadcasted_iota(jnp.int32, (1, cap_k), 1)
    valid = jnp.zeros((1, cap_k), F32)
    off = jnp.int32(0)
    for source in range(sources):
        count = count_of(source)
        off = pl.multiple_of(off, 16)
        kv_buf[pl.ds(off, rows), :128] = kv_ref[source, kv_at : kv_at + rows, :]
        valid = jnp.where((key >= off) & (key < off + count), 1.0, valid)
        off = off + (count + 15) // 16 * 16
    bias = jnp.where(valid > 0.0, 0.0, -1e30)

    offs = []
    off = jnp.int32(0)
    for source in range(HEADS):
        off = pl.multiple_of(off, 16)
        offs.append(off)
        block = q_ref[source, q_at : q_at + half, :]
        zero = jnp.zeros_like(block)
        q_buf[pl.ds(off, half), :] = jnp.where(lane_h < 64, block, zero)
        q_buf[pl.ds(off + half, half), :] = jnp.where(lane_h < 64, swap_halves(block), zero)
        off = off + (count_of(first_ref[0] + source) + 15) // 16 * 16
    total = off

    tile = 128
    scale = LOG2E * 64**-0.5

    @pl.loop(0, cap_q // tile)
    def _(step):
        @pl.when(step * tile < total)
        def _():
            at = pl.ds(pl.multiple_of(step * tile, tile), tile)
            score = dot_t(q_buf[at, :], kv_buf[:cap_k, :128]) + bias
            top = jnp.max(score, axis=1, keepdims=True)
            weight = jnp.exp2((score - top) * scale).astype(BF)
            mixed = dot(weight, kv_buf[:cap_k, :])
            o_buf[at, :] = (mixed[:, :128] / mixed[:, 128:]).astype(BF)

    for source in range(HEADS):
        upper = o_buf[pl.ds(offs[source], half), :]
        lower = o_buf[pl.ds(pl.multiple_of(offs[source] + half, 16), half), :]
        out_ref[source] = jnp.where(lane_h < 64, swap_halves(upper), lower)


def middle_kernel(
    att_ref, tok_ref, w_out_ref, out_gain_ref, w_dec_ref, mask_ref, pos_ref, gain_ref,
    w_qkv_ref, slots_ref, owner_ref, patch_ref,
    send_ref, y_ref, target_ref, flag_ref, att_buf, qkv_buf, *, groups,
):
    rows, width = tok_ref.shape
    half = rows // 2
    block = rows // groups
    for pair in range(HEADS // 2):
        a, b = att_ref[2 * pair], att_ref[2 * pair + 1]
        cols = slice(128 * pair, 128 * pair + 128)
        att_buf[:half, cols] = jnp.concatenate([a[:, :64], b[:, :64]], axis=1)
        att_buf[half:, cols] = jnp.concatenate([a[:, 64:], b[:, 64:]], axis=1)
    pick = slot_of_row(slots_ref[...])
    seen = jnp.sum(pick, axis=1, keepdims=True)
    attended = dot(pick.astype(BF), att_buf[...]).astype(BF)
    encoded = tok_ref[...].astype(F32) + dot(attended, w_out_ref[...])
    dec_normed = layer_norm(encoded, out_gain_ref[...]).astype(BF)
    dec_tok = dot(dec_normed, w_dec_ref[...]).astype(BF).astype(F32)
    filled = jnp.where(seen > 0.0, dec_tok, mask_ref[...].astype(F32))
    decoder_in = (filled + pos_ref[...].astype(F32)).astype(BF)

    owner = owner_ref[...]
    dest = jnp.zeros_like(owner)
    for device in range(1, groups):
        dest = dest + jnp.where(owner >= device * rows, 1, 0)
    local = owner - dest * rows
    first = jnp.min(local.astype(F32), axis=1, keepdims=True).astype(jnp.int32)
    place = dest * block + local - first
    move = slot_of_row(place).astype(BF)
    y = dot(move, decoder_in)
    y_ref[...] = y.astype(BF)
    target_ref[...] = dot(move, patch_ref[...]).astype(BF)
    hidden = jnp.broadcast_to(1.0 - seen, (rows, 128)).astype(BF)
    flag_ref[...] = dot(move, hidden)
    attn_in = layer_norm(y, gain_ref[...]).astype(BF)
    qkv_buf[...] = dot(attn_in, w_qkv_ref[...]).astype(BF).astype(F32)
    att = w_qkv_ref.shape[1] // 3
    size = att // HEADS
    quarter = rows // 4
    for head in range(HEADS):
        at = head * size
        q = qkv_buf[:, at : at + size]
        k = qkv_buf[:, att + at : att + at + size]
        v = qkv_buf[:, 2 * att + at : 2 * att + at + size]
        send_ref[head, :half, :] = jnp.concatenate(
            [k[:half], v[:half], k[half:], v[half:]], axis=1
        ).astype(BF)
        send_ref[head, half:, :] = jnp.concatenate(
            [q[i * quarter : (i + 1) * quarter] for i in range(4)], axis=1
        ).astype(BF)


def dec_attend_kernel(q_ref, kv_ref, out_ref, k_buf, v_buf, *, q_at, rows):
    half = rows // 2
    quarter = rows // 4
    sources = kv_ref.shape[0]
    for source in range(sources):
        for part in range(2):
            block = kv_ref[source, :half, 64 * part : 64 * part + 64]
            at = source * rows + part * half
            k, v = block[:, :32], block[:, 32:]
            k_buf[at : at + half, :] = jnp.concatenate([k, k, k, k], axis=1)
            v_buf[at : at + half, :128] = jnp.concatenate([v, v, v, v], axis=1)
    v_buf[:, 128:] = jnp.ones((v_buf.shape[0], 128), BF)
    scale = LOG2E * 32**-0.5
    lane = lax.broadcasted_iota(jnp.int32, (quarter, 128), 1)
    zone = [(lane >= 32 * i) & (lane < 32 * i + 32) for i in range(4)]

    @pl.loop(0, HEADS)
    def _(source):
        block = q_ref[source, q_at : q_at + quarter, :].astype(F32)
        q = jnp.concatenate([jnp.where(z, block, 0.0) for z in zone], axis=0).astype(BF)
        score = dot_t(q, k_buf[...])
        top = jnp.max(score, axis=1, keepdims=True)
        weight = jnp.exp2((score - top) * scale).astype(BF)
        mixed = dot(weight, v_buf[...])
        mixed = mixed[:, :128] / mixed[:, 128:]
        out = mixed[:quarter]
        for i in range(1, 4):
            out = jnp.where(zone[i], mixed[i * quarter : (i + 1) * quarter], out)
        out_ref[source] = out.astype(BF)


def vmem_call(kernel, outs, scratch, inputs, smem=(), flops=0):
    space = [
        pl.BlockSpec(memory_space=pltpu.SMEM if i in smem else pltpu.VMEM)
        for i in range(len(inputs))
    ]
    moved = sum(a.size * a.dtype.itemsize for a in inputs)
    return pl.pallas_call(
        kernel,
        out_shape=outs,
        in_specs=space,
        out_specs=[pl.BlockSpec(memory_space=pltpu.VMEM)] * len(outs),
        scratch_shapes=scratch,
        compiler_params=pltpu.CompilerParams(vmem_limit_bytes=VMEM_LIMIT),
        cost_estimate=pl.CostEstimate(flops=flops, bytes_accessed=moved, transcendentals=0),
    )(*inputs)


def swap(x, axis, groups=None):
    return lax.all_to_all(
        x, axis, split_axis=0, concat_axis=0, tiled=True, axis_index_groups=groups
    )


def all_sum(x, groups):
    size = lax.axis_size("dp")
    me = lax.axis_index("dp")
    stages = []
    step = 1
    while step < size:
        pairs = [(i, i ^ step) for i in range(size)]
        upper = (me // step) % 2
        half = x.shape[0] // 2
        mine = lax.dynamic_slice_in_dim(x, upper * half, half, 0)
        other = lax.dynamic_slice_in_dim(x, (1 - upper) * half, half, 0)
        x = mine + lax.ppermute(other, "dp", pairs)
        stages.append((pairs, upper))
        step *= 2
    rows, width = x.shape
    blocks = swap(x.reshape(groups, rows // groups, width), "ctx")
    total = jnp.sum(blocks.astype(F32), axis=0).astype(BF)
    x = swap(jnp.broadcast_to(total[None], blocks.shape), "ctx").reshape(rows, width)
    for pairs, upper in reversed(stages):
        other = lax.ppermute(x, "dp", pairs)
        low = jnp.where(upper == 0, x, other)
        high = jnp.where(upper == 0, other, x)
        x = jnp.concatenate([low, high], axis=0)
    return x


def on_device(
    patches,
    enc_pos,
    w_embed,
    enc_gain,
    w_qkv,
    w_out,
    enc_out_gain,
    w_dec_embed,
    mask_token,
    dec_pos,
    dec_attn_gain,
    decoder_query_key_value_weight,
    w_dec_out,
    decoder_feed_gain,
    w_up,
    w_down,
    head_gain,
    w_head,
    visible_rows,
    visible_count,
    owner_slot,
):
    groups = lax.axis_size("ctx")
    repeat = groups // HEADS
    teams = [list(range(HEADS * i, HEADS * i + HEADS)) for i in range(repeat)]
    teams = None if repeat == 1 else teams
    source = patches[0]
    rows, pixels = source.shape
    half, quarter = rows // 2, rows // 4
    share = rows // 3
    width = w_embed.shape[1]
    dec_width = w_dec_embed.shape[1]
    row = lambda vector: vector.reshape(1, -1)
    shape = jax.ShapeDtypeStruct

    send, tok = vmem_call(
        embed_kernel,
        [shape((HEADS, half + rows + 16, 128), BF), shape((rows, width), BF)],
        [pltpu.VMEM((rows, width), BF), pltpu.VMEM((rows, w_qkv.shape[1]), BF)],
        [source, enc_pos, w_embed, row(enc_gain), w_qkv, visible_rows],
        flops=2 * rows * width * (pixels + w_qkv.shape[1]),
    )
    first = (lax.axis_index("ctx") // HEADS * HEADS).astype(jnp.int32).reshape(1)
    if repeat == 1:
        q = kv = swap(send, "ctx")
        q_at, kv_at = 0, half
    else:
        q = swap(send[:, :half], "ctx", teams)
        kv = swap(jnp.tile(send[:, half:], (repeat, 1, 1)), "ctx")
        q_at, kv_at = 0, 0
    cap_k = (share + 16) * groups
    cap_q = min(HEADS * rows, cap_k)
    (att,) = vmem_call(
        functools.partial(
            enc_attend_kernel, q_at=q_at, kv_at=kv_at, rows=rows, cap_q=cap_q, cap_k=cap_k
        ),
        [shape((HEADS, half, 128), BF)],
        [
            pltpu.VMEM((cap_q + rows, 128), BF),
            pltpu.VMEM((cap_k + rows, 256), BF),
            pltpu.VMEM((cap_q + rows, 128), BF),
        ],
        [first, q, kv],
        smem=(0,),
        flops=4 * cap_q * cap_k * 128,
    )
    att = swap(att, "ctx", teams)
    send, y_own, target, flag = vmem_call(
        functools.partial(middle_kernel, groups=groups),
        [
            shape((HEADS, half + quarter, 128), BF),
            shape((rows, dec_width), BF),
            shape((rows, pixels), BF),
            shape((rows, 128), F32),
        ],
        [
            pltpu.VMEM((rows, w_out.shape[0]), BF),
            pltpu.VMEM((rows, decoder_query_key_value_weight.shape[1]), F32),
        ],
        [
            att, tok, w_out, row(enc_out_gain), w_dec_embed, row(mask_token), dec_pos,
            row(dec_attn_gain), decoder_query_key_value_weight, visible_rows, owner_slot, source,
        ],
        flops=2 * rows * width * 1024,
    )
    if repeat == 1:
        q = kv = swap(send, "ctx")
        q_at = half
    else:
        q = swap(send[:, half:], "ctx", teams)
        kv = swap(jnp.tile(send[:, :half], (repeat, 1, 1)), "ctx")
        q_at = 0
    (att,) = vmem_call(
        functools.partial(dec_attend_kernel, q_at=q_at, rows=rows),
        [shape((HEADS, quarter, 128), BF)],
        [pltpu.VMEM((groups * rows, 128), BF), pltpu.VMEM((groups * rows, 256), BF)],
        [q, kv],
        flops=4 * HEADS * rows * groups * rows * 128,
    )
    att = swap(att, "ctx", teams)
    dec_att = (
        att.reshape(HEADS, quarter, 4, 32).transpose(2, 1, 0, 3).reshape(rows, w_dec_out.shape[0])
    )
    y_mid = y_own.astype(F32) + dot(dec_att, w_dec_out)
    feed = layer_norm(y_mid, decoder_feed_gain).astype(BF)
    pre_act = dot(feed, w_up)
    act = jax.nn.gelu(pre_act).astype(BF)
    z = y_mid + dot(act, w_down)
    zn = layer_norm(z, head_gain).astype(BF)
    pred = dot(zn, w_head)
    err = (pred - target.astype(F32)) * flag[:, :1]
    reconstruction = swap(pred.astype(BF).reshape(groups, rows // groups, pixels), "ctx")
    loss_part = jnp.sum(err * err) / pixels
    dpred = (err * (2.0 / pixels)).astype(BF)
    head_part = dot(zn.T, dpred)
    upstream = dot_t(dpred, w_head)
    dz = norm_backward(z, head_gain, upstream).astype(BF)
    back_act = dot_t(dz, w_down)
    gelu_back = jax.vjp(jax.nn.gelu, pre_act)[1]
    pre_grad = gelu_back(back_act)[0].astype(BF)
    back_feed = dot_t(pre_grad, w_up)
    mid_grad = (dz.astype(F32) + norm_backward(y_mid, decoder_feed_gain, back_feed)).astype(BF)
    out_part = dot(dec_att.T, mid_grad)

    depth = out_part.shape[0] // 2
    loss_high = loss_part.astype(BF)
    loss_low = (loss_part - loss_high.astype(F32)).astype(BF)
    used = dec_width + depth + 2
    unit = lax.axis_size("dp") * groups
    padded = -(-used // unit) * unit
    stacked = jnp.concatenate(
        [
            head_part.astype(BF),
            jnp.concatenate([out_part[:depth], out_part[depth:]], axis=1).astype(BF),
            jnp.broadcast_to(loss_high, (1, pixels)),
            jnp.broadcast_to(loss_low, (1, pixels)),
            jnp.zeros((padded - used, pixels), BF),
        ],
        axis=0,
    )
    total = all_sum(stacked, groups)
    grad_head = total[:dec_width].astype(F32)
    tail = total[dec_width : dec_width + depth].astype(F32)
    grad_dec_out = jnp.concatenate([tail[:, :dec_width], tail[:, dec_width:]], axis=0)
    loss = total[used - 2, 0].astype(F32) + total[used - 1, 0].astype(F32)
    masked_total = lax.axis_size("dp") * (groups * rows - share * groups)
    return (reconstruction.reshape(1, rows, pixels), grad_head, grad_dec_out, loss / masked_total)


def solution(mesh):
    in_specs = (
        P("dp", "ctx", None),
        P("ctx", None),
        P(),
        P(),
        P(),
        P(),
        P(),
        P(),
        P(),
        P("ctx", None),
        P(),
        P(),
        P(),
        P(),
        P(),
        P(),
        P(),
        P(),
        P("dp", "ctx"),
        P("dp", "ctx"),
        P("dp", "ctx"),
    )
    out_specs = (P("dp", "ctx", None), P(), P(), P())
    return jax.shard_map(
        on_device, mesh=mesh, in_specs=in_specs, out_specs=out_specs, check_vma=False
    )
```

time: 474 us -> 218 us (0.46)
  waiting for transfers between devices: 256 us -> 63.4 us
  matrix products: 77.6 us -> 14.7 us
  Pallas kernels: 0 us -> 38.5 us
  local copies, waits for them, and re-layouts: 49.2 us -> 17.8 us
  between operations: 17.8 us -> 4.07 us
  starting transfers between devices: 12.2 us -> 21.2 us
  other arithmetic: 18.8 us -> 11.6 us
  blocking collectives: 39.5 us -> 45.2 us
    all_gather x4 -> x0, waiting for transfers between devices: 123 us -> none  [the longest x1 48.5 us: on_device(): lax.all_gather(qkv[:, 2 * enc_width:], 'ctx', axis=0, tiled=True)]
    psum x2 -> x0, waiting for transfers between devices: 95.8 us -> none  [the longest x1 82.6 us: on_device(): lax.psum(head_part.astype(jnp.bfloat16), 'ctx').astype(jnp.float32)]
    dot_general x45 -> x8, matrix products: 77.6 us -> 14.7 us  [the longest x6 7.58 us: dot(): return jnp.dot(a, b, preferred_element_type=F32)]
    all_to_all x0 -> x3, blocking collectives: none -> 45.2 us  [swap(): lax.all_to_all(x, axis, split_axis=0, concat_axis=0, tiled=True, axis_ind...]
    pallas_call x0 -> x4, Pallas kernels: none -> 38.5 us  [vmem_call(): pl.pallas_call(kernel, out_shape=outs, in_specs=space, out_specs=[pl.Bloc...]
    psum x2 -> x0, blocking collectives: 26.3 us -> none  [the longest x1 20 us: on_device(): lax.psum(loss_part.astype(jnp.bfloat16), 'ctx').astype(jnp.float32)]
    all_to_all x3 -> x4, waiting for transfers between devices: 36.9 us -> 51.9 us  [swap(): lax.all_to_all(x, axis, split_axis=0, concat_axis=0, tiled=True, axis_ind...]
    all_gather x4 -> x0, local copies, waits for them, and re-layouts: 13.5 us -> none  [the longest x1 4.38 us: on_device(): lax.all_gather(qkv[:, 2 * enc_width:], 'ctx', axis=0, tiled=True)]
  transfers between devices with their start and end apart: 9 -> 8, of which waited for: 8 -> 7; matrix products, arithmetic and copies ran while one was open for 4% -> 3% of each run, Pallas kernels for 0% -> 0%
where the time goes in v1:
time: 218 us; the launch traced here: 217 us
  waiting for transfers between devices  63.4 us (29%)
  blocking collectives  45.2 us (21%)
  Pallas kernels  38.5 us (18%)
  starting transfers between devices  21.2 us (10%)
  local copies, waits for them, and re-layouts  17.8 us (8%)
  matrix products  14.7 us (7%)
  other arithmetic  11.6 us (5%)
  between operations  4.07 us (2%)
    all_to_all x4, waiting for transfers between devices, swap(): lax.all_to_all(x, axis, split_axis=0, concat_axis=0, tiled=True, axis_ind...  51.9 us
    all_to_all x3, blocking collectives, swap(): lax.all_to_all(x, axis, split_axis=0, concat_axis=0, tiled=True, axis_ind...  45.2 us
    pallas_call x4, Pallas kernels, vmem_call(): pl.pallas_call(kernel, out_shape=outs, in_specs=space, out_specs=[pl.Bloc...  38.5 us
    all_to_all x4, starting transfers between devices, swap(): lax.all_to_all(x, axis, split_axis=0, concat_axis=0, tiled=True, axis_ind...  18 us
    ppermute x2, waiting for transfers between devices, all_sum(): x = mine + lax.ppermute(other, 'dp', pairs)  11.1 us
    dot_general x6, matrix products, dot(): return jnp.dot(a, b, preferred_element_type=F32)  7.58 us
    dot_general x2, matrix products, dot_t(): lax.dot_general(a, b, (((1,), (1,)), ((), ())), preferred_element_type=F32)  7.15 us
    concatenate x1, local copies, waits for them, and re-layouts, on_device(): jnp.concatenate([head_part.astype(BF), jnp.concatenate([out_part[:depth],...  5.02 us
  transfers between devices with their start and end apart: 8, of which 7 were waited for; matrix products, arithmetic and copies ran while one was open for 3% of the time, Pallas kernels for 0%

profile of v1, /device:TPU:0, one launch (start us, length us, event | category | flops | bytes accessed | tf_op | source)
XLA Modules:
  0.0 216.6 jit_solution(12472492482547778396)
XLA Ops:
  0.6 1.4 reshape.90.gain_ref
  2.1 9.8 %shard_map.219 = (bf16[8,448,128]{2,1,0:T(8,128)(2,1)}, bf16[288,1024]{1,0:T(8,128)(2,1)}) custom-call(bf16[288,1024]{1,0:T(8,128)(2,1)} %bitcast.20, bf16[288,1024]{1,0:T(8,128)(2,1)} %pos_ref.2, bf16[1024,1024]{1,0:T(8,128)(2,1)} %w_embed_ref.1, bf16[1,1024]{1,0:T(2,128)(2,1)} %reshape.90.gain_ref, bf16[1024,1536]{1,0:T(8,128)(2,1)} %w_qkv_ref.2, ...), custom_call_target="tpu_custom_call" | custom-call | flops 1509949440 | bytes 6425728 | tf_op jit(solution)/shard_map/pallas_call | solution.py:253
  11.9 7.4 %all-to-all-start = ((bf16[8,448,128]{2,1,0:T(8,128)(2,1)}), bf16[8,448,128]{2,1,0:T(8,128)(2,1)S(1)}, u32[]{:S(2)}, u32[]{:S(2)}) async-start(bf16[8,448,128]{2,1,0:T(8,128)(2,1)} %get-tuple-element.10), calls=%async_computation | async-start | bytes 1835008 | tf_op jit(solution)/shard_map/all_to_all | solution.py:265
  19.4 23.0 %all-to-all-done.q_ref.kv_ref = bf16[8,448,128]{2,1,0:T(8,128)(2,1)S(1)} async-done(((bf16[8,448,128]{2,1,0:T(8,128)(2,1)}), bf16[8,448,128]{2,1,0:T(8,128)(2,1)S(1)}, u32[]{:S(2)}, u32[]{:S(2)}) %all-to-all-start) | async-done | bytes 917536 | tf_op jit(solution)/shard_map/all_to_all | solution.py:265
  42.4 0.9 copy-done.1
  43.3 7.2 %shard_map.220 = bf16[8,144,128]{2,1,0:T(8,128)(2,1)} custom-call(s32[1]{0:T(128)} %bitcast.first_ref, bf16[8,448,128]{2,1,0:T(8,128)(2,1)} %copy-done.1, bf16[8,448,128]{2,1,0:T(8,128)(2,1)} %copy-done.1), custom_call_target="tpu_custom_call" | custom-call | flops 411041792 | bytes 1835012 | tf_op jit(solution)/shard_map/pallas_call | solution.py:253
  50.5 3.5 %all-to-all-start.1 = ((bf16[8,144,128]{2,1,0:T(8,128)(2,1)}), bf16[8,144,128]{2,1,0:T(8,128)(2,1)S(1)}, u32[]{:S(2)}, u32[]{:S(2)}) async-start(bf16[8,144,128]{2,1,0:T(8,128)(2,1)} %shard_map.220), calls=%async_computation.1 | async-start | bytes 589824 | tf_op jit(solution)/shard_map/all_to_all | solution.py:265
  54.0 0.6 reshape.91.out_gain_ref
  54.6 0.6 reshape.92.mask_ref
  55.2 0.6 reshape.93.gain_ref
  55.8 8.0 %all-to-all-done.1.att_ref = bf16[8,144,128]{2,1,0:T(8,128)(2,1)S(1)} async-done(((bf16[8,144,128]{2,1,0:T(8,128)(2,1)}), bf16[8,144,128]{2,1,0:T(8,128)(2,1)S(1)}, u32[]{:S(2)}, u32[]{:S(2)}) %all-to-all-start.1) | async-done | bytes 294944 | tf_op jit(solution)/shard_map/all_to_all | solution.py:265
  63.7 0.7 copy-done.5
  64.5 5.7 %shard_map.221 = (bf16[8,216,128]{2,1,0:T(8,128)(2,1)}, bf16[288,512]{1,0:T(8,128)(2,1)}, bf16[288,1024]{1,0:T(8,128)(2,1)}, f32[288,128]{1,0:T(8,128)}) custom-call(bf16[8,144,128]{2,1,0:T(8,128)(2,1)} %copy-done.5, bf16[288,1024]{1,0:T(8,128)(2,1)} %get-tuple-element.11.tok_ref, bf16[512,1024]{1,0:T(8,128)(2,1)} %w_out_ref.1, ...), custom_call_target="tpu_custom_call" | custom-call | flops 603979776 | bytes 4659456 | tf_op jit(solution)/shard_map/pallas_call | solution.py:253
  70.2 16.3 %all_to_all.35.q_ref.kv_ref = bf16[8,216,128]{2,1,0:T(8,128)(2,1)} all-to-all(bf16[8,216,128]{2,1,0:T(8,128)(2,1)} %get-tuple-element.13), channel_id=1, replica_groups=mesh['dp'=4,'ctx'=8] {'ctx'}, dimensions={0} | all-to-all | bytes 884736 | tf_op jit(solution)/shard_map/all_to_all | solution.py:265
  86.5 15.8 %shard_map.222 = bf16[8,72,128]{2,1,0:T(8,128)(2,1)} custom-call(bf16[8,216,128]{2,1,0:T(8,128)(2,1)} %all_to_all.35.q_ref.kv_ref, bf16[8,216,128]{2,1,0:T(8,128)(2,1)} %all_to_all.35.q_ref.kv_ref), custom_call_target="tpu_custom_call" | custom-call | flops 2717908992 | bytes 884736 | tf_op jit(solution)/shard_map/pallas_call | solution.py:253
  102.3 3.6 %all-to-all-start.3 = ((bf16[8,72,128]{2,1,0:T(8,128)(2,1)}), bf16[8,72,128]{2,1,0:T(8,128)(2,1)S(1)}, u32[]{:S(2)}, u32[]{:S(2)}) async-start(bf16[8,72,128]{2,1,0:T(8,128)(2,1)} %shard_map.222), calls=%async_computation.3 | async-start | bytes 294912 | tf_op jit(solution)/shard_map/all_to_all | solution.py:265
  106.1 7.1 %all-to-all-done.3 = bf16[8,72,128]{2,1,0:T(8,128)(2,1)S(1)} async-done(((bf16[8,72,128]{2,1,0:T(8,128)(2,1)}), bf16[8,72,128]{2,1,0:T(8,128)(2,1)S(1)}, u32[]{:S(2)}, u32[]{:S(2)}) %all-to-all-start.3) | async-done | bytes 147488 | tf_op jit(solution)/shard_map/all_to_all | solution.py:265
  114.4 0.8 fusion.12
  115.2 0.7 copy-done.16
  115.9 1.0 fusion.37
  118.2 2.0 multiply_reduce_fusion
  120.2 1.4 fusion.32
  121.6 1.8 convolution_convert_fusion
  124.1 2.0 multiply_convert_fusion.3
  126.1 5.8 %fusion.31 = (f32[288]{0:T(512)S(1)}, f32[288]{0:T(512)S(1)}, f32[288,512]{1,0:T(8,128)}) fusion(f32[288]{0:T(512)S(1)} %add_rsqrt_fusion.1, f32[288,512]{1,0:T(8,128)S(1)} %get-tuple-element.34, f32[288]{0:T(512)S(1)} %broadcast_multiply_fusion.5, f32[512]{0:T(512)S(1)} %convert_element_type.71, bf16[512,2048]{1,0:T(8,128)(2,1)S(1)} %copy-done, ...), kind=kOutput, calls=%fused_computation.74 | convolution fusion | flops 1220640256 | bytes 8034816 | tf_op jit(solution)/shard_map/dot_general | solution.py:45
  131.8 1.5 convolution_convert_fusion.1
  133.4 0.7 pad_maximum_fusion.3
  134.2 5.0 %concatenate.17 = bf16[672,1024]{1,0:T(8,128)(2,1)S(1)} concatenate(bf16[512,1024]{1,0:T(8,128)(2,1)} %convolution_convert_fusion, bf16[128,1024]{1,0:T(8,128)(2,1)} %pad_maximum_fusion.3, bf16[1,1024]{1,0:T(2,128)(2,1)S(1)} %broadcast_in_dim.8, bf16[1,1024]{1,0:T(2,128)(2,1)S(1)} %broadcast_in_dim.9, bf16[30,1024]{1,0:T(8,128)(2,1)S(1)} %broadcast_in_dim.10), dimensions={0} | concatenate | bytes 2752512 | tf_op jit(solution)/shard_map/concatenate | solution.py:427
  139.2 0.9 constant_dynamic-slice_fusion.1
  140.1 2.5 %collective-permute-done = bf16[336,1024]{1,0:T(8,128)(2,1)} collective-permute-done((bf16[336,1024]{1,0:T(8,128)(2,1)}, bf16[336,1024]{1,0:T(8,128)(2,1)}, u32[]{:S(2)}, u32[]{:S(2)}) %collective-permute-start) | collective-permute-done | bytes 688160 | tf_op jit(solution)/shard_map/ppermute | solution.py:281
  142.6 1.3 dynamic-slice_add_fusion
  144.0 0.8 copy-done.3
  144.8 1.6 collective-permute-start.1
  146.4 8.6 %collective-permute-done.1 = bf16[168,1024]{1,0:T(8,128)(2,1)S(1)} collective-permute-done((bf16[168,1024]{1,0:T(8,128)(2,1)S(1)}, bf16[168,1024]{1,0:T(8,128)(2,1)S(1)}, u32[]{:S(2)}, u32[]{:S(2)}) %collective-permute-start.1) | collective-permute-done | bytes 344096 | tf_op jit(solution)/shard_map/ppermute | solution.py:281
  155.0 1.1 dynamic-slice_add_fusion.1
  156.2 14.2 %all_to_all.36 = bf16[8,21,1024]{2,1,0:T(8,128)(2,1)S(1)} all-to-all(bf16[8,21,1024]{2,1,0:T(8,128)(2,1)S(1)} %reshape.98), channel_id=1, replica_groups=mesh['dp'=4,'ctx'=8] {'ctx'}, dimensions={0} | all-to-all | bytes 688128 | tf_op jit(solution)/shard_map/all_to_all | solution.py:265
  170.6 14.7 %all_to_all.37 = bf16[8,21,1024]{2,1,0:T(8,128)(2,1)S(1)} all-to-all(bf16[8,21,1024]{2,1,0:T(8,128)(2,1)S(1)} %broadcast_in_dim.11), channel_id=1, replica_groups=mesh['dp'=4,'ctx'=8] {'ctx'}, dimensions={0} | all-to-all | bytes 688128 | tf_op jit(solution)/shard_map/all_to_all | solution.py:265
  185.4 1.6 collective-permute-start.2
  187.0 2.0 reshape.96
  189.0 3.5 %all-to-all-start.4 = ((bf16[8,36,1024]{2,1,0:T(8,128)(2,1)}), bf16[8,36,1024]{2,1,0:T(8,128)(2,1)S(1)}, u32[]{:S(2)}, u32[]{:S(2)}) async-start(bf16[8,36,1024]{2,1,0:T(8,128)(2,1)} %reshape.96), calls=%async_computation.4 | async-start | bytes 1310720 | tf_op jit(solution)/shard_map/all_to_all | solution.py:265
  193.0 1.1 broadcast_select_fusion.3
  194.1 0.9 pad_maximum_fusion.1
  195.0 13.8 %all-to-all-done.4 = bf16[8,36,1024]{2,1,0:T(8,128)(2,1)S(1)} async-done(((bf16[8,36,1024]{2,1,0:T(8,128)(2,1)}), bf16[8,36,1024]{2,1,0:T(8,128)(2,1)S(1)}, u32[]{:S(2)}, u32[]{:S(2)}) %all-to-all-start.4) | async-done | bytes 589856 | tf_op jit(solution)/shard_map/all_to_all | solution.py:265
  208.8 0.9 reshape.97
  209.7 1.4 broadcast_select_fusion.1
  211.2 0.5 fusion.33
  211.8 1.6 fusion.11
  214.6 0.8 pad_maximum_fusion.2
  (63 shorter events, 3.5 us)
Async XLA Ops:
  0.6 113.7 %copy-start = (bf16[512,2048]{1,0:T(8,128)(2,1)S(1)}, bf16[512,2048]{1,0:T(8,128)(2,1)}, u32[]{:S(2)}) copy-start(bf16[512,2048]{1,0:T(8,128)(2,1)} %param.35) | copy-start | bytes 6291460
  11.9 42.1 %copy-start.11 = (bf16[1024]{0:T(1024)(128)(2,1)S(1)}, bf16[1024]{0:T(1024)(128)(2,1)}, u32[]{:S(2)}) copy-start(bf16[1024]{0:T(1024)(128)(2,1)} %param.27) | copy-start | bytes 6148
  11.9 42.7 %copy-start.12 = (bf16[512]{0:T(512)(128)(2,1)S(1)}, bf16[512]{0:T(512)(128)(2,1)}, u32[]{:S(2)}) copy-start(bf16[512]{0:T(512)(128)(2,1)} %param.29) | copy-start | bytes 3076
  11.9 43.3 %copy-start.13 = (bf16[512]{0:T(512)(128)(2,1)S(1)}, bf16[512]{0:T(512)(128)(2,1)}, u32[]{:S(2)}) copy-start(bf16[512]{0:T(512)(128)(2,1)} %param.31) | copy-start | bytes 3076
  11.9 30.5 %all-to-all-start = ((bf16[8,448,128]{2,1,0:T(8,128)(2,1)}), bf16[8,448,128]{2,1,0:T(8,128)(2,1)S(1)}, u32[]{:S(2)}, u32[]{:S(2)}) async-start(bf16[8,448,128]{2,1,0:T(8,128)(2,1)} %get-tuple-element.10), calls=%async_computation | async-start | bytes 1835008 | tf_op jit(solution)/shard_map/all_to_all | solution.py:265
  42.4 0.9 copy-start.1
  50.5 13.3 %all-to-all-start.1 = ((bf16[8,144,128]{2,1,0:T(8,128)(2,1)}), bf16[8,144,128]{2,1,0:T(8,128)(2,1)S(1)}, u32[]{:S(2)}, u32[]{:S(2)}) async-start(bf16[8,144,128]{2,1,0:T(8,128)(2,1)} %shard_map.220), calls=%async_computation.1 | async-start | bytes 589824 | tf_op jit(solution)/shard_map/all_to_all | solution.py:265
  63.7 0.7 copy-start.5
  86.5 19.4 %copy-start.14 = (bf16[512]{0:T(512)(128)(2,1)S(1)}, bf16[512]{0:T(512)(128)(2,1)}, u32[]{:S(2)}) copy-start(bf16[512]{0:T(512)(128)(2,1)} %param.34) | copy-start | bytes 3076
  86.5 19.4 %copy-start.15 = (bf16[512]{0:T(512)(128)(2,1)S(1)}, bf16[512]{0:T(512)(128)(2,1)}, u32[]{:S(2)}) copy-start(bf16[512]{0:T(512)(128)(2,1)} %param.37) | copy-start | bytes 3076
  86.5 19.4 %copy-start.10 = (f32[288,128]{1,0:T(8,128)S(1)}, f32[288,128]{1,0:T(8,128)}, u32[]{:S(2)}) copy-start(f32[288,128]{1,0:T(8,128)} %get-tuple-element.15) | copy-start | bytes 442372
  86.5 27.2 %copy-start.8 = (bf16[288,512]{1,0:T(8,128)(2,1)S(1)}, bf16[288,512]{1,0:T(8,128)(2,1)}, u32[]{:S(2)}) copy-start(bf16[288,512]{1,0:T(8,128)(2,1)} %get-tuple-element.12) | copy-start | bytes 884740
  86.5 27.2 %copy-start.9 = (bf16[256,512]{1,0:T(8,128)(2,1)S(1)}, bf16[256,512]{1,0:T(8,128)(2,1)}, u32[]{:S(2)}) copy-start(bf16[256,512]{1,0:T(8,128)(2,1)} %param.33) | copy-start | bytes 786436
  102.3 10.9 %all-to-all-start.3 = ((bf16[8,72,128]{2,1,0:T(8,128)(2,1)}), bf16[8,72,128]{2,1,0:T(8,128)(2,1)S(1)}, u32[]{:S(2)}, u32[]{:S(2)}) async-start(bf16[8,72,128]{2,1,0:T(8,128)(2,1)} %shard_map.222), calls=%async_computation.3 | async-start | bytes 294912 | tf_op jit(solution)/shard_map/all_to_all | solution.py:265
  114.3 1.6 copy-start.16
  115.9 1.4 copy-start.2
  115.9 2.0 copy-start.7
  115.9 2.2 %copy-start.17 = (bf16[288,1024]{1,0:T(8,128)(2,1)S(1)}, bf16[288,1024]{1,0:T(8,128)(2,1)}, u32[]{:S(2)}) copy-start(bf16[288,1024]{1,0:T(8,128)(2,1)} %get-tuple-element.14) | copy-start | bytes 1769476
  126.1 5.8 %copy-start.6 = (bf16[288,512]{1,0:T(8,128)(2,1)S(1)}, bf16[288,512]{1,0:T(8,128)(2,1)}, u32[]{:S(2)}) copy-start(bf16[288,512]{1,0:T(8,128)(2,1)} %multiply_convert_fusion.3) | copy-start | bytes 884740
  140.1 2.5 %collective-permute-start = (bf16[336,1024]{1,0:T(8,128)(2,1)}, bf16[336,1024]{1,0:T(8,128)(2,1)}, u32[]{:S(2)}, u32[]{:S(2)}) collective-permute-start(bf16[336,1024]{1,0:T(8,128)(2,1)} %constant_dynamic-slice_fusion.1), channel_id=1, source_target_pairs={{0,8},{8,0},{16,24},{24,16},{1,9},{9,1},{17,25},{25,17},{2,10},{10... | collective-permute-start | bytes 2064392 | tf_op jit(solution)/shard_map/ppermute | solution.py:281
  143.9 0.8 copy-start.3
  144.8 10.2 %collective-permute-start.1 = (bf16[168,1024]{1,0:T(8,128)(2,1)S(1)}, bf16[168,1024]{1,0:T(8,128)(2,1)S(1)}, u32[]{:S(2)}, u32[]{:S(2)}) collective-permute-start(bf16[168,1024]{1,0:T(8,128)(2,1)S(1)} %constant_dynamic-slice_fusion), channel_id=1, source_target_pairs={{0,16},{8,24},{16,0},{24,8},{1,17},{9,25},{17,1},{25,9},{2,18},{10... | collective-permute-start | bytes 1032200 | tf_op jit(solution)/shard_map/ppermute | solution.py:281
  185.4 7.2 %copy-start.4 = (bf16[168,1024]{1,0:T(8,128)(2,1)}, bf16[168,1024]{1,0:T(8,128)(2,1)S(1)}, u32[]{:S(2)}) copy-start(bf16[168,1024]{1,0:T(8,128)(2,1)S(1)} %reshape.99) | copy-start | bytes 1032196
  185.4 7.6 %collective-permute-start.2 = (bf16[168,1024]{1,0:T(8,128)(2,1)S(1)}, bf16[168,1024]{1,0:T(8,128)(2,1)}, u32[]{:S(2)}, u32[]{:S(2)}) collective-permute-start(bf16[168,1024]{1,0:T(8,128)(2,1)S(1)} %reshape.99), channel_id=1, source_target_pairs={{0,16},{8,24},{16,0},{24,8},{1,17},{9,25},{17,1},{25,9},{2,18},{10... | collective-permute-start | bytes 1032200 | tf_op jit(solution)/shard_map/ppermute | solution.py:289
  189.0 19.8 %all-to-all-start.4 = ((bf16[8,36,1024]{2,1,0:T(8,128)(2,1)}), bf16[8,36,1024]{2,1,0:T(8,128)(2,1)S(1)}, u32[]{:S(2)}, u32[]{:S(2)}) async-start(bf16[8,36,1024]{2,1,0:T(8,128)(2,1)} %reshape.96), calls=%async_computation.4 | async-start | bytes 1310720 | tf_op jit(solution)/shard_map/all_to_all | solution.py:265
  195.0 14.7 %collective-permute-start.3 = (bf16[336,1024]{1,0:T(8,128)(2,1)}, bf16[336,1024]{1,0:T(8,128)(2,1)}, u32[]{:S(2)}, u32[]{:S(2)}) collective-permute-start(bf16[336,1024]{1,0:T(8,128)(2,1)} %pad_maximum_fusion.1), channel_id=1, source_target_pairs={{0,8},{8,0},{16,24},{24,16},{1,9},{9,1},{17,25},{25,17},{2,10},{10... | collective-permute-start | bytes 2064392 | tf_op jit(solution)/shard_map/ppermute | solution.py:289

commit v2 on v1

--- a/solution.py
+++ b/solution.py
@@ -244,6 +244,149 @@
         out_ref[source] = out.astype(BF)
 
 
+def tail_kernel(
+    att_ref, y_ref, w_out_ref, feed_gain_ref, w_up_ref, w_down_ref, head_gain_ref, w_head_ref,
+    target_ref, flag_ref,
+    pred_ref, dec_att_ref, mid_ref, slope_ref, z_ref, zn_ref, dpred_ref, loss_ref, feed_buf, wide_buf,
+):
+    rows, width = y_ref.shape
+    quarter = rows // 4
+    pixels = w_head_ref.shape[1]
+    hidden = w_up_ref.shape[1]
+    blocks = [att_ref[head].astype(F32) for head in range(HEADS)]
+    dec_att_ref[...] = jnp.concatenate(
+        [
+            jnp.concatenate([b[:, 32 * i : 32 * i + 32] for b in blocks], axis=1)
+            for i in range(4)
+        ],
+        axis=0,
+    ).astype(BF)
+    mid_ref[...] = y_ref[...].astype(F32) + dot(dec_att_ref[...], w_out_ref[...])
+    feed_buf[...] = layer_norm(mid_ref[...], feed_gain_ref[...]).astype(BF)
+    z_ref[...] = mid_ref[...]
+    tile = 512
+    c = math.sqrt(2.0 / math.pi)
+
+    @pl.loop(0, hidden // tile)
+    def _(step):
+        cols = pl.ds(pl.multiple_of(step * tile, tile), tile)
+        pre = dot(feed_buf[...], w_up_ref[:, cols])
+        square = pre * pre
+        t = jnp.tanh(pre * (c + (c * 0.044715) * square))
+        gate = 0.5 + 0.5 * t
+        slope = gate + (0.5 * pre) * (1.0 - t * t) * (c + (3 * c * 0.044715) * square)
+        slope_ref[:, cols] = slope.astype(BF)
+        z_ref[...] += dot((pre * gate).astype(BF), w_down_ref[cols, :])
+
+    zn_ref[...] = layer_norm(z_ref[...], head_gain_ref[...]).astype(BF)
+    flag = flag_ref[:, :1]
+    loss_ref[...] = jnp.zeros_like(loss_ref)
+
+    @pl.loop(0, pixels // tile)
+    def _(step):
+        cols = pl.ds(pl.multiple_of(step * tile, tile), tile)
+        pred = dot(zn_ref[...], w_head_ref[:, cols])
+        wide_buf[:, cols] = pred
+        err = (pred - target_ref[:, cols].astype(F32)) * flag
+        dpred_ref[:, cols] = (err * (2.0 / pixels)).astype(BF)
+        part = jnp.sum(jnp.sum(err * err, axis=1, keepdims=True), axis=0, keepdims=True)
+        loss_ref[...] += part * (1.0 / pixels)
+
+    share = pred_ref.shape[1]
+    for dest in range(pred_ref.shape[0]):
+        pred_ref[dest] = wide_buf[dest * share : (dest + 1) * share, :].astype(BF)
+
+
+def backward_kernel(
+    me_ref, dec_att_ref, mid_ref, slope_ref, z_ref, zn_ref, dpred_ref, loss_ref,
+    feed_gain_ref, w_up_ref, w_down_ref, head_gain_ref, w_head_ref,
+    keep_ref, send_ref, back_buf, head_buf, out_buf,
+):
+    hidden = w_up_ref.shape[1]
+    width, pixels = w_head_ref.shape
+    dz = norm_backward(
+        z_ref[...], head_gain_ref[...], dot_t(dpred_ref[...], w_head_ref[...])
+    ).astype(BF)
+    back_buf[...] = jnp.zeros_like(back_buf)
+    tile = 512
+
+    @pl.loop(0, hidden // tile)
+    def _(step):
+        cols = pl.ds(pl.multiple_of(step * tile, tile), tile)
+        back = dot_t(dz, w_down_ref[cols, :]) * slope_ref[:, cols].astype(F32)
+        back_buf[...] += dot_t(back.astype(BF), w_up_ref[:, cols])
+
+    mid_grad = (
+        dz.astype(F32) + norm_backward(mid_ref[...], feed_gain_ref[...], back_buf[...])
+    ).astype(BF)
+    first = (((0,), (0,)), ((), ()))
+    out_buf[...] = lax.dot_general(
+        dec_att_ref[...], mid_grad, first, preferred_element_type=F32
+    )
+
+    @pl.loop(0, pixels // tile)
+    def _(step):
+        cols = pl.ds(pl.multiple_of(step * tile, tile), tile)
+        head_buf[:, cols] = lax.dot_general(
+            zn_ref[...], dpred_ref[:, cols], first, preferred_element_type=F32
+        )
+
+    loss = jnp.broadcast_to(loss_ref[:1, :], (8, 128))
+    high = loss.astype(BF)
+    low = (loss - high.astype(F32)).astype(BF)
+    sums = jnp.concatenate([high.astype(F32), low.astype(F32)], axis=0).astype(BF)
+    deep = out_buf.shape[0] // 32
+    half = out_buf.shape[1] // 2
+    tall = width // 32
+    for index in range(32):
+        block = index ^ me_ref[0]
+        ref = send_ref if index % 2 else keep_ref
+        xy, z = index // 2 % 4, index // 8
+        ref[xy, z, :, :pixels] = head_buf[
+            pl.ds(pl.multiple_of(block * tall, tall), tall), :
+        ].astype(BF)
+        part = out_buf[pl.ds(pl.multiple_of(block * deep, deep), deep), :]
+        ref[xy, z, :, pixels : pixels + half] = jnp.concatenate(
+            [part[:, :half], part[:, half:]], axis=0
+        ).astype(BF)
+        ref[xy, z, :, pixels + half :] = sums
+
+
+def add_kernel(*refs, count):
+    total = refs[0][...].astype(F32)
+    for ref in refs[1:count]:
+        total = total + ref[...].astype(F32)
+    total = total.astype(BF)
+    outs = refs[count:]
+    if len(outs) == 1:
+        outs[0][...] = total
+    else:
+        for i, ref in enumerate(outs):
+            ref[...] = total[i]
+
+
+def join_kernel(*refs):
+    for i, ref in enumerate(refs[:-1]):
+        refs[-1][i] = ref[...]
+
+
+def place_kernel(me_ref, *refs):
+    blocks, (head_ref, out_ref, loss_ref) = refs[:8], refs[8:]
+    pixels = head_ref.shape[1]
+    deep = out_ref.shape[0] // 32
+    half = out_ref.shape[1] // 2
+    tall = head_ref.shape[0] // 32
+    for index in range(32):
+        block = index ^ me_ref[0]
+        value = blocks[index % 2 * 4 + index // 2 % 4][index // 8].astype(F32)
+        head_ref[pl.ds(pl.multiple_of(block * tall, tall), tall), :] = value[:, :pixels]
+        at = pl.ds(pl.multiple_of(block * deep, deep), deep)
+        out_ref[at, :half] = value[:deep, pixels : pixels + half]
+        out_ref[at, half:] = value[deep:, pixels : pixels + half]
+    value = blocks[0][0].astype(F32)
+    loss_ref[...] = value[:8, pixels + half :] + value[8:, pixels + half :]
+
+
 def vmem_call(kernel, outs, scratch, inputs, smem=(), flops=0):
     space = [
         pl.BlockSpec(memory_space=pltpu.SMEM if i in smem else pltpu.VMEM)
@@ -291,6 +434,49 @@
         high = jnp.where(upper == 0, other, x)
         x = jnp.concatenate([low, high], axis=0)
     return x
+
+
+def across(x, dp_bit, ctx_bits):
+    count, groups = lax.axis_size("dp"), lax.axis_size("ctx")
+    pairs = [
+        (i * groups + j, (i ^ dp_bit) * groups + (j ^ ctx_bits))
+        for i in range(count)
+        for j in range(groups)
+    ]
+    return lax.ppermute(x, ("dp", "ctx"), pairs)
+
+
+PLANE = ((2, 0), (0, 1), (2, 1))
+COLUMN = ((0, 2), (0, 4), (0, 6))
+
+
+def sum_by_permutes(keep, send):
+    shape = jax.ShapeDtypeStruct
+    add = lambda parts, outs: vmem_call(
+        functools.partial(add_kernel, count=len(parts)), outs, [], parts
+    )
+    part, block = shape(keep.shape[1:], BF), shape(keep.shape[2:], BF)
+    parts = add([keep, across(send, 1, 0)], [part] * 4)
+    others = [across(p, *bits) for p, bits in zip(parts[1:], PLANE)]
+    blocks = add([parts[0], *others], [block] * 4)
+    others = [across(b, *bits) for b, bits in zip(blocks[1:], COLUMN)]
+    (total,) = add([blocks[0], *others], [block])
+    (column,) = vmem_call(
+        join_kernel, [part], [], [total] + [across(total, *bits) for bits in COLUMN]
+    )
+    ours = [column] + [across(column, *bits) for bits in PLANE]
+    return ours, [across(x, 1, 0) for x in ours]
+
+
+def sum_by_blocks(keep, send, groups):
+    size = keep.shape[0] * keep.shape[1] * keep.shape[2]
+    flat = jnp.concatenate([keep.reshape(size, -1), send.reshape(size, -1)], axis=0)
+    unit = lax.axis_size("dp") * groups
+    used = flat.shape[0]
+    padded = -(-used // unit) * unit
+    total = all_sum(jnp.pad(flat, ((0, padded - used), (0, 0))), groups)[:used]
+    total = total.reshape(2, *keep.shape)
+    return [total[0, i] for i in range(4)], [total[1, i] for i in range(4)]
 
 
 def on_device(
@@ -394,51 +580,61 @@
         flops=4 * HEADS * rows * groups * rows * 128,
     )
     att = swap(att, "ctx", teams)
-    dec_att = (
-        att.reshape(HEADS, quarter, 4, 32).transpose(2, 1, 0, 3).reshape(rows, w_dec_out.shape[0])
-    )
-    y_mid = y_own.astype(F32) + dot(dec_att, w_dec_out)
-    feed = layer_norm(y_mid, decoder_feed_gain).astype(BF)
-    pre_act = dot(feed, w_up)
-    act = jax.nn.gelu(pre_act).astype(BF)
-    z = y_mid + dot(act, w_down)
-    zn = layer_norm(z, head_gain).astype(BF)
-    pred = dot(zn, w_head)
-    err = (pred - target.astype(F32)) * flag[:, :1]
-    reconstruction = swap(pred.astype(BF).reshape(groups, rows // groups, pixels), "ctx")
-    loss_part = jnp.sum(err * err) / pixels
-    dpred = (err * (2.0 / pixels)).astype(BF)
-    head_part = dot(zn.T, dpred)
-    upstream = dot_t(dpred, w_head)
-    dz = norm_backward(z, head_gain, upstream).astype(BF)
-    back_act = dot_t(dz, w_down)
-    gelu_back = jax.vjp(jax.nn.gelu, pre_act)[1]
-    pre_grad = gelu_back(back_act)[0].astype(BF)
-    back_feed = dot_t(pre_grad, w_up)
-    mid_grad = (dz.astype(F32) + norm_backward(y_mid, decoder_feed_gain, back_feed)).astype(BF)
-    out_part = dot(dec_att.T, mid_grad)
-
-    depth = out_part.shape[0] // 2
-    loss_high = loss_part.astype(BF)
-    loss_low = (loss_part - loss_high.astype(F32)).astype(BF)
-    used = dec_width + depth + 2
-    unit = lax.axis_size("dp") * groups
-    padded = -(-used // unit) * unit
-    stacked = jnp.concatenate(
-        [
-            head_part.astype(BF),
-            jnp.concatenate([out_part[:depth], out_part[depth:]], axis=1).astype(BF),
-            jnp.broadcast_to(loss_high, (1, pixels)),
-            jnp.broadcast_to(loss_low, (1, pixels)),
-            jnp.zeros((padded - used, pixels), BF),
-        ],
-        axis=0,
-    )
-    total = all_sum(stacked, groups)
-    grad_head = total[:dec_width].astype(F32)
-    tail = total[dec_width : dec_width + depth].astype(F32)
-    grad_dec_out = jnp.concatenate([tail[:, :dec_width], tail[:, dec_width:]], axis=0)
-    loss = total[used - 2, 0].astype(F32) + total[used - 1, 0].astype(F32)
+    hidden = w_up.shape[1]
+    pred, dec_att, y_mid, slope, z, zn, dpred, loss_part = vmem_call(
+        tail_kernel,
+        [
+            shape((groups, rows // groups, pixels), BF),
+            shape((rows, w_dec_out.shape[0]), BF),
+            shape((rows, dec_width), F32),
+            shape((rows, hidden), BF),
+            shape((rows, dec_width), F32),
+            shape((rows, dec_width), BF),
+            shape((rows, pixels), BF),
+            shape((8, 128), F32),
+        ],
+        [pltpu.VMEM((rows, dec_width), BF), pltpu.VMEM((rows, pixels), F32)],
+        [
+            att, y_own, w_dec_out, row(decoder_feed_gain), w_up, w_down, row(head_gain), w_head,
+            target, flag,
+        ],
+        flops=2 * rows * dec_width * (2 * hidden + pixels),
+    )
+    reconstruction = swap(pred, "ctx")
+    dp_me, ctx_me = lax.axis_index("dp"), lax.axis_index("ctx")
+    if repeat == 1:
+        me = dp_me % 2 + 2 * (dp_me // 2) + 4 * (ctx_me % 2) + 8 * (ctx_me // 2)
+    else:
+        me = jnp.int32(0)
+    me = me.astype(jnp.int32).reshape(1)
+    wide = pixels + dec_width // 2 + 128
+    keep, send = vmem_call(
+        backward_kernel,
+        [shape((4, 4, dec_width // 32, wide), BF)] * 2,
+        [
+            pltpu.VMEM((rows, dec_width), F32),
+            pltpu.VMEM((dec_width, pixels), F32),
+            pltpu.VMEM((w_dec_out.shape[0], dec_width), F32),
+        ],
+        [
+            me, dec_att, y_mid, slope, z, zn, dpred, loss_part, row(decoder_feed_gain),
+            w_up, w_down, row(head_gain), w_head,
+        ],
+        smem=(0,),
+        flops=2 * rows * dec_width * (2 * hidden + 2 * pixels),
+    )
+    if repeat == 1:
+        ours, theirs = sum_by_permutes(keep, send)
+    else:
+        ours, theirs = sum_by_blocks(keep, send, groups)
+    grad_head, grad_dec_out, loss = vmem_call(
+        place_kernel,
+        [shape(w_head.shape, F32), shape(w_dec_out.shape, F32), shape((8, 128), F32)],
+        [],
+        [me, *ours, *theirs],
+        smem=(0,),
+    )
+    loss = loss[0, 0]
     masked_total = lax.axis_size("dp") * (groups * rows - share * groups)
     return (reconstruction.reshape(1, rows, pixels), grad_head, grad_dec_out, loss / masked_total)
 

time: 218 us -> 198 us (0.908)
  blocking collectives: 45.2 us -> 16.3 us
  Pallas kernels: 38.5 us -> 67.2 us
  matrix products: 14.7 us -> 0 us
  starting transfers between devices: 21.2 us -> 34.3 us
  other arithmetic: 11.6 us -> 0 us
  local copies, waits for them, and re-layouts: 17.8 us -> 13.3 us
    all_to_all x3 -> x1, blocking collectives: 45.2 us -> 16.3 us  [swap(): lax.all_to_all(x, axis, split_axis=0, concat_axis=0, tiled=True, axis_ind...]
    pallas_call x4 -> x11, Pallas kernels: 38.5 us -> 67.2 us  [vmem_call(): pl.pallas_call(kernel, out_shape=outs, in_specs=space, out_specs=[pl.Bloc...]
    dot_general x8 -> x0, matrix products: 14.7 us -> none  [the longest x6 7.58 us: dot(): return jnp.dot(a, b, preferred_element_type=F32)]
    all_to_all x4, waiting for transfers between devices: 51.9 us -> 37.3 us  [swap(): lax.all_to_all(x, axis, split_axis=0, concat_axis=0, tiled=True, axis_ind...]
    ppermute x4 -> x17, waiting for transfers between devices: 11.5 us -> 25.7 us  [across(): return lax.ppermute(x, ('dp', 'ctx'), pairs)]
    ppermute x4 -> x17, starting transfers between devices: 3.13 us -> 16.4 us  [across(): return lax.ppermute(x, ('dp', 'ctx'), pairs)]
    concatenate x1 -> x0, local copies, waits for them, and re-layouts: 5.02 us -> none  [on_device(): jnp.concatenate([head_part.astype(BF), jnp.concatenate([out_part[:depth],...]
    convert_element_type x5 -> x0, other arithmetic: 3.62 us -> none  [the longest x1 2.01 us: on_device(): dz = norm_backward(z, head_gain, upstream).astype(BF)]
  transfers between devices with their start and end apart: 8 -> 21, of which waited for: 7 -> 12; matrix products, arithmetic and copies ran while one was open for 3% -> 2% of each run, Pallas kernels for 0% -> 4%
where the time goes in v2:
time: 198 us; the launch traced here: 197 us
  Pallas kernels  67.2 us (34%)
  waiting for transfers between devices  63 us (32%)
  starting transfers between devices  34.3 us (17%)
  blocking collectives  16.3 us (8%)
  local copies, waits for them, and re-layouts  13.3 us (7%)
  between operations  2.56 us (1%)
    pallas_call x11, Pallas kernels, vmem_call(): pl.pallas_call(kernel, out_shape=outs, in_specs=space, out_specs=[pl.Bloc...  67.2 us
    all_to_all x4, waiting for transfers between devices, swap(): lax.all_to_all(x, axis, split_axis=0, concat_axis=0, tiled=True, axis_ind...  37.3 us
    ppermute x17, waiting for transfers between devices, across(): return lax.ppermute(x, ('dp', 'ctx'), pairs)  25.7 us
    all_to_all x4, starting transfers between devices, swap(): lax.all_to_all(x, axis, split_axis=0, concat_axis=0, tiled=True, axis_ind...  17.9 us
    ppermute x17, starting transfers between devices, across(): return lax.ppermute(x, ('dp', 'ctx'), pairs)  16.4 us
    all_to_all x1, blocking collectives, swap(): lax.all_to_all(x, axis, split_axis=0, concat_axis=0, tiled=True, axis_ind...  16.3 us
    unnamed x50, local copies, waits for them, and re-layouts  7.03 us
    reshape x6, local copies, waits for them, and re-layouts, on_device(): row = lambda vector: vector.reshape(1, -1)  4.21 us
  transfers between devices with their start and end apart: 21, of which 12 were waited for; matrix products, arithmetic and copies ran while one was open for 2% of the time, Pallas kernels for 4%

profile of v2, /device:TPU:0, one launch (start us, length us, event | category | flops | bytes accessed | tf_op | source)
XLA Modules:
  0.0 196.7 jit_solution(1378985675687320342)
XLA Ops:
  0.6 1.3 reshape.40.gain_ref
  1.9 9.8 %shard_map.219 = (bf16[8,448,128]{2,1,0:T(8,128)(2,1)}, bf16[288,1024]{1,0:T(8,128)(2,1)}) custom-call(bf16[288,1024]{1,0:T(8,128)(2,1)} %bitcast.4, bf16[288,1024]{1,0:T(8,128)(2,1)} %pos_ref.2, bf16[1024,1024]{1,0:T(8,128)(2,1)} %w_embed_ref.1, bf16[1,1024]{1,0:T(2,128)(2,1)} %reshape.40.gain_ref, bf16[1024,1536]{1,0:T(8,128)(2,1)} %w_qkv_ref.2, ...), custom_call_target="tpu_custom_call" | custom-call | flops 1509949440 | bytes 6425728 | tf_op jit(solution)/shard_map/pallas_call | solution.py:396
  11.8 7.4 %all-to-all-start = ((bf16[8,448,128]{2,1,0:T(8,128)(2,1)}), bf16[8,448,128]{2,1,0:T(8,128)(2,1)S(1)}, u32[]{:S(2)}, u32[]{:S(2)}) async-start(bf16[8,448,128]{2,1,0:T(8,128)(2,1)} %get-tuple-element.31), calls=%async_computation | async-start | bytes 1835008 | tf_op jit(solution)/shard_map/all_to_all | solution.py:408
  19.2 23.0 %all-to-all-done.q_ref.kv_ref = bf16[8,448,128]{2,1,0:T(8,128)(2,1)S(1)} async-done(((bf16[8,448,128]{2,1,0:T(8,128)(2,1)}), bf16[8,448,128]{2,1,0:T(8,128)(2,1)S(1)}, u32[]{:S(2)}, u32[]{:S(2)}) %all-to-all-start) | async-done | bytes 917536 | tf_op jit(solution)/shard_map/all_to_all | solution.py:408
  42.2 0.9 copy-done
  43.1 7.2 %shard_map.220 = bf16[8,144,128]{2,1,0:T(8,128)(2,1)} custom-call(s32[1]{0:T(128)} %bitcast.first_ref, bf16[8,448,128]{2,1,0:T(8,128)(2,1)} %copy-done, bf16[8,448,128]{2,1,0:T(8,128)(2,1)} %copy-done), custom_call_target="tpu_custom_call" | custom-call | flops 411041792 | bytes 1835012 | tf_op jit(solution)/shard_map/pallas_call | solution.py:396
  50.3 3.5 %all-to-all-start.1 = ((bf16[8,144,128]{2,1,0:T(8,128)(2,1)}), bf16[8,144,128]{2,1,0:T(8,128)(2,1)S(1)}, u32[]{:S(2)}, u32[]{:S(2)}) async-start(bf16[8,144,128]{2,1,0:T(8,128)(2,1)} %shard_map.220), calls=%async_computation.1 | async-start | bytes 589824 | tf_op jit(solution)/shard_map/all_to_all | solution.py:408
  54.4 0.6 reshape.43.gain_ref
  55.0 0.6 reshape.41.out_gain_ref
  55.6 8.0 %all-to-all-done.1.att_ref = bf16[8,144,128]{2,1,0:T(8,128)(2,1)S(1)} async-done(((bf16[8,144,128]{2,1,0:T(8,128)(2,1)}), bf16[8,144,128]{2,1,0:T(8,128)(2,1)S(1)}, u32[]{:S(2)}, u32[]{:S(2)}) %all-to-all-start.1) | async-done | bytes 294944 | tf_op jit(solution)/shard_map/all_to_all | solution.py:408
  63.6 0.7 copy-done.1
  64.3 5.7 %shard_map.221 = (bf16[8,216,128]{2,1,0:T(8,128)(2,1)}, bf16[288,512]{1,0:T(8,128)(2,1)}, bf16[288,1024]{1,0:T(8,128)(2,1)}, f32[288,128]{1,0:T(8,128)}) custom-call(bf16[8,144,128]{2,1,0:T(8,128)(2,1)} %copy-done.1, bf16[288,1024]{1,0:T(8,128)(2,1)} %get-tuple-element.32.tok_ref, bf16[512,1024]{1,0:T(8,128)(2,1)} %w_out_ref.2, ...), custom_call_target="tpu_custom_call" | custom-call | flops 603979776 | bytes 4659456 | tf_op jit(solution)/shard_map/pallas_call | solution.py:396
  70.0 16.3 %all_to_all.25.q_ref.kv_ref = bf16[8,216,128]{2,1,0:T(8,128)(2,1)} all-to-all(bf16[8,216,128]{2,1,0:T(8,128)(2,1)} %get-tuple-element.33), channel_id=1, replica_groups=mesh['dp'=4,'ctx'=8] {'ctx'}, dimensions={0} | all-to-all | bytes 884736 | tf_op jit(solution)/shard_map/all_to_all | solution.py:408
  86.3 15.8 %shard_map.222 = bf16[8,72,128]{2,1,0:T(8,128)(2,1)} custom-call(bf16[8,216,128]{2,1,0:T(8,128)(2,1)} %all_to_all.25.q_ref.kv_ref, bf16[8,216,128]{2,1,0:T(8,128)(2,1)} %all_to_all.25.q_ref.kv_ref), custom_call_target="tpu_custom_call" | custom-call | flops 2717908992 | bytes 884736 | tf_op jit(solution)/shard_map/pallas_call | solution.py:396
  102.1 3.4 %all-to-all-start.3 = ((bf16[8,72,128]{2,1,0:T(8,128)(2,1)}), bf16[8,72,128]{2,1,0:T(8,128)(2,1)S(1)}, u32[]{:S(2)}, u32[]{:S(2)}) async-start(bf16[8,72,128]{2,1,0:T(8,128)(2,1)} %shard_map.222), calls=%async_computation.3 | async-start | bytes 294912 | tf_op jit(solution)/shard_map/all_to_all | solution.py:408
  106.1 0.6 reshape.45.head_gain_ref
  106.7 6.3 %all-to-all-done.3.att_ref = bf16[8,72,128]{2,1,0:T(8,128)(2,1)S(1)} async-done(((bf16[8,72,128]{2,1,0:T(8,128)(2,1)}), bf16[8,72,128]{2,1,0:T(8,128)(2,1)S(1)}, u32[]{:S(2)}, u32[]{:S(2)}) %all-to-all-start.3) | async-done | bytes 147488 | tf_op jit(solution)/shard_map/all_to_all | solution.py:408
  112.9 0.6 copy-done.3
  113.6 9.2 %shard_map.223 = (bf16[8,36,1024]{2,1,0:T(8,128)(2,1)}, bf16[288,256]{1,0:T(8,128)(2,1)}, f32[288,512]{1,0:T(8,128)}, bf16[288,2048]{1,0:T(8,128)(2,1)}, f32[288...) custom-call(bf16[8,72,128]{2,1,0:T(8,128)(2,1)} %copy-done.3, ...), custom_call_target="tpu_custom_call" | custom-call | flops 1509949440 | bytes 6686720 | tf_op jit(solution)/shard_map/pallas_call | solution.py:396
  122.8 9.3 %shard_map.224 = (bf16[4,4,16,1408]{3,2,1,0:T(8,128)(2,1)}, bf16[4,4,16,1408]{3,2,1,0:T(8,128)(2,1)}) custom-call(s32[1]{0:T(128)} %bitcast.2.me_ref, bf16[288,256]{1,0:T(8,128)(2,1)} %get-tuple-element.38.dec_att_ref, f32[288,512]{1,0:T(8,128)} %get-tuple-element.39.mid_ref, bf16[288,2048]{1,0:T(8,128)(2,1)} %get-tuple-element.40.slope_ref, ...), custom_call_target="tpu_custom_call" | custom-call | flops 1811939328 | bytes 8640516 | tf_op jit(solution)/shard_map/pallas_call | solution.py:396
  132.1 3.5 %all-to-all-start.4 = ((bf16[8,36,1024]{2,1,0:T(8,128)(2,1)}), bf16[8,36,1024]{2,1,0:T(8,128)(2,1)S(1)}, u32[]{:S(2)}, u32[]{:S(2)}) async-start(bf16[8,36,1024]{2,1,0:T(8,128)(2,1)} %get-tuple-element.37), calls=%async_computation.4 | async-start | bytes 1310720 | tf_op jit(solution)/shard_map/all_to_all | solution.py:408
  135.7 0.8 copy-done.2
  136.5 2.2 %shard_map.225 = (bf16[4,16,1408]{2,1,0:T(8,128)(2,1)}, bf16[4,16,1408]{2,1,0:T(8,128)(2,1)}, bf16[4,16,1408]{2,1,0:T(8,128)(2,1)}, bf16[4,16,1408]{2,1,0:T(8,128)(2,1)}) custom-call(bf16[4,4,16,1408]{3,2,1,0:T(8,128)(2,1)} %get-tuple-element.45.refs_0_, bf16[4,4,16,1408]{3,2,1,0:T(8,128)(2,1)} %copy-done.2), custom_call_target="tpu_custom_call" | custom-call | bytes 1441792 | tf_op jit(solution)/shard_map/pallas_call | solution.py:396
  138.7 1.5 collective-permute-start.1
  140.2 1.9 collective-permute-start.2
  142.2 4.1 %collective-permute-done.1.refs_1_ = bf16[4,16,1408]{2,1,0:T(8,128)(2,1)S(1)} collective-permute-done((bf16[4,16,1408]{2,1,0:T(8,128)(2,1)}, bf16[4,16,1408]{2,1,0:T(8,128)(2,1)S(1)}, u32[]{:S(2)}, u32[]{:S(2)}) %collective-permute-start.1) | collective-permute-done | bytes 180256 | tf_op jit(solution)/shard_map/ppermute | solution.py:446
  146.3 8.2 %collective-permute-done.2.refs_2_ = bf16[4,16,1408]{2,1,0:T(8,128)(2,1)S(1)} collective-permute-done((bf16[4,16,1408]{2,1,0:T(8,128)(2,1)}, bf16[4,16,1408]{2,1,0:T(8,128)(2,1)S(1)}, u32[]{:S(2)}, u32[]{:S(2)}) %collective-permute-start.2) | collective-permute-done | bytes 180256 | tf_op jit(solution)/shard_map/ppermute | solution.py:446
  154.5 0.7 copy-done.12
  155.2 1.9 shard_map.226
  157.1 1.6 collective-permute-start.4
  158.8 2.9 %collective-permute-start.5 = (bf16[16,1408]{1,0:T(8,128)(2,1)}, bf16[16,1408]{1,0:T(8,128)(2,1)S(1)}, u32[]{:S(2)}, u32[]{:S(2)}) collective-permute-start(bf16[16,1408]{1,0:T(8,128)(2,1)} %get-tuple-element.53), channel_id=1, source_target_pairs={{0,4},{1,5},{2,6},{3,7},{4,0},{5,1},{6,2},{7,3},{8,12},{9,13},{10,... | collective-permute-start | bytes 135176 | tf_op jit(solution)/shard_map/ppermute | solution.py:446
  161.7 3.0 %collective-permute-done.5.refs_2_ = bf16[16,1408]{1,0:T(8,128)(2,1)S(1)} collective-permute-done((bf16[16,1408]{1,0:T(8,128)(2,1)}, bf16[16,1408]{1,0:T(8,128)(2,1)S(1)}, u32[]{:S(2)}, u32[]{:S(2)}) %collective-permute-start.5) | collective-permute-done | bytes 45088 | tf_op jit(solution)/shard_map/ppermute | solution.py:446
  164.7 3.0 %collective-permute-done.6.refs_3_ = bf16[16,1408]{1,0:T(8,128)(2,1)S(1)} collective-permute-done((bf16[16,1408]{1,0:T(8,128)(2,1)}, bf16[16,1408]{1,0:T(8,128)(2,1)S(1)}, u32[]{:S(2)}, u32[]{:S(2)}) %collective-permute-start.6) | collective-permute-done | bytes 45088 | tf_op jit(solution)/shard_map/ppermute | solution.py:446
  167.8 0.6 copy-done.16
  168.4 1.5 shard_map.227.refs_0_
  170.4 3.9 %collective-permute-start.7 = (bf16[16,1408]{1,0:T(8,128)(2,1)}, bf16[16,1408]{1,0:T(8,128)(2,1)S(1)}, u32[]{:S(2)}, u32[]{:S(2)}) collective-permute-start(bf16[16,1408]{1,0:T(8,128)(2,1)} %shard_map.227.refs_0_), channel_id=1, source_target_pairs={{0,2},{1,3},{2,0},{3,1},{4,6},{5,7},{6,4},{7,5},{8,10},{9,11},{10,... | collective-permute-start | bytes 135176 | tf_op jit(solution)/shard_map/ppermute | solution.py:446
  174.3 1.8 collective-permute-done.9.refs_3_
  177.1 0.6 copy-done.19
  177.7 1.5 shard_map.228.refs_0_
  179.3 0.8 collective-permute-start.12
  180.1 1.5 collective-permute-start.11
  181.6 1.2 collective-permute-start.10
  182.8 3.4 %collective-permute-done.12.refs_3_ = bf16[4,16,1408]{2,1,0:T(8,128)(2,1)S(1)} collective-permute-done((bf16[4,16,1408]{2,1,0:T(8,128)(2,1)}, bf16[4,16,1408]{2,1,0:T(8,128)(2,1)S(1)}, u32[]{:S(2)}, u32[]{:S(2)}) %collective-permute-start.12) | collective-permute-done | bytes 180256 | tf_op jit(solution)/shard_map/ppermute | solution.py:446
  186.2 1.5 collective-permute-done.11.refs_2_
  188.2 0.9 reshape.46
  190.0 0.7 copy-done.10
  190.7 3.1 %shard_map.229 = (f32[512,1024]{1,0:T(8,128)}, f32[256,512]{1,0:T(8,128)}, f32[8,128]{1,0:T(8,128)}) custom-call(s32[1]{0:T(128)} %bitcast.2.me_ref, bf16[4,16,1408]{2,1,0:T(8,128)(2,1)} %shard_map.228.refs_0_, bf16[4,16,1408]{2,1,0:T(8,128)(2,1)} %copy-done.6, bf16[4,16,1408]{2,1,0:T(8,128)(2,1)} %copy-done.5, bf16[4,16,1408]{2,1,0:T(8,128)(2,1)} %copy-done.4, ...), custom_call_target="tpu_custom_call" | custom-call | bytes 1441796 | tf_op jit(solution)/shard_map/pallas_call | solution.py:396
  193.8 1.2 slice.3
  (64 shorter events, 4.3 us)
Async XLA Ops:
  11.8 42.1 %copy-start.21 = (bf16[512]{0:T(512)(128)(2,1)S(1)}, bf16[512]{0:T(512)(128)(2,1)}, u32[]{:S(2)}) copy-start(bf16[512]{0:T(512)(128)(2,1)} %param.29) | copy-start | bytes 3076
  11.8 42.7 %copy-start.22 = (bf16[512]{0:T(512)(128)(2,1)S(1)}, bf16[512]{0:T(512)(128)(2,1)}, u32[]{:S(2)}) copy-start(bf16[512]{0:T(512)(128)(2,1)} %param.31) | copy-start | bytes 3076
  11.8 43.3 %copy-start.20 = (bf16[1024]{0:T(1024)(128)(2,1)S(1)}, bf16[1024]{0:T(1024)(128)(2,1)}, u32[]{:S(2)}) copy-start(bf16[1024]{0:T(1024)(128)(2,1)} %param.27) | copy-start | bytes 6148
  11.8 30.5 %all-to-all-start = ((bf16[8,448,128]{2,1,0:T(8,128)(2,1)}), bf16[8,448,128]{2,1,0:T(8,128)(2,1)S(1)}, u32[]{:S(2)}, u32[]{:S(2)}) async-start(bf16[8,448,128]{2,1,0:T(8,128)(2,1)} %get-tuple-element.31), calls=%async_computation | async-start | bytes 1835008 | tf_op jit(solution)/shard_map/all_to_all | solution.py:408
  42.2 0.9 copy-start
  50.3 13.3 %all-to-all-start.1 = ((bf16[8,144,128]{2,1,0:T(8,128)(2,1)}), bf16[8,144,128]{2,1,0:T(8,128)(2,1)S(1)}, u32[]{:S(2)}, u32[]{:S(2)}) async-start(bf16[8,144,128]{2,1,0:T(8,128)(2,1)} %shard_map.220), calls=%async_computation.1 | async-start | bytes 589824 | tf_op jit(solution)/shard_map/all_to_all | solution.py:408
  63.6 0.7 copy-start.1
  86.3 19.2 %copy-start.23 = (bf16[512]{0:T(512)(128)(2,1)S(1)}, bf16[512]{0:T(512)(128)(2,1)}, u32[]{:S(2)}) copy-start(bf16[512]{0:T(512)(128)(2,1)} %param.34) | copy-start | bytes 3076
  86.3 19.8 %copy-start.24 = (bf16[512]{0:T(512)(128)(2,1)S(1)}, bf16[512]{0:T(512)(128)(2,1)}, u32[]{:S(2)}) copy-start(bf16[512]{0:T(512)(128)(2,1)} %param.37) | copy-start | bytes 3076
  102.1 10.9 %all-to-all-start.3 = ((bf16[8,72,128]{2,1,0:T(8,128)(2,1)}), bf16[8,72,128]{2,1,0:T(8,128)(2,1)S(1)}, u32[]{:S(2)}, u32[]{:S(2)}) async-start(bf16[8,72,128]{2,1,0:T(8,128)(2,1)} %shard_map.222), calls=%async_computation.3 | async-start | bytes 294912 | tf_op jit(solution)/shard_map/all_to_all | solution.py:408
  112.9 0.6 copy-start.3
  132.1 3.6 %collective-permute-start = (bf16[4,4,16,1408]{3,2,1,0:T(8,128)(2,1)}, bf16[4,4,16,1408]{3,2,1,0:T(8,128)(2,1)S(1)}, u32[]{:S(2)}, u32[]{:S(2)}) collective-permute-start(bf16[4,4,16,1408]{3,2,1,0:T(8,128)(2,1)} %get-tuple-element.46), channel_id=1, source_target_pairs={{0,8},{1,9},{2,10},{3,11},{4,12},{5,13},{6,14},{7,15},{8,0},{9,1},... | collective-permute-start | bytes 2162696 | tf_op jit(solution)/shard_map/ppermute | solution.py:446
  132.1 56.1 %all-to-all-start.4 = ((bf16[8,36,1024]{2,1,0:T(8,128)(2,1)}), bf16[8,36,1024]{2,1,0:T(8,128)(2,1)S(1)}, u32[]{:S(2)}, u32[]{:S(2)}) async-start(bf16[8,36,1024]{2,1,0:T(8,128)(2,1)} %get-tuple-element.37), calls=%async_computation.4 | async-start | bytes 1310720 | tf_op jit(solution)/shard_map/all_to_all | solution.py:408
  135.7 0.9 copy-start.2
  138.7 7.6 %collective-permute-start.1 = (bf16[4,16,1408]{2,1,0:T(8,128)(2,1)}, bf16[4,16,1408]{2,1,0:T(8,128)(2,1)S(1)}, u32[]{:S(2)}, u32[]{:S(2)}) collective-permute-start(bf16[4,16,1408]{2,1,0:T(8,128)(2,1)} %get-tuple-element.48), channel_id=1, source_target_pairs={{0,16},{1,17},{2,18},{3,19},{4,20},{5,21},{6,22},{7,23},{8,24},{9,... | collective-permute-start | bytes 540680 | tf_op jit(solution)/shard_map/ppermute | solution.py:446
  140.2 14.3 %collective-permute-start.2 = (bf16[4,16,1408]{2,1,0:T(8,128)(2,1)}, bf16[4,16,1408]{2,1,0:T(8,128)(2,1)S(1)}, u32[]{:S(2)}, u32[]{:S(2)}) collective-permute-start(bf16[4,16,1408]{2,1,0:T(8,128)(2,1)} %get-tuple-element.49), channel_id=1, source_target_pairs={{0,1},{1,0},{2,3},{3,2},{4,5},{5,4},{6,7},{7,6},{8,9},{9,8},{10,11... | collective-permute-start | bytes 540680 | tf_op jit(solution)/shard_map/ppermute | solution.py:446
  142.1 12.4 %collective-permute-start.3 = (bf16[4,16,1408]{2,1,0:T(8,128)(2,1)}, bf16[4,16,1408]{2,1,0:T(8,128)(2,1)S(1)}, u32[]{:S(2)}, u32[]{:S(2)}) collective-permute-start(bf16[4,16,1408]{2,1,0:T(8,128)(2,1)} %get-tuple-element.50), channel_id=1, source_target_pairs={{0,17},{1,16},{2,19},{3,18},{4,21},{5,20},{6,23},{7,22},{8,25},{9,... | collective-permute-start | bytes 540680 | tf_op jit(solution)/shard_map/ppermute | solution.py:446
  146.3 8.2 %copy-start.11 = (bf16[4,16,1408]{2,1,0:T(8,128)(2,1)}, bf16[4,16,1408]{2,1,0:T(8,128)(2,1)S(1)}, u32[]{:S(2)}) copy-start(bf16[4,16,1408]{2,1,0:T(8,128)(2,1)S(1)} %collective-permute-done.1.refs_1_) | copy-start | bytes 540676
  154.5 0.7 copy-start.12
  154.5 0.7 copy-start.13
  157.1 4.6 %collective-permute-start.4 = (bf16[16,1408]{1,0:T(8,128)(2,1)}, bf16[16,1408]{1,0:T(8,128)(2,1)S(1)}, u32[]{:S(2)}, u32[]{:S(2)}) collective-permute-start(bf16[16,1408]{1,0:T(8,128)(2,1)} %get-tuple-element.52), channel_id=1, source_target_pairs={{0,2},{1,3},{2,0},{3,1},{4,6},{5,7},{6,4},{7,5},{8,10},{9,11},{10,... | collective-permute-start | bytes 135176 | tf_op jit(solution)/shard_map/ppermute | solution.py:446
  158.8 6.0 %collective-permute-start.5 = (bf16[16,1408]{1,0:T(8,128)(2,1)}, bf16[16,1408]{1,0:T(8,128)(2,1)S(1)}, u32[]{:S(2)}, u32[]{:S(2)}) collective-permute-start(bf16[16,1408]{1,0:T(8,128)(2,1)} %get-tuple-element.53), channel_id=1, source_target_pairs={{0,4},{1,5},{2,6},{3,7},{4,0},{5,1},{6,2},{7,3},{8,12},{9,13},{10,... | collective-permute-start | bytes 135176 | tf_op jit(solution)/shard_map/ppermute | solution.py:446
  161.7 6.1 %collective-permute-start.6 = (bf16[16,1408]{1,0:T(8,128)(2,1)}, bf16[16,1408]{1,0:T(8,128)(2,1)S(1)}, u32[]{:S(2)}, u32[]{:S(2)}) collective-permute-start(bf16[16,1408]{1,0:T(8,128)(2,1)} %get-tuple-element.54), channel_id=1, source_target_pairs={{0,6},{1,7},{2,4},{3,5},{4,2},{5,3},{6,0},{7,1},{8,14},{9,15},{10,... | collective-permute-start | bytes 135176 | tf_op jit(solution)/shard_map/ppermute | solution.py:446
  161.7 6.1 %copy-start.14 = (bf16[16,1408]{1,0:T(8,128)(2,1)}, bf16[16,1408]{1,0:T(8,128)(2,1)S(1)}, u32[]{:S(2)}) copy-start(bf16[16,1408]{1,0:T(8,128)(2,1)S(1)} %collective-permute-done.4.refs_1_) | copy-start | bytes 135172
  164.7 3.0 %copy-start.15 = (bf16[16,1408]{1,0:T(8,128)(2,1)}, bf16[16,1408]{1,0:T(8,128)(2,1)S(1)}, u32[]{:S(2)}) copy-start(bf16[16,1408]{1,0:T(8,128)(2,1)S(1)} %collective-permute-done.5.refs_2_) | copy-start | bytes 135172
  167.8 0.6 copy-start.16
  169.9 6.2 %collective-permute-start.9 = (bf16[16,1408]{1,0:T(8,128)(2,1)}, bf16[16,1408]{1,0:T(8,128)(2,1)S(1)}, u32[]{:S(2)}, u32[]{:S(2)}) collective-permute-start(bf16[16,1408]{1,0:T(8,128)(2,1)} %shard_map.227.refs_0_), channel_id=1, source_target_pairs={{0,6},{1,7},{2,4},{3,5},{4,2},{5,3},{6,0},{7,1},{8,14},{9,15},{10,... | collective-permute-start | bytes 135176 | tf_op jit(solution)/shard_map/ppermute | solution.py:446
  170.4 6.1 %collective-permute-start.8 = (bf16[16,1408]{1,0:T(8,128)(2,1)}, bf16[16,1408]{1,0:T(8,128)(2,1)S(1)}, u32[]{:S(2)}, u32[]{:S(2)}) collective-permute-start(bf16[16,1408]{1,0:T(8,128)(2,1)} %shard_map.227.refs_0_), channel_id=1, source_target_pairs={{0,4},{1,5},{2,6},{3,7},{4,0},{5,1},{6,2},{7,3},{8,12},{9,13},{10,... | collective-permute-start | bytes 135176 | tf_op jit(solution)/shard_map/ppermute | solution.py:446
  170.4 6.1 %collective-permute-start.7 = (bf16[16,1408]{1,0:T(8,128)(2,1)}, bf16[16,1408]{1,0:T(8,128)(2,1)S(1)}, u32[]{:S(2)}, u32[]{:S(2)}) collective-permute-start(bf16[16,1408]{1,0:T(8,128)(2,1)} %shard_map.227.refs_0_), channel_id=1, source_target_pairs={{0,2},{1,3},{2,0},{3,1},{4,6},{5,7},{6,4},{7,5},{8,10},{9,11},{10,... | collective-permute-start | bytes 135176 | tf_op jit(solution)/shard_map/ppermute | solution.py:446
  176.0 0.6 copy-start.17
  176.5 0.6 copy-start.18
  177.1 0.6 copy-start.19
  179.3 6.9 %collective-permute-start.12 = (bf16[4,16,1408]{2,1,0:T(8,128)(2,1)}, bf16[4,16,1408]{2,1,0:T(8,128)(2,1)S(1)}, u32[]{:S(2)}, u32[]{:S(2)}) collective-permute-start(bf16[4,16,1408]{2,1,0:T(8,128)(2,1)} %shard_map.228.refs_0_), channel_id=1, source_target_pairs={{0,17},{1,16},{2,19},{3,18},{4,21},{5,20},{6,23},{7,22},{8,25},{9,... | collective-permute-start | bytes 540680 | tf_op jit(solution)/shard_map/ppermute | solution.py:446
  180.1 7.6 %collective-permute-start.11 = (bf16[4,16,1408]{2,1,0:T(8,128)(2,1)}, bf16[4,16,1408]{2,1,0:T(8,128)(2,1)S(1)}, u32[]{:S(2)}, u32[]{:S(2)}) collective-permute-start(bf16[4,16,1408]{2,1,0:T(8,128)(2,1)} %shard_map.228.refs_0_), channel_id=1, source_target_pairs={{0,1},{1,0},{2,3},{3,2},{4,5},{5,4},{6,7},{7,6},{8,9},{9,8},{10,11... | collective-permute-start | bytes 540680 | tf_op jit(solution)/shard_map/ppermute | solution.py:446
  181.6 6.1 %collective-permute-start.10 = (bf16[4,16,1408]{2,1,0:T(8,128)(2,1)}, bf16[4,16,1408]{2,1,0:T(8,128)(2,1)S(1)}, u32[]{:S(2)}, u32[]{:S(2)}) collective-permute-start(bf16[4,16,1408]{2,1,0:T(8,128)(2,1)} %shard_map.228.refs_0_), channel_id=1, source_target_pairs={{0,16},{1,17},{2,18},{3,19},{4,20},{5,21},{6,22},{7,23},{8,24},{9,... | collective-permute-start | bytes 540680 | tf_op jit(solution)/shard_map/ppermute | solution.py:446
  182.8 6.4 %collective-permute-start.13 = (bf16[4,16,1408]{2,1,0:T(8,128)(2,1)}, bf16[4,16,1408]{2,1,0:T(8,128)(2,1)S(1)}, u32[]{:S(2)}, u32[]{:S(2)}) collective-permute-start(bf16[4,16,1408]{2,1,0:T(8,128)(2,1)} %shard_map.228.refs_0_), channel_id=1, source_target_pairs={{0,8},{1,9},{2,10},{3,11},{4,12},{5,13},{6,14},{7,15},{8,0},{9,1},... | collective-permute-start | bytes 540680 | tf_op jit(solution)/shard_map/ppermute | solution.py:446
  186.2 3.2 %copy-start.4 = (bf16[4,16,1408]{2,1,0:T(8,128)(2,1)}, bf16[4,16,1408]{2,1,0:T(8,128)(2,1)S(1)}, u32[]{:S(2)}) copy-start(bf16[4,16,1408]{2,1,0:T(8,128)(2,1)S(1)} %collective-permute-done.12.refs_3_) | copy-start | bytes 540676
  186.2 3.0 %collective-permute-start.16 = (bf16[4,16,1408]{2,1,0:T(8,128)(2,1)S(1)}, bf16[4,16,1408]{2,1,0:T(8,128)(2,1)S(1)}, u32[]{:S(2)}, u32[]{:S(2)}) collective-permute-start(bf16[4,16,1408]{2,1,0:T(8,128)(2,1)S(1)} %collective-permute-done.12.refs_3_), channel_id=1, source_target_pairs={{0,8},{1,9},{2,10},{3,11},{4,12},{5,13},{6,14},{7,15},{8,0},{9,1},... | collective-permute-start | bytes 540680 | tf_op jit(solution)/shard_map/ppermute | solution.py:446
  187.7 1.7 copy-start.5
  187.7 1.5 collective-permute-start.15
  187.7 1.7 copy-start.6
  187.7 1.7 collective-permute-start.14
  189.2 0.7 copy-start.7
  189.2 0.8 copy-start.8
  189.2 0.8 copy-start.9
  190.0 0.7 copy-start.10

commit v3 on v2

--- a/solution.py
+++ b/solution.py
@@ -12,14 +12,18 @@
 BF = jnp.bfloat16
 F32 = jnp.float32
 LOG2E = math.log2(math.e)
-VMEM_LIMIT = 56 << 20
+VMEM_LIMIT = 24 << 20
+
+
+def as_row(vector):
+    return vector.astype(F32).reshape(1, -1)
 
 
 def layer_norm(x, gain):
     row_mean = jnp.mean(x, axis=-1, keepdims=True)
     centered_input = x - row_mean
     var = jnp.mean(centered_input * centered_input, axis=-1, keepdims=True)
-    return centered_input * lax.rsqrt(var + 1e-06) * gain.astype(F32)
+    return centered_input * lax.rsqrt(var + 1e-06) * as_row(gain)
 
 
 def norm_backward(z, gain, upstream):
@@ -29,7 +33,7 @@
         jnp.mean(centered_input * centered_input, axis=-1, keepdims=True) + 1e-06
     )
     normalized_input = centered_input * inverse_scale
-    input_gradient = upstream * gain.astype(F32)
+    input_gradient = upstream * as_row(gain)
     return inverse_scale * (
         input_gradient
         - jnp.mean(input_gradient, axis=-1, keepdims=True)
@@ -179,7 +183,7 @@
     encoded = tok_ref[...].astype(F32) + dot(attended, w_out_ref[...])
     dec_normed = layer_norm(encoded, out_gain_ref[...]).astype(BF)
     dec_tok = dot(dec_normed, w_dec_ref[...]).astype(BF).astype(F32)
-    filled = jnp.where(seen > 0.0, dec_tok, mask_ref[...].astype(F32))
+    filled = jnp.where(seen > 0.0, dec_tok, as_row(mask_ref[...]))
     decoder_in = (filled + pos_ref[...].astype(F32)).astype(BF)
 
     owner = owner_ref[...]
@@ -370,7 +374,7 @@
         refs[-1][i] = ref[...]
 
 
-def place_kernel(me_ref, *refs):
+def place_kernel(me_ref, *refs, masked_total):
     blocks, (head_ref, out_ref, loss_ref) = refs[:8], refs[8:]
     pixels = head_ref.shape[1]
     deep = out_ref.shape[0] // 32
@@ -384,10 +388,11 @@
         out_ref[at, :half] = value[:deep, pixels : pixels + half]
         out_ref[at, half:] = value[deep:, pixels : pixels + half]
     value = blocks[0][0].astype(F32)
-    loss_ref[...] = value[:8, pixels + half :] + value[8:, pixels + half :]
-
-
-def vmem_call(kernel, outs, scratch, inputs, smem=(), flops=0):
+    total = value[:8, pixels + half :] + value[8:, pixels + half :]
+    loss_ref[0, 0] = jnp.max(total) * (1.0 / masked_total)
+
+
+def vmem_call(kernel, outs, scratch, inputs, smem=(), smem_out=(), flops=0):
     space = [
         pl.BlockSpec(memory_space=pltpu.SMEM if i in smem else pltpu.VMEM)
         for i in range(len(inputs))
@@ -397,7 +402,10 @@
         kernel,
         out_shape=outs,
         in_specs=space,
-        out_specs=[pl.BlockSpec(memory_space=pltpu.VMEM)] * len(outs),
+        out_specs=[
+            pl.BlockSpec(memory_space=pltpu.SMEM if i in smem_out else pltpu.VMEM)
+            for i in range(len(outs))
+        ],
         scratch_shapes=scratch,
         compiler_params=pltpu.CompilerParams(vmem_limit_bytes=VMEM_LIMIT),
         cost_estimate=pl.CostEstimate(flops=flops, bytes_accessed=moved, transcendentals=0),
@@ -450,7 +458,7 @@
 COLUMN = ((0, 2), (0, 4), (0, 6))
 
 
-def sum_by_permutes(keep, send):
+def sum_by_permutes(keep, send, ahead):
     shape = jax.ShapeDtypeStruct
     add = lambda parts, outs: vmem_call(
         functools.partial(add_kernel, count=len(parts)), outs, [], parts
@@ -458,14 +466,15 @@
     part, block = shape(keep.shape[1:], BF), shape(keep.shape[2:], BF)
     parts = add([keep, across(send, 1, 0)], [part] * 4)
     others = [across(p, *bits) for p, bits in zip(parts[1:], PLANE)]
-    blocks = add([parts[0], *others], [block] * 4)
+    first, ahead = lax.optimization_barrier((parts[0], ahead))
+    blocks = add([first, *others], [block] * 4)
     others = [across(b, *bits) for b, bits in zip(blocks[1:], COLUMN)]
     (total,) = add([blocks[0], *others], [block])
     (column,) = vmem_call(
         join_kernel, [part], [], [total] + [across(total, *bits) for bits in COLUMN]
     )
     ours = [column] + [across(column, *bits) for bits in PLANE]
-    return ours, [across(x, 1, 0) for x in ours]
+    return ours, [across(x, 1, 0) for x in ours], ahead
 
 
 def sum_by_blocks(keep, send, groups):
@@ -512,14 +521,13 @@
     share = rows // 3
     width = w_embed.shape[1]
     dec_width = w_dec_embed.shape[1]
-    row = lambda vector: vector.reshape(1, -1)
     shape = jax.ShapeDtypeStruct
 
     send, tok = vmem_call(
         embed_kernel,
         [shape((HEADS, half + rows + 16, 128), BF), shape((rows, width), BF)],
         [pltpu.VMEM((rows, width), BF), pltpu.VMEM((rows, w_qkv.shape[1]), BF)],
-        [source, enc_pos, w_embed, row(enc_gain), w_qkv, visible_rows],
+        [source, enc_pos, w_embed, enc_gain, w_qkv, visible_rows],
         flops=2 * rows * width * (pixels + w_qkv.shape[1]),
     )
     first = (lax.axis_index("ctx") // HEADS * HEADS).astype(jnp.int32).reshape(1)
@@ -560,8 +568,8 @@
             pltpu.VMEM((rows, decoder_query_key_value_weight.shape[1]), F32),
         ],
         [
-            att, tok, w_out, row(enc_out_gain), w_dec_embed, row(mask_token), dec_pos,
-            row(dec_attn_gain), decoder_query_key_value_weight, visible_rows, owner_slot, source,
+            att, tok, w_out, enc_out_gain, w_dec_embed, mask_token, dec_pos,
+            dec_attn_gain, decoder_query_key_value_weight, visible_rows, owner_slot, source,
         ],
         flops=2 * rows * width * 1024,
     )
@@ -595,7 +603,7 @@
         ],
         [pltpu.VMEM((rows, dec_width), BF), pltpu.VMEM((rows, pixels), F32)],
         [
-            att, y_own, w_dec_out, row(decoder_feed_gain), w_up, w_down, row(head_gain), w_head,
+            att, y_own, w_dec_out, decoder_feed_gain, w_up, w_down, head_gain, w_head,
             target, flag,
         ],
         flops=2 * rows * dec_width * (2 * hidden + pixels),
@@ -617,26 +625,26 @@
             pltpu.VMEM((w_dec_out.shape[0], dec_width), F32),
         ],
         [
-            me, dec_att, y_mid, slope, z, zn, dpred, loss_part, row(decoder_feed_gain),
-            w_up, w_down, row(head_gain), w_head,
+            me, dec_att, y_mid, slope, z, zn, dpred, loss_part, decoder_feed_gain,
+            w_up, w_down, head_gain, w_head,
         ],
         smem=(0,),
         flops=2 * rows * dec_width * (2 * hidden + 2 * pixels),
     )
     if repeat == 1:
-        ours, theirs = sum_by_permutes(keep, send)
+        ours, theirs, reconstruction = sum_by_permutes(keep, send, reconstruction)
     else:
         ours, theirs = sum_by_blocks(keep, send, groups)
+    masked_total = lax.axis_size("dp") * (groups * rows - share * groups)
     grad_head, grad_dec_out, loss = vmem_call(
-        place_kernel,
-        [shape(w_head.shape, F32), shape(w_dec_out.shape, F32), shape((8, 128), F32)],
+        functools.partial(place_kernel, masked_total=masked_total),
+        [shape(w_head.shape, F32), shape(w_dec_out.shape, F32), shape((1, 1), F32)],
         [],
         [me, *ours, *theirs],
         smem=(0,),
-    )
-    loss = loss[0, 0]
-    masked_total = lax.axis_size("dp") * (groups * rows - share * groups)
-    return (reconstruction.reshape(1, rows, pixels), grad_head, grad_dec_out, loss / masked_total)
+        smem_out=(2,),
+    )
+    return (reconstruction.reshape(1, rows, pixels), grad_head, grad_dec_out, loss.reshape(()))
 
 
 def solution(mesh):

time: 198 us -> 190 us (0.960)
  Pallas kernels: 67.2 us -> 39.9 us
  local copies, waits for them, and re-layouts: 13.3 us -> 33.4 us
  blocking collectives: 16.3 us -> 29.3 us
  waiting for transfers between devices: 63 us -> 53.4 us
  starting transfers between devices: 34.3 us -> 31.8 us
    pallas_call x11, Pallas kernels: 67.2 us -> 39.9 us  [vmem_call(): pl.pallas_call(kernel, out_shape=outs, in_specs=space, out_specs=[pl.Bloc...]
    unnamed x50 -> x98, local copies, waits for them, and re-layouts: 7.03 us -> 31.4 us
    all_to_all x1 -> x2, blocking collectives: 16.3 us -> 29.3 us  [swap(): lax.all_to_all(x, axis, split_axis=0, concat_axis=0, tiled=True, axis_ind...]
    all_to_all x4 -> x3, waiting for transfers between devices: 37.3 us -> 30.5 us  [swap(): lax.all_to_all(x, axis, split_axis=0, concat_axis=0, tiled=True, axis_ind...]
    reshape x6 -> x0, local copies, waits for them, and re-layouts: 4.21 us -> none  [on_device(): row = lambda vector: vector.reshape(1, -1)]
    ppermute x17, waiting for transfers between devices: 25.7 us -> 22.9 us  [across(): return lax.ppermute(x, ('dp', 'ctx'), pairs)]
    all_to_all x4 -> x3, starting transfers between devices: 17.9 us -> 15.2 us  [swap(): lax.all_to_all(x, axis, split_axis=0, concat_axis=0, tiled=True, axis_ind...]
  transfers between devices with their start and end apart: 21 -> 20, of which waited for: 12 -> 12; matrix products, arithmetic and copies ran while one was open for 2% -> 1% of each run, Pallas kernels for 4% -> 3%
where the time goes in v3:
time: 190 us; the launch traced here: 189 us
  waiting for transfers between devices  53.4 us (28%)
  Pallas kernels  39.9 us (21%)
  local copies, waits for them, and re-layouts  33.4 us (18%)
  starting transfers between devices  31.8 us (17%)
  blocking collectives  29.3 us (15%)
    pallas_call x11, Pallas kernels, vmem_call(): pl.pallas_call(kernel, out_shape=outs, in_specs=space, out_specs=[pl.Bloc...  39.9 us
    unnamed x98, local copies, waits for them, and re-layouts  31.4 us
    all_to_all x3, waiting for transfers between devices, swap(): lax.all_to_all(x, axis, split_axis=0, concat_axis=0, tiled=True, axis_ind...  30.5 us
    all_to_all x2, blocking collectives, swap(): lax.all_to_all(x, axis, split_axis=0, concat_axis=0, tiled=True, axis_ind...  29.3 us
    ppermute x17, waiting for transfers between devices, across(): return lax.ppermute(x, ('dp', 'ctx'), pairs)  22.9 us
    ppermute x17, starting transfers between devices, across(): return lax.ppermute(x, ('dp', 'ctx'), pairs)  16.6 us
    all_to_all x3, starting transfers between devices, swap(): lax.all_to_all(x, axis, split_axis=0, concat_axis=0, tiled=True, axis_ind...  15.2 us
  transfers between devices with their start and end apart: 20, of which 12 were waited for; matrix products, arithmetic and copies ran while one was open for 1% of the time, Pallas kernels for 3%

profile of v3, /device:TPU:0, one launch (start us, length us, event | category | flops | bytes accessed | tf_op | source)
XLA Modules:
  0.0 188.9 jit_solution(8365482413597593865)
XLA Ops:
  0.6 1.9 copy-done.4
  2.5 1.1 copy-done.5
  3.6 1.6 copy-done.7
  5.2 1.1 copy-done.22
  7.6 6.9 %shard_map.219 = (bf16[8,448,128]{2,1,0:T(8,128)(2,1)}, bf16[288,1024]{1,0:T(8,128)(2,1)S(1)}) custom-call(bf16[288,1024]{1,0:T(8,128)(2,1)S(1)} %bitcast.4, bf16[288,1024]{1,0:T(8,128)(2,1)S(1)} %copy-done.22, bf16[1024,1024]{1,0:T(8,128)(2,1)S(1)} %copy-done.7, bf16[1024]{0:T(1024)(128)(2,1)S(1)} %copy-done.44, bf16[1024,1536]{1,0:T(8,128)(2,1)S(1)} %copy-done.4, ...), custom_call_target="tpu_custom_call" | custom-call | flops 1509949440 | bytes 6425728 | tf_op jit(solution)/shard_map/pallas_call | solution.py:401
  15.4 7.4 %all-to-all-start = ((bf16[8,448,128]{2,1,0:T(8,128)(2,1)}), bf16[8,448,128]{2,1,0:T(8,128)(2,1)S(1)}, u32[]{:S(2)}, u32[]{:S(2)}) async-start(bf16[8,448,128]{2,1,0:T(8,128)(2,1)} %get-tuple-element.33), calls=%async_computation | async-start | bytes 1835008 | tf_op jit(solution)/shard_map/all_to_all | solution.py:416
  22.8 23.0 %all-to-all-done.q_ref.kv_ref = bf16[8,448,128]{2,1,0:T(8,128)(2,1)S(1)} async-done(((bf16[8,448,128]{2,1,0:T(8,128)(2,1)}), bf16[8,448,128]{2,1,0:T(8,128)(2,1)S(1)}, u32[]{:S(2)}, u32[]{:S(2)}) %all-to-all-start) | async-done | bytes 917536 | tf_op jit(solution)/shard_map/all_to_all | solution.py:416
  45.9 5.0 %shard_map.220 = bf16[8,144,128]{2,1,0:T(8,128)(2,1)S(1)} custom-call(s32[1]{0:T(128)} %bitcast.1.first_ref, bf16[8,448,128]{2,1,0:T(8,128)(2,1)S(1)} %all-to-all-done.q_ref.kv_ref, bf16[8,448,128]{2,1,0:T(8,128)(2,1)S(1)} %all-to-all-done.q_ref.kv_ref), custom_call_target="tpu_custom_call" | custom-call | flops 411041792 | bytes 1835012 | tf_op jit(solution)/shard_map/pallas_call | solution.py:401
  50.8 13.8 %all_to_all.25.att_ref = bf16[8,144,128]{2,1,0:T(8,128)(2,1)S(1)} all-to-all(bf16[8,144,128]{2,1,0:T(8,128)(2,1)S(1)} %shard_map.220), channel_id=1, replica_groups=mesh['dp'=4,'ctx'=8] {'ctx'}, dimensions={0} | all-to-all | bytes 589824 | tf_op jit(solution)/shard_map/all_to_all | solution.py:416
  64.7 2.6 %shard_map.221 = (bf16[8,216,128]{2,1,0:T(8,128)(2,1)S(1)}, bf16[288,512]{1,0:T(8,128)(2,1)S(1)}, bf16[288,1024]{1,0:T(8,128)(2,1)S(1)}, f32[288,128]{1,0:T(8,128)S(1)}) custom-call(bf16[8,144,128]{2,1,0:T(8,128)(2,1)S(1)} %all_to_all.25.att_ref, bf16[288,1024]{1,0:T(8,128)(2,1)S(1)} %copy-done.24, bf16[512,1024]{1,0:T(8,128)(2,1)S(1)} %copy-done.10, ...), custom_call_target="tpu_custom_call" | custom-call | flops 603979776 | bytes 4659456 | tf_op jit(solution)/shard_map/pallas_call | solution.py:401
  68.2 15.5 %all_to_all.26.q_ref.kv_ref = bf16[8,216,128]{2,1,0:T(8,128)(2,1)S(1)} all-to-all(bf16[8,216,128]{2,1,0:T(8,128)(2,1)S(1)} %get-tuple-element.35), channel_id=1, replica_groups=mesh['dp'=4,'ctx'=8] {'ctx'}, dimensions={0} | all-to-all | bytes 884736 | tf_op jit(solution)/shard_map/all_to_all | solution.py:416
  83.7 14.0 %shard_map.222 = bf16[8,72,128]{2,1,0:T(8,128)(2,1)S(1)} custom-call(bf16[8,216,128]{2,1,0:T(8,128)(2,1)S(1)} %all_to_all.26.q_ref.kv_ref, bf16[8,216,128]{2,1,0:T(8,128)(2,1)S(1)} %all_to_all.26.q_ref.kv_ref), custom_call_target="tpu_custom_call" | custom-call | flops 2717908992 | bytes 884736 | tf_op jit(solution)/shard_map/pallas_call | solution.py:401
  98.3 3.4 %all-to-all-start.3 = ((bf16[8,72,128]{2,1,0:T(8,128)(2,1)}), bf16[8,72,128]{2,1,0:T(8,128)(2,1)S(1)}, u32[]{:S(2)}, u32[]{:S(2)}) async-start(bf16[8,72,128]{2,1,0:T(8,128)(2,1)} %copy-done.33), calls=%async_computation.3 | async-start | bytes 294912 | tf_op jit(solution)/shard_map/all_to_all | solution.py:416
  101.8 7.4 %all-to-all-done.3.att_ref = bf16[8,72,128]{2,1,0:T(8,128)(2,1)S(1)} async-done(((bf16[8,72,128]{2,1,0:T(8,128)(2,1)}), bf16[8,72,128]{2,1,0:T(8,128)(2,1)S(1)}, u32[]{:S(2)}, u32[]{:S(2)}) %all-to-all-start.3) | async-done | bytes 147488 | tf_op jit(solution)/shard_map/all_to_all | solution.py:416
  109.2 1.6 copy-done.1
  110.8 1.1 copy-done.15
  111.9 1.0 copy-done.27
  112.8 0.9 copy-done.32
  115.1 4.8 %shard_map.223 = (bf16[8,36,1024]{2,1,0:T(8,128)(2,1)S(1)}, bf16[288,256]{1,0:T(8,128)(2,1)S(1)}, f32[288,512]{1,0:T(8,128)S(1)}, bf16[288,2048]{1,0:T(8,128)(2,...) custom-call(bf16[8,72,128]{2,1,0:T(8,128)(2,1)S(1)} %all-to-all-done, ...), custom_call_target="tpu_custom_call" | custom-call | flops 1509949440 | bytes 6686720 | tf_op jit(solution)/shard_map/pallas_call | solution.py:401
  120.0 1.0 copy-done.8
  121.0 0.9 copy-done.13
  126.2 4.4 %all-to-all-start.4 = ((bf16[8,36,1024]{2,1,0:T(8,128)(2,1)}), bf16[8,36,1024]{2,1,0:T(8,128)(2,1)}, u32[]{:S(2)}, u32[]{:S(2)}) async-start(bf16[8,36,1024]{2,1,0:T(8,128)(2,1)} %copy-done.13), calls=%async_computation.4 | async-start | bytes 1310720 | tf_op jit(solution)/shard_map/all_to_all | solution.py:416
  130.6 1.6 copy-done.2
  132.2 1.3 copy-done.9
  133.5 1.1 copy-done.17
  134.6 1.1 copy-done.19
  135.6 1.1 copy-done.21
  136.7 1.0 copy-done.29
  137.7 0.9 copy-done.35
  140.6 4.7 %shard_map.224 = (bf16[4,4,16,1408]{3,2,1,0:T(8,128)(2,1)S(1)}, bf16[4,4,16,1408]{3,2,1,0:T(8,128)(2,1)S(1)}) custom-call(s32[1]{0:T(128)} %bitcast.me_ref, bf16[288,256]{1,0:T(8,128)(2,1)S(1)} %copy-done.35, f32[288,512]{1,0:T(8,128)S(1)} %copy-done.17, bf16[288,2048]{1,0:T(8,128)(2,1)S(1)} %copy-done.9, f32[288,512]{1,0:T(8,128)S(1)} %copy-done.19, ...), custom_call_target="tpu_custom_call" | custom-call | flops 1811939328 | bytes 8640516 | tf_op jit(solution)/shard_map/pallas_call | solution.py:401
  145.3 2.2 %collective-permute-done.refs_1_ = bf16[4,4,16,1408]{3,2,1,0:T(8,128)(2,1)S(1)} collective-permute-done((bf16[4,4,16,1408]{3,2,1,0:T(8,128)(2,1)S(1)}, bf16[4,4,16,1408]{3,2,1,0:T(8,128)(2,1)S(1)}, u32[]{:S(2)}, u32[]{:S(2)}) %collective-permute-start) | collective-permute-done | bytes 720928 | tf_op jit(solution)/shard_map/ppermute | solution.py:454
  147.7 1.6 collective-permute-start.1
  149.2 1.7 collective-permute-start.2
  151.2 3.9 %collective-permute-done.1.refs_1_ = bf16[4,16,1408]{2,1,0:T(8,128)(2,1)S(1)} collective-permute-done((bf16[4,16,1408]{2,1,0:T(8,128)(2,1)S(1)}, bf16[4,16,1408]{2,1,0:T(8,128)(2,1)S(1)}, u32[]{:S(2)}, u32[]{:S(2)}) %collective-permute-start.1) | collective-permute-done | bytes 180256 | tf_op jit(solution)/shard_map/ppermute | solution.py:454
  155.1 3.5 %collective-permute-done.2.refs_2_ = bf16[4,16,1408]{2,1,0:T(8,128)(2,1)S(1)} collective-permute-done((bf16[4,16,1408]{2,1,0:T(8,128)(2,1)S(1)}, bf16[4,16,1408]{2,1,0:T(8,128)(2,1)S(1)}, u32[]{:S(2)}, u32[]{:S(2)}) %collective-permute-start.2) | collective-permute-done | bytes 180256 | tf_op jit(solution)/shard_map/ppermute | solution.py:454
  159.5 1.8 collective-permute-start.4
  161.3 2.4 %collective-permute-start.5 = (bf16[16,1408]{1,0:T(8,128)(2,1)S(1)}, bf16[16,1408]{1,0:T(8,128)(2,1)S(1)}, u32[]{:S(2)}, u32[]{:S(2)}) collective-permute-start(bf16[16,1408]{1,0:T(8,128)(2,1)S(1)} %get-tuple-element.57), channel_id=1, source_target_pairs={{0,4},{1,5},{2,6},{3,7},{4,0},{5,1},{6,2},{7,3},{8,12},{9,13},{10,... | collective-permute-start | bytes 135176 | tf_op jit(solution)/shard_map/ppermute | solution.py:454
  164.0 3.2 %collective-permute-done.5.refs_2_ = bf16[16,1408]{1,0:T(8,128)(2,1)S(1)} collective-permute-done((bf16[16,1408]{1,0:T(8,128)(2,1)S(1)}, bf16[16,1408]{1,0:T(8,128)(2,1)S(1)}, u32[]{:S(2)}, u32[]{:S(2)}) %collective-permute-start.5) | collective-permute-done | bytes 45088 | tf_op jit(solution)/shard_map/ppermute | solution.py:454
  167.2 2.4 %collective-permute-done.6.refs_3_ = bf16[16,1408]{1,0:T(8,128)(2,1)S(1)} collective-permute-done((bf16[16,1408]{1,0:T(8,128)(2,1)S(1)}, bf16[16,1408]{1,0:T(8,128)(2,1)S(1)}, u32[]{:S(2)}, u32[]{:S(2)}) %collective-permute-start.6) | collective-permute-done | bytes 45088 | tf_op jit(solution)/shard_map/ppermute | solution.py:454
  170.2 3.8 %collective-permute-start.7 = (bf16[16,1408]{1,0:T(8,128)(2,1)S(1)}, bf16[16,1408]{1,0:T(8,128)(2,1)S(1)}, u32[]{:S(2)}, u32[]{:S(2)}) collective-permute-start(bf16[16,1408]{1,0:T(8,128)(2,1)S(1)} %shard_map.227.refs_0_), channel_id=1, source_target_pairs={{0,2},{1,3},{2,0},{3,1},{4,6},{5,7},{6,4},{7,5},{8,10},{9,11},{10,... | collective-permute-start | bytes 135176 | tf_op jit(solution)/shard_map/ppermute | solution.py:454
  174.0 1.6 collective-permute-done.9.refs_3_
  176.2 1.5 collective-permute-start.12
  177.7 1.2 collective-permute-start.11
  178.9 0.9 collective-permute-start.10
  179.7 3.0 %collective-permute-done.12.refs_3_ = bf16[4,16,1408]{2,1,0:T(8,128)(2,1)S(1)} collective-permute-done((bf16[4,16,1408]{2,1,0:T(8,128)(2,1)S(1)}, bf16[4,16,1408]{2,1,0:T(8,128)(2,1)S(1)}, u32[]{:S(2)}, u32[]{:S(2)}) %collective-permute-start.12) | collective-permute-done | bytes 180256 | tf_op jit(solution)/shard_map/ppermute | solution.py:454
  182.7 1.8 collective-permute-done.11.refs_2_
  185.1 2.0 %reshape.22 = bf16[1,288,1024]{2,1,0:T(8,128)(2,1)} reshape(bf16[8,36,1024]{2,1,0:T(8,128)(2,1)} %all-to-all-done.4) | data formatting | bytes 1179648 | tf_op jit(solution)/shard_map/reshape | solution.py:647
  187.1 1.7 shard_map.229
  (104 shorter events, 15.0 us)
Async XLA Ops:
  0.6 1.9 %copy-start.4 = (bf16[1024,1536]{1,0:T(8,128)(2,1)S(1)}, bf16[1024,1536]{1,0:T(8,128)(2,1)}, u32[]{:S(2)}) copy-start(bf16[1024,1536]{1,0:T(8,128)(2,1)} %w_qkv_ref.2) | copy-start | bytes 9437188
  2.5 1.1 copy-start.5
  3.6 1.6 copy-start.7
  5.2 1.1 copy-start.22
  15.3 49.3 %copy-start.6 = (bf16[1,288,1024]{2,1,0:T(8,128)(2,1)S(1)}, bf16[1,288,1024]{2,1,0:T(8,128)(2,1)}, u32[]{:S(2)}) copy-start(bf16[1,288,1024]{2,1,0:T(8,128)(2,1)} %param.21) | copy-start | bytes 1769476
  15.3 49.3 %copy-start.10 = (bf16[512,1024]{1,0:T(8,128)(2,1)S(1)}, bf16[512,1024]{1,0:T(8,128)(2,1)}, u32[]{:S(2)}) copy-start(bf16[512,1024]{1,0:T(8,128)(2,1)} %w_out_ref.2) | copy-start | bytes 3145732
  15.3 49.3 %copy-start.12 = (bf16[512,768]{1,0:T(8,128)(2,1)S(1)}, bf16[512,768]{1,0:T(8,128)(2,1)}, u32[]{:S(2)}) copy-start(bf16[512,768]{1,0:T(8,128)(2,1)} %w_qkv_ref.3) | copy-start | bytes 2359300
  15.3 49.3 %copy-start.37 = (s32[1,288]{1,0:T(1,128)S(1)}, s32[1,288]{1,0:T(1,128)}, u32[]{:S(2)}) copy-start(s32[1,288]{1,0:T(1,128)} %slots_ref.3) | copy-start | bytes 3460
  15.3 49.3 %copy-start.45 = (bf16[1024]{0:T(1024)(128)(2,1)S(1)}, bf16[1024]{0:T(1024)(128)(2,1)}, u32[]{:S(2)}) copy-start(bf16[1024]{0:T(1024)(128)(2,1)} %out_gain_ref.1) | copy-start | bytes 6148
  15.4 49.3 %copy-start.46 = (s32[1,288]{1,0:T(1,128)S(1)}, s32[1,288]{1,0:T(1,128)}, u32[]{:S(2)}) copy-start(s32[1,288]{1,0:T(1,128)} %owner_ref.1) | copy-start | bytes 3460
  15.4 49.3 %copy-start.47 = (bf16[512]{0:T(512)(128)(2,1)S(1)}, bf16[512]{0:T(512)(128)(2,1)}, u32[]{:S(2)}) copy-start(bf16[512]{0:T(512)(128)(2,1)} %mask_ref.1) | copy-start | bytes 3076
  15.4 49.3 %copy-start.48 = (bf16[512]{0:T(512)(128)(2,1)S(1)}, bf16[512]{0:T(512)(128)(2,1)}, u32[]{:S(2)}) copy-start(bf16[512]{0:T(512)(128)(2,1)} %gain_ref.3) | copy-start | bytes 3076
  15.4 30.5 %all-to-all-start = ((bf16[8,448,128]{2,1,0:T(8,128)(2,1)}), bf16[8,448,128]{2,1,0:T(8,128)(2,1)S(1)}, u32[]{:S(2)}, u32[]{:S(2)}) async-start(bf16[8,448,128]{2,1,0:T(8,128)(2,1)} %get-tuple-element.33), calls=%async_computation | async-start | bytes 1835008 | tf_op jit(solution)/shard_map/all_to_all | solution.py:416
  45.8 18.9 %copy-start.11 = (bf16[1024,512]{1,0:T(8,128)(2,1)S(1)}, bf16[1024,512]{1,0:T(8,128)(2,1)}, u32[]{:S(2)}) copy-start(bf16[1024,512]{1,0:T(8,128)(2,1)} %w_dec_ref.1) | copy-start | bytes 3145732
  45.9 18.9 %copy-start.24 = (bf16[288,1024]{1,0:T(8,128)(2,1)S(1)}, bf16[288,1024]{1,0:T(8,128)(2,1)}, u32[]{:S(2)}) copy-start(bf16[288,1024]{1,0:T(8,128)(2,1)} %copy-done.23) | copy-start | bytes 1769476
  45.9 18.9 %copy-start.25 = (bf16[288,512]{1,0:T(8,128)(2,1)S(1)}, bf16[288,512]{1,0:T(8,128)(2,1)}, u32[]{:S(2)}) copy-start(bf16[288,512]{1,0:T(8,128)(2,1)} %pos_ref.3) | copy-start | bytes 884740
  68.2 15.5 %copy-start.26 = (bf16[288,512]{1,0:T(8,128)(2,1)}, bf16[288,512]{1,0:T(8,128)(2,1)S(1)}, u32[]{:S(2)}) copy-start(bf16[288,512]{1,0:T(8,128)(2,1)S(1)} %get-tuple-element.36.y_ref) | copy-start | bytes 884740
  68.2 15.5 %copy-start.31 = (f32[288,128]{1,0:T(8,128)}, f32[288,128]{1,0:T(8,128)S(1)}, u32[]{:S(2)}) copy-start(f32[288,128]{1,0:T(8,128)S(1)} %get-tuple-element.38.flag_ref) | copy-start | bytes 442372
  83.7 25.5 %copy-start = (bf16[512,2048]{1,0:T(8,128)(2,1)S(1)}, bf16[512,2048]{1,0:T(8,128)(2,1)}, u32[]{:S(2)}) copy-start(bf16[512,2048]{1,0:T(8,128)(2,1)} %w_up_ref.3) | copy-start | bytes 6291460
  83.7 25.5 %copy-start.3 = (bf16[512,1024]{1,0:T(8,128)(2,1)S(1)}, bf16[512,1024]{1,0:T(8,128)(2,1)}, u32[]{:S(2)}) copy-start(bf16[512,1024]{1,0:T(8,128)(2,1)} %w_head_ref.3) | copy-start | bytes 3145732
  83.7 25.5 %copy-start.30 = (bf16[256,512]{1,0:T(8,128)(2,1)S(1)}, bf16[256,512]{1,0:T(8,128)(2,1)}, u32[]{:S(2)}) copy-start(bf16[256,512]{1,0:T(8,128)(2,1)} %w_out_ref.3) | copy-start | bytes 786436
  98.3 10.9 %all-to-all-start.3 = ((bf16[8,72,128]{2,1,0:T(8,128)(2,1)}), bf16[8,72,128]{2,1,0:T(8,128)(2,1)S(1)}, u32[]{:S(2)}, u32[]{:S(2)}) async-start(bf16[8,72,128]{2,1,0:T(8,128)(2,1)} %copy-done.33), calls=%async_computation.3 | async-start | bytes 294912 | tf_op jit(solution)/shard_map/all_to_all | solution.py:416
  109.2 1.6 copy-start.1
  110.8 1.1 copy-start.15
  120.0 1.0 copy-start.8
  126.2 25.0 %all-to-all-start.4 = ((bf16[8,36,1024]{2,1,0:T(8,128)(2,1)}), bf16[8,36,1024]{2,1,0:T(8,128)(2,1)}, u32[]{:S(2)}, u32[]{:S(2)}) async-start(bf16[8,36,1024]{2,1,0:T(8,128)(2,1)} %copy-done.13), calls=%async_computation.4 | async-start | bytes 1310720 | tf_op jit(solution)/shard_map/all_to_all | solution.py:416
  130.6 1.6 copy-start.2
  132.2 1.3 copy-start.9
  133.5 1.1 copy-start.17
  134.6 1.1 copy-start.19
  135.6 1.1 copy-start.21
  145.3 2.3 %collective-permute-start = (bf16[4,4,16,1408]{3,2,1,0:T(8,128)(2,1)S(1)}, bf16[4,4,16,1408]{3,2,1,0:T(8,128)(2,1)S(1)}, u32[]{:S(2)}, u32[]{:S(2)}) collective-permute-start(bf16[4,4,16,1408]{3,2,1,0:T(8,128)(2,1)S(1)} %get-tuple-element.47), channel_id=1, source_target_pairs={{0,8},{1,9},{2,10},{3,11},{4,12},{5,13},{6,14},{7,15},{8,0},{9,1},... | collective-permute-start | bytes 2162696 | tf_op jit(solution)/shard_map/ppermute | solution.py:454
  147.7 7.5 %collective-permute-start.1 = (bf16[4,16,1408]{2,1,0:T(8,128)(2,1)S(1)}, bf16[4,16,1408]{2,1,0:T(8,128)(2,1)S(1)}, u32[]{:S(2)}, u32[]{:S(2)}) collective-permute-start(bf16[4,16,1408]{2,1,0:T(8,128)(2,1)S(1)} %get-tuple-element.52), channel_id=1, source_target_pairs={{0,16},{1,17},{2,18},{3,19},{4,20},{5,21},{6,22},{7,23},{8,24},{9,... | collective-permute-start | bytes 540680 | tf_op jit(solution)/shard_map/ppermute | solution.py:454
  149.2 9.4 %collective-permute-start.2 = (bf16[4,16,1408]{2,1,0:T(8,128)(2,1)S(1)}, bf16[4,16,1408]{2,1,0:T(8,128)(2,1)S(1)}, u32[]{:S(2)}, u32[]{:S(2)}) collective-permute-start(bf16[4,16,1408]{2,1,0:T(8,128)(2,1)S(1)} %get-tuple-element.53), channel_id=1, source_target_pairs={{0,1},{1,0},{2,3},{3,2},{4,5},{5,4},{6,7},{7,6},{8,9},{9,8},{10,11... | collective-permute-start | bytes 540680 | tf_op jit(solution)/shard_map/ppermute | solution.py:454
  151.0 8.5 %collective-permute-start.3 = (bf16[4,16,1408]{2,1,0:T(8,128)(2,1)S(1)}, bf16[4,16,1408]{2,1,0:T(8,128)(2,1)S(1)}, u32[]{:S(2)}, u32[]{:S(2)}) collective-permute-start(bf16[4,16,1408]{2,1,0:T(8,128)(2,1)S(1)} %get-tuple-element.54), channel_id=1, source_target_pairs={{0,17},{1,16},{2,19},{3,18},{4,21},{5,20},{6,23},{7,22},{8,25},{9,... | collective-permute-start | bytes 540680 | tf_op jit(solution)/shard_map/ppermute | solution.py:454
  159.5 4.5 %collective-permute-start.4 = (bf16[16,1408]{1,0:T(8,128)(2,1)S(1)}, bf16[16,1408]{1,0:T(8,128)(2,1)S(1)}, u32[]{:S(2)}, u32[]{:S(2)}) collective-permute-start(bf16[16,1408]{1,0:T(8,128)(2,1)S(1)} %get-tuple-element.56), channel_id=1, source_target_pairs={{0,2},{1,3},{2,0},{3,1},{4,6},{5,7},{6,4},{7,5},{8,10},{9,11},{10,... | collective-permute-start | bytes 135176 | tf_op jit(solution)/shard_map/ppermute | solution.py:454
  161.3 5.8 %collective-permute-start.5 = (bf16[16,1408]{1,0:T(8,128)(2,1)S(1)}, bf16[16,1408]{1,0:T(8,128)(2,1)S(1)}, u32[]{:S(2)}, u32[]{:S(2)}) collective-permute-start(bf16[16,1408]{1,0:T(8,128)(2,1)S(1)} %get-tuple-element.57), channel_id=1, source_target_pairs={{0,4},{1,5},{2,6},{3,7},{4,0},{5,1},{6,2},{7,3},{8,12},{9,13},{10,... | collective-permute-start | bytes 135176 | tf_op jit(solution)/shard_map/ppermute | solution.py:454
  163.7 5.8 %collective-permute-start.6 = (bf16[16,1408]{1,0:T(8,128)(2,1)S(1)}, bf16[16,1408]{1,0:T(8,128)(2,1)S(1)}, u32[]{:S(2)}, u32[]{:S(2)}) collective-permute-start(bf16[16,1408]{1,0:T(8,128)(2,1)S(1)} %get-tuple-element.58), channel_id=1, source_target_pairs={{0,6},{1,7},{2,4},{3,5},{4,2},{5,3},{6,0},{7,1},{8,14},{9,15},{10,... | collective-permute-start | bytes 135176 | tf_op jit(solution)/shard_map/ppermute | solution.py:454
  169.6 6.0 %collective-permute-start.9 = (bf16[16,1408]{1,0:T(8,128)(2,1)S(1)}, bf16[16,1408]{1,0:T(8,128)(2,1)S(1)}, u32[]{:S(2)}, u32[]{:S(2)}) collective-permute-start(bf16[16,1408]{1,0:T(8,128)(2,1)S(1)} %shard_map.227.refs_0_), channel_id=1, source_target_pairs={{0,6},{1,7},{2,4},{3,5},{4,2},{5,3},{6,0},{7,1},{8,14},{9,15},{10,... | collective-permute-start | bytes 135176 | tf_op jit(solution)/shard_map/ppermute | solution.py:454
  170.2 5.9 %collective-permute-start.8 = (bf16[16,1408]{1,0:T(8,128)(2,1)S(1)}, bf16[16,1408]{1,0:T(8,128)(2,1)S(1)}, u32[]{:S(2)}, u32[]{:S(2)}) collective-permute-start(bf16[16,1408]{1,0:T(8,128)(2,1)S(1)} %shard_map.227.refs_0_), channel_id=1, source_target_pairs={{0,4},{1,5},{2,6},{3,7},{4,0},{5,1},{6,2},{7,3},{8,12},{9,13},{10,... | collective-permute-start | bytes 135176 | tf_op jit(solution)/shard_map/ppermute | solution.py:454
  170.2 5.9 %collective-permute-start.7 = (bf16[16,1408]{1,0:T(8,128)(2,1)S(1)}, bf16[16,1408]{1,0:T(8,128)(2,1)S(1)}, u32[]{:S(2)}, u32[]{:S(2)}) collective-permute-start(bf16[16,1408]{1,0:T(8,128)(2,1)S(1)} %shard_map.227.refs_0_), channel_id=1, source_target_pairs={{0,2},{1,3},{2,0},{3,1},{4,6},{5,7},{6,4},{7,5},{8,10},{9,11},{10,... | collective-permute-start | bytes 135176 | tf_op jit(solution)/shard_map/ppermute | solution.py:454
  176.2 6.6 %collective-permute-start.12 = (bf16[4,16,1408]{2,1,0:T(8,128)(2,1)S(1)}, bf16[4,16,1408]{2,1,0:T(8,128)(2,1)S(1)}, u32[]{:S(2)}, u32[]{:S(2)}) collective-permute-start(bf16[4,16,1408]{2,1,0:T(8,128)(2,1)S(1)} %shard_map.228.refs_0_), channel_id=1, source_target_pairs={{0,17},{1,16},{2,19},{3,18},{4,21},{5,20},{6,23},{7,22},{8,25},{9,... | collective-permute-start | bytes 540680 | tf_op jit(solution)/shard_map/ppermute | solution.py:454
  177.7 6.9 %collective-permute-start.11 = (bf16[4,16,1408]{2,1,0:T(8,128)(2,1)S(1)}, bf16[4,16,1408]{2,1,0:T(8,128)(2,1)S(1)}, u32[]{:S(2)}, u32[]{:S(2)}) collective-permute-start(bf16[4,16,1408]{2,1,0:T(8,128)(2,1)S(1)} %shard_map.228.refs_0_), channel_id=1, source_target_pairs={{0,1},{1,0},{2,3},{3,2},{4,5},{5,4},{6,7},{7,6},{8,9},{9,8},{10,11... | collective-permute-start | bytes 540680 | tf_op jit(solution)/shard_map/ppermute | solution.py:454
  178.9 5.7 %collective-permute-start.10 = (bf16[4,16,1408]{2,1,0:T(8,128)(2,1)S(1)}, bf16[4,16,1408]{2,1,0:T(8,128)(2,1)S(1)}, u32[]{:S(2)}, u32[]{:S(2)}) collective-permute-start(bf16[4,16,1408]{2,1,0:T(8,128)(2,1)S(1)} %shard_map.228.refs_0_), channel_id=1, source_target_pairs={{0,16},{1,17},{2,18},{3,19},{4,20},{5,21},{6,22},{7,23},{8,24},{9,... | collective-permute-start | bytes 540680 | tf_op jit(solution)/shard_map/ppermute | solution.py:454
  179.7 7.4 %collective-permute-start.13 = (bf16[4,16,1408]{2,1,0:T(8,128)(2,1)S(1)}, bf16[4,16,1408]{2,1,0:T(8,128)(2,1)S(1)}, u32[]{:S(2)}, u32[]{:S(2)}) collective-permute-start(bf16[4,16,1408]{2,1,0:T(8,128)(2,1)S(1)} %shard_map.228.refs_0_), channel_id=1, source_target_pairs={{0,8},{1,9},{2,10},{3,11},{4,12},{5,13},{6,14},{7,15},{8,0},{9,1},... | collective-permute-start | bytes 540680 | tf_op jit(solution)/shard_map/ppermute | solution.py:454
  182.7 4.4 %collective-permute-start.16 = (bf16[4,16,1408]{2,1,0:T(8,128)(2,1)S(1)}, bf16[4,16,1408]{2,1,0:T(8,128)(2,1)S(1)}, u32[]{:S(2)}, u32[]{:S(2)}) collective-permute-start(bf16[4,16,1408]{2,1,0:T(8,128)(2,1)S(1)} %collective-permute-done.12.refs_3_), channel_id=1, source_target_pairs={{0,8},{1,9},{2,10},{3,11},{4,12},{5,13},{6,14},{7,15},{8,0},{9,1},... | collective-permute-start | bytes 540680 | tf_op jit(solution)/shard_map/ppermute | solution.py:454
  184.6 2.5 %collective-permute-start.15 = (bf16[4,16,1408]{2,1,0:T(8,128)(2,1)S(1)}, bf16[4,16,1408]{2,1,0:T(8,128)(2,1)S(1)}, u32[]{:S(2)}, u32[]{:S(2)}) collective-permute-start(bf16[4,16,1408]{2,1,0:T(8,128)(2,1)S(1)} %collective-permute-done.11.refs_2_), channel_id=1, source_target_pairs={{0,8},{1,9},{2,10},{3,11},{4,12},{5,13},{6,14},{7,15},{8,0},{9,1},... | collective-permute-start | bytes 540680 | tf_op jit(solution)/shard_map/ppermute | solution.py:454
  184.6 2.5 %collective-permute-start.14 = (bf16[4,16,1408]{2,1,0:T(8,128)(2,1)S(1)}, bf16[4,16,1408]{2,1,0:T(8,128)(2,1)S(1)}, u32[]{:S(2)}, u32[]{:S(2)}) collective-permute-start(bf16[4,16,1408]{2,1,0:T(8,128)(2,1)S(1)} %collective-permute-done.10.refs_1_), channel_id=1, source_target_pairs={{0,8},{1,9},{2,10},{3,11},{4,12},{5,13},{6,14},{7,15},{8,0},{9,1},... | collective-permute-start | bytes 540680 | tf_op jit(solution)/shard_map/ppermute | solution.py:454
  (21 other events, 16.0 us)

commit v4 on v3

--- a/solution.py
+++ b/solution.py
@@ -61,8 +61,9 @@
 
 
 def embed_kernel(
-    patch_ref, pos_ref, w_embed_ref, gain_ref, w_qkv_ref, slots_ref,
-    send_ref, tok_ref, normed_ref, qkv_ref,
+    patch_hbm, pos_hbm, w_embed_hbm, gain_ref, w_qkv_hbm, slots_ref,
+    send_ref, tok_ref, normed_ref, qkv_ref, patch_ref, pos_ref, w_embed_ref, w_qkv_ref,
+    patch_sem, pos_sem, embed_sem, qkv_sem,
 ):
     rows, width = patch_ref.shape
     half = rows // 2
@@ -70,19 +71,33 @@
     size = att // HEADS
     tile = 256
 
-    @pl.loop(0, width // tile)
-    def _(step):
-        cols = pl.ds(pl.multiple_of(step * tile, tile), tile)
+    def piece(hbm, buf, sem, step):
+        cols = slice(step * tile, (step + 1) * tile)
+        return pltpu.make_async_copy(hbm.at[:, cols], buf.at[:, cols], sem.at[step])
+
+    embed_copies = [
+        piece(w_embed_hbm, w_embed_ref, embed_sem, i) for i in range(width // tile)
+    ]
+    qkv_copies = [piece(w_qkv_hbm, w_qkv_ref, qkv_sem, i) for i in range(3 * att // tile)]
+    patch_copy = pltpu.make_async_copy(patch_hbm, patch_ref, patch_sem)
+    pos_copy = pltpu.make_async_copy(pos_hbm, pos_ref, pos_sem)
+    for copy in [patch_copy, embed_copies[0], pos_copy, *embed_copies[1:], *qkv_copies]:
+        copy.start()
+    patch_copy.wait()
+    for step in range(width // tile):
+        embed_copies[step].wait()
+        if step == 0:
+            pos_copy.wait()
+        cols = slice(step * tile, (step + 1) * tile)
         tok_ref[:, cols] = (
             dot(patch_ref[...], w_embed_ref[:, cols]) + pos_ref[:, cols].astype(F32)
         ).astype(BF)
 
     normed_ref[...] = layer_norm(tok_ref[...].astype(F32), gain_ref[...]).astype(BF)
     pick = slot_of_row(slots_ref[...]).astype(BF)
-
-    @pl.loop(0, 3 * att // tile)
-    def _(step):
-        cols = pl.ds(pl.multiple_of(step * tile, tile), tile)
+    for step in range(3 * att // tile):
+        qkv_copies[step].wait()
+        cols = slice(step * tile, (step + 1) * tile)
         part = dot(normed_ref[...], w_qkv_ref[:, cols]).astype(BF)
         qkv_ref[:, cols] = lax.dot_general(
             pick, part, (((0,), (0,)), ((), ())), preferred_element_type=F32
@@ -103,7 +118,7 @@
 
 
 def enc_attend_kernel(
-    first_ref, q_ref, kv_ref, out_ref, q_buf, kv_buf, o_buf, *, q_at, kv_at, rows, cap_q, cap_k
+    me_ref, q_ref, kv_ref, out_ref, q_buf, kv_buf, o_buf, *, q_at, kv_at, rows, cap_q, cap_k
 ):
     half = rows // 2
     sources = kv_ref.shape[0]
@@ -141,7 +156,7 @@
         zero = jnp.zeros_like(block)
         q_buf[pl.ds(off, half), :] = jnp.where(lane_h < 64, block, zero)
         q_buf[pl.ds(off + half, half), :] = jnp.where(lane_h < 64, swap_halves(block), zero)
-        off = off + (count_of(first_ref[0] + source) + 15) // 16 * 16
+        off = off + (count_of(me_ref[2] + source) + 15) // 16 * 16
     total = off
 
     tile = 128
@@ -249,10 +264,11 @@
 
 
 def tail_kernel(
-    att_ref, y_ref, w_out_ref, feed_gain_ref, w_up_ref, w_down_ref, head_gain_ref, w_head_ref,
-    target_ref, flag_ref,
-    pred_ref, dec_att_ref, mid_ref, slope_ref, z_ref, zn_ref, dpred_ref, loss_ref, feed_buf, wide_buf,
+    me_ref, att_ref, y_ref, w_out_ref, feed_gain_ref, w_up_ref, w_down_ref, head_gain_ref,
+    w_head_ref, target_ref, flag_ref,
+    dec_att_ref, mid_ref, slope_ref, z_ref, zn_ref, dpred_ref, loss_ref, *refs,
 ):
+    *pred_refs, feed_buf, wide_buf, pred_buf = refs
     rows, width = y_ref.shape
     quarter = rows // 4
     pixels = w_head_ref.shape[1]
@@ -296,9 +312,23 @@
         part = jnp.sum(jnp.sum(err * err, axis=1, keepdims=True), axis=0, keepdims=True)
         loss_ref[...] += part * (1.0 / pixels)
 
-    share = pred_ref.shape[1]
-    for dest in range(pred_ref.shape[0]):
-        pred_ref[dest] = wide_buf[dest * share : (dest + 1) * share, :].astype(BF)
+    share = pred_buf.shape[1]
+    for dest in range(pred_buf.shape[0]):
+        pred_buf[dest] = wide_buf[dest * share : (dest + 1) * share, :].astype(BF)
+    if len(pred_refs) == 1:
+        pred_refs[0][...] = pred_buf[...]
+    else:
+        for index, ref in enumerate(pred_refs):
+            ref[...] = pred_buf[me_ref[1] ^ index]
+
+
+def gather_kernel(me_ref, *refs):
+    *parts, out_ref, buf = refs
+    share = buf.shape[1]
+    for index, ref in enumerate(parts):
+        buf[me_ref[1] ^ index] = ref[...].astype(F32)
+    for device in range(buf.shape[0]):
+        out_ref[device * share : (device + 1) * share, :] = buf[device].astype(BF)
 
 
 def backward_kernel(
@@ -392,9 +422,12 @@
     loss_ref[0, 0] = jnp.max(total) * (1.0 / masked_total)
 
 
-def vmem_call(kernel, outs, scratch, inputs, smem=(), smem_out=(), flops=0):
+def vmem_call(kernel, outs, scratch, inputs, smem=(), smem_out=(), anywhere=(),
+              vmem=VMEM_LIMIT, flops=0):
     space = [
-        pl.BlockSpec(memory_space=pltpu.SMEM if i in smem else pltpu.VMEM)
+        pl.BlockSpec(
+            memory_space=pltpu.SMEM if i in smem else pl.ANY if i in anywhere else pltpu.VMEM
+        )
         for i in range(len(inputs))
     ]
     moved = sum(a.size * a.dtype.itemsize for a in inputs)
@@ -407,7 +440,7 @@
             for i in range(len(outs))
         ],
         scratch_shapes=scratch,
-        compiler_params=pltpu.CompilerParams(vmem_limit_bytes=VMEM_LIMIT),
+        compiler_params=pltpu.CompilerParams(vmem_limit_bytes=vmem),
         cost_estimate=pl.CostEstimate(flops=flops, bytes_accessed=moved, transcendentals=0),
     )(*inputs)
 
@@ -515,7 +548,12 @@
     repeat = groups // HEADS
     teams = [list(range(HEADS * i, HEADS * i + HEADS)) for i in range(repeat)]
     teams = None if repeat == 1 else teams
-    source = patches[0]
+    dp_me, ctx_me = lax.axis_index("dp"), lax.axis_index("ctx")
+    place = dp_me % 2 + 2 * (dp_me // 2) + 4 * (ctx_me % 2) + 8 * (ctx_me // 2)
+    if repeat > 1:
+        place = jnp.zeros_like(place)
+    me = jnp.stack([place, ctx_me, ctx_me // HEADS * HEADS]).astype(jnp.int32)
+    source, me = lax.optimization_barrier((patches[0], me))
     rows, pixels = source.shape
     half, quarter = rows // 2, rows // 4
     share = rows // 3
@@ -526,11 +564,23 @@
     send, tok = vmem_call(
         embed_kernel,
         [shape((HEADS, half + rows + 16, 128), BF), shape((rows, width), BF)],
-        [pltpu.VMEM((rows, width), BF), pltpu.VMEM((rows, w_qkv.shape[1]), BF)],
+        [
+            pltpu.VMEM((rows, width), BF),
+            pltpu.VMEM((rows, w_qkv.shape[1]), BF),
+            pltpu.VMEM(source.shape, BF),
+            pltpu.VMEM(enc_pos.shape, BF),
+            pltpu.VMEM(w_embed.shape, BF),
+            pltpu.VMEM(w_qkv.shape, BF),
+            pltpu.SemaphoreType.DMA,
+            pltpu.SemaphoreType.DMA,
+            pltpu.SemaphoreType.DMA((width // 256,)),
+            pltpu.SemaphoreType.DMA((w_qkv.shape[1] // 256,)),
+        ],
         [source, enc_pos, w_embed, enc_gain, w_qkv, visible_rows],
+        anywhere=(0, 1, 2, 4),
+        vmem=56 << 20,
         flops=2 * rows * width * (pixels + w_qkv.shape[1]),
     )
-    first = (lax.axis_index("ctx") // HEADS * HEADS).astype(jnp.int32).reshape(1)
     if repeat == 1:
         q = kv = swap(send, "ctx")
         q_at, kv_at = 0, half
@@ -550,7 +600,7 @@
             pltpu.VMEM((cap_k + rows, 256), BF),
             pltpu.VMEM((cap_q + rows, 128), BF),
         ],
-        [first, q, kv],
+        [me, q, kv],
         smem=(0,),
         flops=4 * cap_q * cap_k * 128,
     )
@@ -589,10 +639,10 @@
     )
     att = swap(att, "ctx", teams)
     hidden = w_up.shape[1]
-    pred, dec_att, y_mid, slope, z, zn, dpred, loss_part = vmem_call(
+    share_rows = rows // groups
+    dec_att, y_mid, slope, z, zn, dpred, loss_part, *preds = vmem_call(
         tail_kernel,
         [
-            shape((groups, rows // groups, pixels), BF),
             shape((rows, w_dec_out.shape[0]), BF),
             shape((rows, dec_width), F32),
             shape((rows, hidden), BF),
@@ -600,21 +650,26 @@
             shape((rows, dec_width), BF),
             shape((rows, pixels), BF),
             shape((8, 128), F32),
-        ],
-        [pltpu.VMEM((rows, dec_width), BF), pltpu.VMEM((rows, pixels), F32)],
-        [
-            att, y_own, w_dec_out, decoder_feed_gain, w_up, w_down, head_gain, w_head,
+        ]
+        + (
+            [shape((share_rows, pixels), BF)] * groups
+            if repeat == 1
+            else [shape((groups, share_rows, pixels), BF)]
+        ),
+        [
+            pltpu.VMEM((rows, dec_width), BF),
+            pltpu.VMEM((rows, pixels), F32),
+            pltpu.VMEM((groups, share_rows, pixels), BF),
+        ],
+        [
+            me, att, y_own, w_dec_out, decoder_feed_gain, w_up, w_down, head_gain, w_head,
             target, flag,
         ],
+        smem=(0,),
         flops=2 * rows * dec_width * (2 * hidden + pixels),
     )
-    reconstruction = swap(pred, "ctx")
-    dp_me, ctx_me = lax.axis_index("dp"), lax.axis_index("ctx")
     if repeat == 1:
-        me = dp_me % 2 + 2 * (dp_me // 2) + 4 * (ctx_me % 2) + 8 * (ctx_me // 2)
-    else:
-        me = jnp.int32(0)
-    me = me.astype(jnp.int32).reshape(1)
+        preds = [preds[0]] + [across(preds[i], 0, i) for i in range(1, groups)]
     wide = pixels + dec_width // 2 + 128
     keep, send = vmem_call(
         backward_kernel,
@@ -632,9 +687,17 @@
         flops=2 * rows * dec_width * (2 * hidden + 2 * pixels),
     )
     if repeat == 1:
-        ours, theirs, reconstruction = sum_by_permutes(keep, send, reconstruction)
+        ours, theirs, preds = sum_by_permutes(keep, send, preds)
+        (reconstruction,) = vmem_call(
+            gather_kernel,
+            [shape((rows, pixels), BF)],
+            [pltpu.VMEM((groups, share_rows, pixels), F32)],
+            [me, *preds],
+            smem=(0,),
+        )
     else:
         ours, theirs = sum_by_blocks(keep, send, groups)
+        reconstruction = swap(preds[0], "ctx")
     masked_total = lax.axis_size("dp") * (groups * rows - share * groups)
     grad_head, grad_dec_out, loss = vmem_call(
         functools.partial(place_kernel, masked_total=masked_total),

time: 190 us -> 170 us (0.89)
  blocking collectives: 29.3 us -> 70 us
  local copies, waits for them, and re-layouts: 33.4 us -> 0.1 us
  waiting for transfers between devices: 53.4 us -> 23.6 us
  Pallas kernels: 39.9 us -> 47.7 us
  starting transfers between devices: 31.8 us -> 26.6 us
    all_to_all x2 -> x4, blocking collectives: 29.3 us -> 70 us  [swap(): lax.all_to_all(x, axis, split_axis=0, concat_axis=0, tiled=True, axis_ind...]
    unnamed x98 -> x34, local copies, waits for them, and re-layouts: 31.4 us -> 0.1 us
    all_to_all x3 -> x0, waiting for transfers between devices: 30.5 us -> none  [swap(): lax.all_to_all(x, axis, split_axis=0, concat_axis=0, tiled=True, axis_ind...]
    all_to_all x3 -> x0, starting transfers between devices: 15.2 us -> none  [swap(): lax.all_to_all(x, axis, split_axis=0, concat_axis=0, tiled=True, axis_ind...]
    ppermute x17 -> x24, starting transfers between devices: 16.6 us -> 26.6 us  [across(): return lax.ppermute(x, ('dp', 'ctx'), pairs)]
    pallas_call x11 -> x12, Pallas kernels: 39.9 us -> 47.7 us  [vmem_call(): pl.pallas_call(kernel, out_shape=outs, in_specs=space, out_specs=[pl.Bloc...]
    reshape x1 -> x0, local copies, waits for them, and re-layouts: 2.01 us -> none  [on_device(): reconstruction.reshape(1, rows, pixels)]
    ppermute x17 -> x24, waiting for transfers between devices: 22.9 us -> 23.6 us  [across(): return lax.ppermute(x, ('dp', 'ctx'), pairs)]
  transfers between devices with their start and end apart: 20 -> 24, of which waited for: 12 -> 11; matrix products, arithmetic and copies ran while one was open for 1% -> 0% of each run, Pallas kernels for 3% -> 1%
where the time goes in v4:
time: 170 us; the launch traced here: 169 us
  blocking collectives  70 us (41%)
  Pallas kernels  47.7 us (28%)
  starting transfers between devices  26.6 us (16%)
  waiting for transfers between devices  23.6 us (14%)
    all_to_all x4, blocking collectives, swap(): lax.all_to_all(x, axis, split_axis=0, concat_axis=0, tiled=True, axis_ind...  70 us
    pallas_call x12, Pallas kernels, vmem_call(): pl.pallas_call(kernel, out_shape=outs, in_specs=space, out_specs=[pl.Bloc...  47.7 us
    ppermute x24, starting transfers between devices, across(): return lax.ppermute(x, ('dp', 'ctx'), pairs)  26.6 us
    ppermute x24, waiting for transfers between devices, across(): return lax.ppermute(x, ('dp', 'ctx'), pairs)  23.6 us
  transfers between devices with their start and end apart: 24, of which 11 were waited for; matrix products, arithmetic and copies ran while one was open for 0% of the time, Pallas kernels for 1%

profile of v4, /device:TPU:0, one launch (start us, length us, event | category | flops | bytes accessed | tf_op | source)
XLA Modules:
  0.0 169.3 jit_solution(18046118173842333525)
XLA Ops:
  0.7 0.1 pad_add_fusion.me_ref
  0.7 10.9 %shard_map.219 = (bf16[8,448,128]{2,1,0:T(8,128)(2,1)}, bf16[288,1024]{1,0:T(8,128)(2,1)}) custom-call(bf16[288,1024]{1,0:T(8,128)(2,1)} %bitcast.6, bf16[288,1024]{1,0:T(8,128)(2,1)} %pos_hbm.1, bf16[1024,1024]{1,0:T(8,128)(2,1)} %w_embed_hbm.1, bf16[1024]{0:T(1024)(128)(2,1)} %gain_ref.2, bf16[1024,1536]{1,0:T(8,128)(2,1)} %w_qkv_hbm.1, s32[1,288]{1,0:T(1,128)} %slots_ref.3), custom_call_target="tpu_custom_call" | custom-call | flops 1509949440 | bytes 6425728 | tf_op jit(solution)/shard_map/pallas_call | solution.py:434
  11.6 0.0 copy-start.3
  11.6 0.0 copy-start.4
  11.8 30.9 %all_to_all.20.q_ref.kv_ref = bf16[8,448,128]{2,1,0:T(8,128)(2,1)S(1)} all-to-all(bf16[8,448,128]{2,1,0:T(8,128)(2,1)} %get-tuple-element.51), channel_id=1, replica_groups=mesh['dp'=4,'ctx'=8] {'ctx'}, dimensions={0} | all-to-all | bytes 1835008 | tf_op jit(solution)/shard_map/all_to_all | solution.py:449
  42.6 5.5 %shard_map.220 = bf16[8,144,128]{2,1,0:T(8,128)(2,1)S(1)} custom-call(s32[3]{0:T(128)S(1)} %pad_add_fusion.me_ref, bf16[8,448,128]{2,1,0:T(8,128)(2,1)S(1)} %all_to_all.20.q_ref.kv_ref, bf16[8,448,128]{2,1,0:T(8,128)(2,1)S(1)} %all_to_all.20.q_ref.kv_ref), custom_call_target="tpu_custom_call" | custom-call | flops 411041792 | bytes 1835020 | tf_op jit(solution)/shard_map/pallas_call | solution.py:434
  48.1 13.2 %all_to_all.21.att_ref = bf16[8,144,128]{2,1,0:T(8,128)(2,1)S(1)} all-to-all(bf16[8,144,128]{2,1,0:T(8,128)(2,1)S(1)} %shard_map.220), channel_id=1, replica_groups=mesh['dp'=4,'ctx'=8] {'ctx'}, dimensions={0} | all-to-all | bytes 589824 | tf_op jit(solution)/shard_map/all_to_all | solution.py:449
  61.4 2.6 %shard_map.221 = (bf16[8,216,128]{2,1,0:T(8,128)(2,1)S(1)}, bf16[288,512]{1,0:T(8,128)(2,1)S(1)}, bf16[288,1024]{1,0:T(8,128)(2,1)S(1)}, f32[288,128]{1,0:T(8,128)S(1)}) custom-call(bf16[8,144,128]{2,1,0:T(8,128)(2,1)S(1)} %all_to_all.21.att_ref, bf16[288,1024]{1,0:T(8,128)(2,1)S(1)} %copy-done.7, bf16[512,1024]{1,0:T(8,128)(2,1)S(1)} %copy-done.4, ...), custom_call_target="tpu_custom_call" | custom-call | flops 603979776 | bytes 4659456 | tf_op jit(solution)/shard_map/pallas_call | solution.py:434
  64.1 15.3 %all_to_all.22.q_ref.kv_ref = bf16[8,216,128]{2,1,0:T(8,128)(2,1)S(1)} all-to-all(bf16[8,216,128]{2,1,0:T(8,128)(2,1)S(1)} %get-tuple-element.53), channel_id=1, replica_groups=mesh['dp'=4,'ctx'=8] {'ctx'}, dimensions={0} | all-to-all | bytes 884736 | tf_op jit(solution)/shard_map/all_to_all | solution.py:449
  79.4 14.0 %shard_map.222 = bf16[8,72,128]{2,1,0:T(8,128)(2,1)S(1)} custom-call(bf16[8,216,128]{2,1,0:T(8,128)(2,1)S(1)} %all_to_all.22.q_ref.kv_ref, bf16[8,216,128]{2,1,0:T(8,128)(2,1)S(1)} %all_to_all.22.q_ref.kv_ref), custom_call_target="tpu_custom_call" | custom-call | flops 2717908992 | bytes 884736 | tf_op jit(solution)/shard_map/pallas_call | solution.py:434
  93.4 10.7 %all_to_all.23.att_ref = bf16[8,72,128]{2,1,0:T(8,128)(2,1)S(1)} all-to-all(bf16[8,72,128]{2,1,0:T(8,128)(2,1)S(1)} %shard_map.222), channel_id=1, replica_groups=mesh['dp'=4,'ctx'=8] {'ctx'}, dimensions={0} | all-to-all | bytes 294912 | tf_op jit(solution)/shard_map/all_to_all | solution.py:449
  104.1 5.5 %shard_map.223 = (bf16[288,256]{1,0:T(8,128)(2,1)S(1)}, f32[288,512]{1,0:T(8,128)S(1)}, bf16[288,2048]{1,0:T(8,128)(2,1)S(1)}, f32[288,512]{1,0:T(8,128)S(1)}, b...) custom-call(s32[3]{0:T(128)S(1)} %pad_add_fusion.me_ref, ...), custom_call_target="tpu_custom_call" | custom-call | flops 1509949440 | bytes 6686732 | tf_op jit(solution)/shard_map/pallas_call | solution.py:434
  109.5 5.2 %shard_map.224 = (bf16[4,4,16,1408]{3,2,1,0:T(8,128)(2,1)S(1)}, bf16[4,4,16,1408]{3,2,1,0:T(8,128)(2,1)S(1)}) custom-call(s32[3]{0:T(128)S(1)} %pad_add_fusion.me_ref, bf16[288,256]{1,0:T(8,128)(2,1)S(1)} %get-tuple-element.57.dec_att_ref, f32[288,512]{1,0:T(8,128)S(1)} %get-tuple-element.58.mid_ref, bf16[288,2048]{1,0:T(8,128)(2,1)S(1)} %get-tuple-element.59.slope_ref, ...), custom_call_target="tpu_custom_call" | custom-call | flops 1811939328 | bytes 8640524 | tf_op jit(solution)/shard_map/pallas_call | solution.py:434
  114.8 0.1 collective-permute-start
  114.9 0.2 collective-permute-start.1
  115.1 1.2 collective-permute-start.2
  116.2 2.2 %collective-permute-start.3 = (bf16[36,1024]{1,0:T(8,128)(2,1)S(1)}, bf16[36,1024]{1,0:T(8,128)(2,1)S(1)}, u32[]{:S(2)}, u32[]{:S(2)}) collective-permute-start(bf16[36,1024]{1,0:T(8,128)(2,1)S(1)} %get-tuple-element.70), channel_id=1, source_target_pairs={{0,3},{1,2},{2,1},{3,0},{4,7},{5,6},{6,5},{7,4},{8,11},{9,10},{10,... | collective-permute-start | bytes 221192 | tf_op jit(solution)/shard_map/ppermute | solution.py:487
  118.4 0.2 shard_map.225
  118.6 1.6 collective-permute-start.8
  120.1 0.2 collective-permute-start.9
  120.3 1.8 %collective-permute-start.10 = (bf16[4,16,1408]{2,1,0:T(8,128)(2,1)S(1)}, bf16[4,16,1408]{2,1,0:T(8,128)(2,1)S(1)}, u32[]{:S(2)}, u32[]{:S(2)}) collective-permute-start(bf16[4,16,1408]{2,1,0:T(8,128)(2,1)S(1)} %get-tuple-element.86), channel_id=1, source_target_pairs={{0,17},{1,16},{2,19},{3,18},{4,21},{5,20},{6,23},{7,22},{8,25},{9,... | collective-permute-start | bytes 540680 | tf_op jit(solution)/shard_map/ppermute | solution.py:487
  122.1 0.4 collective-permute-start.4
  122.5 0.2 collective-permute-done.3.refs_3_
  122.7 2.3 %collective-permute-start.5 = (bf16[36,1024]{1,0:T(8,128)(2,1)S(1)}, bf16[36,1024]{1,0:T(8,128)(2,1)S(1)}, u32[]{:S(2)}, u32[]{:S(2)}) collective-permute-start(bf16[36,1024]{1,0:T(8,128)(2,1)S(1)} %get-tuple-element.72), channel_id=1, source_target_pairs={{0,5},{1,4},{2,7},{3,6},{4,1},{5,0},{6,3},{7,2},{8,13},{9,12},{10,... | collective-permute-start | bytes 221192 | tf_op jit(solution)/shard_map/ppermute | solution.py:487
  125.0 4.8 %collective-permute-done.4.refs_4_ = bf16[36,1024]{1,0:T(8,128)(2,1)S(1)} collective-permute-done((bf16[36,1024]{1,0:T(8,128)(2,1)S(1)}, bf16[36,1024]{1,0:T(8,128)(2,1)S(1)}, u32[]{:S(2)}, u32[]{:S(2)}) %collective-permute-start.4) | collective-permute-done | bytes 73760 | tf_op jit(solution)/shard_map/ppermute | solution.py:487
  129.8 1.7 collective-permute-start.6
  131.5 2.1 %collective-permute-done.5.refs_5_ = bf16[36,1024]{1,0:T(8,128)(2,1)S(1)} collective-permute-done((bf16[36,1024]{1,0:T(8,128)(2,1)S(1)}, bf16[36,1024]{1,0:T(8,128)(2,1)S(1)}, u32[]{:S(2)}, u32[]{:S(2)}) %collective-permute-start.5) | collective-permute-done | bytes 73760 | tf_op jit(solution)/shard_map/ppermute | solution.py:487
  133.5 2.1 %collective-permute-start.7 = (bf16[36,1024]{1,0:T(8,128)(2,1)S(1)}, bf16[36,1024]{1,0:T(8,128)(2,1)S(1)}, u32[]{:S(2)}, u32[]{:S(2)}) collective-permute-start(bf16[36,1024]{1,0:T(8,128)(2,1)S(1)} %get-tuple-element.74), channel_id=1, source_target_pairs={{0,7},{1,6},{2,5},{3,4},{4,3},{5,2},{6,1},{7,0},{8,15},{9,14},{10,... | collective-permute-start | bytes 221192 | tf_op jit(solution)/shard_map/ppermute | solution.py:487
  135.6 0.4 collective-permute-done.6.refs_6_
  136.0 4.9 %collective-permute-done.7.refs_7_ = bf16[36,1024]{1,0:T(8,128)(2,1)S(1)} collective-permute-done((bf16[36,1024]{1,0:T(8,128)(2,1)S(1)}, bf16[36,1024]{1,0:T(8,128)(2,1)S(1)}, u32[]{:S(2)}, u32[]{:S(2)}) %collective-permute-start.7) | collective-permute-done | bytes 73760 | tf_op jit(solution)/shard_map/ppermute | solution.py:487
  141.0 0.1 shard_map.227
  141.1 0.1 collective-permute-start.11
  141.2 1.5 collective-permute-start.12
  142.6 2.9 %collective-permute-start.13 = (bf16[16,1408]{1,0:T(8,128)(2,1)S(1)}, bf16[16,1408]{1,0:T(8,128)(2,1)S(1)}, u32[]{:S(2)}, u32[]{:S(2)}) collective-permute-start(bf16[16,1408]{1,0:T(8,128)(2,1)S(1)} %get-tuple-element.90), channel_id=1, source_target_pairs={{0,6},{1,7},{2,4},{3,5},{4,2},{5,3},{6,0},{7,1},{8,14},{9,15},{10,... | collective-permute-start | bytes 135176 | tf_op jit(solution)/shard_map/ppermute | solution.py:487
  145.5 0.6 collective-permute-done.12.refs_2_
  146.2 2.3 %collective-permute-done.13.refs_3_ = bf16[16,1408]{1,0:T(8,128)(2,1)S(1)} collective-permute-done((bf16[16,1408]{1,0:T(8,128)(2,1)S(1)}, bf16[16,1408]{1,0:T(8,128)(2,1)S(1)}, u32[]{:S(2)}, u32[]{:S(2)}) %collective-permute-start.13) | collective-permute-done | bytes 45088 | tf_op jit(solution)/shard_map/ppermute | solution.py:487
  148.5 3.0 %collective-permute-start.16 = (bf16[16,1408]{1,0:T(8,128)(2,1)S(1)}, bf16[16,1408]{1,0:T(8,128)(2,1)S(1)}, u32[]{:S(2)}, u32[]{:S(2)}) collective-permute-start(bf16[16,1408]{1,0:T(8,128)(2,1)S(1)} %shard_map.228.refs_0_), channel_id=1, source_target_pairs={{0,6},{1,7},{2,4},{3,5},{4,2},{5,3},{6,0},{7,1},{8,14},{9,15},{10,... | collective-permute-start | bytes 135176 | tf_op jit(solution)/shard_map/ppermute | solution.py:487
  151.5 1.4 collective-permute-start.14
  153.0 1.5 collective-permute-done.16.refs_3_
  154.4 2.0 %collective-permute-done.15.refs_2_ = bf16[16,1408]{1,0:T(8,128)(2,1)S(1)} collective-permute-done((bf16[16,1408]{1,0:T(8,128)(2,1)S(1)}, bf16[16,1408]{1,0:T(8,128)(2,1)S(1)}, u32[]{:S(2)}, u32[]{:S(2)}) %collective-permute-start.15) | collective-permute-done | bytes 45088 | tf_op jit(solution)/shard_map/ppermute | solution.py:487
  156.5 0.9 collective-permute-start.19
  157.4 1.3 collective-permute-start.18
  158.7 1.3 collective-permute-start.17
  160.0 3.0 %collective-permute-done.19.refs_3_ = bf16[4,16,1408]{2,1,0:T(8,128)(2,1)S(1)} collective-permute-done((bf16[4,16,1408]{2,1,0:T(8,128)(2,1)S(1)}, bf16[4,16,1408]{2,1,0:T(8,128)(2,1)S(1)}, u32[]{:S(2)}, u32[]{:S(2)}) %collective-permute-start.19) | collective-permute-done | bytes 180256 | tf_op jit(solution)/shard_map/ppermute | solution.py:487
  163.1 1.8 %collective-permute-done.18.refs_2_ = bf16[4,16,1408]{2,1,0:T(8,128)(2,1)S(1)} collective-permute-done((bf16[4,16,1408]{2,1,0:T(8,128)(2,1)S(1)}, bf16[4,16,1408]{2,1,0:T(8,128)(2,1)S(1)}, u32[]{:S(2)}, u32[]{:S(2)}) %collective-permute-start.18) | collective-permute-done | bytes 180256 | tf_op jit(solution)/shard_map/ppermute | solution.py:487
  164.9 0.5 collective-permute-start.21
  165.4 1.5 shard_map.226
  166.9 2.2 %shard_map.230 = (f32[512,1024]{1,0:T(8,128)}, f32[256,512]{1,0:T(8,128)}, f32[1,1]{1,0:T(1,128)}) custom-call(s32[3]{0:T(128)S(1)} %pad_add_fusion.me_ref, bf16[4,16,1408]{2,1,0:T(8,128)(2,1)S(1)} %shard_map.229.refs_0_, bf16[4,16,1408]{2,1,0:T(8,128)(2,1)S(1)} %collective-permute-done.17.refs_1_, bf16[4,16,1408]{2,1,0:T(8,128)(2,1)S(1)} %collective-permute-done.18.refs_2_, ...), custom_call_target="tpu_custom_call" | custom-call | bytes 1441804 | tf_op jit(solution)/shard_map/pallas_call | solution.py:434
  (51 shorter events, 0.2 us)
Async XLA Ops:
  11.6 49.7 %copy-start.3 = (bf16[1,288,1024]{2,1,0:T(8,128)(2,1)S(1)}, bf16[1,288,1024]{2,1,0:T(8,128)(2,1)}, u32[]{:S(2)}) copy-start(bf16[1,288,1024]{2,1,0:T(8,128)(2,1)} %param.21) | copy-start | bytes 1769476
  11.6 49.7 %copy-start.4 = (bf16[512,1024]{1,0:T(8,128)(2,1)S(1)}, bf16[512,1024]{1,0:T(8,128)(2,1)}, u32[]{:S(2)}) copy-start(bf16[512,1024]{1,0:T(8,128)(2,1)} %w_out_ref.2) | copy-start | bytes 3145732
  11.7 49.7 %copy-start.5 = (bf16[1024,512]{1,0:T(8,128)(2,1)S(1)}, bf16[1024,512]{1,0:T(8,128)(2,1)}, u32[]{:S(2)}) copy-start(bf16[1024,512]{1,0:T(8,128)(2,1)} %w_dec_ref.1) | copy-start | bytes 3145732
  11.7 49.7 %copy-start.6 = (bf16[512,768]{1,0:T(8,128)(2,1)S(1)}, bf16[512,768]{1,0:T(8,128)(2,1)}, u32[]{:S(2)}) copy-start(bf16[512,768]{1,0:T(8,128)(2,1)} %w_qkv_ref.1) | copy-start | bytes 2359300
  11.7 49.7 %copy-start.7 = (bf16[288,1024]{1,0:T(8,128)(2,1)S(1)}, bf16[288,1024]{1,0:T(8,128)(2,1)}, u32[]{:S(2)}) copy-start(bf16[288,1024]{1,0:T(8,128)(2,1)} %get-tuple-element.52.tok_ref) | copy-start | bytes 1769476
  11.7 49.7 %copy-start.8 = (bf16[288,512]{1,0:T(8,128)(2,1)S(1)}, bf16[288,512]{1,0:T(8,128)(2,1)}, u32[]{:S(2)}) copy-start(bf16[288,512]{1,0:T(8,128)(2,1)} %pos_ref.1) | copy-start | bytes 884740
  11.7 49.7 %copy-start.10 = (s32[1,288]{1,0:T(1,128)S(1)}, s32[1,288]{1,0:T(1,128)}, u32[]{:S(2)}) copy-start(s32[1,288]{1,0:T(1,128)} %slots_ref.3) | copy-start | bytes 3460
  11.7 49.7 %copy-start.13 = (bf16[1024]{0:T(1024)(128)(2,1)S(1)}, bf16[1024]{0:T(1024)(128)(2,1)}, u32[]{:S(2)}) copy-start(bf16[1024]{0:T(1024)(128)(2,1)} %out_gain_ref.1) | copy-start | bytes 6148
  11.7 49.7 %copy-start.14 = (s32[1,288]{1,0:T(1,128)S(1)}, s32[1,288]{1,0:T(1,128)}, u32[]{:S(2)}) copy-start(s32[1,288]{1,0:T(1,128)} %owner_ref.1) | copy-start | bytes 3460
  11.7 49.7 %copy-start.15 = (bf16[512]{0:T(512)(128)(2,1)S(1)}, bf16[512]{0:T(512)(128)(2,1)}, u32[]{:S(2)}) copy-start(bf16[512]{0:T(512)(128)(2,1)} %mask_ref.1) | copy-start | bytes 3076
  11.8 49.7 %copy-start.16 = (bf16[512]{0:T(512)(128)(2,1)S(1)}, bf16[512]{0:T(512)(128)(2,1)}, u32[]{:S(2)}) copy-start(bf16[512]{0:T(512)(128)(2,1)} %gain_ref.3) | copy-start | bytes 3076
  79.3 24.7 %copy-start = (bf16[512,2048]{1,0:T(8,128)(2,1)S(1)}, bf16[512,2048]{1,0:T(8,128)(2,1)}, u32[]{:S(2)}) copy-start(bf16[512,2048]{1,0:T(8,128)(2,1)} %w_up_ref.3) | copy-start | bytes 6291460
  79.4 24.7 %copy-start.1 = (bf16[2048,512]{1,0:T(8,128)(2,1)S(1)}, bf16[2048,512]{1,0:T(8,128)(2,1)}, u32[]{:S(2)}) copy-start(bf16[2048,512]{1,0:T(8,128)(2,1)} %w_down_ref.3) | copy-start | bytes 6291460
  79.4 24.7 %copy-start.2 = (bf16[512,1024]{1,0:T(8,128)(2,1)S(1)}, bf16[512,1024]{1,0:T(8,128)(2,1)}, u32[]{:S(2)}) copy-start(bf16[512,1024]{1,0:T(8,128)(2,1)} %w_head_ref.3) | copy-start | bytes 3145732
  79.4 24.7 %copy-start.9 = (bf16[256,512]{1,0:T(8,128)(2,1)S(1)}, bf16[256,512]{1,0:T(8,128)(2,1)}, u32[]{:S(2)}) copy-start(bf16[256,512]{1,0:T(8,128)(2,1)} %w_out_ref.3) | copy-start | bytes 786436
  79.4 24.7 %copy-start.11 = (bf16[512]{0:T(512)(128)(2,1)S(1)}, bf16[512]{0:T(512)(128)(2,1)}, u32[]{:S(2)}) copy-start(bf16[512]{0:T(512)(128)(2,1)} %feed_gain_ref.3) | copy-start | bytes 3076
  79.4 24.7 %copy-start.12 = (bf16[512]{0:T(512)(128)(2,1)S(1)}, bf16[512]{0:T(512)(128)(2,1)}, u32[]{:S(2)}) copy-start(bf16[512]{0:T(512)(128)(2,1)} %head_gain_ref.3) | copy-start | bytes 3076
  114.8 3.6 %collective-permute-start = (bf16[4,4,16,1408]{3,2,1,0:T(8,128)(2,1)S(1)}, bf16[4,4,16,1408]{3,2,1,0:T(8,128)(2,1)S(1)}, u32[]{:S(2)}, u32[]{:S(2)}) collective-permute-start(bf16[4,4,16,1408]{3,2,1,0:T(8,128)(2,1)S(1)} %get-tuple-element.65), channel_id=1, source_target_pairs={{0,8},{1,9},{2,10},{3,11},{4,12},{5,13},{6,14},{7,15},{8,0},{9,1},... | collective-permute-start | bytes 2162696 | tf_op jit(solution)/shard_map/ppermute | solution.py:487
  114.9 5.5 %collective-permute-start.1 = (bf16[36,1024]{1,0:T(8,128)(2,1)S(1)}, bf16[36,1024]{1,0:T(8,128)(2,1)S(1)}, u32[]{:S(2)}, u32[]{:S(2)}) collective-permute-start(bf16[36,1024]{1,0:T(8,128)(2,1)S(1)} %get-tuple-element.68), channel_id=1, source_target_pairs={{0,1},{1,0},{2,3},{3,2},{4,5},{5,4},{6,7},{7,6},{8,9},{9,8},{10,11... | collective-permute-start | bytes 221192 | tf_op jit(solution)/shard_map/ppermute | solution.py:487
  115.1 7.1 %collective-permute-start.2 = (bf16[36,1024]{1,0:T(8,128)(2,1)S(1)}, bf16[36,1024]{1,0:T(8,128)(2,1)S(1)}, u32[]{:S(2)}, u32[]{:S(2)}) collective-permute-start(bf16[36,1024]{1,0:T(8,128)(2,1)S(1)} %get-tuple-element.69), channel_id=1, source_target_pairs={{0,2},{1,3},{2,0},{3,1},{4,6},{5,7},{6,4},{7,5},{8,10},{9,11},{10,... | collective-permute-start | bytes 221192 | tf_op jit(solution)/shard_map/ppermute | solution.py:487
  116.2 6.5 %collective-permute-start.3 = (bf16[36,1024]{1,0:T(8,128)(2,1)S(1)}, bf16[36,1024]{1,0:T(8,128)(2,1)S(1)}, u32[]{:S(2)}, u32[]{:S(2)}) collective-permute-start(bf16[36,1024]{1,0:T(8,128)(2,1)S(1)} %get-tuple-element.70), channel_id=1, source_target_pairs={{0,3},{1,2},{2,1},{3,0},{4,7},{5,6},{6,5},{7,4},{8,11},{9,10},{10,... | collective-permute-start | bytes 221192 | tf_op jit(solution)/shard_map/ppermute | solution.py:487
  118.6 22.4 %collective-permute-start.8 = (bf16[4,16,1408]{2,1,0:T(8,128)(2,1)S(1)}, bf16[4,16,1408]{2,1,0:T(8,128)(2,1)S(1)}, u32[]{:S(2)}, u32[]{:S(2)}) collective-permute-start(bf16[4,16,1408]{2,1,0:T(8,128)(2,1)S(1)} %get-tuple-element.84), channel_id=1, source_target_pairs={{0,16},{1,17},{2,18},{3,19},{4,20},{5,21},{6,22},{7,23},{8,24},{9,... | collective-permute-start | bytes 540680 | tf_op jit(solution)/shard_map/ppermute | solution.py:487
  120.1 20.8 %collective-permute-start.9 = (bf16[4,16,1408]{2,1,0:T(8,128)(2,1)S(1)}, bf16[4,16,1408]{2,1,0:T(8,128)(2,1)S(1)}, u32[]{:S(2)}, u32[]{:S(2)}) collective-permute-start(bf16[4,16,1408]{2,1,0:T(8,128)(2,1)S(1)} %get-tuple-element.85), channel_id=1, source_target_pairs={{0,1},{1,0},{2,3},{3,2},{4,5},{5,4},{6,7},{7,6},{8,9},{9,8},{10,11... | collective-permute-start | bytes 540680 | tf_op jit(solution)/shard_map/ppermute | solution.py:487
  120.3 20.7 %collective-permute-start.10 = (bf16[4,16,1408]{2,1,0:T(8,128)(2,1)S(1)}, bf16[4,16,1408]{2,1,0:T(8,128)(2,1)S(1)}, u32[]{:S(2)}, u32[]{:S(2)}) collective-permute-start(bf16[4,16,1408]{2,1,0:T(8,128)(2,1)S(1)} %get-tuple-element.86), channel_id=1, source_target_pairs={{0,17},{1,16},{2,19},{3,18},{4,21},{5,20},{6,23},{7,22},{8,25},{9,... | collective-permute-start | bytes 540680 | tf_op jit(solution)/shard_map/ppermute | solution.py:487
  122.1 7.7 %collective-permute-start.4 = (bf16[36,1024]{1,0:T(8,128)(2,1)S(1)}, bf16[36,1024]{1,0:T(8,128)(2,1)S(1)}, u32[]{:S(2)}, u32[]{:S(2)}) collective-permute-start(bf16[36,1024]{1,0:T(8,128)(2,1)S(1)} %get-tuple-element.71), channel_id=1, source_target_pairs={{0,4},{1,5},{2,6},{3,7},{4,0},{5,1},{6,2},{7,3},{8,12},{9,13},{10,... | collective-permute-start | bytes 221192 | tf_op jit(solution)/shard_map/ppermute | solution.py:487
  122.7 10.8 %collective-permute-start.5 = (bf16[36,1024]{1,0:T(8,128)(2,1)S(1)}, bf16[36,1024]{1,0:T(8,128)(2,1)S(1)}, u32[]{:S(2)}, u32[]{:S(2)}) collective-permute-start(bf16[36,1024]{1,0:T(8,128)(2,1)S(1)} %get-tuple-element.72), channel_id=1, source_target_pairs={{0,5},{1,4},{2,7},{3,6},{4,1},{5,0},{6,3},{7,2},{8,13},{9,12},{10,... | collective-permute-start | bytes 221192 | tf_op jit(solution)/shard_map/ppermute | solution.py:487
  129.8 6.2 %collective-permute-start.6 = (bf16[36,1024]{1,0:T(8,128)(2,1)S(1)}, bf16[36,1024]{1,0:T(8,128)(2,1)S(1)}, u32[]{:S(2)}, u32[]{:S(2)}) collective-permute-start(bf16[36,1024]{1,0:T(8,128)(2,1)S(1)} %get-tuple-element.73), channel_id=1, source_target_pairs={{0,6},{1,7},{2,4},{3,5},{4,2},{5,3},{6,0},{7,1},{8,14},{9,15},{10,... | collective-permute-start | bytes 221192 | tf_op jit(solution)/shard_map/ppermute | solution.py:487
  133.5 7.4 %collective-permute-start.7 = (bf16[36,1024]{1,0:T(8,128)(2,1)S(1)}, bf16[36,1024]{1,0:T(8,128)(2,1)S(1)}, u32[]{:S(2)}, u32[]{:S(2)}) collective-permute-start(bf16[36,1024]{1,0:T(8,128)(2,1)S(1)} %get-tuple-element.74), channel_id=1, source_target_pairs={{0,7},{1,6},{2,5},{3,4},{4,3},{5,2},{6,1},{7,0},{8,15},{9,14},{10,... | collective-permute-start | bytes 221192 | tf_op jit(solution)/shard_map/ppermute | solution.py:487
  141.1 4.5 %collective-permute-start.11 = (bf16[16,1408]{1,0:T(8,128)(2,1)S(1)}, bf16[16,1408]{1,0:T(8,128)(2,1)S(1)}, u32[]{:S(2)}, u32[]{:S(2)}) collective-permute-start(bf16[16,1408]{1,0:T(8,128)(2,1)S(1)} %get-tuple-element.88), channel_id=1, source_target_pairs={{0,2},{1,3},{2,0},{3,1},{4,6},{5,7},{6,4},{7,5},{8,10},{9,11},{10,... | collective-permute-start | bytes 135176 | tf_op jit(solution)/shard_map/ppermute | solution.py:487
  141.2 5.0 %collective-permute-start.12 = (bf16[16,1408]{1,0:T(8,128)(2,1)S(1)}, bf16[16,1408]{1,0:T(8,128)(2,1)S(1)}, u32[]{:S(2)}, u32[]{:S(2)}) collective-permute-start(bf16[16,1408]{1,0:T(8,128)(2,1)S(1)} %get-tuple-element.89), channel_id=1, source_target_pairs={{0,4},{1,5},{2,6},{3,7},{4,0},{5,1},{6,2},{7,3},{8,12},{9,13},{10,... | collective-permute-start | bytes 135176 | tf_op jit(solution)/shard_map/ppermute | solution.py:487
  142.6 5.8 %collective-permute-start.13 = (bf16[16,1408]{1,0:T(8,128)(2,1)S(1)}, bf16[16,1408]{1,0:T(8,128)(2,1)S(1)}, u32[]{:S(2)}, u32[]{:S(2)}) collective-permute-start(bf16[16,1408]{1,0:T(8,128)(2,1)S(1)} %get-tuple-element.90), channel_id=1, source_target_pairs={{0,6},{1,7},{2,4},{3,5},{4,2},{5,3},{6,0},{7,1},{8,14},{9,15},{10,... | collective-permute-start | bytes 135176 | tf_op jit(solution)/shard_map/ppermute | solution.py:487
  148.5 5.9 %collective-permute-start.16 = (bf16[16,1408]{1,0:T(8,128)(2,1)S(1)}, bf16[16,1408]{1,0:T(8,128)(2,1)S(1)}, u32[]{:S(2)}, u32[]{:S(2)}) collective-permute-start(bf16[16,1408]{1,0:T(8,128)(2,1)S(1)} %shard_map.228.refs_0_), channel_id=1, source_target_pairs={{0,6},{1,7},{2,4},{3,5},{4,2},{5,3},{6,0},{7,1},{8,14},{9,15},{10,... | collective-permute-start | bytes 135176 | tf_op jit(solution)/shard_map/ppermute | solution.py:487
  151.5 4.9 %collective-permute-start.15 = (bf16[16,1408]{1,0:T(8,128)(2,1)S(1)}, bf16[16,1408]{1,0:T(8,128)(2,1)S(1)}, u32[]{:S(2)}, u32[]{:S(2)}) collective-permute-start(bf16[16,1408]{1,0:T(8,128)(2,1)S(1)} %shard_map.228.refs_0_), channel_id=1, source_target_pairs={{0,4},{1,5},{2,6},{3,7},{4,0},{5,1},{6,2},{7,3},{8,12},{9,13},{10,... | collective-permute-start | bytes 135176 | tf_op jit(solution)/shard_map/ppermute | solution.py:487
  151.5 4.9 %collective-permute-start.14 = (bf16[16,1408]{1,0:T(8,128)(2,1)S(1)}, bf16[16,1408]{1,0:T(8,128)(2,1)S(1)}, u32[]{:S(2)}, u32[]{:S(2)}) collective-permute-start(bf16[16,1408]{1,0:T(8,128)(2,1)S(1)} %shard_map.228.refs_0_), channel_id=1, source_target_pairs={{0,2},{1,3},{2,0},{3,1},{4,6},{5,7},{6,4},{7,5},{8,10},{9,11},{10,... | collective-permute-start | bytes 135176 | tf_op jit(solution)/shard_map/ppermute | solution.py:487
  156.5 6.6 %collective-permute-start.19 = (bf16[4,16,1408]{2,1,0:T(8,128)(2,1)S(1)}, bf16[4,16,1408]{2,1,0:T(8,128)(2,1)S(1)}, u32[]{:S(2)}, u32[]{:S(2)}) collective-permute-start(bf16[4,16,1408]{2,1,0:T(8,128)(2,1)S(1)} %shard_map.229.refs_0_), channel_id=1, source_target_pairs={{0,17},{1,16},{2,19},{3,18},{4,21},{5,20},{6,23},{7,22},{8,25},{9,... | collective-permute-start | bytes 540680 | tf_op jit(solution)/shard_map/ppermute | solution.py:487
  157.4 7.4 %collective-permute-start.18 = (bf16[4,16,1408]{2,1,0:T(8,128)(2,1)S(1)}, bf16[4,16,1408]{2,1,0:T(8,128)(2,1)S(1)}, u32[]{:S(2)}, u32[]{:S(2)}) collective-permute-start(bf16[4,16,1408]{2,1,0:T(8,128)(2,1)S(1)} %shard_map.229.refs_0_), channel_id=1, source_target_pairs={{0,1},{1,0},{2,3},{3,2},{4,5},{5,4},{6,7},{7,6},{8,9},{9,8},{10,11... | collective-permute-start | bytes 540680 | tf_op jit(solution)/shard_map/ppermute | solution.py:487
  158.7 6.2 %collective-permute-start.17 = (bf16[4,16,1408]{2,1,0:T(8,128)(2,1)S(1)}, bf16[4,16,1408]{2,1,0:T(8,128)(2,1)S(1)}, u32[]{:S(2)}, u32[]{:S(2)}) collective-permute-start(bf16[4,16,1408]{2,1,0:T(8,128)(2,1)S(1)} %shard_map.229.refs_0_), channel_id=1, source_target_pairs={{0,16},{1,17},{2,18},{3,19},{4,20},{5,21},{6,22},{7,23},{8,24},{9,... | collective-permute-start | bytes 540680 | tf_op jit(solution)/shard_map/ppermute | solution.py:487
  160.0 6.8 %collective-permute-start.20 = (bf16[4,16,1408]{2,1,0:T(8,128)(2,1)S(1)}, bf16[4,16,1408]{2,1,0:T(8,128)(2,1)S(1)}, u32[]{:S(2)}, u32[]{:S(2)}) collective-permute-start(bf16[4,16,1408]{2,1,0:T(8,128)(2,1)S(1)} %shard_map.229.refs_0_), channel_id=1, source_target_pairs={{0,8},{1,9},{2,10},{3,11},{4,12},{5,13},{6,14},{7,15},{8,0},{9,1},... | collective-permute-start | bytes 540680 | tf_op jit(solution)/shard_map/ppermute | solution.py:487
  163.0 3.8 %collective-permute-start.23 = (bf16[4,16,1408]{2,1,0:T(8,128)(2,1)S(1)}, bf16[4,16,1408]{2,1,0:T(8,128)(2,1)S(1)}, u32[]{:S(2)}, u32[]{:S(2)}) collective-permute-start(bf16[4,16,1408]{2,1,0:T(8,128)(2,1)S(1)} %collective-permute-done.19.refs_3_), channel_id=1, source_target_pairs={{0,8},{1,9},{2,10},{3,11},{4,12},{5,13},{6,14},{7,15},{8,0},{9,1},... | collective-permute-start | bytes 540680 | tf_op jit(solution)/shard_map/ppermute | solution.py:487
  164.8 2.0 %collective-permute-start.22 = (bf16[4,16,1408]{2,1,0:T(8,128)(2,1)S(1)}, bf16[4,16,1408]{2,1,0:T(8,128)(2,1)S(1)}, u32[]{:S(2)}, u32[]{:S(2)}) collective-permute-start(bf16[4,16,1408]{2,1,0:T(8,128)(2,1)S(1)} %collective-permute-done.18.refs_2_), channel_id=1, source_target_pairs={{0,8},{1,9},{2,10},{3,11},{4,12},{5,13},{6,14},{7,15},{8,0},{9,1},... | collective-permute-start | bytes 540680 | tf_op jit(solution)/shard_map/ppermute | solution.py:487
  164.9 2.0 %collective-permute-start.21 = (bf16[4,16,1408]{2,1,0:T(8,128)(2,1)S(1)}, bf16[4,16,1408]{2,1,0:T(8,128)(2,1)S(1)}, u32[]{:S(2)}, u32[]{:S(2)}) collective-permute-start(bf16[4,16,1408]{2,1,0:T(8,128)(2,1)S(1)} %collective-permute-done.17.refs_1_), channel_id=1, source_target_pairs={{0,8},{1,9},{2,10},{3,11},{4,12},{5,13},{6,14},{7,15},{8,0},{9,1},... | collective-permute-start | bytes 540680 | tf_op jit(solution)/shard_map/ppermute | solution.py:487

commit v5 on v4

--- a/solution.py
+++ b/solution.py
@@ -93,15 +93,15 @@
             dot(patch_ref[...], w_embed_ref[:, cols]) + pos_ref[:, cols].astype(F32)
         ).astype(BF)
 
-    normed_ref[...] = layer_norm(tok_ref[...].astype(F32), gain_ref[...]).astype(BF)
     pick = slot_of_row(slots_ref[...]).astype(BF)
+    normed = layer_norm(tok_ref[...].astype(F32), gain_ref[...]).astype(BF)
+    normed_ref[...] = lax.dot_general(
+        pick, normed, (((0,), (0,)), ((), ())), preferred_element_type=F32
+    ).astype(BF)
     for step in range(3 * att // tile):
         qkv_copies[step].wait()
         cols = slice(step * tile, (step + 1) * tile)
-        part = dot(normed_ref[...], w_qkv_ref[:, cols]).astype(BF)
-        qkv_ref[:, cols] = lax.dot_general(
-            pick, part, (((0,), (0,)), ((), ())), preferred_element_type=F32
-        ).astype(BF)
+        qkv_ref[:, cols] = dot(normed_ref[...], w_qkv_ref[:, cols]).astype(BF)
 
     count = jnp.sum(jnp.where(slots_ref[...] >= 0, 1.0, 0.0), axis=1, keepdims=True)
     high = jnp.floor(count * (1.0 / 16))
@@ -248,29 +248,40 @@
     lane = lax.broadcasted_iota(jnp.int32, (quarter, 128), 1)
     zone = [(lane >= 32 * i) & (lane < 32 * i + 32) for i in range(4)]
 
-    @pl.loop(0, HEADS)
-    def _(source):
+    chunk = 256
+    unroll = 4 if sources == HEADS else 1
+
+    def attend(source):
         block = q_ref[source, q_at : q_at + quarter, :].astype(F32)
         q = jnp.concatenate([jnp.where(z, block, 0.0) for z in zone], axis=0).astype(BF)
-        score = dot_t(q, k_buf[...])
-        top = jnp.max(score, axis=1, keepdims=True)
-        weight = jnp.exp2((score - top) * scale).astype(BF)
-        mixed = dot(weight, v_buf[...])
+        top = mixed = None
+        for at in range(0, k_buf.shape[0], chunk):
+            score = dot_t(q, k_buf[at : at + chunk, :])
+            peak = jnp.max(score, axis=1, keepdims=True)
+            new = peak if top is None else jnp.maximum(top, peak)
+            weight = jnp.exp2((score - new) * scale).astype(BF)
+            part = dot(weight, v_buf[at : at + chunk, :])
+            mixed = part if top is None else mixed * jnp.exp2((top - new) * scale) + part
+            top = new
         mixed = mixed[:, :128] / mixed[:, 128:]
         out = mixed[:quarter]
         for i in range(1, 4):
             out = jnp.where(zone[i], mixed[i * quarter : (i + 1) * quarter], out)
         out_ref[source] = out.astype(BF)
 
+    @pl.loop(0, HEADS // unroll)
+    def _(step):
+        for i in range(unroll):
+            attend(step * unroll + i)
+
 
 def tail_kernel(
     me_ref, att_ref, y_ref, w_out_ref, feed_gain_ref, w_up_ref, w_down_ref, head_gain_ref,
     w_head_ref, target_ref, flag_ref,
-    dec_att_ref, mid_ref, slope_ref, z_ref, zn_ref, dpred_ref, loss_ref, *refs,
+    dec_att_ref, mid_ref, slope_ref, z_ref, dpred_ref, loss_ref, keep_ref, send_ref, *refs,
 ):
-    *pred_refs, feed_buf, wide_buf, pred_buf = refs
+    *zn_refs, feed_buf, zn_buf, split_buf, head_buf = refs
     rows, width = y_ref.shape
-    quarter = rows // 4
     pixels = w_head_ref.shape[1]
     hidden = w_up_ref.shape[1]
     blocks = [att_ref[head].astype(F32) for head in range(HEADS)]
@@ -286,10 +297,8 @@
     z_ref[...] = mid_ref[...]
     tile = 512
     c = math.sqrt(2.0 / math.pi)
-
-    @pl.loop(0, hidden // tile)
-    def _(step):
-        cols = pl.ds(pl.multiple_of(step * tile, tile), tile)
+    for at in range(0, hidden, tile):
+        cols = slice(at, at + tile)
         pre = dot(feed_buf[...], w_up_ref[:, cols])
         square = pre * pre
         t = jnp.tanh(pre * (c + (c * 0.044715) * square))
@@ -298,92 +307,106 @@
         slope_ref[:, cols] = slope.astype(BF)
         z_ref[...] += dot((pre * gate).astype(BF), w_down_ref[cols, :])
 
-    zn_ref[...] = layer_norm(z_ref[...], head_gain_ref[...]).astype(BF)
+    zn = layer_norm(z_ref[...], head_gain_ref[...])
+    zn_buf[...] = zn.astype(BF)
+    share = split_buf.shape[1]
+    for dest in range(split_buf.shape[0]):
+        split_buf[dest] = zn[dest * share : (dest + 1) * share, :].astype(BF)
+    if len(zn_refs) == 1:
+        zn_refs[0][...] = split_buf[...]
+    else:
+        for index in range(2 * zn_refs[0].shape[0]):
+            zn_refs[index % 2][index // 2] = split_buf[me_ref[1] ^ index]
     flag = flag_ref[:, :1]
-    loss_ref[...] = jnp.zeros_like(loss_ref)
-
-    @pl.loop(0, pixels // tile)
-    def _(step):
-        cols = pl.ds(pl.multiple_of(step * tile, tile), tile)
-        pred = dot(zn_ref[...], w_head_ref[:, cols])
-        wide_buf[:, cols] = pred
+    loss = jnp.zeros((1, 1), F32)
+    for at in range(0, pixels, tile):
+        cols = slice(at, at + tile)
+        pred = dot(zn_buf[...], w_head_ref[:, cols])
         err = (pred - target_ref[:, cols].astype(F32)) * flag
         dpred_ref[:, cols] = (err * (2.0 / pixels)).astype(BF)
-        part = jnp.sum(jnp.sum(err * err, axis=1, keepdims=True), axis=0, keepdims=True)
-        loss_ref[...] += part * (1.0 / pixels)
-
-    share = pred_buf.shape[1]
-    for dest in range(pred_buf.shape[0]):
-        pred_buf[dest] = wide_buf[dest * share : (dest + 1) * share, :].astype(BF)
-    if len(pred_refs) == 1:
-        pred_refs[0][...] = pred_buf[...]
-    else:
-        for index, ref in enumerate(pred_refs):
-            ref[...] = pred_buf[me_ref[1] ^ index]
-
-
-def gather_kernel(me_ref, *refs):
-    *parts, out_ref, buf = refs
-    share = buf.shape[1]
-    for index, ref in enumerate(parts):
-        buf[me_ref[1] ^ index] = ref[...].astype(F32)
-    for device in range(buf.shape[0]):
-        out_ref[device * share : (device + 1) * share, :] = buf[device].astype(BF)
+        loss += jnp.sum(jnp.sum(err * err, axis=1, keepdims=True), axis=0, keepdims=True)
+        head_buf[:, cols] = lax.dot_general(
+            zn_buf[...], dpred_ref[:, cols], (((0,), (0,)), ((), ())), preferred_element_type=F32
+        )
+    loss_ref[...] = jnp.broadcast_to(loss * (1.0 / pixels), loss_ref.shape)
+    tall = width // 32
+    for index in range(32):
+        at = pl.multiple_of((index ^ me_ref[0]) * tall, tall)
+        ref = send_ref if index % 2 else keep_ref
+        ref[index // 2 % 4, index // 8] = head_buf[pl.ds(at, tall), :].astype(BF)
+
+
+def gather_kernel(me_ref, w_head_ref, *refs, places):
+    *parts, out_ref, split_buf, zn_buf = refs
+    share = split_buf.shape[1]
+    for ref, indices in zip(parts, places):
+        for i, index in enumerate(indices):
+            split_buf[me_ref[3] ^ index] = ref[i].astype(F32)
+    zn_buf[...] = jnp.concatenate(
+        [split_buf[device] for device in range(split_buf.shape[0])], axis=0
+    ).astype(BF)
+    tile = 512
+    for at in range(0, w_head_ref.shape[1], tile):
+        cols = slice(at, at + tile)
+        out_ref[:, cols] = dot(zn_buf[...], w_head_ref[:, cols]).astype(BF)
+
+
+def head_back_kernel(dpred_ref, z_ref, head_gain_ref, w_head_ref, dz_ref):
+    dz_ref[...] = norm_backward(
+        z_ref[...], head_gain_ref[...], dot_t(dpred_ref[...], w_head_ref[...])
+    ).astype(BF)
 
 
 def backward_kernel(
-    me_ref, dec_att_ref, mid_ref, slope_ref, z_ref, zn_ref, dpred_ref, loss_ref,
-    feed_gain_ref, w_up_ref, w_down_ref, head_gain_ref, w_head_ref,
-    keep_ref, send_ref, back_buf, head_buf, out_buf,
+    me_ref, dec_att_ref, mid_ref, slope_ref, dz_ref, loss_ref, feed_gain_ref, w_up_ref, w_down_ref,
+    keep_ref, send_ref, back_buf, out_buf,
 ):
     hidden = w_up_ref.shape[1]
-    width, pixels = w_head_ref.shape
-    dz = norm_backward(
-        z_ref[...], head_gain_ref[...], dot_t(dpred_ref[...], w_head_ref[...])
-    ).astype(BF)
-    back_buf[...] = jnp.zeros_like(back_buf)
+    dz = dz_ref[...]
     tile = 512
-
-    @pl.loop(0, hidden // tile)
-    def _(step):
-        cols = pl.ds(pl.multiple_of(step * tile, tile), tile)
+    for at in range(0, hidden, tile):
+        cols = slice(at, at + tile)
         back = dot_t(dz, w_down_ref[cols, :]) * slope_ref[:, cols].astype(F32)
-        back_buf[...] += dot_t(back.astype(BF), w_up_ref[:, cols])
+        part = dot_t(back.astype(BF), w_up_ref[:, cols])
+        back_buf[...] = part if at == 0 else back_buf[...] + part
 
     mid_grad = (
         dz.astype(F32) + norm_backward(mid_ref[...], feed_gain_ref[...], back_buf[...])
     ).astype(BF)
-    first = (((0,), (0,)), ((), ()))
     out_buf[...] = lax.dot_general(
-        dec_att_ref[...], mid_grad, first, preferred_element_type=F32
-    )
-
-    @pl.loop(0, pixels // tile)
-    def _(step):
-        cols = pl.ds(pl.multiple_of(step * tile, tile), tile)
-        head_buf[:, cols] = lax.dot_general(
-            zn_ref[...], dpred_ref[:, cols], first, preferred_element_type=F32
-        )
-
-    loss = jnp.broadcast_to(loss_ref[:1, :], (8, 128))
+        dec_att_ref[...], mid_grad, (((0,), (0,)), ((), ())), preferred_element_type=F32
+    )
+    loss = loss_ref[...]
     high = loss.astype(BF)
     low = (loss - high.astype(F32)).astype(BF)
     sums = jnp.concatenate([high.astype(F32), low.astype(F32)], axis=0).astype(BF)
     deep = out_buf.shape[0] // 32
     half = out_buf.shape[1] // 2
-    tall = width // 32
     for index in range(32):
-        block = index ^ me_ref[0]
+        at = pl.multiple_of((index ^ me_ref[0]) * deep, deep)
         ref = send_ref if index % 2 else keep_ref
         xy, z = index // 2 % 4, index // 8
-        ref[xy, z, :, :pixels] = head_buf[
-            pl.ds(pl.multiple_of(block * tall, tall), tall), :
-        ].astype(BF)
-        part = out_buf[pl.ds(pl.multiple_of(block * deep, deep), deep), :]
-        ref[xy, z, :, pixels : pixels + half] = jnp.concatenate(
-            [part[:, :half], part[:, half:]], axis=0
-        ).astype(BF)
-        ref[xy, z, :, pixels + half :] = sums
+        part = out_buf[pl.ds(at, deep), :]
+        ref[xy, z, :, :half] = jnp.concatenate([part[:, :half], part[:, half:]], axis=0).astype(BF)
+        ref[xy, z, :, half:] = sums
+
+
+def pair_kernel(keep_ref, got_ref, mine_ref, other_ref, *refs):
+    total = (keep_ref[...].astype(F32) + got_ref[...].astype(F32)).astype(BF)
+    for i in range(4):
+        refs[i][...] = total[i]
+    for i in range(1, 4):
+        refs[3 + i][0] = mine_ref[i]
+        refs[3 + i][1] = other_ref[i]
+
+
+def merge_kernel(*refs):
+    head = sum(ref[...].astype(F32) for ref in refs[:4]).astype(BF)
+    out = sum(ref[...].astype(F32) for ref in refs[4:8]).astype(BF)
+    pixels = head.shape[2]
+    for i, ref in enumerate(refs[8:]):
+        ref[:, :pixels] = head[i]
+        ref[:, pixels:] = out[i]
 
 
 def add_kernel(*refs, count):
@@ -491,23 +514,44 @@
 COLUMN = ((0, 2), (0, 4), (0, 6))
 
 
-def sum_by_permutes(keep, send, ahead):
+def sum_by_permutes(head_keep, head_send, zn_keep, zn_send, head_back, backward):
     shape = jax.ShapeDtypeStruct
-    add = lambda parts, outs: vmem_call(
-        functools.partial(add_kernel, count=len(parts)), outs, [], parts
-    )
-    part, block = shape(keep.shape[1:], BF), shape(keep.shape[2:], BF)
-    parts = add([keep, across(send, 1, 0)], [part] * 4)
-    others = [across(p, *bits) for p, bits in zip(parts[1:], PLANE)]
-    first, ahead = lax.optimization_barrier((parts[0], ahead))
-    blocks = add([first, *others], [block] * 4)
+    head_got = across(head_send, 1, 0)
+    zn_got = across(zn_send, 0, 1)
+    dz = head_back()
+    heads = vmem_call(
+        functools.partial(add_kernel, count=2),
+        [shape(head_keep.shape[1:], BF)] * 4,
+        [],
+        [head_keep, head_got],
+    )
+    mine, dz = lax.optimization_barrier((heads[0], dz))
+    heads = [mine] + [across(p, *bits) for p, bits in zip(heads[1:], PLANE)]
+    out_keep, out_send = backward(dz)
+    out_got = across(out_send, 1, 0)
+    *outs, zn1, zn2, zn3 = vmem_call(
+        pair_kernel,
+        [shape(out_keep.shape[1:], BF)] * 4 + [shape((2, *zn_keep.shape[1:]), BF)] * 3,
+        [],
+        [out_keep, out_got, zn_keep, zn_got],
+    )
+    outs = [outs[0]] + [across(p, *bits) for p, bits in zip(outs[1:], PLANE)]
+    rest = [across(p, *bits) for p, bits in zip((zn1, zn2, zn3), COLUMN)]
+    block = shape((head_keep.shape[2], head_keep.shape[3] + out_keep.shape[3]), BF)
+    blocks = vmem_call(merge_kernel, [block] * 4, [], [*heads, *outs])
     others = [across(b, *bits) for b, bits in zip(blocks[1:], COLUMN)]
-    (total,) = add([blocks[0], *others], [block])
+    (total,) = vmem_call(
+        functools.partial(add_kernel, count=4), [block], [], [blocks[0], *others]
+    )
+    total, *rest = lax.optimization_barrier((total, *rest))
     (column,) = vmem_call(
-        join_kernel, [part], [], [total] + [across(total, *bits) for bits in COLUMN]
+        join_kernel,
+        [shape((4, *block.shape), BF)],
+        [],
+        [total] + [across(total, *bits) for bits in COLUMN],
     )
     ours = [column] + [across(column, *bits) for bits in PLANE]
-    return ours, [across(x, 1, 0) for x in ours], ahead
+    return ours, [across(x, 1, 0) for x in ours], [zn_keep, zn_got, *rest]
 
 
 def sum_by_blocks(keep, send, groups):
@@ -552,7 +596,9 @@
     place = dp_me % 2 + 2 * (dp_me // 2) + 4 * (ctx_me % 2) + 8 * (ctx_me // 2)
     if repeat > 1:
         place = jnp.zeros_like(place)
-    me = jnp.stack([place, ctx_me, ctx_me // HEADS * HEADS]).astype(jnp.int32)
+    me = jnp.stack(
+        [place, ctx_me, ctx_me // HEADS * HEADS, ctx_me if repeat == 1 else place]
+    ).astype(jnp.int32)
     source, me = lax.optimization_barrier((patches[0], me))
     rows, pixels = source.shape
     half, quarter = rows // 2, rows // 4
@@ -640,64 +686,76 @@
     att = swap(att, "ctx", teams)
     hidden = w_up.shape[1]
     share_rows = rows // groups
-    dec_att, y_mid, slope, z, zn, dpred, loss_part, *preds = vmem_call(
+    tall = dec_width // 32
+    split = (groups, share_rows, dec_width)
+    dec_att, y_mid, slope, z, dpred, loss_part, head_keep, head_send, *zn = vmem_call(
         tail_kernel,
         [
             shape((rows, w_dec_out.shape[0]), BF),
             shape((rows, dec_width), F32),
             shape((rows, hidden), BF),
             shape((rows, dec_width), F32),
-            shape((rows, dec_width), BF),
             shape((rows, pixels), BF),
             shape((8, 128), F32),
         ]
-        + (
-            [shape((share_rows, pixels), BF)] * groups
-            if repeat == 1
-            else [shape((groups, share_rows, pixels), BF)]
-        ),
+        + [shape((4, 4, tall, pixels), BF)] * 2
+        + ([shape((4, *split[1:]), BF)] * 2 if repeat == 1 else [shape(split, BF)]),
         [
             pltpu.VMEM((rows, dec_width), BF),
-            pltpu.VMEM((rows, pixels), F32),
-            pltpu.VMEM((groups, share_rows, pixels), BF),
+            pltpu.VMEM((rows, dec_width), BF),
+            pltpu.VMEM(split, BF),
+            pltpu.VMEM((dec_width, pixels), F32),
         ],
         [
             me, att, y_own, w_dec_out, decoder_feed_gain, w_up, w_down, head_gain, w_head,
             target, flag,
         ],
         smem=(0,),
-        flops=2 * rows * dec_width * (2 * hidden + pixels),
-    )
+        flops=2 * rows * dec_width * (2 * hidden + 2 * pixels),
+    )
+
+    def head_back():
+        return vmem_call(
+            head_back_kernel,
+            [shape((rows, dec_width), BF)],
+            [],
+            [dpred, z, head_gain, w_head],
+            flops=2 * rows * dec_width * pixels,
+        )[0]
+
+    def backward(dz):
+        return vmem_call(
+            backward_kernel,
+            [shape((4, 4, tall, dec_width // 2 + 128), BF)] * 2,
+            [
+                pltpu.VMEM((rows, dec_width), F32),
+                pltpu.VMEM((w_dec_out.shape[0], dec_width), F32),
+            ],
+            [me, dec_att, y_mid, slope, dz, loss_part, decoder_feed_gain, w_up, w_down],
+            smem=(0,),
+            flops=40 * rows * dec_width * hidden,
+        )
+
     if repeat == 1:
-        preds = [preds[0]] + [across(preds[i], 0, i) for i in range(1, groups)]
-    wide = pixels + dec_width // 2 + 128
-    keep, send = vmem_call(
-        backward_kernel,
-        [shape((4, 4, dec_width // 32, wide), BF)] * 2,
-        [
-            pltpu.VMEM((rows, dec_width), F32),
-            pltpu.VMEM((dec_width, pixels), F32),
-            pltpu.VMEM((w_dec_out.shape[0], dec_width), F32),
-        ],
-        [
-            me, dec_att, y_mid, slope, z, zn, dpred, loss_part, decoder_feed_gain,
-            w_up, w_down, head_gain, w_head,
-        ],
+        ours, theirs, zn = sum_by_permutes(head_keep, head_send, *zn, head_back, backward)
+        places = [(0,), (1,), (2, 3), (4, 5), (6, 7)]
+    else:
+        out_keep, out_send = backward(head_back())
+        ours, theirs = sum_by_blocks(
+            jnp.concatenate([head_keep, out_keep], axis=3),
+            jnp.concatenate([head_send, out_send], axis=3),
+            groups,
+        )
+        zn = [swap(zn[0], "ctx")]
+        places = [tuple(range(groups))]
+    (reconstruction,) = vmem_call(
+        functools.partial(gather_kernel, places=places),
+        [shape((rows, pixels), BF)],
+        [pltpu.VMEM(split, F32), pltpu.VMEM((rows, dec_width), BF)],
+        [me, w_head, *zn],
         smem=(0,),
-        flops=2 * rows * dec_width * (2 * hidden + 2 * pixels),
-    )
-    if repeat == 1:
-        ours, theirs, preds = sum_by_permutes(keep, send, preds)
-        (reconstruction,) = vmem_call(
-            gather_kernel,
-            [shape((rows, pixels), BF)],
-            [pltpu.VMEM((groups, share_rows, pixels), F32)],
-            [me, *preds],
-            smem=(0,),
-        )
-    else:
-        ours, theirs = sum_by_blocks(keep, send, groups)
-        reconstruction = swap(preds[0], "ctx")
+        flops=2 * rows * dec_width * pixels,
+    )
     masked_total = lax.axis_size("dp") * (groups * rows - share * groups)
     grad_head, grad_dec_out, loss = vmem_call(
         functools.partial(place_kernel, masked_total=masked_total),

time: 170 us -> 156 us (0.918)
  Pallas kernels: 47.7 us -> 38.2 us
  starting transfers between devices: 26.6 us -> 24 us
    pallas_call x12 -> x14, Pallas kernels: 47.7 us -> 38.2 us  [vmem_call(): pl.pallas_call(kernel, out_shape=outs, in_specs=space, out_specs=[pl.Bloc...]
    ppermute x24 -> x25, starting transfers between devices: 26.6 us -> 24 us  [across(): return lax.ppermute(x, ('dp', 'ctx'), pairs)]
    ppermute x24 -> x25, waiting for transfers between devices: 23.6 us -> 22.2 us  [across(): return lax.ppermute(x, ('dp', 'ctx'), pairs)]
  transfers between devices with their start and end apart: 24 -> 25, of which waited for: 11 -> 11; matrix products, arithmetic and copies ran while one was open for 0% -> 0% of each run, Pallas kernels for 1% -> 2%
where the time goes in v5:
time: 156 us
  blocking collectives  70 us (45%)
  Pallas kernels  38.2 us (24%)
  starting transfers between devices  24 us (15%)
  waiting for transfers between devices  22.2 us (14%)
    all_to_all x4, blocking collectives, swap(): lax.all_to_all(x, axis, split_axis=0, concat_axis=0, tiled=True, axis_ind...  70 us
    pallas_call x14, Pallas kernels, vmem_call(): pl.pallas_call(kernel, out_shape=outs, in_specs=space, out_specs=[pl.Bloc...  38.2 us
    ppermute x25, starting transfers between devices, across(): return lax.ppermute(x, ('dp', 'ctx'), pairs)  24 us
    ppermute x25, waiting for transfers between devices, across(): return lax.ppermute(x, ('dp', 'ctx'), pairs)  22.2 us
  transfers between devices with their start and end apart: 25, of which 11 were waited for; matrix products, arithmetic and copies ran while one was open for 0% of the time, Pallas kernels for 2%

profile of v5, /device:TPU:0, one launch (start us, length us, event | category | flops | bytes accessed | tf_op | source)
XLA Modules:
  0.0 155.8 jit_solution(2952936811072435922)
XLA Ops:
  0.7 0.1 pad_add_fusion.me_ref
  0.8 9.7 %shard_map.219 = (bf16[8,448,128]{2,1,0:T(8,128)(2,1)}, bf16[288,1024]{1,0:T(8,128)(2,1)}) custom-call(bf16[288,1024]{1,0:T(8,128)(2,1)} %bitcast.6, bf16[288,1024]{1,0:T(8,128)(2,1)} %pos_hbm.1, bf16[1024,1024]{1,0:T(8,128)(2,1)} %w_embed_hbm.1, bf16[1024]{0:T(1024)(128)(2,1)} %gain_ref.2, bf16[1024,1536]{1,0:T(8,128)(2,1)} %w_qkv_hbm.1, s32[1,288]{1,0:T(1,128)} %slots_ref.3), custom_call_target="tpu_custom_call" | custom-call | flops 1509949440 | bytes 6425728 | tf_op jit(solution)/shard_map/pallas_call | solution.py:457
  10.6 30.9 %all_to_all.20.q_ref.kv_ref = bf16[8,448,128]{2,1,0:T(8,128)(2,1)S(1)} all-to-all(bf16[8,448,128]{2,1,0:T(8,128)(2,1)} %get-tuple-element.50), channel_id=1, replica_groups=mesh['dp'=4,'ctx'=8] {'ctx'}, dimensions={0} | all-to-all | bytes 1835008 | tf_op jit(solution)/shard_map/all_to_all | solution.py:472
  41.5 5.5 %shard_map.220 = bf16[8,144,128]{2,1,0:T(8,128)(2,1)S(1)} custom-call(s32[4]{0:T(128)S(1)} %pad_add_fusion.me_ref, bf16[8,448,128]{2,1,0:T(8,128)(2,1)S(1)} %all_to_all.20.q_ref.kv_ref, bf16[8,448,128]{2,1,0:T(8,128)(2,1)S(1)} %all_to_all.20.q_ref.kv_ref), custom_call_target="tpu_custom_call" | custom-call | flops 411041792 | bytes 1835024 | tf_op jit(solution)/shard_map/pallas_call | solution.py:457
  47.0 13.2 %all_to_all.21.att_ref = bf16[8,144,128]{2,1,0:T(8,128)(2,1)S(1)} all-to-all(bf16[8,144,128]{2,1,0:T(8,128)(2,1)S(1)} %shard_map.220), channel_id=1, replica_groups=mesh['dp'=4,'ctx'=8] {'ctx'}, dimensions={0} | all-to-all | bytes 589824 | tf_op jit(solution)/shard_map/all_to_all | solution.py:472
  60.2 2.6 %shard_map.221 = (bf16[8,216,128]{2,1,0:T(8,128)(2,1)S(1)}, bf16[288,512]{1,0:T(8,128)(2,1)S(1)}, bf16[288,1024]{1,0:T(8,128)(2,1)S(1)}, f32[288,128]{1,0:T(8,128)S(1)}) custom-call(bf16[8,144,128]{2,1,0:T(8,128)(2,1)S(1)} %all_to_all.21.att_ref, bf16[288,1024]{1,0:T(8,128)(2,1)S(1)} %copy-done.5, bf16[512,1024]{1,0:T(8,128)(2,1)S(1)} %copy-done.2, ...), custom_call_target="tpu_custom_call" | custom-call | flops 603979776 | bytes 4659456 | tf_op jit(solution)/shard_map/pallas_call | solution.py:457
  62.9 15.3 %all_to_all.22.q_ref.kv_ref = bf16[8,216,128]{2,1,0:T(8,128)(2,1)S(1)} all-to-all(bf16[8,216,128]{2,1,0:T(8,128)(2,1)S(1)} %get-tuple-element.52), channel_id=1, replica_groups=mesh['dp'=4,'ctx'=8] {'ctx'}, dimensions={0} | all-to-all | bytes 884736 | tf_op jit(solution)/shard_map/all_to_all | solution.py:472
  78.2 7.7 %shard_map.222 = bf16[8,72,128]{2,1,0:T(8,128)(2,1)S(1)} custom-call(bf16[8,216,128]{2,1,0:T(8,128)(2,1)S(1)} %all_to_all.22.q_ref.kv_ref, bf16[8,216,128]{2,1,0:T(8,128)(2,1)S(1)} %all_to_all.22.q_ref.kv_ref), custom_call_target="tpu_custom_call" | custom-call | flops 2717908992 | bytes 884736 | tf_op jit(solution)/shard_map/pallas_call | solution.py:457
  85.9 10.7 %all_to_all.23.att_ref = bf16[8,72,128]{2,1,0:T(8,128)(2,1)S(1)} all-to-all(bf16[8,72,128]{2,1,0:T(8,128)(2,1)S(1)} %shard_map.222), channel_id=1, replica_groups=mesh['dp'=4,'ctx'=8] {'ctx'}, dimensions={0} | all-to-all | bytes 294912 | tf_op jit(solution)/shard_map/all_to_all | solution.py:472
  96.7 5.0 %shard_map.223 = (bf16[288,256]{1,0:T(8,128)(2,1)S(1)}, f32[288,512]{1,0:T(8,128)S(1)}, bf16[288,2048]{1,0:T(8,128)(2,1)S(1)}, f32[288,512]{1,0:T(8,128)S(1)}, b...) custom-call(s32[4]{0:T(128)S(1)} %pad_add_fusion.me_ref, ...), custom_call_target="tpu_custom_call" | custom-call | flops 1811939328 | bytes 6686736 | tf_op jit(solution)/shard_map/pallas_call | solution.py:457
  101.6 0.1 collective-permute-start.1
  101.7 0.6 shard_map.225.dz_ref
  102.4 1.3 collective-permute-done.1.refs_1_
  103.6 0.1 shard_map.224
  103.7 2.7 %shard_map.226 = (bf16[4,4,16,384]{3,2,1,0:T(8,128)(2,1)S(1)}, bf16[4,4,16,384]{3,2,1,0:T(8,128)(2,1)S(1)}) custom-call(s32[4]{0:T(128)S(1)} %pad_add_fusion.me_ref, bf16[288,256]{1,0:T(8,128)(2,1)S(1)} %get-tuple-element.67.dec_att_ref, f32[288,512]{1,0:T(8,128)S(1)} %get-tuple-element.68.mid_ref, bf16[288,2048]{1,0:T(8,128)(2,1)S(1)} %get-tuple-element.69.slope_ref, ...), custom_call_target="tpu_custom_call" | custom-call | flops 12079595520 | bytes 6411280 | tf_op jit(solution)/shard_map/pallas_call | solution.py:457
  106.4 0.2 collective-permute-start.5
  106.6 0.2 collective-permute-start
  106.8 1.5 collective-permute-start.2
  108.3 1.9 %collective-permute-start.3 = (bf16[4,16,1024]{2,1,0:T(8,128)(2,1)S(1)}, bf16[4,16,1024]{2,1,0:T(8,128)(2,1)S(1)}, u32[]{:S(2)}, u32[]{:S(2)}) collective-permute-start(bf16[4,16,1024]{2,1,0:T(8,128)(2,1)S(1)} %get-tuple-element.65), channel_id=1, source_target_pairs={{0,1},{1,0},{2,3},{3,2},{4,5},{5,4},{6,7},{7,6},{8,9},{9,8},{10,11... | collective-permute-start | bytes 393224 | tf_op jit(solution)/shard_map/ppermute | solution.py:510
  110.2 0.1 collective-permute-start.4
  110.3 3.7 %collective-permute-done.other_ref.refs_1_ = bf16[4,36,512]{2,1,0:T(8,128)(2,1)S(1)} collective-permute-done((bf16[4,36,512]{2,1,0:T(8,128)(2,1)S(1)}, bf16[4,36,512]{2,1,0:T(8,128)(2,1)S(1)}, u32[]{:S(2)}, u32[]{:S(2)}) %collective-permute-start) | collective-permute-done | bytes 147488 | tf_op jit(solution)/shard_map/ppermute | solution.py:510
  114.1 2.1 %collective-permute-start.6 = (bf16[4,16,384]{2,1,0:T(8,128)(2,1)S(1)}, bf16[4,16,384]{2,1,0:T(8,128)(2,1)S(1)}, u32[]{:S(2)}, u32[]{:S(2)}) collective-permute-start(bf16[4,16,384]{2,1,0:T(8,128)(2,1)S(1)} %get-tuple-element.75), channel_id=1, source_target_pairs={{0,16},{1,17},{2,18},{3,19},{4,20},{5,21},{6,22},{7,23},{8,24},{9,... | collective-permute-start | bytes 147464 | tf_op jit(solution)/shard_map/ppermute | solution.py:510
  116.2 1.5 collective-permute-start.8
  117.7 2.1 %collective-permute-done.3.refs_2_ = bf16[4,16,1024]{2,1,0:T(8,128)(2,1)S(1)} collective-permute-done((bf16[4,16,1024]{2,1,0:T(8,128)(2,1)S(1)}, bf16[4,16,1024]{2,1,0:T(8,128)(2,1)S(1)}, u32[]{:S(2)}, u32[]{:S(2)}) %collective-permute-start.3) | collective-permute-done | bytes 131104 | tf_op jit(solution)/shard_map/ppermute | solution.py:510
  119.8 0.5 collective-permute-done.7.refs_6_
  120.3 0.9 collective-permute-done.8.refs_7_
  121.2 0.1 shard_map.228
  121.3 1.4 collective-permute-start.9
  122.7 0.7 collective-permute-start.12
  123.4 0.4 collective-permute-start.13
  123.7 3.3 %collective-permute-start.14 = (bf16[2,36,512]{2,1,0:T(8,128)(2,1)S(1)}, bf16[2,36,512]{2,1,0:T(8,128)(2,1)S(1)}, u32[]{:S(2)}, u32[]{:S(2)}) collective-permute-start(bf16[2,36,512]{2,1,0:T(8,128)(2,1)S(1)} %get-tuple-element.84), channel_id=1, source_target_pairs={{0,6},{1,7},{2,4},{3,5},{4,2},{5,3},{6,0},{7,1},{8,14},{9,15},{10,... | collective-permute-start | bytes 221192 | tf_op jit(solution)/shard_map/ppermute | solution.py:510
  127.1 0.1 collective-permute-start.10
  127.1 2.1 %collective-permute-start.11 = (bf16[16,1408]{1,0:T(8,128)(2,1)S(1)}, bf16[16,1408]{1,0:T(8,128)(2,1)S(1)}, u32[]{:S(2)}, u32[]{:S(2)}) collective-permute-start(bf16[16,1408]{1,0:T(8,128)(2,1)S(1)} %get-tuple-element.81), channel_id=1, source_target_pairs={{0,6},{1,7},{2,4},{3,5},{4,2},{5,3},{6,0},{7,1},{8,14},{9,15},{10,... | collective-permute-start | bytes 135176 | tf_op jit(solution)/shard_map/ppermute | solution.py:510
  129.2 6.1 %collective-permute-done.10.refs_2_ = bf16[16,1408]{1,0:T(8,128)(2,1)S(1)} collective-permute-done((bf16[16,1408]{1,0:T(8,128)(2,1)S(1)}, bf16[16,1408]{1,0:T(8,128)(2,1)S(1)}, u32[]{:S(2)}, u32[]{:S(2)}) %collective-permute-start.10) | collective-permute-done | bytes 45088 | tf_op jit(solution)/shard_map/ppermute | solution.py:510
  135.4 1.3 collective-permute-start.17
  136.7 1.2 collective-permute-start.16
  137.9 1.9 %collective-permute-start.15 = (bf16[16,1408]{1,0:T(8,128)(2,1)S(1)}, bf16[16,1408]{1,0:T(8,128)(2,1)S(1)}, u32[]{:S(2)}, u32[]{:S(2)}) collective-permute-start(bf16[16,1408]{1,0:T(8,128)(2,1)S(1)} %shard_map.229.refs_0_), channel_id=1, source_target_pairs={{0,2},{1,3},{2,0},{3,1},{4,6},{5,7},{6,4},{7,5},{8,10},{9,11},{10,... | collective-permute-start | bytes 135176 | tf_op jit(solution)/shard_map/ppermute | solution.py:510
  139.8 1.5 collective-permute-done.17.refs_3_
  141.3 1.1 collective-permute-done.16.refs_2_
  142.3 0.1 collective-permute-done.15.refs_1_
  142.5 1.5 collective-permute-start.20
  144.0 1.5 collective-permute-start.19
  145.5 0.5 collective-permute-start.18
  146.0 3.2 %collective-permute-done.20.refs_3_ = bf16[4,16,1408]{2,1,0:T(8,128)(2,1)S(1)} collective-permute-done((bf16[4,16,1408]{2,1,0:T(8,128)(2,1)S(1)}, bf16[4,16,1408]{2,1,0:T(8,128)(2,1)S(1)}, u32[]{:S(2)}, u32[]{:S(2)}) %collective-permute-start.20) | collective-permute-done | bytes 180256 | tf_op jit(solution)/shard_map/ppermute | solution.py:510
  149.2 1.8 %collective-permute-done.19.refs_2_ = bf16[4,16,1408]{2,1,0:T(8,128)(2,1)S(1)} collective-permute-done((bf16[4,16,1408]{2,1,0:T(8,128)(2,1)S(1)}, bf16[4,16,1408]{2,1,0:T(8,128)(2,1)S(1)}, u32[]{:S(2)}, u32[]{:S(2)}) %collective-permute-start.19) | collective-permute-done | bytes 180256 | tf_op jit(solution)/shard_map/ppermute | solution.py:510
  151.0 0.5 collective-permute-start.22
  151.6 1.9 %shard_map.230 = bf16[288,1024]{1,0:T(8,128)(2,1)} custom-call(s32[4]{0:T(128)S(1)} %pad_add_fusion.me_ref, bf16[512,1024]{1,0:T(8,128)(2,1)S(1)} %copy-done, bf16[4,36,512]{2,1,0:T(8,128)(2,1)S(1)} %get-tuple-element.56.mine_ref.refs_0_, bf16[4,36,512]{2,1,0:T(8,128)(2,1)S(1)} %collective-permute-done.other_ref.refs_1_, ...), custom_call_target="tpu_custom_call" | custom-call | flops 301989888 | bytes 1564688 | tf_op jit(solution)/shard_map/pallas_call | solution.py:457
  153.4 2.2 %shard_map.232 = (f32[512,1024]{1,0:T(8,128)}, f32[256,512]{1,0:T(8,128)}, f32[1,1]{1,0:T(1,128)}) custom-call(s32[4]{0:T(128)S(1)} %pad_add_fusion.me_ref, bf16[4,16,1408]{2,1,0:T(8,128)(2,1)S(1)} %shard_map.231.refs_0_, bf16[4,16,1408]{2,1,0:T(8,128)(2,1)S(1)} %collective-permute-done.18.refs_1_, bf16[4,16,1408]{2,1,0:T(8,128)(2,1)S(1)} %collective-permute-done.19.refs_2_, ...), custom_call_target="tpu_custom_call" | custom-call | bytes 1441808 | tf_op jit(solution)/shard_map/pallas_call | solution.py:457
  (55 shorter events, 0.3 us)
Async XLA Ops:
  10.4 49.7 %copy-start.1 = (bf16[1,288,1024]{2,1,0:T(8,128)(2,1)S(1)}, bf16[1,288,1024]{2,1,0:T(8,128)(2,1)}, u32[]{:S(2)}) copy-start(bf16[1,288,1024]{2,1,0:T(8,128)(2,1)} %param.21) | copy-start | bytes 1769476
  10.5 49.7 %copy-start.2 = (bf16[512,1024]{1,0:T(8,128)(2,1)S(1)}, bf16[512,1024]{1,0:T(8,128)(2,1)}, u32[]{:S(2)}) copy-start(bf16[512,1024]{1,0:T(8,128)(2,1)} %w_out_ref.2) | copy-start | bytes 3145732
  10.5 49.7 %copy-start.3 = (bf16[1024,512]{1,0:T(8,128)(2,1)S(1)}, bf16[1024,512]{1,0:T(8,128)(2,1)}, u32[]{:S(2)}) copy-start(bf16[1024,512]{1,0:T(8,128)(2,1)} %w_dec_ref.1) | copy-start | bytes 3145732
  10.5 49.7 %copy-start.4 = (bf16[512,768]{1,0:T(8,128)(2,1)S(1)}, bf16[512,768]{1,0:T(8,128)(2,1)}, u32[]{:S(2)}) copy-start(bf16[512,768]{1,0:T(8,128)(2,1)} %w_qkv_ref.1) | copy-start | bytes 2359300
  10.5 49.7 %copy-start.5 = (bf16[288,1024]{1,0:T(8,128)(2,1)S(1)}, bf16[288,1024]{1,0:T(8,128)(2,1)}, u32[]{:S(2)}) copy-start(bf16[288,1024]{1,0:T(8,128)(2,1)} %get-tuple-element.51.tok_ref) | copy-start | bytes 1769476
  10.5 49.7 %copy-start.6 = (bf16[288,512]{1,0:T(8,128)(2,1)S(1)}, bf16[288,512]{1,0:T(8,128)(2,1)}, u32[]{:S(2)}) copy-start(bf16[288,512]{1,0:T(8,128)(2,1)} %pos_ref.1) | copy-start | bytes 884740
  10.5 49.7 %copy-start.7 = (s32[1,288]{1,0:T(1,128)S(1)}, s32[1,288]{1,0:T(1,128)}, u32[]{:S(2)}) copy-start(s32[1,288]{1,0:T(1,128)} %slots_ref.3) | copy-start | bytes 3460
  10.5 49.7 %copy-start.8 = (bf16[1024]{0:T(1024)(128)(2,1)S(1)}, bf16[1024]{0:T(1024)(128)(2,1)}, u32[]{:S(2)}) copy-start(bf16[1024]{0:T(1024)(128)(2,1)} %out_gain_ref.1) | copy-start | bytes 6148
  10.5 49.7 %copy-start.9 = (s32[1,288]{1,0:T(1,128)S(1)}, s32[1,288]{1,0:T(1,128)}, u32[]{:S(2)}) copy-start(s32[1,288]{1,0:T(1,128)} %owner_ref.1) | copy-start | bytes 3460
  10.6 49.7 %copy-start.11 = (bf16[512]{0:T(512)(128)(2,1)S(1)}, bf16[512]{0:T(512)(128)(2,1)}, u32[]{:S(2)}) copy-start(bf16[512]{0:T(512)(128)(2,1)} %mask_ref.1) | copy-start | bytes 3076
  10.6 49.7 %copy-start.12 = (bf16[512]{0:T(512)(128)(2,1)S(1)}, bf16[512]{0:T(512)(128)(2,1)}, u32[]{:S(2)}) copy-start(bf16[512]{0:T(512)(128)(2,1)} %gain_ref.3) | copy-start | bytes 3076
  78.2 18.5 %copy-start = (bf16[512,1024]{1,0:T(8,128)(2,1)S(1)}, bf16[512,1024]{1,0:T(8,128)(2,1)}, u32[]{:S(2)}) copy-start(bf16[512,1024]{1,0:T(8,128)(2,1)} %w_head_ref.5) | copy-start | bytes 3145732
  78.2 18.5 %copy-start.10 = (bf16[512]{0:T(512)(128)(2,1)S(1)}, bf16[512]{0:T(512)(128)(2,1)}, u32[]{:S(2)}) copy-start(bf16[512]{0:T(512)(128)(2,1)} %head_gain_ref.3) | copy-start | bytes 3076
  78.2 18.5 %copy-start.13 = (bf16[512,2048]{1,0:T(8,128)(2,1)S(1)}, bf16[512,2048]{1,0:T(8,128)(2,1)}, u32[]{:S(2)}) copy-start(bf16[512,2048]{1,0:T(8,128)(2,1)} %w_up_ref.3) | copy-start | bytes 6291460
  78.2 18.5 %copy-start.14 = (bf16[2048,512]{1,0:T(8,128)(2,1)S(1)}, bf16[2048,512]{1,0:T(8,128)(2,1)}, u32[]{:S(2)}) copy-start(bf16[2048,512]{1,0:T(8,128)(2,1)} %w_down_ref.3) | copy-start | bytes 6291460
  78.2 18.5 %copy-start.15 = (bf16[256,512]{1,0:T(8,128)(2,1)S(1)}, bf16[256,512]{1,0:T(8,128)(2,1)}, u32[]{:S(2)}) copy-start(bf16[256,512]{1,0:T(8,128)(2,1)} %w_out_ref.3) | copy-start | bytes 786436
  78.2 18.5 %copy-start.16 = (bf16[512]{0:T(512)(128)(2,1)S(1)}, bf16[512]{0:T(512)(128)(2,1)}, u32[]{:S(2)}) copy-start(bf16[512]{0:T(512)(128)(2,1)} %feed_gain_ref.3) | copy-start | bytes 3076
  101.6 2.0 %collective-permute-start.1 = (bf16[4,4,16,1024]{3,2,1,0:T(8,128)(2,1)S(1)}, bf16[4,4,16,1024]{3,2,1,0:T(8,128)(2,1)S(1)}, u32[]{:S(2)}, u32[]{:S(2)}) collective-permute-start(bf16[4,4,16,1024]{3,2,1,0:T(8,128)(2,1)S(1)} %get-tuple-element.59), channel_id=1, source_target_pairs={{0,8},{1,9},{2,10},{3,11},{4,12},{5,13},{6,14},{7,15},{8,0},{9,1},... | collective-permute-start | bytes 1572872 | tf_op jit(solution)/shard_map/ppermute | solution.py:510
  106.4 7.6 %collective-permute-start.5 = (bf16[4,4,16,384]{3,2,1,0:T(8,128)(2,1)S(1)}, bf16[4,4,16,384]{3,2,1,0:T(8,128)(2,1)S(1)}, u32[]{:S(2)}, u32[]{:S(2)}) collective-permute-start(bf16[4,4,16,384]{3,2,1,0:T(8,128)(2,1)S(1)} %get-tuple-element.73), channel_id=1, source_target_pairs={{0,8},{1,9},{2,10},{3,11},{4,12},{5,13},{6,14},{7,15},{8,0},{9,1},... | collective-permute-start | bytes 589832 | tf_op jit(solution)/shard_map/ppermute | solution.py:510
  106.6 7.4 %collective-permute-start = (bf16[4,36,512]{2,1,0:T(8,128)(2,1)S(1)}, bf16[4,36,512]{2,1,0:T(8,128)(2,1)S(1)}, u32[]{:S(2)}, u32[]{:S(2)}) collective-permute-start(bf16[4,36,512]{2,1,0:T(8,128)(2,1)S(1)} %get-tuple-element.57), channel_id=1, source_target_pairs={{0,1},{1,0},{2,3},{3,2},{4,5},{5,4},{6,7},{7,6},{8,9},{9,8},{10,11... | collective-permute-start | bytes 442376 | tf_op jit(solution)/shard_map/ppermute | solution.py:510
  106.8 9.4 %collective-permute-start.2 = (bf16[4,16,1024]{2,1,0:T(8,128)(2,1)S(1)}, bf16[4,16,1024]{2,1,0:T(8,128)(2,1)S(1)}, u32[]{:S(2)}, u32[]{:S(2)}) collective-permute-start(bf16[4,16,1024]{2,1,0:T(8,128)(2,1)S(1)} %get-tuple-element.64), channel_id=1, source_target_pairs={{0,16},{1,17},{2,18},{3,19},{4,20},{5,21},{6,22},{7,23},{8,24},{9,... | collective-permute-start | bytes 393224 | tf_op jit(solution)/shard_map/ppermute | solution.py:510
  108.3 11.5 %collective-permute-start.3 = (bf16[4,16,1024]{2,1,0:T(8,128)(2,1)S(1)}, bf16[4,16,1024]{2,1,0:T(8,128)(2,1)S(1)}, u32[]{:S(2)}, u32[]{:S(2)}) collective-permute-start(bf16[4,16,1024]{2,1,0:T(8,128)(2,1)S(1)} %get-tuple-element.65), channel_id=1, source_target_pairs={{0,1},{1,0},{2,3},{3,2},{4,5},{5,4},{6,7},{7,6},{8,9},{9,8},{10,11... | collective-permute-start | bytes 393224 | tf_op jit(solution)/shard_map/ppermute | solution.py:510
  110.2 9.6 %collective-permute-start.4 = (bf16[4,16,1024]{2,1,0:T(8,128)(2,1)S(1)}, bf16[4,16,1024]{2,1,0:T(8,128)(2,1)S(1)}, u32[]{:S(2)}, u32[]{:S(2)}) collective-permute-start(bf16[4,16,1024]{2,1,0:T(8,128)(2,1)S(1)} %get-tuple-element.66), channel_id=1, source_target_pairs={{0,17},{1,16},{2,19},{3,18},{4,21},{5,20},{6,23},{7,22},{8,25},{9,... | collective-permute-start | bytes 393224 | tf_op jit(solution)/shard_map/ppermute | solution.py:510
  114.1 5.7 %collective-permute-start.6 = (bf16[4,16,384]{2,1,0:T(8,128)(2,1)S(1)}, bf16[4,16,384]{2,1,0:T(8,128)(2,1)S(1)}, u32[]{:S(2)}, u32[]{:S(2)}) collective-permute-start(bf16[4,16,384]{2,1,0:T(8,128)(2,1)S(1)} %get-tuple-element.75), channel_id=1, source_target_pairs={{0,16},{1,17},{2,18},{3,19},{4,20},{5,21},{6,22},{7,23},{8,24},{9,... | collective-permute-start | bytes 147464 | tf_op jit(solution)/shard_map/ppermute | solution.py:510
  116.2 4.1 %collective-permute-start.7 = (bf16[4,16,384]{2,1,0:T(8,128)(2,1)S(1)}, bf16[4,16,384]{2,1,0:T(8,128)(2,1)S(1)}, u32[]{:S(2)}, u32[]{:S(2)}) collective-permute-start(bf16[4,16,384]{2,1,0:T(8,128)(2,1)S(1)} %get-tuple-element.76), channel_id=1, source_target_pairs={{0,1},{1,0},{2,3},{3,2},{4,5},{5,4},{6,7},{7,6},{8,9},{9,8},{10,11... | collective-permute-start | bytes 147464 | tf_op jit(solution)/shard_map/ppermute | solution.py:510
  116.2 5.0 %collective-permute-start.8 = (bf16[4,16,384]{2,1,0:T(8,128)(2,1)S(1)}, bf16[4,16,384]{2,1,0:T(8,128)(2,1)S(1)}, u32[]{:S(2)}, u32[]{:S(2)}) collective-permute-start(bf16[4,16,384]{2,1,0:T(8,128)(2,1)S(1)} %get-tuple-element.77), channel_id=1, source_target_pairs={{0,17},{1,16},{2,19},{3,18},{4,21},{5,20},{6,23},{7,22},{8,25},{9,... | collective-permute-start | bytes 147464 | tf_op jit(solution)/shard_map/ppermute | solution.py:510
  121.3 5.8 %collective-permute-start.9 = (bf16[16,1408]{1,0:T(8,128)(2,1)S(1)}, bf16[16,1408]{1,0:T(8,128)(2,1)S(1)}, u32[]{:S(2)}, u32[]{:S(2)}) collective-permute-start(bf16[16,1408]{1,0:T(8,128)(2,1)S(1)} %get-tuple-element.79), channel_id=1, source_target_pairs={{0,2},{1,3},{2,0},{3,1},{4,6},{5,7},{6,4},{7,5},{8,10},{9,11},{10,... | collective-permute-start | bytes 135176 | tf_op jit(solution)/shard_map/ppermute | solution.py:510
  122.7 12.7 %collective-permute-start.12 = (bf16[2,36,512]{2,1,0:T(8,128)(2,1)S(1)}, bf16[2,36,512]{2,1,0:T(8,128)(2,1)S(1)}, u32[]{:S(2)}, u32[]{:S(2)}) collective-permute-start(bf16[2,36,512]{2,1,0:T(8,128)(2,1)S(1)} %get-tuple-element.82), channel_id=1, source_target_pairs={{0,2},{1,3},{2,0},{3,1},{4,6},{5,7},{6,4},{7,5},{8,10},{9,11},{10,... | collective-permute-start | bytes 221192 | tf_op jit(solution)/shard_map/ppermute | solution.py:510
  123.4 12.0 %collective-permute-start.13 = (bf16[2,36,512]{2,1,0:T(8,128)(2,1)S(1)}, bf16[2,36,512]{2,1,0:T(8,128)(2,1)S(1)}, u32[]{:S(2)}, u32[]{:S(2)}) collective-permute-start(bf16[2,36,512]{2,1,0:T(8,128)(2,1)S(1)} %get-tuple-element.83), channel_id=1, source_target_pairs={{0,4},{1,5},{2,6},{3,7},{4,0},{5,1},{6,2},{7,3},{8,12},{9,13},{10,... | collective-permute-start | bytes 221192 | tf_op jit(solution)/shard_map/ppermute | solution.py:510
  123.7 11.6 %collective-permute-start.14 = (bf16[2,36,512]{2,1,0:T(8,128)(2,1)S(1)}, bf16[2,36,512]{2,1,0:T(8,128)(2,1)S(1)}, u32[]{:S(2)}, u32[]{:S(2)}) collective-permute-start(bf16[2,36,512]{2,1,0:T(8,128)(2,1)S(1)} %get-tuple-element.84), channel_id=1, source_target_pairs={{0,6},{1,7},{2,4},{3,5},{4,2},{5,3},{6,0},{7,1},{8,14},{9,15},{10,... | collective-permute-start | bytes 221192 | tf_op jit(solution)/shard_map/ppermute | solution.py:510
  127.1 8.2 %collective-permute-start.10 = (bf16[16,1408]{1,0:T(8,128)(2,1)S(1)}, bf16[16,1408]{1,0:T(8,128)(2,1)S(1)}, u32[]{:S(2)}, u32[]{:S(2)}) collective-permute-start(bf16[16,1408]{1,0:T(8,128)(2,1)S(1)} %get-tuple-element.80), channel_id=1, source_target_pairs={{0,4},{1,5},{2,6},{3,7},{4,0},{5,1},{6,2},{7,3},{8,12},{9,13},{10,... | collective-permute-start | bytes 135176 | tf_op jit(solution)/shard_map/ppermute | solution.py:510
  127.1 8.2 %collective-permute-start.11 = (bf16[16,1408]{1,0:T(8,128)(2,1)S(1)}, bf16[16,1408]{1,0:T(8,128)(2,1)S(1)}, u32[]{:S(2)}, u32[]{:S(2)}) collective-permute-start(bf16[16,1408]{1,0:T(8,128)(2,1)S(1)} %get-tuple-element.81), channel_id=1, source_target_pairs={{0,6},{1,7},{2,4},{3,5},{4,2},{5,3},{6,0},{7,1},{8,14},{9,15},{10,... | collective-permute-start | bytes 135176 | tf_op jit(solution)/shard_map/ppermute | solution.py:510
  135.4 5.9 %collective-permute-start.17 = (bf16[16,1408]{1,0:T(8,128)(2,1)S(1)}, bf16[16,1408]{1,0:T(8,128)(2,1)S(1)}, u32[]{:S(2)}, u32[]{:S(2)}) collective-permute-start(bf16[16,1408]{1,0:T(8,128)(2,1)S(1)} %shard_map.229.refs_0_), channel_id=1, source_target_pairs={{0,6},{1,7},{2,4},{3,5},{4,2},{5,3},{6,0},{7,1},{8,14},{9,15},{10,... | collective-permute-start | bytes 135176 | tf_op jit(solution)/shard_map/ppermute | solution.py:510
  136.7 5.6 %collective-permute-start.16 = (bf16[16,1408]{1,0:T(8,128)(2,1)S(1)}, bf16[16,1408]{1,0:T(8,128)(2,1)S(1)}, u32[]{:S(2)}, u32[]{:S(2)}) collective-permute-start(bf16[16,1408]{1,0:T(8,128)(2,1)S(1)} %shard_map.229.refs_0_), channel_id=1, source_target_pairs={{0,4},{1,5},{2,6},{3,7},{4,0},{5,1},{6,2},{7,3},{8,12},{9,13},{10,... | collective-permute-start | bytes 135176 | tf_op jit(solution)/shard_map/ppermute | solution.py:510
  137.9 4.5 %collective-permute-start.15 = (bf16[16,1408]{1,0:T(8,128)(2,1)S(1)}, bf16[16,1408]{1,0:T(8,128)(2,1)S(1)}, u32[]{:S(2)}, u32[]{:S(2)}) collective-permute-start(bf16[16,1408]{1,0:T(8,128)(2,1)S(1)} %shard_map.229.refs_0_), channel_id=1, source_target_pairs={{0,2},{1,3},{2,0},{3,1},{4,6},{5,7},{6,4},{7,5},{8,10},{9,11},{10,... | collective-permute-start | bytes 135176 | tf_op jit(solution)/shard_map/ppermute | solution.py:510
  142.5 6.8 %collective-permute-start.20 = (bf16[4,16,1408]{2,1,0:T(8,128)(2,1)S(1)}, bf16[4,16,1408]{2,1,0:T(8,128)(2,1)S(1)}, u32[]{:S(2)}, u32[]{:S(2)}) collective-permute-start(bf16[4,16,1408]{2,1,0:T(8,128)(2,1)S(1)} %shard_map.231.refs_0_), channel_id=1, source_target_pairs={{0,17},{1,16},{2,19},{3,18},{4,21},{5,20},{6,23},{7,22},{8,25},{9,... | collective-permute-start | bytes 540680 | tf_op jit(solution)/shard_map/ppermute | solution.py:510
  144.0 7.1 %collective-permute-start.19 = (bf16[4,16,1408]{2,1,0:T(8,128)(2,1)S(1)}, bf16[4,16,1408]{2,1,0:T(8,128)(2,1)S(1)}, u32[]{:S(2)}, u32[]{:S(2)}) collective-permute-start(bf16[4,16,1408]{2,1,0:T(8,128)(2,1)S(1)} %shard_map.231.refs_0_), channel_id=1, source_target_pairs={{0,1},{1,0},{2,3},{3,2},{4,5},{5,4},{6,7},{7,6},{8,9},{9,8},{10,11... | collective-permute-start | bytes 540680 | tf_op jit(solution)/shard_map/ppermute | solution.py:510
  145.5 5.6 %collective-permute-start.18 = (bf16[4,16,1408]{2,1,0:T(8,128)(2,1)S(1)}, bf16[4,16,1408]{2,1,0:T(8,128)(2,1)S(1)}, u32[]{:S(2)}, u32[]{:S(2)}) collective-permute-start(bf16[4,16,1408]{2,1,0:T(8,128)(2,1)S(1)} %shard_map.231.refs_0_), channel_id=1, source_target_pairs={{0,16},{1,17},{2,18},{3,19},{4,20},{5,21},{6,22},{7,23},{8,24},{9,... | collective-permute-start | bytes 540680 | tf_op jit(solution)/shard_map/ppermute | solution.py:510
  146.0 7.4 %collective-permute-start.21 = (bf16[4,16,1408]{2,1,0:T(8,128)(2,1)S(1)}, bf16[4,16,1408]{2,1,0:T(8,128)(2,1)S(1)}, u32[]{:S(2)}, u32[]{:S(2)}) collective-permute-start(bf16[4,16,1408]{2,1,0:T(8,128)(2,1)S(1)} %shard_map.231.refs_0_), channel_id=1, source_target_pairs={{0,8},{1,9},{2,10},{3,11},{4,12},{5,13},{6,14},{7,15},{8,0},{9,1},... | collective-permute-start | bytes 540680 | tf_op jit(solution)/shard_map/ppermute | solution.py:510
  149.2 4.2 %collective-permute-start.24 = (bf16[4,16,1408]{2,1,0:T(8,128)(2,1)S(1)}, bf16[4,16,1408]{2,1,0:T(8,128)(2,1)S(1)}, u32[]{:S(2)}, u32[]{:S(2)}) collective-permute-start(bf16[4,16,1408]{2,1,0:T(8,128)(2,1)S(1)} %collective-permute-done.20.refs_3_), channel_id=1, source_target_pairs={{0,8},{1,9},{2,10},{3,11},{4,12},{5,13},{6,14},{7,15},{8,0},{9,1},... | collective-permute-start | bytes 540680 | tf_op jit(solution)/shard_map/ppermute | solution.py:510
  151.0 2.4 %collective-permute-start.23 = (bf16[4,16,1408]{2,1,0:T(8,128)(2,1)S(1)}, bf16[4,16,1408]{2,1,0:T(8,128)(2,1)S(1)}, u32[]{:S(2)}, u32[]{:S(2)}) collective-permute-start(bf16[4,16,1408]{2,1,0:T(8,128)(2,1)S(1)} %collective-permute-done.19.refs_2_), channel_id=1, source_target_pairs={{0,8},{1,9},{2,10},{3,11},{4,12},{5,13},{6,14},{7,15},{8,0},{9,1},... | collective-permute-start | bytes 540680 | tf_op jit(solution)/shard_map/ppermute | solution.py:510
  151.0 2.4 %collective-permute-start.22 = (bf16[4,16,1408]{2,1,0:T(8,128)(2,1)S(1)}, bf16[4,16,1408]{2,1,0:T(8,128)(2,1)S(1)}, u32[]{:S(2)}, u32[]{:S(2)}) collective-permute-start(bf16[4,16,1408]{2,1,0:T(8,128)(2,1)S(1)} %collective-permute-done.18.refs_1_), channel_id=1, source_target_pairs={{0,8},{1,9},{2,10},{3,11},{4,12},{5,13},{6,14},{7,15},{8,0},{9,1},... | collective-permute-start | bytes 540680 | tf_op jit(solution)/shard_map/ppermute | solution.py:510

commit v6 on v5

--- a/solution.py
+++ b/solution.py
@@ -9,6 +9,7 @@
 from jax.sharding import PartitionSpec as P
 
 HEADS = 8
+ORDER = (6, 7, 4, 5, 2, 3, 1, 0)
 BF = jnp.bfloat16
 F32 = jnp.float32
 LOG2E = math.log2(math.e)
@@ -61,45 +62,48 @@
 
 
 def embed_kernel(
-    patch_hbm, pos_hbm, w_embed_hbm, gain_ref, w_qkv_hbm, slots_ref,
-    send_ref, tok_ref, normed_ref, qkv_ref, patch_ref, pos_ref, w_embed_ref, w_qkv_ref,
-    patch_sem, pos_sem, embed_sem, qkv_sem,
+    me_ref, patch_hbm, pos_hbm, w_embed_hbm, gain_ref, w_qkv_hbm, slots_ref, *refs,
 ):
+    tok_ref, *send_refs = refs[:-12]
+    normed_ref, qkv_ref, patch_ref, pos_ref, w_embed_ref, w_qkv_ref, send_buf = refs[-12:-5]
+    patch_sem, pos_sem, embed_sem, qkv_sem, send_sem = refs[-5:]
     rows, width = patch_ref.shape
     half = rows // 2
     att = w_qkv_ref.shape[1] // 3
     size = att // HEADS
     tile = 256
 
-    def piece(hbm, buf, sem, step):
-        cols = slice(step * tile, (step + 1) * tile)
-        return pltpu.make_async_copy(hbm.at[:, cols], buf.at[:, cols], sem.at[step])
-
-    embed_copies = [
-        piece(w_embed_hbm, w_embed_ref, embed_sem, i) for i in range(width // tile)
-    ]
-    qkv_copies = [piece(w_qkv_hbm, w_qkv_ref, qkv_sem, i) for i in range(3 * att // tile)]
+    def pieces(hbm, buf, sem):
+        return [
+            pltpu.make_async_copy(
+                hbm.at[at : at + tile], buf.at[at : at + tile], sem.at[at // tile]
+            )
+            for at in range(0, buf.shape[0], tile)
+        ]
+
+    embed_copies = pieces(w_embed_hbm, w_embed_ref, embed_sem)
+    qkv_copies = pieces(w_qkv_hbm, w_qkv_ref, qkv_sem)
     patch_copy = pltpu.make_async_copy(patch_hbm, patch_ref, patch_sem)
     pos_copy = pltpu.make_async_copy(pos_hbm, pos_ref, pos_sem)
-    for copy in [patch_copy, embed_copies[0], pos_copy, *embed_copies[1:], *qkv_copies]:
+    for copy in [patch_copy, *embed_copies, pos_copy, *qkv_copies]:
         copy.start()
     patch_copy.wait()
-    for step in range(width // tile):
-        embed_copies[step].wait()
-        if step == 0:
-            pos_copy.wait()
+    total = None
+    for step, copy in enumerate(embed_copies):
+        copy.wait()
         cols = slice(step * tile, (step + 1) * tile)
-        tok_ref[:, cols] = (
-            dot(patch_ref[...], w_embed_ref[:, cols]) + pos_ref[:, cols].astype(F32)
-        ).astype(BF)
-
+        part = dot(patch_ref[:, cols], w_embed_ref[cols, :])
+        total = part if total is None else total + part
+    pos_copy.wait()
+    tok_ref[...] = (total + pos_ref[...].astype(F32)).astype(BF)
     pick = slot_of_row(slots_ref[...]).astype(BF)
     normed = layer_norm(tok_ref[...].astype(F32), gain_ref[...]).astype(BF)
     normed_ref[...] = lax.dot_general(
         pick, normed, (((0,), (0,)), ((), ())), preferred_element_type=F32
     ).astype(BF)
+    for copy in qkv_copies:
+        copy.wait()
     for step in range(3 * att // tile):
-        qkv_copies[step].wait()
         cols = slice(step * tile, (step + 1) * tile)
         qkv_ref[:, cols] = dot(normed_ref[...], w_qkv_ref[:, cols]).astype(BF)
 
@@ -112,21 +116,38 @@
         q = qkv_ref[:, at : at + size]
         k = qkv_ref[:, att + at : att + at + size]
         v = qkv_ref[:, 2 * att + at : 2 * att + at + size]
-        send_ref[head, :half, :] = jnp.concatenate([q[:half], q[half:]], axis=1)
-        send_ref[head, half : half + rows, :] = jnp.concatenate([k, v], axis=1)
-        send_ref[head, half + rows :, :] = info
-
-
-def enc_attend_kernel(
-    me_ref, q_ref, kv_ref, out_ref, q_buf, kv_buf, o_buf, *, q_at, kv_at, rows, cap_q, cap_k
-):
+        send_buf[head, :half, :] = jnp.concatenate([q[:half], q[half:]], axis=1)
+        send_buf[head, half : half + rows, :] = jnp.concatenate([k, v], axis=1)
+        send_buf[head, half + rows :, :] = info
+    if len(send_refs) == 1:
+        copies = [pltpu.make_async_copy(send_buf, send_refs[0], send_sem.at[0])]
+    else:
+        copies = [
+            pltpu.make_async_copy(send_buf.at[me_ref[1] ^ index], ref, send_sem.at[index])
+            for index, ref in enumerate(send_refs)
+        ]
+    for copy in copies:
+        copy.start()
+    for copy in copies:
+        copy.wait()
+
+
+def enc_attend_kernel(me_ref, *refs, q_at, kv_at, rows, cap_q, cap_k):
+    *blocks, out_ref, q_buf, kv_buf, o_buf = refs
+    if len(blocks) == HEADS:
+        q_of = kv_of = lambda source: blocks[source]
+        place_of = lambda source: me_ref[1] ^ ORDER[source]
+        sources, first = HEADS, 0
+    else:
+        q_of, kv_of = blocks[0].at.__getitem__, blocks[1].at.__getitem__
+        place_of = lambda source: source
+        sources, first = blocks[1].shape[0], me_ref[2]
     half = rows // 2
-    sources = kv_ref.shape[0]
     lane16 = lax.broadcasted_iota(jnp.int32, (16, 128), 1)
     lane_h = lax.broadcasted_iota(jnp.int32, (half, 128), 1)
 
     def count_of(source):
-        info = kv_ref[source, kv_at + rows : kv_at + rows + 16, :].astype(F32)
+        info = kv_of(source)[kv_at + rows : kv_at + rows + 16, :].astype(F32)
         high = jnp.max(jnp.where(lane16 < 64, info, 0.0)).astype(jnp.int32)
         low = jnp.max(jnp.where(lane16 >= 64, info, 0.0)).astype(jnp.int32)
         return high * 16 + low
@@ -142,7 +163,7 @@
     for source in range(sources):
         count = count_of(source)
         off = pl.multiple_of(off, 16)
-        kv_buf[pl.ds(off, rows), :128] = kv_ref[source, kv_at : kv_at + rows, :]
+        kv_buf[pl.ds(off, rows), :128] = kv_of(source)[kv_at : kv_at + rows, :]
         valid = jnp.where((key >= off) & (key < off + count), 1.0, valid)
         off = off + (count + 15) // 16 * 16
     bias = jnp.where(valid > 0.0, 0.0, -1e30)
@@ -152,11 +173,11 @@
     for source in range(HEADS):
         off = pl.multiple_of(off, 16)
         offs.append(off)
-        block = q_ref[source, q_at : q_at + half, :]
+        block = q_of(source)[q_at : q_at + half, :]
         zero = jnp.zeros_like(block)
         q_buf[pl.ds(off, half), :] = jnp.where(lane_h < 64, block, zero)
         q_buf[pl.ds(off + half, half), :] = jnp.where(lane_h < 64, swap_halves(block), zero)
-        off = off + (count_of(me_ref[2] + source) + 15) // 16 * 16
+        off = off + (count_of(first + source) + 15) // 16 * 16
     total = off
 
     tile = 128
@@ -176,7 +197,7 @@
     for source in range(HEADS):
         upper = o_buf[pl.ds(offs[source], half), :]
         lower = o_buf[pl.ds(pl.multiple_of(offs[source] + half, 16), half), :]
-        out_ref[source] = jnp.where(lane_h < 64, swap_halves(upper), lower)
+        out_ref[place_of(source)] = jnp.where(lane_h < 64, swap_halves(upper), lower)
 
 
 def middle_kernel(
@@ -391,22 +412,18 @@
         ref[xy, z, :, half:] = sums
 
 
-def pair_kernel(keep_ref, got_ref, mine_ref, other_ref, *refs):
-    total = (keep_ref[...].astype(F32) + got_ref[...].astype(F32)).astype(BF)
+def merge_kernel(
+    head_keep_ref, head_got_ref, out_keep_ref, out_got_ref, mine_ref, other_ref, *refs
+):
+    head = (head_keep_ref[...].astype(F32) + head_got_ref[...].astype(F32)).astype(BF)
+    out = (out_keep_ref[...].astype(F32) + out_got_ref[...].astype(F32)).astype(BF)
+    pixels = head.shape[3]
     for i in range(4):
-        refs[i][...] = total[i]
+        refs[i][:, :, :pixels] = head[i]
+        refs[i][:, :, pixels:] = out[i]
     for i in range(1, 4):
         refs[3 + i][0] = mine_ref[i]
         refs[3 + i][1] = other_ref[i]
-
-
-def merge_kernel(*refs):
-    head = sum(ref[...].astype(F32) for ref in refs[:4]).astype(BF)
-    out = sum(ref[...].astype(F32) for ref in refs[4:8]).astype(BF)
-    pixels = head.shape[2]
-    for i, ref in enumerate(refs[8:]):
-        ref[:, :pixels] = head[i]
-        ref[:, pixels:] = out[i]
 
 
 def add_kernel(*refs, count):
@@ -446,7 +463,7 @@
 
 
 def vmem_call(kernel, outs, scratch, inputs, smem=(), smem_out=(), anywhere=(),
-              vmem=VMEM_LIMIT, flops=0):
+              anywhere_out=(), vmem=VMEM_LIMIT, flops=0):
     space = [
         pl.BlockSpec(
             memory_space=pltpu.SMEM if i in smem else pl.ANY if i in anywhere else pltpu.VMEM
@@ -459,7 +476,13 @@
         out_shape=outs,
         in_specs=space,
         out_specs=[
-            pl.BlockSpec(memory_space=pltpu.SMEM if i in smem_out else pltpu.VMEM)
+            pl.BlockSpec(
+                memory_space=pltpu.SMEM
+                if i in smem_out
+                else pl.ANY
+                if i in anywhere_out
+                else pltpu.VMEM
+            )
             for i in range(len(outs))
         ],
         scratch_shapes=scratch,
@@ -514,44 +537,44 @@
 COLUMN = ((0, 2), (0, 4), (0, 6))
 
 
-def sum_by_permutes(head_keep, head_send, zn_keep, zn_send, head_back, backward):
+def sum_by_permutes(head_keep, head_send, zn_keep, zn_send, head_back, backward, rebuild):
     shape = jax.ShapeDtypeStruct
     head_got = across(head_send, 1, 0)
     zn_got = across(zn_send, 0, 1)
-    dz = head_back()
-    heads = vmem_call(
-        functools.partial(add_kernel, count=2),
-        [shape(head_keep.shape[1:], BF)] * 4,
+    dz, head_got = lax.optimization_barrier((head_back(), head_got))
+    out_keep, out_send = backward(dz)
+    out_send, zn_got = lax.optimization_barrier((out_send, zn_got))
+    out_got = across(out_send, 1, 0)
+    block = shape((head_keep.shape[2], head_keep.shape[3] + out_keep.shape[3]), BF)
+    part = shape((4, *block.shape), BF)
+    pair = shape((2, *zn_keep.shape[1:]), BF)
+    *parts, zn1, zn2, zn3 = vmem_call(
+        merge_kernel,
+        [part] * 4 + [pair] * 3,
         [],
-        [head_keep, head_got],
-    )
-    mine, dz = lax.optimization_barrier((heads[0], dz))
-    heads = [mine] + [across(p, *bits) for p, bits in zip(heads[1:], PLANE)]
-    out_keep, out_send = backward(dz)
-    out_got = across(out_send, 1, 0)
-    *outs, zn1, zn2, zn3 = vmem_call(
-        pair_kernel,
-        [shape(out_keep.shape[1:], BF)] * 4 + [shape((2, *zn_keep.shape[1:]), BF)] * 3,
-        [],
-        [out_keep, out_got, zn_keep, zn_got],
-    )
-    outs = [outs[0]] + [across(p, *bits) for p, bits in zip(outs[1:], PLANE)]
+        [head_keep, head_got, out_keep, out_got, zn_keep, zn_got],
+    )
     rest = [across(p, *bits) for p, bits in zip((zn1, zn2, zn3), COLUMN)]
-    block = shape((head_keep.shape[2], head_keep.shape[3] + out_keep.shape[3]), BF)
-    blocks = vmem_call(merge_kernel, [block] * 4, [], [*heads, *outs])
+    others = [across(p, *bits) for p, bits in zip(parts[1:], PLANE)]
+    mine, *rest = lax.optimization_barrier((parts[0], *rest))
+    blocks = vmem_call(
+        functools.partial(add_kernel, count=4), [block] * 4, [], [*reversed(others), mine]
+    )
     others = [across(b, *bits) for b, bits in zip(blocks[1:], COLUMN)]
     (total,) = vmem_call(
-        functools.partial(add_kernel, count=4), [block], [], [blocks[0], *others]
-    )
-    total, *rest = lax.optimization_barrier((total, *rest))
+        functools.partial(add_kernel, count=4), [block], [], [*reversed(others), blocks[0]]
+    )
     (column,) = vmem_call(
         join_kernel,
-        [shape((4, *block.shape), BF)],
+        [part],
         [],
         [total] + [across(total, *bits) for bits in COLUMN],
     )
+    column, reconstruction = lax.optimization_barrier(
+        (column, rebuild([zn_keep, zn_got, *rest]))
+    )
     ours = [column] + [across(column, *bits) for bits in PLANE]
-    return ours, [across(x, 1, 0) for x in ours], [zn_keep, zn_got, *rest]
+    return ours, [across(x, 1, 0) for x in ours], reconstruction
 
 
 def sum_by_blocks(keep, send, groups):
@@ -607,9 +630,15 @@
     dec_width = w_dec_embed.shape[1]
     shape = jax.ShapeDtypeStruct
 
-    send, tok = vmem_call(
+    tall_block = half + rows + 16
+    tok, *send = vmem_call(
         embed_kernel,
-        [shape((HEADS, half + rows + 16, 128), BF), shape((rows, width), BF)],
+        [shape((rows, width), BF)]
+        + (
+            [shape((tall_block, 128), BF)] * HEADS
+            if repeat == 1
+            else [shape((HEADS, tall_block, 128), BF)]
+        ),
         [
             pltpu.VMEM((rows, width), BF),
             pltpu.VMEM((rows, w_qkv.shape[1]), BF),
@@ -617,22 +646,28 @@
             pltpu.VMEM(enc_pos.shape, BF),
             pltpu.VMEM(w_embed.shape, BF),
             pltpu.VMEM(w_qkv.shape, BF),
+            pltpu.VMEM((HEADS, tall_block, 128), BF),
             pltpu.SemaphoreType.DMA,
             pltpu.SemaphoreType.DMA,
+            pltpu.SemaphoreType.DMA((pixels // 256,)),
             pltpu.SemaphoreType.DMA((width // 256,)),
-            pltpu.SemaphoreType.DMA((w_qkv.shape[1] // 256,)),
+            pltpu.SemaphoreType.DMA((HEADS,)),
         ],
-        [source, enc_pos, w_embed, enc_gain, w_qkv, visible_rows],
-        anywhere=(0, 1, 2, 4),
+        [me, source, enc_pos, w_embed, enc_gain, w_qkv, visible_rows],
+        smem=(0,),
+        anywhere=(1, 2, 3, 5),
+        anywhere_out=range(1, 1 + HEADS),
         vmem=56 << 20,
         flops=2 * rows * width * (pixels + w_qkv.shape[1]),
     )
     if repeat == 1:
-        q = kv = swap(send, "ctx")
+        blocks = [across(send[i], 0, i) if i else send[0] for i in ORDER]
         q_at, kv_at = 0, half
     else:
-        q = swap(send[:, :half], "ctx", teams)
-        kv = swap(jnp.tile(send[:, half:], (repeat, 1, 1)), "ctx")
+        blocks = [
+            swap(send[0][:, :half], "ctx", teams),
+            swap(jnp.tile(send[0][:, half:], (repeat, 1, 1)), "ctx"),
+        ]
         q_at, kv_at = 0, 0
     cap_k = (share + 16) * groups
     cap_q = min(HEADS * rows, cap_k)
@@ -646,7 +681,7 @@
             pltpu.VMEM((cap_k + rows, 256), BF),
             pltpu.VMEM((cap_q + rows, 128), BF),
         ],
-        [me, q, kv],
+        [me, *blocks],
         smem=(0,),
         flops=4 * cap_q * cap_k * 128,
     )
@@ -736,9 +771,22 @@
             flops=40 * rows * dec_width * hidden,
         )
 
+    places = [(0,), (1,), (2, 3), (4, 5), (6, 7)] if repeat == 1 else [tuple(range(groups))]
+
+    def rebuild(parts):
+        return vmem_call(
+            functools.partial(gather_kernel, places=places),
+            [shape((rows, pixels), BF)],
+            [pltpu.VMEM(split, F32), pltpu.VMEM((rows, dec_width), BF)],
+            [me, w_head, *parts],
+            smem=(0,),
+            flops=2 * rows * dec_width * pixels,
+        )[0]
+
     if repeat == 1:
-        ours, theirs, zn = sum_by_permutes(head_keep, head_send, *zn, head_back, backward)
-        places = [(0,), (1,), (2, 3), (4, 5), (6, 7)]
+        ours, theirs, reconstruction = sum_by_permutes(
+            head_keep, head_send, *zn, head_back, backward, rebuild
+        )
     else:
         out_keep, out_send = backward(head_back())
         ours, theirs = sum_by_blocks(
@@ -746,16 +794,7 @@
             jnp.concatenate([head_send, out_send], axis=3),
             groups,
         )
-        zn = [swap(zn[0], "ctx")]
-        places = [tuple(range(groups))]
-    (reconstruction,) = vmem_call(
-        functools.partial(gather_kernel, places=places),
-        [shape((rows, pixels), BF)],
-        [pltpu.VMEM(split, F32), pltpu.VMEM((rows, dec_width), BF)],
-        [me, w_head, *zn],
-        smem=(0,),
-        flops=2 * rows * dec_width * pixels,
-    )
+        reconstruction = rebuild([swap(zn[0], "ctx")])
     masked_total = lax.axis_size("dp") * (groups * rows - share * groups)
     grad_head, grad_dec_out, loss = vmem_call(
         functools.partial(place_kernel, masked_total=masked_total),

time: 156 us -> 146 us (0.936)
  blocking collectives: 70 us -> 35.1 us
  starting transfers between devices: 24 us -> 38.8 us
  waiting for transfers between devices: 22.2 us -> 31.4 us
  local copies, waits for them, and re-layouts: 0.1 us -> 2.05 us
  Pallas kernels: 38.2 us -> 36.6 us
    all_to_all x4 -> x3, blocking collectives: 70 us -> 35.1 us  [swap(): lax.all_to_all(x, axis, split_axis=0, concat_axis=0, tiled=True, axis_ind...]
    ppermute x25 -> x29, starting transfers between devices: 24 us -> 38.8 us  [across(): return lax.ppermute(x, ('dp', 'ctx'), pairs)]
    ppermute x25 -> x29, waiting for transfers between devices: 22.2 us -> 31.4 us  [across(): return lax.ppermute(x, ('dp', 'ctx'), pairs)]
    unnamed x34 -> x38, local copies, waits for them, and re-layouts: 0.1 us -> 2.05 us
    pallas_call x14 -> x13, Pallas kernels: 38.2 us -> 36.6 us  [vmem_call(): pl.pallas_call(kernel, out_shape=outs, in_specs=space, out_specs=[pl.Bloc...]
  transfers between devices with their start and end apart: 25 -> 29, of which waited for: 11 -> 19; matrix products, arithmetic and copies ran while one was open for 0% -> 0% of each run, Pallas kernels for 2% -> 4%
where the time goes in v6:
time: 146 us
  starting transfers between devices  38.8 us (27%)
  Pallas kernels  36.6 us (25%)
  blocking collectives  35.1 us (24%)
  waiting for transfers between devices  31.4 us (22%)
  local copies, waits for them, and re-layouts  2.05 us (1%)
    ppermute x29, starting transfers between devices, across(): return lax.ppermute(x, ('dp', 'ctx'), pairs)  38.8 us
    pallas_call x13, Pallas kernels, vmem_call(): pl.pallas_call(kernel, out_shape=outs, in_specs=space, out_specs=[pl.Bloc...  36.6 us
    all_to_all x3, blocking collectives, swap(): lax.all_to_all(x, axis, split_axis=0, concat_axis=0, tiled=True, axis_ind...  35.1 us
    ppermute x29, waiting for transfers between devices, across(): return lax.ppermute(x, ('dp', 'ctx'), pairs)  31.4 us
  transfers between devices with their start and end apart: 29, of which 19 were waited for; matrix products, arithmetic and copies ran while one was open for 0% of the time, Pallas kernels for 4%

profile of v6, /device:TPU:0, one launch (start us, length us, event | category | flops | bytes accessed | tf_op | source)
XLA Modules:
  0.0 145.7 jit_solution(5920948813493113226)
XLA Ops:
  0.7 0.7 pad_add_fusion.me_ref
  1.3 8.1 %shard_map.219 = (bf16[288,1024]{1,0:T(8,128)(2,1)}, bf16[448,128]{1,0:T(8,128)(2,1)}, bf16[448,128]{1,0:T(8,128)(2,1)}, bf16[448,128]{1,0:T(8,128)(2,1)}, bf16[...) custom-call(s32[4]{0:T(128)} %pad_add_fusion.me_ref, ...), custom_call_target="tpu_custom_call" | custom-call | flops 1509949440 | bytes 6425744 | tf_op jit(solution)/shard_map/pallas_call | solution.py:474
  9.5 5.1 %collective-permute-start = (bf16[448,128]{1,0:T(8,128)(2,1)}, bf16[448,128]{1,0:T(8,128)(2,1)S(1)}, u32[]{:S(2)}, u32[]{:S(2)}) collective-permute-start(bf16[448,128]{1,0:T(8,128)(2,1)} %get-tuple-element.57), channel_id=1, source_target_pairs={{0,6},{1,7},{2,4},{3,5},{4,2},{5,3},{6,0},{7,1},{8,14},{9,15},{10,... | collective-permute-start | bytes 344072 | tf_op jit(solution)/shard_map/ppermute | solution.py:533
  14.6 1.2 collective-permute-start.1
  15.8 0.8 collective-permute-start.2
  16.6 1.9 %collective-permute-start.3 = (bf16[448,128]{1,0:T(8,128)(2,1)}, bf16[448,128]{1,0:T(8,128)(2,1)S(1)}, u32[]{:S(2)}, u32[]{:S(2)}) collective-permute-start(bf16[448,128]{1,0:T(8,128)(2,1)} %get-tuple-element.60), channel_id=1, source_target_pairs={{0,5},{1,4},{2,7},{3,6},{4,1},{5,0},{6,3},{7,2},{8,13},{9,12},{10,... | collective-permute-start | bytes 344072 | tf_op jit(solution)/shard_map/ppermute | solution.py:533
  18.5 1.4 collective-permute-start.4
  20.0 9.5 %collective-permute-start.5 = (bf16[448,128]{1,0:T(8,128)(2,1)}, bf16[448,128]{1,0:T(8,128)(2,1)S(1)}, u32[]{:S(2)}, u32[]{:S(2)}) collective-permute-start(bf16[448,128]{1,0:T(8,128)(2,1)} %get-tuple-element.62), channel_id=1, source_target_pairs={{0,3},{1,2},{2,1},{3,0},{4,7},{5,6},{6,5},{7,4},{8,11},{9,10},{10,... | collective-permute-start | bytes 344072 | tf_op jit(solution)/shard_map/ppermute | solution.py:533
  29.4 3.5 %collective-permute-done.2.refs_2_ = bf16[448,128]{1,0:T(8,128)(2,1)S(1)} collective-permute-done((bf16[448,128]{1,0:T(8,128)(2,1)}, bf16[448,128]{1,0:T(8,128)(2,1)S(1)}, u32[]{:S(2)}, u32[]{:S(2)}) %collective-permute-start.2) | collective-permute-done | bytes 114720 | tf_op jit(solution)/shard_map/ppermute | solution.py:533
  32.9 2.6 %collective-permute-done.3.refs_3_ = bf16[448,128]{1,0:T(8,128)(2,1)S(1)} collective-permute-done((bf16[448,128]{1,0:T(8,128)(2,1)}, bf16[448,128]{1,0:T(8,128)(2,1)S(1)}, u32[]{:S(2)}, u32[]{:S(2)}) %collective-permute-start.3) | collective-permute-done | bytes 114720 | tf_op jit(solution)/shard_map/ppermute | solution.py:533
  35.5 1.1 collective-permute-done.5.refs_5_
  36.5 0.8 collective-permute-done.6.refs_6_
  37.3 0.9 copy-done.17
  38.2 5.5 %shard_map.220 = bf16[8,144,128]{2,1,0:T(8,128)(2,1)S(1)} custom-call(s32[4]{0:T(128)S(1)} %copy-done.7, bf16[448,128]{1,0:T(8,128)(2,1)S(1)} %collective-permute-done.refs_0_, bf16[448,128]{1,0:T(8,128)(2,1)S(1)} %collective-permute-done.1.refs_1_, bf16[448,128]{1,0:T(8,128)(2,1)S(1)} %collective-permute-done.2.refs_2_, ...), custom_call_target="tpu_custom_call" | custom-call | flops 411041792 | bytes 917520 | tf_op jit(solution)/shard_map/pallas_call | solution.py:474
  43.7 12.3 %all_to_all.15.att_ref = bf16[8,144,128]{2,1,0:T(8,128)(2,1)S(1)} all-to-all(bf16[8,144,128]{2,1,0:T(8,128)(2,1)S(1)} %shard_map.220), channel_id=1, replica_groups=mesh['dp'=4,'ctx'=8] {'ctx'}, dimensions={0} | all-to-all | bytes 589824 | tf_op jit(solution)/shard_map/all_to_all | solution.py:495
  56.2 1.1 copy-done.5
  57.2 2.6 %shard_map.221 = (bf16[8,216,128]{2,1,0:T(8,128)(2,1)S(1)}, bf16[288,512]{1,0:T(8,128)(2,1)S(1)}, bf16[288,1024]{1,0:T(8,128)(2,1)S(1)}, f32[288,128]{1,0:T(8,128)S(1)}) custom-call(bf16[8,144,128]{2,1,0:T(8,128)(2,1)S(1)} %all_to_all.15.att_ref, bf16[288,1024]{1,0:T(8,128)(2,1)S(1)} %copy-done.5, bf16[512,1024]{1,0:T(8,128)(2,1)S(1)} %copy-done.2, ...), custom_call_target="tpu_custom_call" | custom-call | flops 603979776 | bytes 4659456 | tf_op jit(solution)/shard_map/pallas_call | solution.py:474
  59.8 12.3 %all_to_all.16.q_ref.kv_ref = bf16[8,216,128]{2,1,0:T(8,128)(2,1)S(1)} all-to-all(bf16[8,216,128]{2,1,0:T(8,128)(2,1)S(1)} %get-tuple-element.66), channel_id=1, replica_groups=mesh['dp'=4,'ctx'=8] {'ctx'}, dimensions={0} | all-to-all | bytes 884736 | tf_op jit(solution)/shard_map/all_to_all | solution.py:495
  72.1 7.7 %shard_map.222 = bf16[8,72,128]{2,1,0:T(8,128)(2,1)S(1)} custom-call(bf16[8,216,128]{2,1,0:T(8,128)(2,1)S(1)} %all_to_all.16.q_ref.kv_ref, bf16[8,216,128]{2,1,0:T(8,128)(2,1)S(1)} %all_to_all.16.q_ref.kv_ref), custom_call_target="tpu_custom_call" | custom-call | flops 2717908992 | bytes 884736 | tf_op jit(solution)/shard_map/pallas_call | solution.py:474
  79.9 10.5 %all_to_all.17.att_ref = bf16[8,72,128]{2,1,0:T(8,128)(2,1)S(1)} all-to-all(bf16[8,72,128]{2,1,0:T(8,128)(2,1)S(1)} %shard_map.222), channel_id=1, replica_groups=mesh['dp'=4,'ctx'=8] {'ctx'}, dimensions={0} | all-to-all | bytes 294912 | tf_op jit(solution)/shard_map/all_to_all | solution.py:495
  90.4 5.0 %shard_map.223 = (bf16[288,256]{1,0:T(8,128)(2,1)S(1)}, f32[288,512]{1,0:T(8,128)S(1)}, bf16[288,2048]{1,0:T(8,128)(2,1)S(1)}, f32[288,512]{1,0:T(8,128)S(1)}, b...) custom-call(s32[4]{0:T(128)S(1)} %copy-done.7, ...), custom_call_target="tpu_custom_call" | custom-call | flops 1811939328 | bytes 6686736 | tf_op jit(solution)/shard_map/pallas_call | solution.py:474
  95.7 0.6 shard_map.224.dz_ref
  96.3 1.0 collective-permute-done.7.head_got_ref
  97.4 2.7 %shard_map.225 = (bf16[4,4,16,384]{3,2,1,0:T(8,128)(2,1)S(1)}, bf16[4,4,16,384]{3,2,1,0:T(8,128)(2,1)S(1)}) custom-call(s32[4]{0:T(128)S(1)} %copy-done.7, bf16[288,256]{1,0:T(8,128)(2,1)S(1)} %get-tuple-element.75.dec_att_ref, f32[288,512]{1,0:T(8,128)S(1)} %get-tuple-element.76.mid_ref, bf16[288,2048]{1,0:T(8,128)(2,1)S(1)} %get-tuple-element.77.slope_ref, ...), custom_call_target="tpu_custom_call" | custom-call | flops 12079595520 | bytes 6411280 | tf_op jit(solution)/shard_map/pallas_call | solution.py:474
  100.1 2.0 %collective-permute-done.8.other_ref.refs_1_ = bf16[4,36,512]{2,1,0:T(8,128)(2,1)S(1)} collective-permute-done((bf16[4,36,512]{2,1,0:T(8,128)(2,1)S(1)}, bf16[4,36,512]{2,1,0:T(8,128)(2,1)S(1)}, u32[]{:S(2)}, u32[]{:S(2)}) %collective-permute-start.8) | collective-permute-done | bytes 147488 | tf_op jit(solution)/shard_map/ppermute | solution.py:533
  102.1 1.4 collective-permute-done.9.out_got_ref
  103.7 1.3 collective-permute-start.10
  105.0 1.8 %collective-permute-start.11 = (bf16[4,16,1408]{2,1,0:T(8,128)(2,1)S(1)}, bf16[4,16,1408]{2,1,0:T(8,128)(2,1)S(1)}, u32[]{:S(2)}, u32[]{:S(2)}) collective-permute-start(bf16[4,16,1408]{2,1,0:T(8,128)(2,1)S(1)} %get-tuple-element.87), channel_id=1, source_target_pairs={{0,1},{1,0},{2,3},{3,2},{4,5},{5,4},{6,7},{7,6},{8,9},{9,8},{10,11... | collective-permute-start | bytes 540680 | tf_op jit(solution)/shard_map/ppermute | solution.py:533
  107.3 1.1 collective-permute-start.14
  108.4 3.5 %collective-permute-done.13.refs_2_ = bf16[2,36,512]{2,1,0:T(8,128)(2,1)S(1)} collective-permute-done((bf16[2,36,512]{2,1,0:T(8,128)(2,1)S(1)}, bf16[2,36,512]{2,1,0:T(8,128)(2,1)S(1)}, u32[]{:S(2)}, u32[]{:S(2)}) %collective-permute-start.13) | collective-permute-done | bytes 73760 | tf_op jit(solution)/shard_map/ppermute | solution.py:533
  111.9 1.0 collective-permute-start.15
  112.9 2.8 %collective-permute-done.14.refs_3_ = bf16[2,36,512]{2,1,0:T(8,128)(2,1)S(1)} collective-permute-done((bf16[2,36,512]{2,1,0:T(8,128)(2,1)S(1)}, bf16[2,36,512]{2,1,0:T(8,128)(2,1)S(1)}, u32[]{:S(2)}, u32[]{:S(2)}) %collective-permute-start.14) | collective-permute-done | bytes 73760 | tf_op jit(solution)/shard_map/ppermute | solution.py:533
  115.7 2.4 %collective-permute-done.15.refs_4_ = bf16[2,36,512]{2,1,0:T(8,128)(2,1)S(1)} collective-permute-done((bf16[2,36,512]{2,1,0:T(8,128)(2,1)S(1)}, bf16[2,36,512]{2,1,0:T(8,128)(2,1)S(1)}, u32[]{:S(2)}, u32[]{:S(2)}) %collective-permute-start.15) | collective-permute-done | bytes 73760 | tf_op jit(solution)/shard_map/ppermute | solution.py:533
  118.2 1.1 collective-permute-start.16
  119.3 3.4 %collective-permute-start.18 = (bf16[16,1408]{1,0:T(8,128)(2,1)S(1)}, bf16[16,1408]{1,0:T(8,128)(2,1)S(1)}, u32[]{:S(2)}, u32[]{:S(2)}) collective-permute-start(bf16[16,1408]{1,0:T(8,128)(2,1)S(1)} %get-tuple-element.96), channel_id=1, source_target_pairs={{0,2},{1,3},{2,0},{3,1},{4,6},{5,7},{6,4},{7,5},{8,10},{9,11},{10,... | collective-permute-start | bytes 135176 | tf_op jit(solution)/shard_map/ppermute | solution.py:533
  122.7 1.5 %collective-permute-done.16.refs_0_ = bf16[16,1408]{1,0:T(8,128)(2,1)S(1)} collective-permute-done((bf16[16,1408]{1,0:T(8,128)(2,1)S(1)}, bf16[16,1408]{1,0:T(8,128)(2,1)S(1)}, u32[]{:S(2)}, u32[]{:S(2)}) %collective-permute-start.16) | collective-permute-done | bytes 45088 | tf_op jit(solution)/shard_map/ppermute | solution.py:533
  124.2 1.9 %collective-permute-done.17.refs_1_ = bf16[16,1408]{1,0:T(8,128)(2,1)S(1)} collective-permute-done((bf16[16,1408]{1,0:T(8,128)(2,1)S(1)}, bf16[16,1408]{1,0:T(8,128)(2,1)S(1)}, u32[]{:S(2)}, u32[]{:S(2)}) %collective-permute-start.17) | collective-permute-done | bytes 45088 | tf_op jit(solution)/shard_map/ppermute | solution.py:533
  126.1 1.1 collective-permute-start.21
  127.2 1.6 %collective-permute-start.20 = (bf16[16,1408]{1,0:T(8,128)(2,1)S(1)}, bf16[16,1408]{1,0:T(8,128)(2,1)S(1)}, u32[]{:S(2)}, u32[]{:S(2)}) collective-permute-start(bf16[16,1408]{1,0:T(8,128)(2,1)S(1)} %shard_map.228.refs_0_), channel_id=1, source_target_pairs={{0,4},{1,5},{2,6},{3,7},{4,0},{5,1},{6,2},{7,3},{8,12},{9,13},{10,... | collective-permute-start | bytes 135176 | tf_op jit(solution)/shard_map/ppermute | solution.py:533
  128.8 1.8 %collective-permute-start.19 = (bf16[16,1408]{1,0:T(8,128)(2,1)S(1)}, bf16[16,1408]{1,0:T(8,128)(2,1)S(1)}, u32[]{:S(2)}, u32[]{:S(2)}) collective-permute-start(bf16[16,1408]{1,0:T(8,128)(2,1)S(1)} %shard_map.228.refs_0_), channel_id=1, source_target_pairs={{0,2},{1,3},{2,0},{3,1},{4,6},{5,7},{6,4},{7,5},{8,10},{9,11},{10,... | collective-permute-start | bytes 135176 | tf_op jit(solution)/shard_map/ppermute | solution.py:533
  130.6 1.9 %shard_map.230 = bf16[288,1024]{1,0:T(8,128)(2,1)} custom-call(s32[4]{0:T(128)S(1)} %copy-done.7, bf16[512,1024]{1,0:T(8,128)(2,1)S(1)} %copy-done, bf16[4,36,512]{2,1,0:T(8,128)(2,1)S(1)} %get-tuple-element.84.mine_ref.refs_0_, bf16[4,36,512]{2,1,0:T(8,128)(2,1)S(1)} %collective-permute-done.8.other_ref.refs_1_, ...), custom_call_target="tpu_custom_call" | custom-call | flops 301989888 | bytes 1564688 | tf_op jit(solution)/shard_map/pallas_call | solution.py:474
  132.4 0.7 collective-permute-done.20.refs_2_
  133.3 1.4 collective-permute-start.24
  134.7 1.6 %collective-permute-start.23 = (bf16[4,16,1408]{2,1,0:T(8,128)(2,1)S(1)}, bf16[4,16,1408]{2,1,0:T(8,128)(2,1)S(1)}, u32[]{:S(2)}, u32[]{:S(2)}) collective-permute-start(bf16[4,16,1408]{2,1,0:T(8,128)(2,1)S(1)} %shard_map.229.refs_0_), channel_id=1, source_target_pairs={{0,1},{1,0},{2,3},{3,2},{4,5},{5,4},{6,7},{7,6},{8,9},{9,8},{10,11... | collective-permute-start | bytes 540680 | tf_op jit(solution)/shard_map/ppermute | solution.py:533
  136.8 3.0 %collective-permute-done.24.refs_3_ = bf16[4,16,1408]{2,1,0:T(8,128)(2,1)S(1)} collective-permute-done((bf16[4,16,1408]{2,1,0:T(8,128)(2,1)S(1)}, bf16[4,16,1408]{2,1,0:T(8,128)(2,1)S(1)}, u32[]{:S(2)}, u32[]{:S(2)}) %collective-permute-start.24) | collective-permute-done | bytes 180256 | tf_op jit(solution)/shard_map/ppermute | solution.py:533
  139.8 1.8 %collective-permute-done.23.refs_2_ = bf16[4,16,1408]{2,1,0:T(8,128)(2,1)S(1)} collective-permute-done((bf16[4,16,1408]{2,1,0:T(8,128)(2,1)S(1)}, bf16[4,16,1408]{2,1,0:T(8,128)(2,1)S(1)}, u32[]{:S(2)}, u32[]{:S(2)}) %collective-permute-start.23) | collective-permute-done | bytes 180256 | tf_op jit(solution)/shard_map/ppermute | solution.py:533
  142.2 0.9 collective-permute-done.27.refs_6_
  143.3 2.2 %shard_map.231 = (f32[512,1024]{1,0:T(8,128)}, f32[256,512]{1,0:T(8,128)}, f32[1,1]{1,0:T(1,128)}) custom-call(s32[4]{0:T(128)S(1)} %copy-done.7, bf16[4,16,1408]{2,1,0:T(8,128)(2,1)S(1)} %shard_map.229.refs_0_, bf16[4,16,1408]{2,1,0:T(8,128)(2,1)S(1)} %collective-permute-done.22.refs_1_, bf16[4,16,1408]{2,1,0:T(8,128)(2,1)S(1)} %collective-permute-done.23.refs_2_, ...), custom_call_target="tpu_custom_call" | custom-call | bytes 1441808 | tf_op jit(solution)/shard_map/pallas_call | solution.py:474
  (65 shorter events, 2.7 us)
Async XLA Ops:
  1.3 36.0 %copy-start.7 = (s32[4]{0:T(128)S(1)}, s32[4]{0:T(128)}, u32[]{:S(2)}) copy-start(s32[4]{0:T(128)} %pad_add_fusion.me_ref) | copy-start | bytes 52
  1.3 54.7 %copy-start.3 = (bf16[1024,512]{1,0:T(8,128)(2,1)S(1)}, bf16[1024,512]{1,0:T(8,128)(2,1)}, u32[]{:S(2)}) copy-start(bf16[1024,512]{1,0:T(8,128)(2,1)} %w_dec_ref.1) | copy-start | bytes 3145732
  1.3 54.7 %copy-start.4 = (bf16[512,768]{1,0:T(8,128)(2,1)S(1)}, bf16[512,768]{1,0:T(8,128)(2,1)}, u32[]{:S(2)}) copy-start(bf16[512,768]{1,0:T(8,128)(2,1)} %w_qkv_ref.1) | copy-start | bytes 2359300
  9.4 46.7 %copy-start.1 = (bf16[1,288,1024]{2,1,0:T(8,128)(2,1)S(1)}, bf16[1,288,1024]{2,1,0:T(8,128)(2,1)}, u32[]{:S(2)}) copy-start(bf16[1,288,1024]{2,1,0:T(8,128)(2,1)} %param.21) | copy-start | bytes 1769476
  9.4 46.7 %copy-start.2 = (bf16[512,1024]{1,0:T(8,128)(2,1)S(1)}, bf16[512,1024]{1,0:T(8,128)(2,1)}, u32[]{:S(2)}) copy-start(bf16[512,1024]{1,0:T(8,128)(2,1)} %w_out_ref.2) | copy-start | bytes 3145732
  9.4 46.7 %copy-start.6 = (bf16[288,512]{1,0:T(8,128)(2,1)S(1)}, bf16[288,512]{1,0:T(8,128)(2,1)}, u32[]{:S(2)}) copy-start(bf16[288,512]{1,0:T(8,128)(2,1)} %pos_ref.1) | copy-start | bytes 884740
  9.4 46.7 %copy-start.8 = (s32[1,288]{1,0:T(1,128)S(1)}, s32[1,288]{1,0:T(1,128)}, u32[]{:S(2)}) copy-start(s32[1,288]{1,0:T(1,128)} %slots_ref.3) | copy-start | bytes 3460
  9.4 46.7 %copy-start.9 = (bf16[1024]{0:T(1024)(128)(2,1)S(1)}, bf16[1024]{0:T(1024)(128)(2,1)}, u32[]{:S(2)}) copy-start(bf16[1024]{0:T(1024)(128)(2,1)} %out_gain_ref.1) | copy-start | bytes 6148
  9.5 46.7 %copy-start.10 = (s32[1,288]{1,0:T(1,128)S(1)}, s32[1,288]{1,0:T(1,128)}, u32[]{:S(2)}) copy-start(s32[1,288]{1,0:T(1,128)} %owner_ref.1) | copy-start | bytes 3460
  9.5 46.7 %copy-start.12 = (bf16[512]{0:T(512)(128)(2,1)S(1)}, bf16[512]{0:T(512)(128)(2,1)}, u32[]{:S(2)}) copy-start(bf16[512]{0:T(512)(128)(2,1)} %mask_ref.1) | copy-start | bytes 3076
  9.5 46.7 %copy-start.13 = (bf16[512]{0:T(512)(128)(2,1)S(1)}, bf16[512]{0:T(512)(128)(2,1)}, u32[]{:S(2)}) copy-start(bf16[512]{0:T(512)(128)(2,1)} %gain_ref.3) | copy-start | bytes 3076
  9.5 10.5 %collective-permute-start = (bf16[448,128]{1,0:T(8,128)(2,1)}, bf16[448,128]{1,0:T(8,128)(2,1)S(1)}, u32[]{:S(2)}, u32[]{:S(2)}) collective-permute-start(bf16[448,128]{1,0:T(8,128)(2,1)} %get-tuple-element.57), channel_id=1, source_target_pairs={{0,6},{1,7},{2,4},{3,5},{4,2},{5,3},{6,0},{7,1},{8,14},{9,15},{10,... | collective-permute-start | bytes 344072 | tf_op jit(solution)/shard_map/ppermute | solution.py:533
  14.6 14.8 %collective-permute-start.1 = (bf16[448,128]{1,0:T(8,128)(2,1)}, bf16[448,128]{1,0:T(8,128)(2,1)S(1)}, u32[]{:S(2)}, u32[]{:S(2)}) collective-permute-start(bf16[448,128]{1,0:T(8,128)(2,1)} %get-tuple-element.58), channel_id=1, source_target_pairs={{0,7},{1,6},{2,5},{3,4},{4,3},{5,2},{6,1},{7,0},{8,15},{9,14},{10,... | collective-permute-start | bytes 344072 | tf_op jit(solution)/shard_map/ppermute | solution.py:533
  15.8 17.1 %collective-permute-start.2 = (bf16[448,128]{1,0:T(8,128)(2,1)}, bf16[448,128]{1,0:T(8,128)(2,1)S(1)}, u32[]{:S(2)}, u32[]{:S(2)}) collective-permute-start(bf16[448,128]{1,0:T(8,128)(2,1)} %get-tuple-element.59), channel_id=1, source_target_pairs={{0,4},{1,5},{2,6},{3,7},{4,0},{5,1},{6,2},{7,3},{8,12},{9,13},{10,... | collective-permute-start | bytes 344072 | tf_op jit(solution)/shard_map/ppermute | solution.py:533
  16.6 18.9 %collective-permute-start.3 = (bf16[448,128]{1,0:T(8,128)(2,1)}, bf16[448,128]{1,0:T(8,128)(2,1)S(1)}, u32[]{:S(2)}, u32[]{:S(2)}) collective-permute-start(bf16[448,128]{1,0:T(8,128)(2,1)} %get-tuple-element.60), channel_id=1, source_target_pairs={{0,5},{1,4},{2,7},{3,6},{4,1},{5,0},{6,3},{7,2},{8,13},{9,12},{10,... | collective-permute-start | bytes 344072 | tf_op jit(solution)/shard_map/ppermute | solution.py:533
  18.5 17.0 %collective-permute-start.4 = (bf16[448,128]{1,0:T(8,128)(2,1)}, bf16[448,128]{1,0:T(8,128)(2,1)S(1)}, u32[]{:S(2)}, u32[]{:S(2)}) collective-permute-start(bf16[448,128]{1,0:T(8,128)(2,1)} %get-tuple-element.61), channel_id=1, source_target_pairs={{0,2},{1,3},{2,0},{3,1},{4,6},{5,7},{6,4},{7,5},{8,10},{9,11},{10,... | collective-permute-start | bytes 344072 | tf_op jit(solution)/shard_map/ppermute | solution.py:533
  20.0 16.6 %collective-permute-start.5 = (bf16[448,128]{1,0:T(8,128)(2,1)}, bf16[448,128]{1,0:T(8,128)(2,1)S(1)}, u32[]{:S(2)}, u32[]{:S(2)}) collective-permute-start(bf16[448,128]{1,0:T(8,128)(2,1)} %get-tuple-element.62), channel_id=1, source_target_pairs={{0,3},{1,2},{2,1},{3,0},{4,7},{5,6},{6,5},{7,4},{8,11},{9,10},{10,... | collective-permute-start | bytes 344072 | tf_op jit(solution)/shard_map/ppermute | solution.py:533
  29.4 7.9 %collective-permute-start.6 = (bf16[448,128]{1,0:T(8,128)(2,1)}, bf16[448,128]{1,0:T(8,128)(2,1)S(1)}, u32[]{:S(2)}, u32[]{:S(2)}) collective-permute-start(bf16[448,128]{1,0:T(8,128)(2,1)} %get-tuple-element.63), channel_id=1, source_target_pairs={{0,1},{1,0},{2,3},{3,2},{4,5},{5,4},{6,7},{7,6},{8,9},{9,8},{10,11... | collective-permute-start | bytes 344072 | tf_op jit(solution)/shard_map/ppermute | solution.py:533
  37.3 0.9 copy-start.17
  56.1 1.1 copy-start.5
  72.1 18.3 %copy-start = (bf16[512,1024]{1,0:T(8,128)(2,1)S(1)}, bf16[512,1024]{1,0:T(8,128)(2,1)}, u32[]{:S(2)}) copy-start(bf16[512,1024]{1,0:T(8,128)(2,1)} %w_head_ref.5) | copy-start | bytes 3145732
  72.1 18.3 %copy-start.11 = (bf16[512]{0:T(512)(128)(2,1)S(1)}, bf16[512]{0:T(512)(128)(2,1)}, u32[]{:S(2)}) copy-start(bf16[512]{0:T(512)(128)(2,1)} %head_gain_ref.3) | copy-start | bytes 3076
  72.1 18.3 %copy-start.14 = (bf16[512,2048]{1,0:T(8,128)(2,1)S(1)}, bf16[512,2048]{1,0:T(8,128)(2,1)}, u32[]{:S(2)}) copy-start(bf16[512,2048]{1,0:T(8,128)(2,1)} %w_up_ref.3) | copy-start | bytes 6291460
  72.1 18.3 %copy-start.15 = (bf16[2048,512]{1,0:T(8,128)(2,1)S(1)}, bf16[2048,512]{1,0:T(8,128)(2,1)}, u32[]{:S(2)}) copy-start(bf16[2048,512]{1,0:T(8,128)(2,1)} %w_down_ref.3) | copy-start | bytes 6291460
  72.1 18.3 %copy-start.16 = (bf16[256,512]{1,0:T(8,128)(2,1)S(1)}, bf16[256,512]{1,0:T(8,128)(2,1)}, u32[]{:S(2)}) copy-start(bf16[256,512]{1,0:T(8,128)(2,1)} %w_out_ref.3) | copy-start | bytes 786436
  72.1 18.3 %copy-start.18 = (bf16[512]{0:T(512)(128)(2,1)S(1)}, bf16[512]{0:T(512)(128)(2,1)}, u32[]{:S(2)}) copy-start(bf16[512]{0:T(512)(128)(2,1)} %feed_gain_ref.3) | copy-start | bytes 3076
  95.4 2.0 %collective-permute-start.7 = (bf16[4,4,16,1024]{3,2,1,0:T(8,128)(2,1)S(1)}, bf16[4,4,16,1024]{3,2,1,0:T(8,128)(2,1)S(1)}, u32[]{:S(2)}, u32[]{:S(2)}) collective-permute-start(bf16[4,4,16,1024]{3,2,1,0:T(8,128)(2,1)S(1)} %get-tuple-element.73), channel_id=1, source_target_pairs={{0,8},{1,9},{2,10},{3,11},{4,12},{5,13},{6,14},{7,15},{8,0},{9,1},... | collective-permute-start | bytes 1572872 | tf_op jit(solution)/shard_map/ppermute | solution.py:533
  95.5 6.6 %collective-permute-start.8 = (bf16[4,36,512]{2,1,0:T(8,128)(2,1)S(1)}, bf16[4,36,512]{2,1,0:T(8,128)(2,1)S(1)}, u32[]{:S(2)}, u32[]{:S(2)}) collective-permute-start(bf16[4,36,512]{2,1,0:T(8,128)(2,1)S(1)} %get-tuple-element.82), channel_id=1, source_target_pairs={{0,1},{1,0},{2,3},{3,2},{4,5},{5,4},{6,7},{7,6},{8,9},{9,8},{10,11... | collective-permute-start | bytes 442376 | tf_op jit(solution)/shard_map/ppermute | solution.py:533
  102.1 1.4 collective-permute-start.9
  103.7 14.4 %collective-permute-start.10 = (bf16[4,16,1408]{2,1,0:T(8,128)(2,1)S(1)}, bf16[4,16,1408]{2,1,0:T(8,128)(2,1)S(1)}, u32[]{:S(2)}, u32[]{:S(2)}) collective-permute-start(bf16[4,16,1408]{2,1,0:T(8,128)(2,1)S(1)} %get-tuple-element.86), channel_id=1, source_target_pairs={{0,17},{1,16},{2,19},{3,18},{4,21},{5,20},{6,23},{7,22},{8,25},{9,... | collective-permute-start | bytes 540680 | tf_op jit(solution)/shard_map/ppermute | solution.py:533
  105.0 13.2 %collective-permute-start.11 = (bf16[4,16,1408]{2,1,0:T(8,128)(2,1)S(1)}, bf16[4,16,1408]{2,1,0:T(8,128)(2,1)S(1)}, u32[]{:S(2)}, u32[]{:S(2)}) collective-permute-start(bf16[4,16,1408]{2,1,0:T(8,128)(2,1)S(1)} %get-tuple-element.87), channel_id=1, source_target_pairs={{0,1},{1,0},{2,3},{3,2},{4,5},{5,4},{6,7},{7,6},{8,9},{9,8},{10,11... | collective-permute-start | bytes 540680 | tf_op jit(solution)/shard_map/ppermute | solution.py:533
  106.7 11.4 %collective-permute-start.12 = (bf16[4,16,1408]{2,1,0:T(8,128)(2,1)S(1)}, bf16[4,16,1408]{2,1,0:T(8,128)(2,1)S(1)}, u32[]{:S(2)}, u32[]{:S(2)}) collective-permute-start(bf16[4,16,1408]{2,1,0:T(8,128)(2,1)S(1)} %get-tuple-element.88), channel_id=1, source_target_pairs={{0,16},{1,17},{2,18},{3,19},{4,20},{5,21},{6,22},{7,23},{8,24},{9,... | collective-permute-start | bytes 540680 | tf_op jit(solution)/shard_map/ppermute | solution.py:533
  107.3 4.6 %collective-permute-start.13 = (bf16[2,36,512]{2,1,0:T(8,128)(2,1)S(1)}, bf16[2,36,512]{2,1,0:T(8,128)(2,1)S(1)}, u32[]{:S(2)}, u32[]{:S(2)}) collective-permute-start(bf16[2,36,512]{2,1,0:T(8,128)(2,1)S(1)} %get-tuple-element.90), channel_id=1, source_target_pairs={{0,2},{1,3},{2,0},{3,1},{4,6},{5,7},{6,4},{7,5},{8,10},{9,11},{10,... | collective-permute-start | bytes 221192 | tf_op jit(solution)/shard_map/ppermute | solution.py:533
  107.3 8.4 %collective-permute-start.14 = (bf16[2,36,512]{2,1,0:T(8,128)(2,1)S(1)}, bf16[2,36,512]{2,1,0:T(8,128)(2,1)S(1)}, u32[]{:S(2)}, u32[]{:S(2)}) collective-permute-start(bf16[2,36,512]{2,1,0:T(8,128)(2,1)S(1)} %get-tuple-element.91), channel_id=1, source_target_pairs={{0,4},{1,5},{2,6},{3,7},{4,0},{5,1},{6,2},{7,3},{8,12},{9,13},{10,... | collective-permute-start | bytes 221192 | tf_op jit(solution)/shard_map/ppermute | solution.py:533
  111.9 6.2 %collective-permute-start.15 = (bf16[2,36,512]{2,1,0:T(8,128)(2,1)S(1)}, bf16[2,36,512]{2,1,0:T(8,128)(2,1)S(1)}, u32[]{:S(2)}, u32[]{:S(2)}) collective-permute-start(bf16[2,36,512]{2,1,0:T(8,128)(2,1)S(1)} %get-tuple-element.92), channel_id=1, source_target_pairs={{0,6},{1,7},{2,4},{3,5},{4,2},{5,3},{6,0},{7,1},{8,14},{9,15},{10,... | collective-permute-start | bytes 221192 | tf_op jit(solution)/shard_map/ppermute | solution.py:533
  118.2 5.9 %collective-permute-start.16 = (bf16[16,1408]{1,0:T(8,128)(2,1)S(1)}, bf16[16,1408]{1,0:T(8,128)(2,1)S(1)}, u32[]{:S(2)}, u32[]{:S(2)}) collective-permute-start(bf16[16,1408]{1,0:T(8,128)(2,1)S(1)} %get-tuple-element.94), channel_id=1, source_target_pairs={{0,6},{1,7},{2,4},{3,5},{4,2},{5,3},{6,0},{7,1},{8,14},{9,15},{10,... | collective-permute-start | bytes 135176 | tf_op jit(solution)/shard_map/ppermute | solution.py:533
  119.3 6.8 %collective-permute-start.17 = (bf16[16,1408]{1,0:T(8,128)(2,1)S(1)}, bf16[16,1408]{1,0:T(8,128)(2,1)S(1)}, u32[]{:S(2)}, u32[]{:S(2)}) collective-permute-start(bf16[16,1408]{1,0:T(8,128)(2,1)S(1)} %get-tuple-element.95), channel_id=1, source_target_pairs={{0,4},{1,5},{2,6},{3,7},{4,0},{5,1},{6,2},{7,3},{8,12},{9,13},{10,... | collective-permute-start | bytes 135176 | tf_op jit(solution)/shard_map/ppermute | solution.py:533
  119.3 6.8 %collective-permute-start.18 = (bf16[16,1408]{1,0:T(8,128)(2,1)S(1)}, bf16[16,1408]{1,0:T(8,128)(2,1)S(1)}, u32[]{:S(2)}, u32[]{:S(2)}) collective-permute-start(bf16[16,1408]{1,0:T(8,128)(2,1)S(1)} %get-tuple-element.96), channel_id=1, source_target_pairs={{0,2},{1,3},{2,0},{3,1},{4,6},{5,7},{6,4},{7,5},{8,10},{9,11},{10,... | collective-permute-start | bytes 135176 | tf_op jit(solution)/shard_map/ppermute | solution.py:533
  126.1 6.3 %collective-permute-start.21 = (bf16[16,1408]{1,0:T(8,128)(2,1)S(1)}, bf16[16,1408]{1,0:T(8,128)(2,1)S(1)}, u32[]{:S(2)}, u32[]{:S(2)}) collective-permute-start(bf16[16,1408]{1,0:T(8,128)(2,1)S(1)} %shard_map.228.refs_0_), channel_id=1, source_target_pairs={{0,6},{1,7},{2,4},{3,5},{4,2},{5,3},{6,0},{7,1},{8,14},{9,15},{10,... | collective-permute-start | bytes 135176 | tf_op jit(solution)/shard_map/ppermute | solution.py:533
  127.2 5.9 %collective-permute-start.20 = (bf16[16,1408]{1,0:T(8,128)(2,1)S(1)}, bf16[16,1408]{1,0:T(8,128)(2,1)S(1)}, u32[]{:S(2)}, u32[]{:S(2)}) collective-permute-start(bf16[16,1408]{1,0:T(8,128)(2,1)S(1)} %shard_map.228.refs_0_), channel_id=1, source_target_pairs={{0,4},{1,5},{2,6},{3,7},{4,0},{5,1},{6,2},{7,3},{8,12},{9,13},{10,... | collective-permute-start | bytes 135176 | tf_op jit(solution)/shard_map/ppermute | solution.py:533
  128.8 4.5 %collective-permute-start.19 = (bf16[16,1408]{1,0:T(8,128)(2,1)S(1)}, bf16[16,1408]{1,0:T(8,128)(2,1)S(1)}, u32[]{:S(2)}, u32[]{:S(2)}) collective-permute-start(bf16[16,1408]{1,0:T(8,128)(2,1)S(1)} %shard_map.228.refs_0_), channel_id=1, source_target_pairs={{0,2},{1,3},{2,0},{3,1},{4,6},{5,7},{6,4},{7,5},{8,10},{9,11},{10,... | collective-permute-start | bytes 135176 | tf_op jit(solution)/shard_map/ppermute | solution.py:533
  133.3 6.6 %collective-permute-start.24 = (bf16[4,16,1408]{2,1,0:T(8,128)(2,1)S(1)}, bf16[4,16,1408]{2,1,0:T(8,128)(2,1)S(1)}, u32[]{:S(2)}, u32[]{:S(2)}) collective-permute-start(bf16[4,16,1408]{2,1,0:T(8,128)(2,1)S(1)} %shard_map.229.refs_0_), channel_id=1, source_target_pairs={{0,17},{1,16},{2,19},{3,18},{4,21},{5,20},{6,23},{7,22},{8,25},{9,... | collective-permute-start | bytes 540680 | tf_op jit(solution)/shard_map/ppermute | solution.py:533
  134.7 7.0 %collective-permute-start.23 = (bf16[4,16,1408]{2,1,0:T(8,128)(2,1)S(1)}, bf16[4,16,1408]{2,1,0:T(8,128)(2,1)S(1)}, u32[]{:S(2)}, u32[]{:S(2)}) collective-permute-start(bf16[4,16,1408]{2,1,0:T(8,128)(2,1)S(1)} %shard_map.229.refs_0_), channel_id=1, source_target_pairs={{0,1},{1,0},{2,3},{3,2},{4,5},{5,4},{6,7},{7,6},{8,9},{9,8},{10,11... | collective-permute-start | bytes 540680 | tf_op jit(solution)/shard_map/ppermute | solution.py:533
  136.3 5.5 %collective-permute-start.22 = (bf16[4,16,1408]{2,1,0:T(8,128)(2,1)S(1)}, bf16[4,16,1408]{2,1,0:T(8,128)(2,1)S(1)}, u32[]{:S(2)}, u32[]{:S(2)}) collective-permute-start(bf16[4,16,1408]{2,1,0:T(8,128)(2,1)S(1)} %shard_map.229.refs_0_), channel_id=1, source_target_pairs={{0,16},{1,17},{2,18},{3,19},{4,20},{5,21},{6,22},{7,23},{8,24},{9,... | collective-permute-start | bytes 540680 | tf_op jit(solution)/shard_map/ppermute | solution.py:533
  136.8 5.4 %collective-permute-start.25 = (bf16[4,16,1408]{2,1,0:T(8,128)(2,1)S(1)}, bf16[4,16,1408]{2,1,0:T(8,128)(2,1)S(1)}, u32[]{:S(2)}, u32[]{:S(2)}) collective-permute-start(bf16[4,16,1408]{2,1,0:T(8,128)(2,1)S(1)} %shard_map.229.refs_0_), channel_id=1, source_target_pairs={{0,8},{1,9},{2,10},{3,11},{4,12},{5,13},{6,14},{7,15},{8,0},{9,1},... | collective-permute-start | bytes 540680 | tf_op jit(solution)/shard_map/ppermute | solution.py:533
  139.8 2.3 %collective-permute-start.28 = (bf16[4,16,1408]{2,1,0:T(8,128)(2,1)S(1)}, bf16[4,16,1408]{2,1,0:T(8,128)(2,1)S(1)}, u32[]{:S(2)}, u32[]{:S(2)}) collective-permute-start(bf16[4,16,1408]{2,1,0:T(8,128)(2,1)S(1)} %collective-permute-done.24.refs_3_), channel_id=1, source_target_pairs={{0,8},{1,9},{2,10},{3,11},{4,12},{5,13},{6,14},{7,15},{8,0},{9,1},... | collective-permute-start | bytes 540680 | tf_op jit(solution)/shard_map/ppermute | solution.py:533
  141.7 1.4 collective-permute-start.27
  141.8 1.6 %collective-permute-start.26 = (bf16[4,16,1408]{2,1,0:T(8,128)(2,1)S(1)}, bf16[4,16,1408]{2,1,0:T(8,128)(2,1)S(1)}, u32[]{:S(2)}, u32[]{:S(2)}) collective-permute-start(bf16[4,16,1408]{2,1,0:T(8,128)(2,1)S(1)} %collective-permute-done.22.refs_1_), channel_id=1, source_target_pairs={{0,8},{1,9},{2,10},{3,11},{4,12},{5,13},{6,14},{7,15},{8,0},{9,1},... | collective-permute-start | bytes 540680 | tf_op jit(solution)/shard_map/ppermute | solution.py:533

commit v7 on v6

--- a/solution.py
+++ b/solution.py
@@ -180,19 +180,26 @@
         off = off + (count_of(first + source) + 15) // 16 * 16
     total = off
 
-    tile = 128
     scale = LOG2E * 64**-0.5
 
-    @pl.loop(0, cap_q // tile)
-    def _(step):
-        @pl.when(step * tile < total)
-        def _():
-            at = pl.ds(pl.multiple_of(step * tile, tile), tile)
-            score = dot_t(q_buf[at, :], kv_buf[:cap_k, :128]) + bias
-            top = jnp.max(score, axis=1, keepdims=True)
-            weight = jnp.exp2((score - top) * scale).astype(BF)
-            mixed = dot(weight, kv_buf[:cap_k, :])
-            o_buf[at, :] = (mixed[:, :128] / mixed[:, 128:]).astype(BF)
+    def attend(at):
+        score = dot_t(q_buf[at, :], kv_buf[:cap_k, :128]) + bias
+        top = jnp.max(score, axis=1, keepdims=True)
+        weight = jnp.exp2((score - top) * scale).astype(BF)
+        mixed = dot(weight, kv_buf[:cap_k, :])
+        o_buf[at, :] = (mixed[:, :128] / mixed[:, 128:]).astype(BF)
+
+    if cap_q == cap_k:
+        for at in range(0, cap_q, cap_q // 4):
+            attend(slice(at, at + cap_q // 4))
+    else:
+        tile = 128
+
+        @pl.loop(0, cap_q // tile)
+        def _(step):
+            @pl.when(step * tile < total)
+            def _():
+                attend(pl.ds(pl.multiple_of(step * tile, tile), tile))
 
     for source in range(HEADS):
         upper = o_buf[pl.ds(offs[source], half), :]
@@ -466,7 +473,7 @@
               anywhere_out=(), vmem=VMEM_LIMIT, flops=0):
     space = [
         pl.BlockSpec(
-            memory_space=pltpu.SMEM if i in smem else pl.ANY if i in anywhere else pltpu.VMEM
+            memory_space=pltpu.SMEM if i in smem else pltpu.HBM if i in anywhere else pltpu.VMEM
         )
         for i in range(len(inputs))
     ]
@@ -489,6 +496,10 @@
         compiler_params=pltpu.CompilerParams(vmem_limit_bytes=vmem),
         cost_estimate=pl.CostEstimate(flops=flops, bytes_accessed=moved, transcendentals=0),
     )(*inputs)
+
+
+def pinned(x):
+    return pltpu.with_memory_space_constraint(x, pltpu.HBM)
 
 
 def swap(x, axis, groups=None):
@@ -556,7 +567,8 @@
     )
     rest = [across(p, *bits) for p, bits in zip((zn1, zn2, zn3), COLUMN)]
     others = [across(p, *bits) for p, bits in zip(parts[1:], PLANE)]
-    mine, *rest = lax.optimization_barrier((parts[0], *rest))
+    mine, *far = lax.optimization_barrier((parts[0], *rest[1:]))
+    rest = [rest[0], *far]
     blocks = vmem_call(
         functools.partial(add_kernel, count=4), [block] * 4, [], [*reversed(others), mine]
     )
@@ -653,11 +665,12 @@
             pltpu.SemaphoreType.DMA((width // 256,)),
             pltpu.SemaphoreType.DMA((HEADS,)),
         ],
-        [me, source, enc_pos, w_embed, enc_gain, w_qkv, visible_rows],
+        [me]
+        + [pinned(x) for x in (source, enc_pos, w_embed, enc_gain, w_qkv, visible_rows)],
         smem=(0,),
         anywhere=(1, 2, 3, 5),
         anywhere_out=range(1, 1 + HEADS),
-        vmem=56 << 20,
+        vmem=28 << 20,
         flops=2 * rows * width * (pixels + w_qkv.shape[1]),
     )
     if repeat == 1:

time: 146 us -> 137 us (0.938)
  Pallas kernels: 36.6 us -> 33.4 us
  waiting for transfers between devices: 31.4 us -> 28.3 us
  local copies, waits for them, and re-layouts: 2.05 us -> 0.09 us
    ppermute x29, waiting for transfers between devices: 31.4 us -> 28.3 us  [across(): return lax.ppermute(x, ('dp', 'ctx'), pairs)]
    pallas_call x13, Pallas kernels: 36.6 us -> 33.4 us  [vmem_call(): pl.pallas_call(kernel, out_shape=outs, in_specs=space, out_specs=[pl.Bloc...]
    unnamed x38 -> x32, local copies, waits for them, and re-layouts: 2.05 us -> 0.09 us
  transfers between devices with their start and end apart: 29 -> 29, of which waited for: 19 -> 16; matrix products, arithmetic and copies ran while one was open for 0% -> 0% of each run, Pallas kernels for 4% -> 4%
where the time goes in v7:
time: 137 us
  starting transfers between devices  38.8 us (28%)
  blocking collectives  35.1 us (26%)
  Pallas kernels  33.4 us (24%)
  waiting for transfers between devices  28.3 us (21%)
    ppermute x29, starting transfers between devices, across(): return lax.ppermute(x, ('dp', 'ctx'), pairs)  38.8 us
    all_to_all x3, blocking collectives, swap(): lax.all_to_all(x, axis, split_axis=0, concat_axis=0, tiled=True, axis_ind...  35.1 us
    pallas_call x13, Pallas kernels, vmem_call(): pl.pallas_call(kernel, out_shape=outs, in_specs=space, out_specs=[pl.Bloc...  33.4 us
    ppermute x29, waiting for transfers between devices, across(): return lax.ppermute(x, ('dp', 'ctx'), pairs)  28.3 us
  transfers between devices with their start and end apart: 29, of which 16 were waited for; matrix products, arithmetic and copies ran while one was open for 0% of the time, Pallas kernels for 4%

profile of v7, /device:TPU:0, one launch (start us, length us, event | category | flops | bytes accessed | tf_op | source)
XLA Modules:
  0.0 136.9 jit_solution(3389584535614861012)
XLA Ops:
  0.8 7.5 %shard_map.219 = (bf16[288,1024]{1,0:T(8,128)(2,1)S(1)}, bf16[448,128]{1,0:T(8,128)(2,1)S(1)}, bf16[448,128]{1,0:T(8,128)(2,1)S(1)}, bf16[448,128]{1,0:T(8,128)(...) custom-call(s32[4]{0:T(128)S(1)} %pad_add_fusion.me_ref, ...), custom_call_target="tpu_custom_call" | custom-call | flops 1509949440 | bytes 6425744 | tf_op jit(solution)/shard_map/pallas_call | solution.py:481
  8.4 5.1 %collective-permute-start = (bf16[448,128]{1,0:T(8,128)(2,1)S(1)}, bf16[448,128]{1,0:T(8,128)(2,1)S(1)}, u32[]{:S(2)}, u32[]{:S(2)}) collective-permute-start(bf16[448,128]{1,0:T(8,128)(2,1)S(1)} %get-tuple-element.56), channel_id=1, source_target_pairs={{0,6},{1,7},{2,4},{3,5},{4,2},{5,3},{6,0},{7,1},{8,14},{9,15},{10,... | collective-permute-start | bytes 344072 | tf_op jit(solution)/shard_map/ppermute | solution.py:544
  13.5 1.2 collective-permute-start.1
  14.7 0.8 collective-permute-start.2
  15.5 1.9 %collective-permute-start.3 = (bf16[448,128]{1,0:T(8,128)(2,1)S(1)}, bf16[448,128]{1,0:T(8,128)(2,1)S(1)}, u32[]{:S(2)}, u32[]{:S(2)}) collective-permute-start(bf16[448,128]{1,0:T(8,128)(2,1)S(1)} %get-tuple-element.59), channel_id=1, source_target_pairs={{0,5},{1,4},{2,7},{3,6},{4,1},{5,0},{6,3},{7,2},{8,13},{9,12},{10,... | collective-permute-start | bytes 344072 | tf_op jit(solution)/shard_map/ppermute | solution.py:544
  17.4 1.4 %collective-permute-start.4 = (bf16[448,128]{1,0:T(8,128)(2,1)S(1)}, bf16[448,128]{1,0:T(8,128)(2,1)S(1)}, u32[]{:S(2)}, u32[]{:S(2)}) collective-permute-start(bf16[448,128]{1,0:T(8,128)(2,1)S(1)} %get-tuple-element.60), channel_id=1, source_target_pairs={{0,2},{1,3},{2,0},{3,1},{4,6},{5,7},{6,4},{7,5},{8,10},{9,11},{10,... | collective-permute-start | bytes 344072 | tf_op jit(solution)/shard_map/ppermute | solution.py:544
  18.8 9.3 %collective-permute-start.5 = (bf16[448,128]{1,0:T(8,128)(2,1)S(1)}, bf16[448,128]{1,0:T(8,128)(2,1)S(1)}, u32[]{:S(2)}, u32[]{:S(2)}) collective-permute-start(bf16[448,128]{1,0:T(8,128)(2,1)S(1)} %get-tuple-element.61), channel_id=1, source_target_pairs={{0,3},{1,2},{2,1},{3,0},{4,7},{5,6},{6,5},{7,4},{8,11},{9,10},{10,... | collective-permute-start | bytes 344072 | tf_op jit(solution)/shard_map/ppermute | solution.py:544
  28.1 3.5 %collective-permute-done.2.refs_2_ = bf16[448,128]{1,0:T(8,128)(2,1)S(1)} collective-permute-done((bf16[448,128]{1,0:T(8,128)(2,1)S(1)}, bf16[448,128]{1,0:T(8,128)(2,1)S(1)}, u32[]{:S(2)}, u32[]{:S(2)}) %collective-permute-start.2) | collective-permute-done | bytes 114720 | tf_op jit(solution)/shard_map/ppermute | solution.py:544
  31.6 2.5 %collective-permute-done.3.refs_3_ = bf16[448,128]{1,0:T(8,128)(2,1)S(1)} collective-permute-done((bf16[448,128]{1,0:T(8,128)(2,1)S(1)}, bf16[448,128]{1,0:T(8,128)(2,1)S(1)}, u32[]{:S(2)}, u32[]{:S(2)}) %collective-permute-start.3) | collective-permute-done | bytes 114720 | tf_op jit(solution)/shard_map/ppermute | solution.py:544
  34.2 1.0 collective-permute-done.5.refs_5_
  35.1 0.7 collective-permute-done.6.refs_6_
  35.8 2.8 %shard_map.220 = bf16[8,144,128]{2,1,0:T(8,128)(2,1)S(1)} custom-call(s32[4]{0:T(128)S(1)} %pad_add_fusion.me_ref, bf16[448,128]{1,0:T(8,128)(2,1)S(1)} %collective-permute-done.refs_0_, bf16[448,128]{1,0:T(8,128)(2,1)S(1)} %collective-permute-done.1.refs_1_, bf16[448,128]{1,0:T(8,128)(2,1)S(1)} %collective-permute-done.2.refs_2_, ...), custom_call_target="tpu_custom_call" | custom-call | flops 411041792 | bytes 917520 | tf_op jit(solution)/shard_map/pallas_call | solution.py:481
  38.6 12.3 %all_to_all.15.att_ref = bf16[8,144,128]{2,1,0:T(8,128)(2,1)S(1)} all-to-all(bf16[8,144,128]{2,1,0:T(8,128)(2,1)S(1)} %shard_map.220), channel_id=1, replica_groups=mesh['dp'=4,'ctx'=8] {'ctx'}, dimensions={0} | all-to-all | bytes 589824 | tf_op jit(solution)/shard_map/all_to_all | solution.py:506
  51.0 2.6 %shard_map.221 = (bf16[8,216,128]{2,1,0:T(8,128)(2,1)S(1)}, bf16[288,512]{1,0:T(8,128)(2,1)S(1)}, bf16[288,1024]{1,0:T(8,128)(2,1)S(1)}, f32[288,128]{1,0:T(8,128)S(1)}) custom-call(bf16[8,144,128]{2,1,0:T(8,128)(2,1)S(1)} %all_to_all.15.att_ref, bf16[288,1024]{1,0:T(8,128)(2,1)S(1)} %get-tuple-element.64.tok_ref, bf16[512,1024]{1,0:T(8,128)(2,1)S(1)} %copy-done.2, ...), custom_call_target="tpu_custom_call" | custom-call | flops 603979776 | bytes 4659456 | tf_op jit(solution)/shard_map/pallas_call | solution.py:481
  53.6 12.3 %all_to_all.16.q_ref.kv_ref = bf16[8,216,128]{2,1,0:T(8,128)(2,1)S(1)} all-to-all(bf16[8,216,128]{2,1,0:T(8,128)(2,1)S(1)} %get-tuple-element.65), channel_id=1, replica_groups=mesh['dp'=4,'ctx'=8] {'ctx'}, dimensions={0} | all-to-all | bytes 884736 | tf_op jit(solution)/shard_map/all_to_all | solution.py:506
  65.9 7.7 %shard_map.222 = bf16[8,72,128]{2,1,0:T(8,128)(2,1)S(1)} custom-call(bf16[8,216,128]{2,1,0:T(8,128)(2,1)S(1)} %all_to_all.16.q_ref.kv_ref, bf16[8,216,128]{2,1,0:T(8,128)(2,1)S(1)} %all_to_all.16.q_ref.kv_ref), custom_call_target="tpu_custom_call" | custom-call | flops 2717908992 | bytes 884736 | tf_op jit(solution)/shard_map/pallas_call | solution.py:481
  73.7 10.5 %all_to_all.17.att_ref = bf16[8,72,128]{2,1,0:T(8,128)(2,1)S(1)} all-to-all(bf16[8,72,128]{2,1,0:T(8,128)(2,1)S(1)} %shard_map.222), channel_id=1, replica_groups=mesh['dp'=4,'ctx'=8] {'ctx'}, dimensions={0} | all-to-all | bytes 294912 | tf_op jit(solution)/shard_map/all_to_all | solution.py:506
  84.2 5.0 %shard_map.223 = (bf16[288,256]{1,0:T(8,128)(2,1)S(1)}, f32[288,512]{1,0:T(8,128)S(1)}, bf16[288,2048]{1,0:T(8,128)(2,1)S(1)}, f32[288,512]{1,0:T(8,128)S(1)}, b...) custom-call(s32[4]{0:T(128)S(1)} %pad_add_fusion.me_ref, ...), custom_call_target="tpu_custom_call" | custom-call | flops 1811939328 | bytes 6686736 | tf_op jit(solution)/shard_map/pallas_call | solution.py:481
  89.6 0.6 shard_map.224.dz_ref
  90.2 1.0 collective-permute-done.7.head_got_ref
  91.2 2.7 %shard_map.225 = (bf16[4,4,16,384]{3,2,1,0:T(8,128)(2,1)S(1)}, bf16[4,4,16,384]{3,2,1,0:T(8,128)(2,1)S(1)}) custom-call(s32[4]{0:T(128)S(1)} %pad_add_fusion.me_ref, bf16[288,256]{1,0:T(8,128)(2,1)S(1)} %get-tuple-element.74.dec_att_ref, f32[288,512]{1,0:T(8,128)S(1)} %get-tuple-element.75.mid_ref, bf16[288,2048]{1,0:T(8,128)(2,1)S(1)} %get-tuple-element.76.slope_ref, ...), custom_call_target="tpu_custom_call" | custom-call | flops 12079595520 | bytes 6411280 | tf_op jit(solution)/shard_map/pallas_call | solution.py:481
  94.0 2.0 %collective-permute-done.8.other_ref.refs_1_ = bf16[4,36,512]{2,1,0:T(8,128)(2,1)S(1)} collective-permute-done((bf16[4,36,512]{2,1,0:T(8,128)(2,1)S(1)}, bf16[4,36,512]{2,1,0:T(8,128)(2,1)S(1)}, u32[]{:S(2)}, u32[]{:S(2)}) %collective-permute-start.8) | collective-permute-done | bytes 147488 | tf_op jit(solution)/shard_map/ppermute | solution.py:544
  96.0 1.4 %collective-permute-done.9.out_got_ref = bf16[4,4,16,384]{3,2,1,0:T(8,128)(2,1)S(1)} collective-permute-done((bf16[4,4,16,384]{3,2,1,0:T(8,128)(2,1)S(1)}, bf16[4,4,16,384]{3,2,1,0:T(8,128)(2,1)S(1)}, u32[]{:S(2)}, u32[]{:S(2)}) %collective-permute-start.9) | collective-permute-done | bytes 196640 | tf_op jit(solution)/shard_map/ppermute | solution.py:544
  97.6 1.3 collective-permute-start.10
  98.8 1.8 %collective-permute-start.11 = (bf16[4,16,1408]{2,1,0:T(8,128)(2,1)S(1)}, bf16[4,16,1408]{2,1,0:T(8,128)(2,1)S(1)}, u32[]{:S(2)}, u32[]{:S(2)}) collective-permute-start(bf16[4,16,1408]{2,1,0:T(8,128)(2,1)S(1)} %get-tuple-element.86), channel_id=1, source_target_pairs={{0,1},{1,0},{2,3},{3,2},{4,5},{5,4},{6,7},{7,6},{8,9},{9,8},{10,11... | collective-permute-start | bytes 540680 | tf_op jit(solution)/shard_map/ppermute | solution.py:544
  100.6 0.5 collective-permute-start.12
  101.1 0.4 collective-permute-start.13
  101.5 1.9 %collective-permute-start.14 = (bf16[2,36,512]{2,1,0:T(8,128)(2,1)S(1)}, bf16[2,36,512]{2,1,0:T(8,128)(2,1)S(1)}, u32[]{:S(2)}, u32[]{:S(2)}) collective-permute-start(bf16[2,36,512]{2,1,0:T(8,128)(2,1)S(1)} %get-tuple-element.90), channel_id=1, source_target_pairs={{0,6},{1,7},{2,4},{3,5},{4,2},{5,3},{6,0},{7,1},{8,14},{9,15},{10,... | collective-permute-start | bytes 221192 | tf_op jit(solution)/shard_map/ppermute | solution.py:544
  103.4 6.0 %collective-permute-done.13.refs_3_ = bf16[2,36,512]{2,1,0:T(8,128)(2,1)S(1)} collective-permute-done((bf16[2,36,512]{2,1,0:T(8,128)(2,1)S(1)}, bf16[2,36,512]{2,1,0:T(8,128)(2,1)S(1)}, u32[]{:S(2)}, u32[]{:S(2)}) %collective-permute-start.13) | collective-permute-done | bytes 73760 | tf_op jit(solution)/shard_map/ppermute | solution.py:544
  109.5 1.1 collective-permute-start.15
  110.6 2.5 %collective-permute-start.16 = (bf16[16,1408]{1,0:T(8,128)(2,1)S(1)}, bf16[16,1408]{1,0:T(8,128)(2,1)S(1)}, u32[]{:S(2)}, u32[]{:S(2)}) collective-permute-start(bf16[16,1408]{1,0:T(8,128)(2,1)S(1)} %get-tuple-element.93), channel_id=1, source_target_pairs={{0,4},{1,5},{2,6},{3,7},{4,0},{5,1},{6,2},{7,3},{8,12},{9,13},{10,... | collective-permute-start | bytes 135176 | tf_op jit(solution)/shard_map/ppermute | solution.py:544
  113.1 0.9 collective-permute-start.17
  114.0 1.7 %collective-permute-done.15.refs_0_ = bf16[16,1408]{1,0:T(8,128)(2,1)S(1)} collective-permute-done((bf16[16,1408]{1,0:T(8,128)(2,1)S(1)}, bf16[16,1408]{1,0:T(8,128)(2,1)S(1)}, u32[]{:S(2)}, u32[]{:S(2)}) %collective-permute-start.15) | collective-permute-done | bytes 45088 | tf_op jit(solution)/shard_map/ppermute | solution.py:544
  115.7 0.9 collective-permute-done.16.refs_1_
  116.5 0.6 collective-permute-done.17.refs_2_
  117.2 1.5 %collective-permute-start.20 = (bf16[16,1408]{1,0:T(8,128)(2,1)S(1)}, bf16[16,1408]{1,0:T(8,128)(2,1)S(1)}, u32[]{:S(2)}, u32[]{:S(2)}) collective-permute-start(bf16[16,1408]{1,0:T(8,128)(2,1)S(1)} %shard_map.228.refs_0_), channel_id=1, source_target_pairs={{0,6},{1,7},{2,4},{3,5},{4,2},{5,3},{6,0},{7,1},{8,14},{9,15},{10,... | collective-permute-start | bytes 135176 | tf_op jit(solution)/shard_map/ppermute | solution.py:544
  118.7 0.9 collective-permute-start.19
  119.6 2.0 %collective-permute-start.18 = (bf16[16,1408]{1,0:T(8,128)(2,1)S(1)}, bf16[16,1408]{1,0:T(8,128)(2,1)S(1)}, u32[]{:S(2)}, u32[]{:S(2)}) collective-permute-start(bf16[16,1408]{1,0:T(8,128)(2,1)S(1)} %shard_map.228.refs_0_), channel_id=1, source_target_pairs={{0,2},{1,3},{2,0},{3,1},{4,6},{5,7},{6,4},{7,5},{8,10},{9,11},{10,... | collective-permute-start | bytes 135176 | tf_op jit(solution)/shard_map/ppermute | solution.py:544
  121.6 1.9 %shard_map.230 = bf16[288,1024]{1,0:T(8,128)(2,1)} custom-call(s32[4]{0:T(128)S(1)} %pad_add_fusion.me_ref, bf16[512,1024]{1,0:T(8,128)(2,1)S(1)} %copy-done, bf16[4,36,512]{2,1,0:T(8,128)(2,1)S(1)} %get-tuple-element.83.mine_ref.refs_0_, bf16[4,36,512]{2,1,0:T(8,128)(2,1)S(1)} %collective-permute-done.8.other_ref.refs_1_, ...), custom_call_target="tpu_custom_call" | custom-call | flops 301989888 | bytes 1564688 | tf_op jit(solution)/shard_map/pallas_call | solution.py:481
  123.5 0.6 collective-permute-done.19.refs_2_
  124.1 1.7 %collective-permute-start.24 = (bf16[4,16,1408]{2,1,0:T(8,128)(2,1)S(1)}, bf16[4,16,1408]{2,1,0:T(8,128)(2,1)S(1)}, u32[]{:S(2)}, u32[]{:S(2)}) collective-permute-start(bf16[4,16,1408]{2,1,0:T(8,128)(2,1)S(1)} %shard_map.229.refs_0_), channel_id=1, source_target_pairs={{0,17},{1,16},{2,19},{3,18},{4,21},{5,20},{6,23},{7,22},{8,25},{9,... | collective-permute-start | bytes 540680 | tf_op jit(solution)/shard_map/ppermute | solution.py:544
  125.8 1.3 collective-permute-start.23
  127.1 0.6 collective-permute-start.22
  127.7 3.3 %collective-permute-done.24.refs_3_ = bf16[4,16,1408]{2,1,0:T(8,128)(2,1)S(1)} collective-permute-done((bf16[4,16,1408]{2,1,0:T(8,128)(2,1)S(1)}, bf16[4,16,1408]{2,1,0:T(8,128)(2,1)S(1)}, u32[]{:S(2)}, u32[]{:S(2)}) %collective-permute-start.24) | collective-permute-done | bytes 180256 | tf_op jit(solution)/shard_map/ppermute | solution.py:544
  131.0 1.8 %collective-permute-done.23.refs_2_ = bf16[4,16,1408]{2,1,0:T(8,128)(2,1)S(1)} collective-permute-done((bf16[4,16,1408]{2,1,0:T(8,128)(2,1)S(1)}, bf16[4,16,1408]{2,1,0:T(8,128)(2,1)S(1)}, u32[]{:S(2)}, u32[]{:S(2)}) %collective-permute-start.23) | collective-permute-done | bytes 180256 | tf_op jit(solution)/shard_map/ppermute | solution.py:544
  132.8 0.5 collective-permute-start.26
  133.3 0.9 collective-permute-done.27.refs_6_
  134.5 2.2 %shard_map.231 = (f32[512,1024]{1,0:T(8,128)}, f32[256,512]{1,0:T(8,128)}, f32[1,1]{1,0:T(1,128)}) custom-call(s32[4]{0:T(128)S(1)} %pad_add_fusion.me_ref, bf16[4,16,1408]{2,1,0:T(8,128)(2,1)S(1)} %shard_map.229.refs_0_, bf16[4,16,1408]{2,1,0:T(8,128)(2,1)S(1)} %collective-permute-done.22.refs_1_, bf16[4,16,1408]{2,1,0:T(8,128)(2,1)S(1)} %collective-permute-done.23.refs_2_, ...), custom_call_target="tpu_custom_call" | custom-call | bytes 1441808 | tf_op jit(solution)/shard_map/pallas_call | solution.py:481
  (59 shorter events, 1.1 us)
Async XLA Ops:
  0.8 50.1 %copy-start.3 = (bf16[1024,512]{1,0:T(8,128)(2,1)S(1)}, bf16[1024,512]{1,0:T(8,128)(2,1)}, u32[]{:S(2)}) copy-start(bf16[1024,512]{1,0:T(8,128)(2,1)} %w_dec_ref.1) | copy-start | bytes 3145732
  0.8 50.1 %copy-start.4 = (bf16[512,768]{1,0:T(8,128)(2,1)S(1)}, bf16[512,768]{1,0:T(8,128)(2,1)}, u32[]{:S(2)}) copy-start(bf16[512,768]{1,0:T(8,128)(2,1)} %w_qkv_ref.1) | copy-start | bytes 2359300
  8.3 42.6 %copy-start.1 = (bf16[1,288,1024]{2,1,0:T(8,128)(2,1)S(1)}, bf16[1,288,1024]{2,1,0:T(8,128)(2,1)}, u32[]{:S(2)}) copy-start(bf16[1,288,1024]{2,1,0:T(8,128)(2,1)} %param.21) | copy-start | bytes 1769476
  8.3 42.6 %copy-start.2 = (bf16[512,1024]{1,0:T(8,128)(2,1)S(1)}, bf16[512,1024]{1,0:T(8,128)(2,1)}, u32[]{:S(2)}) copy-start(bf16[512,1024]{1,0:T(8,128)(2,1)} %w_out_ref.2) | copy-start | bytes 3145732
  8.3 42.6 %copy-start.5 = (bf16[288,512]{1,0:T(8,128)(2,1)S(1)}, bf16[288,512]{1,0:T(8,128)(2,1)}, u32[]{:S(2)}) copy-start(bf16[288,512]{1,0:T(8,128)(2,1)} %pos_ref.1) | copy-start | bytes 884740
  8.3 42.6 %copy-start.6 = (s32[1,288]{1,0:T(1,128)S(1)}, s32[1,288]{1,0:T(1,128)}, u32[]{:S(2)}) copy-start(s32[1,288]{1,0:T(1,128)} %slots_ref.3) | copy-start | bytes 3460
  8.3 42.6 %copy-start.7 = (bf16[1024]{0:T(1024)(128)(2,1)S(1)}, bf16[1024]{0:T(1024)(128)(2,1)}, u32[]{:S(2)}) copy-start(bf16[1024]{0:T(1024)(128)(2,1)} %out_gain_ref.1) | copy-start | bytes 6148
  8.3 42.6 %copy-start.8 = (s32[1,288]{1,0:T(1,128)S(1)}, s32[1,288]{1,0:T(1,128)}, u32[]{:S(2)}) copy-start(s32[1,288]{1,0:T(1,128)} %owner_ref.1) | copy-start | bytes 3460
  8.4 42.6 %copy-start.10 = (bf16[512]{0:T(512)(128)(2,1)S(1)}, bf16[512]{0:T(512)(128)(2,1)}, u32[]{:S(2)}) copy-start(bf16[512]{0:T(512)(128)(2,1)} %mask_ref.1) | copy-start | bytes 3076
  8.4 42.6 %copy-start.11 = (bf16[512]{0:T(512)(128)(2,1)S(1)}, bf16[512]{0:T(512)(128)(2,1)}, u32[]{:S(2)}) copy-start(bf16[512]{0:T(512)(128)(2,1)} %gain_ref.3) | copy-start | bytes 3076
  8.4 10.5 %collective-permute-start = (bf16[448,128]{1,0:T(8,128)(2,1)S(1)}, bf16[448,128]{1,0:T(8,128)(2,1)S(1)}, u32[]{:S(2)}, u32[]{:S(2)}) collective-permute-start(bf16[448,128]{1,0:T(8,128)(2,1)S(1)} %get-tuple-element.56), channel_id=1, source_target_pairs={{0,6},{1,7},{2,4},{3,5},{4,2},{5,3},{6,0},{7,1},{8,14},{9,15},{10,... | collective-permute-start | bytes 344072 | tf_op jit(solution)/shard_map/ppermute | solution.py:544
  13.5 14.6 %collective-permute-start.1 = (bf16[448,128]{1,0:T(8,128)(2,1)S(1)}, bf16[448,128]{1,0:T(8,128)(2,1)S(1)}, u32[]{:S(2)}, u32[]{:S(2)}) collective-permute-start(bf16[448,128]{1,0:T(8,128)(2,1)S(1)} %get-tuple-element.57), channel_id=1, source_target_pairs={{0,7},{1,6},{2,5},{3,4},{4,3},{5,2},{6,1},{7,0},{8,15},{9,14},{10,... | collective-permute-start | bytes 344072 | tf_op jit(solution)/shard_map/ppermute | solution.py:544
  14.7 16.9 %collective-permute-start.2 = (bf16[448,128]{1,0:T(8,128)(2,1)S(1)}, bf16[448,128]{1,0:T(8,128)(2,1)S(1)}, u32[]{:S(2)}, u32[]{:S(2)}) collective-permute-start(bf16[448,128]{1,0:T(8,128)(2,1)S(1)} %get-tuple-element.58), channel_id=1, source_target_pairs={{0,4},{1,5},{2,6},{3,7},{4,0},{5,1},{6,2},{7,3},{8,12},{9,13},{10,... | collective-permute-start | bytes 344072 | tf_op jit(solution)/shard_map/ppermute | solution.py:544
  15.5 18.7 %collective-permute-start.3 = (bf16[448,128]{1,0:T(8,128)(2,1)S(1)}, bf16[448,128]{1,0:T(8,128)(2,1)S(1)}, u32[]{:S(2)}, u32[]{:S(2)}) collective-permute-start(bf16[448,128]{1,0:T(8,128)(2,1)S(1)} %get-tuple-element.59), channel_id=1, source_target_pairs={{0,5},{1,4},{2,7},{3,6},{4,1},{5,0},{6,3},{7,2},{8,13},{9,12},{10,... | collective-permute-start | bytes 344072 | tf_op jit(solution)/shard_map/ppermute | solution.py:544
  17.4 16.8 %collective-permute-start.4 = (bf16[448,128]{1,0:T(8,128)(2,1)S(1)}, bf16[448,128]{1,0:T(8,128)(2,1)S(1)}, u32[]{:S(2)}, u32[]{:S(2)}) collective-permute-start(bf16[448,128]{1,0:T(8,128)(2,1)S(1)} %get-tuple-element.60), channel_id=1, source_target_pairs={{0,2},{1,3},{2,0},{3,1},{4,6},{5,7},{6,4},{7,5},{8,10},{9,11},{10,... | collective-permute-start | bytes 344072 | tf_op jit(solution)/shard_map/ppermute | solution.py:544
  18.8 16.3 %collective-permute-start.5 = (bf16[448,128]{1,0:T(8,128)(2,1)S(1)}, bf16[448,128]{1,0:T(8,128)(2,1)S(1)}, u32[]{:S(2)}, u32[]{:S(2)}) collective-permute-start(bf16[448,128]{1,0:T(8,128)(2,1)S(1)} %get-tuple-element.61), channel_id=1, source_target_pairs={{0,3},{1,2},{2,1},{3,0},{4,7},{5,6},{6,5},{7,4},{8,11},{9,10},{10,... | collective-permute-start | bytes 344072 | tf_op jit(solution)/shard_map/ppermute | solution.py:544
  28.1 7.7 %collective-permute-start.6 = (bf16[448,128]{1,0:T(8,128)(2,1)S(1)}, bf16[448,128]{1,0:T(8,128)(2,1)S(1)}, u32[]{:S(2)}, u32[]{:S(2)}) collective-permute-start(bf16[448,128]{1,0:T(8,128)(2,1)S(1)} %get-tuple-element.62), channel_id=1, source_target_pairs={{0,1},{1,0},{2,3},{3,2},{4,5},{5,4},{6,7},{7,6},{8,9},{9,8},{10,11... | collective-permute-start | bytes 344072 | tf_op jit(solution)/shard_map/ppermute | solution.py:544
  65.9 18.3 %copy-start = (bf16[512,1024]{1,0:T(8,128)(2,1)S(1)}, bf16[512,1024]{1,0:T(8,128)(2,1)}, u32[]{:S(2)}) copy-start(bf16[512,1024]{1,0:T(8,128)(2,1)} %w_head_ref.5) | copy-start | bytes 3145732
  65.9 18.3 %copy-start.9 = (bf16[512]{0:T(512)(128)(2,1)S(1)}, bf16[512]{0:T(512)(128)(2,1)}, u32[]{:S(2)}) copy-start(bf16[512]{0:T(512)(128)(2,1)} %head_gain_ref.3) | copy-start | bytes 3076
  65.9 18.3 %copy-start.12 = (bf16[512,2048]{1,0:T(8,128)(2,1)S(1)}, bf16[512,2048]{1,0:T(8,128)(2,1)}, u32[]{:S(2)}) copy-start(bf16[512,2048]{1,0:T(8,128)(2,1)} %w_up_ref.3) | copy-start | bytes 6291460
  65.9 18.3 %copy-start.13 = (bf16[2048,512]{1,0:T(8,128)(2,1)S(1)}, bf16[2048,512]{1,0:T(8,128)(2,1)}, u32[]{:S(2)}) copy-start(bf16[2048,512]{1,0:T(8,128)(2,1)} %w_down_ref.3) | copy-start | bytes 6291460
  65.9 18.3 %copy-start.14 = (bf16[256,512]{1,0:T(8,128)(2,1)S(1)}, bf16[256,512]{1,0:T(8,128)(2,1)}, u32[]{:S(2)}) copy-start(bf16[256,512]{1,0:T(8,128)(2,1)} %w_out_ref.3) | copy-start | bytes 786436
  65.9 18.3 %copy-start.15 = (bf16[512]{0:T(512)(128)(2,1)S(1)}, bf16[512]{0:T(512)(128)(2,1)}, u32[]{:S(2)}) copy-start(bf16[512]{0:T(512)(128)(2,1)} %feed_gain_ref.3) | copy-start | bytes 3076
  89.3 2.0 %collective-permute-start.7 = (bf16[4,4,16,1024]{3,2,1,0:T(8,128)(2,1)S(1)}, bf16[4,4,16,1024]{3,2,1,0:T(8,128)(2,1)S(1)}, u32[]{:S(2)}, u32[]{:S(2)}) collective-permute-start(bf16[4,4,16,1024]{3,2,1,0:T(8,128)(2,1)S(1)} %get-tuple-element.72), channel_id=1, source_target_pairs={{0,8},{1,9},{2,10},{3,11},{4,12},{5,13},{6,14},{7,15},{8,0},{9,1},... | collective-permute-start | bytes 1572872 | tf_op jit(solution)/shard_map/ppermute | solution.py:544
  89.4 6.6 %collective-permute-start.8 = (bf16[4,36,512]{2,1,0:T(8,128)(2,1)S(1)}, bf16[4,36,512]{2,1,0:T(8,128)(2,1)S(1)}, u32[]{:S(2)}, u32[]{:S(2)}) collective-permute-start(bf16[4,36,512]{2,1,0:T(8,128)(2,1)S(1)} %get-tuple-element.81), channel_id=1, source_target_pairs={{0,1},{1,0},{2,3},{3,2},{4,5},{5,4},{6,7},{7,6},{8,9},{9,8},{10,11... | collective-permute-start | bytes 442376 | tf_op jit(solution)/shard_map/ppermute | solution.py:544
  96.0 1.4 %collective-permute-start.9 = (bf16[4,4,16,384]{3,2,1,0:T(8,128)(2,1)S(1)}, bf16[4,4,16,384]{3,2,1,0:T(8,128)(2,1)S(1)}, u32[]{:S(2)}, u32[]{:S(2)}) collective-permute-start(bf16[4,4,16,384]{3,2,1,0:T(8,128)(2,1)S(1)} %get-tuple-element.82), channel_id=1, source_target_pairs={{0,8},{1,9},{2,10},{3,11},{4,12},{5,13},{6,14},{7,15},{8,0},{9,1},... | collective-permute-start | bytes 589832 | tf_op jit(solution)/shard_map/ppermute | solution.py:544
  97.6 11.8 %collective-permute-start.10 = (bf16[4,16,1408]{2,1,0:T(8,128)(2,1)S(1)}, bf16[4,16,1408]{2,1,0:T(8,128)(2,1)S(1)}, u32[]{:S(2)}, u32[]{:S(2)}) collective-permute-start(bf16[4,16,1408]{2,1,0:T(8,128)(2,1)S(1)} %get-tuple-element.85), channel_id=1, source_target_pairs={{0,17},{1,16},{2,19},{3,18},{4,21},{5,20},{6,23},{7,22},{8,25},{9,... | collective-permute-start | bytes 540680 | tf_op jit(solution)/shard_map/ppermute | solution.py:544
  98.8 10.6 %collective-permute-start.11 = (bf16[4,16,1408]{2,1,0:T(8,128)(2,1)S(1)}, bf16[4,16,1408]{2,1,0:T(8,128)(2,1)S(1)}, u32[]{:S(2)}, u32[]{:S(2)}) collective-permute-start(bf16[4,16,1408]{2,1,0:T(8,128)(2,1)S(1)} %get-tuple-element.86), channel_id=1, source_target_pairs={{0,1},{1,0},{2,3},{3,2},{4,5},{5,4},{6,7},{7,6},{8,9},{9,8},{10,11... | collective-permute-start | bytes 540680 | tf_op jit(solution)/shard_map/ppermute | solution.py:544
  100.6 8.8 %collective-permute-start.12 = (bf16[4,16,1408]{2,1,0:T(8,128)(2,1)S(1)}, bf16[4,16,1408]{2,1,0:T(8,128)(2,1)S(1)}, u32[]{:S(2)}, u32[]{:S(2)}) collective-permute-start(bf16[4,16,1408]{2,1,0:T(8,128)(2,1)S(1)} %get-tuple-element.87), channel_id=1, source_target_pairs={{0,16},{1,17},{2,18},{3,19},{4,20},{5,21},{6,22},{7,23},{8,24},{9,... | collective-permute-start | bytes 540680 | tf_op jit(solution)/shard_map/ppermute | solution.py:544
  101.1 8.3 %collective-permute-start.13 = (bf16[2,36,512]{2,1,0:T(8,128)(2,1)S(1)}, bf16[2,36,512]{2,1,0:T(8,128)(2,1)S(1)}, u32[]{:S(2)}, u32[]{:S(2)}) collective-permute-start(bf16[2,36,512]{2,1,0:T(8,128)(2,1)S(1)} %get-tuple-element.89), channel_id=1, source_target_pairs={{0,4},{1,5},{2,6},{3,7},{4,0},{5,1},{6,2},{7,3},{8,12},{9,13},{10,... | collective-permute-start | bytes 221192 | tf_op jit(solution)/shard_map/ppermute | solution.py:544
  101.5 7.9 %collective-permute-start.14 = (bf16[2,36,512]{2,1,0:T(8,128)(2,1)S(1)}, bf16[2,36,512]{2,1,0:T(8,128)(2,1)S(1)}, u32[]{:S(2)}, u32[]{:S(2)}) collective-permute-start(bf16[2,36,512]{2,1,0:T(8,128)(2,1)S(1)} %get-tuple-element.90), channel_id=1, source_target_pairs={{0,6},{1,7},{2,4},{3,5},{4,2},{5,3},{6,0},{7,1},{8,14},{9,15},{10,... | collective-permute-start | bytes 221192 | tf_op jit(solution)/shard_map/ppermute | solution.py:544
  109.4 12.2 %collective-permute-start.21 = (bf16[2,36,512]{2,1,0:T(8,128)(2,1)S(1)}, bf16[2,36,512]{2,1,0:T(8,128)(2,1)S(1)}, u32[]{:S(2)}, u32[]{:S(2)}) collective-permute-start(bf16[2,36,512]{2,1,0:T(8,128)(2,1)S(1)} %get-tuple-element.96), channel_id=1, source_target_pairs={{0,2},{1,3},{2,0},{3,1},{4,6},{5,7},{6,4},{7,5},{8,10},{9,11},{10,... | collective-permute-start | bytes 221192 | tf_op jit(solution)/shard_map/ppermute | solution.py:544
  109.5 6.1 %collective-permute-start.15 = (bf16[16,1408]{1,0:T(8,128)(2,1)S(1)}, bf16[16,1408]{1,0:T(8,128)(2,1)S(1)}, u32[]{:S(2)}, u32[]{:S(2)}) collective-permute-start(bf16[16,1408]{1,0:T(8,128)(2,1)S(1)} %get-tuple-element.92), channel_id=1, source_target_pairs={{0,6},{1,7},{2,4},{3,5},{4,2},{5,3},{6,0},{7,1},{8,14},{9,15},{10,... | collective-permute-start | bytes 135176 | tf_op jit(solution)/shard_map/ppermute | solution.py:544
  110.6 6.0 %collective-permute-start.16 = (bf16[16,1408]{1,0:T(8,128)(2,1)S(1)}, bf16[16,1408]{1,0:T(8,128)(2,1)S(1)}, u32[]{:S(2)}, u32[]{:S(2)}) collective-permute-start(bf16[16,1408]{1,0:T(8,128)(2,1)S(1)} %get-tuple-element.93), channel_id=1, source_target_pairs={{0,4},{1,5},{2,6},{3,7},{4,0},{5,1},{6,2},{7,3},{8,12},{9,13},{10,... | collective-permute-start | bytes 135176 | tf_op jit(solution)/shard_map/ppermute | solution.py:544
  113.1 4.0 %collective-permute-start.17 = (bf16[16,1408]{1,0:T(8,128)(2,1)S(1)}, bf16[16,1408]{1,0:T(8,128)(2,1)S(1)}, u32[]{:S(2)}, u32[]{:S(2)}) collective-permute-start(bf16[16,1408]{1,0:T(8,128)(2,1)S(1)} %get-tuple-element.94), channel_id=1, source_target_pairs={{0,2},{1,3},{2,0},{3,1},{4,6},{5,7},{6,4},{7,5},{8,10},{9,11},{10,... | collective-permute-start | bytes 135176 | tf_op jit(solution)/shard_map/ppermute | solution.py:544
  117.2 6.3 %collective-permute-start.20 = (bf16[16,1408]{1,0:T(8,128)(2,1)S(1)}, bf16[16,1408]{1,0:T(8,128)(2,1)S(1)}, u32[]{:S(2)}, u32[]{:S(2)}) collective-permute-start(bf16[16,1408]{1,0:T(8,128)(2,1)S(1)} %shard_map.228.refs_0_), channel_id=1, source_target_pairs={{0,6},{1,7},{2,4},{3,5},{4,2},{5,3},{6,0},{7,1},{8,14},{9,15},{10,... | collective-permute-start | bytes 135176 | tf_op jit(solution)/shard_map/ppermute | solution.py:544
  118.7 5.4 %collective-permute-start.19 = (bf16[16,1408]{1,0:T(8,128)(2,1)S(1)}, bf16[16,1408]{1,0:T(8,128)(2,1)S(1)}, u32[]{:S(2)}, u32[]{:S(2)}) collective-permute-start(bf16[16,1408]{1,0:T(8,128)(2,1)S(1)} %shard_map.228.refs_0_), channel_id=1, source_target_pairs={{0,4},{1,5},{2,6},{3,7},{4,0},{5,1},{6,2},{7,3},{8,12},{9,13},{10,... | collective-permute-start | bytes 135176 | tf_op jit(solution)/shard_map/ppermute | solution.py:544
  119.6 4.5 %collective-permute-start.18 = (bf16[16,1408]{1,0:T(8,128)(2,1)S(1)}, bf16[16,1408]{1,0:T(8,128)(2,1)S(1)}, u32[]{:S(2)}, u32[]{:S(2)}) collective-permute-start(bf16[16,1408]{1,0:T(8,128)(2,1)S(1)} %shard_map.228.refs_0_), channel_id=1, source_target_pairs={{0,2},{1,3},{2,0},{3,1},{4,6},{5,7},{6,4},{7,5},{8,10},{9,11},{10,... | collective-permute-start | bytes 135176 | tf_op jit(solution)/shard_map/ppermute | solution.py:544
  124.1 6.8 %collective-permute-start.24 = (bf16[4,16,1408]{2,1,0:T(8,128)(2,1)S(1)}, bf16[4,16,1408]{2,1,0:T(8,128)(2,1)S(1)}, u32[]{:S(2)}, u32[]{:S(2)}) collective-permute-start(bf16[4,16,1408]{2,1,0:T(8,128)(2,1)S(1)} %shard_map.229.refs_0_), channel_id=1, source_target_pairs={{0,17},{1,16},{2,19},{3,18},{4,21},{5,20},{6,23},{7,22},{8,25},{9,... | collective-permute-start | bytes 540680 | tf_op jit(solution)/shard_map/ppermute | solution.py:544
  125.8 7.0 %collective-permute-start.23 = (bf16[4,16,1408]{2,1,0:T(8,128)(2,1)S(1)}, bf16[4,16,1408]{2,1,0:T(8,128)(2,1)S(1)}, u32[]{:S(2)}, u32[]{:S(2)}) collective-permute-start(bf16[4,16,1408]{2,1,0:T(8,128)(2,1)S(1)} %shard_map.229.refs_0_), channel_id=1, source_target_pairs={{0,1},{1,0},{2,3},{3,2},{4,5},{5,4},{6,7},{7,6},{8,9},{9,8},{10,11... | collective-permute-start | bytes 540680 | tf_op jit(solution)/shard_map/ppermute | solution.py:544
  127.1 5.7 %collective-permute-start.22 = (bf16[4,16,1408]{2,1,0:T(8,128)(2,1)S(1)}, bf16[4,16,1408]{2,1,0:T(8,128)(2,1)S(1)}, u32[]{:S(2)}, u32[]{:S(2)}) collective-permute-start(bf16[4,16,1408]{2,1,0:T(8,128)(2,1)S(1)} %shard_map.229.refs_0_), channel_id=1, source_target_pairs={{0,16},{1,17},{2,18},{3,19},{4,20},{5,21},{6,22},{7,23},{8,24},{9,... | collective-permute-start | bytes 540680 | tf_op jit(solution)/shard_map/ppermute | solution.py:544
  127.7 5.6 %collective-permute-start.25 = (bf16[4,16,1408]{2,1,0:T(8,128)(2,1)S(1)}, bf16[4,16,1408]{2,1,0:T(8,128)(2,1)S(1)}, u32[]{:S(2)}, u32[]{:S(2)}) collective-permute-start(bf16[4,16,1408]{2,1,0:T(8,128)(2,1)S(1)} %shard_map.229.refs_0_), channel_id=1, source_target_pairs={{0,8},{1,9},{2,10},{3,11},{4,12},{5,13},{6,14},{7,15},{8,0},{9,1},... | collective-permute-start | bytes 540680 | tf_op jit(solution)/shard_map/ppermute | solution.py:544
  131.0 2.3 %collective-permute-start.28 = (bf16[4,16,1408]{2,1,0:T(8,128)(2,1)S(1)}, bf16[4,16,1408]{2,1,0:T(8,128)(2,1)S(1)}, u32[]{:S(2)}, u32[]{:S(2)}) collective-permute-start(bf16[4,16,1408]{2,1,0:T(8,128)(2,1)S(1)} %collective-permute-done.24.refs_3_), channel_id=1, source_target_pairs={{0,8},{1,9},{2,10},{3,11},{4,12},{5,13},{6,14},{7,15},{8,0},{9,1},... | collective-permute-start | bytes 540680 | tf_op jit(solution)/shard_map/ppermute | solution.py:544
  132.8 1.4 %collective-permute-start.27 = (bf16[4,16,1408]{2,1,0:T(8,128)(2,1)S(1)}, bf16[4,16,1408]{2,1,0:T(8,128)(2,1)S(1)}, u32[]{:S(2)}, u32[]{:S(2)}) collective-permute-start(bf16[4,16,1408]{2,1,0:T(8,128)(2,1)S(1)} %collective-permute-done.23.refs_2_), channel_id=1, source_target_pairs={{0,8},{1,9},{2,10},{3,11},{4,12},{5,13},{6,14},{7,15},{8,0},{9,1},... | collective-permute-start | bytes 540680 | tf_op jit(solution)/shard_map/ppermute | solution.py:544
  132.8 1.7 %collective-permute-start.26 = (bf16[4,16,1408]{2,1,0:T(8,128)(2,1)S(1)}, bf16[4,16,1408]{2,1,0:T(8,128)(2,1)S(1)}, u32[]{:S(2)}, u32[]{:S(2)}) collective-permute-start(bf16[4,16,1408]{2,1,0:T(8,128)(2,1)S(1)} %collective-permute-done.22.refs_1_), channel_id=1, source_target_pairs={{0,8},{1,9},{2,10},{3,11},{4,12},{5,13},{6,14},{7,15},{8,0},{9,1},... | collective-permute-start | bytes 540680 | tf_op jit(solution)/shard_map/ppermute | solution.py:544

commit v8 on v7

--- a/solution.py
+++ b/solution.py
@@ -552,9 +552,8 @@
     shape = jax.ShapeDtypeStruct
     head_got = across(head_send, 1, 0)
     zn_got = across(zn_send, 0, 1)
-    dz, head_got = lax.optimization_barrier((head_back(), head_got))
-    out_keep, out_send = backward(dz)
-    out_send, zn_got = lax.optimization_barrier((out_send, zn_got))
+    out_keep, out_send = backward(head_back())
+    out_send, head_got, zn_got = lax.optimization_barrier((out_send, head_got, zn_got))
     out_got = across(out_send, 1, 0)
     block = shape((head_keep.shape[2], head_keep.shape[3] + out_keep.shape[3]), BF)
     part = shape((4, *block.shape), BF)

time: 137 us -> 136 us (level)
  transfers between devices with their start and end apart: 29 -> 29, of which waited for: 16 -> 15; matrix products, arithmetic and copies ran while one was open for 0% -> 0% of each run, Pallas kernels for 4% -> 4%
where the time goes in v8:
time: 136 us
  starting transfers between devices  38.7 us (28%)
  blocking collectives  35.1 us (26%)
  Pallas kernels  33.4 us (25%)
  waiting for transfers between devices  27.3 us (20%)
    ppermute x29, starting transfers between devices, across(): return lax.ppermute(x, ('dp', 'ctx'), pairs)  38.7 us
    all_to_all x3, blocking collectives, swap(): lax.all_to_all(x, axis, split_axis=0, concat_axis=0, tiled=True, axis_ind...  35.1 us
    pallas_call x13, Pallas kernels, vmem_call(): pl.pallas_call(kernel, out_shape=outs, in_specs=space, out_specs=[pl.Bloc...  33.4 us
    ppermute x29, waiting for transfers between devices, across(): return lax.ppermute(x, ('dp', 'ctx'), pairs)  27.3 us
  transfers between devices with their start and end apart: 29, of which 15 were waited for; matrix products, arithmetic and copies ran while one was open for 0% of the time, Pallas kernels for 4%

profile of v8, /device:TPU:0, one launch (start us, length us, event | category | flops | bytes accessed | tf_op | source)
XLA Modules:
  0.0 135.8 jit_solution(15329339861566185642)
XLA Ops:
  0.8 7.5 %shard_map.219 = (bf16[288,1024]{1,0:T(8,128)(2,1)S(1)}, bf16[448,128]{1,0:T(8,128)(2,1)S(1)}, bf16[448,128]{1,0:T(8,128)(2,1)S(1)}, bf16[448,128]{1,0:T(8,128)(...) custom-call(s32[4]{0:T(128)S(1)} %pad_add_fusion.me_ref, ...), custom_call_target="tpu_custom_call" | custom-call | flops 1509949440 | bytes 6425744 | tf_op jit(solution)/shard_map/pallas_call | solution.py:481
  8.4 5.1 %collective-permute-start = (bf16[448,128]{1,0:T(8,128)(2,1)S(1)}, bf16[448,128]{1,0:T(8,128)(2,1)S(1)}, u32[]{:S(2)}, u32[]{:S(2)}) collective-permute-start(bf16[448,128]{1,0:T(8,128)(2,1)S(1)} %get-tuple-element.55), channel_id=1, source_target_pairs={{0,6},{1,7},{2,4},{3,5},{4,2},{5,3},{6,0},{7,1},{8,14},{9,15},{10,... | collective-permute-start | bytes 344072 | tf_op jit(solution)/shard_map/ppermute | solution.py:544
  13.5 1.2 collective-permute-start.1
  14.7 0.8 collective-permute-start.2
  15.5 1.9 %collective-permute-start.3 = (bf16[448,128]{1,0:T(8,128)(2,1)S(1)}, bf16[448,128]{1,0:T(8,128)(2,1)S(1)}, u32[]{:S(2)}, u32[]{:S(2)}) collective-permute-start(bf16[448,128]{1,0:T(8,128)(2,1)S(1)} %get-tuple-element.58), channel_id=1, source_target_pairs={{0,5},{1,4},{2,7},{3,6},{4,1},{5,0},{6,3},{7,2},{8,13},{9,12},{10,... | collective-permute-start | bytes 344072 | tf_op jit(solution)/shard_map/ppermute | solution.py:544
  17.4 1.4 %collective-permute-start.4 = (bf16[448,128]{1,0:T(8,128)(2,1)S(1)}, bf16[448,128]{1,0:T(8,128)(2,1)S(1)}, u32[]{:S(2)}, u32[]{:S(2)}) collective-permute-start(bf16[448,128]{1,0:T(8,128)(2,1)S(1)} %get-tuple-element.59), channel_id=1, source_target_pairs={{0,2},{1,3},{2,0},{3,1},{4,6},{5,7},{6,4},{7,5},{8,10},{9,11},{10,... | collective-permute-start | bytes 344072 | tf_op jit(solution)/shard_map/ppermute | solution.py:544
  18.8 9.3 %collective-permute-start.5 = (bf16[448,128]{1,0:T(8,128)(2,1)S(1)}, bf16[448,128]{1,0:T(8,128)(2,1)S(1)}, u32[]{:S(2)}, u32[]{:S(2)}) collective-permute-start(bf16[448,128]{1,0:T(8,128)(2,1)S(1)} %get-tuple-element.60), channel_id=1, source_target_pairs={{0,3},{1,2},{2,1},{3,0},{4,7},{5,6},{6,5},{7,4},{8,11},{9,10},{10,... | collective-permute-start | bytes 344072 | tf_op jit(solution)/shard_map/ppermute | solution.py:544
  28.1 3.5 %collective-permute-done.2.refs_2_ = bf16[448,128]{1,0:T(8,128)(2,1)S(1)} collective-permute-done((bf16[448,128]{1,0:T(8,128)(2,1)S(1)}, bf16[448,128]{1,0:T(8,128)(2,1)S(1)}, u32[]{:S(2)}, u32[]{:S(2)}) %collective-permute-start.2) | collective-permute-done | bytes 114720 | tf_op jit(solution)/shard_map/ppermute | solution.py:544
  31.6 2.5 %collective-permute-done.3.refs_3_ = bf16[448,128]{1,0:T(8,128)(2,1)S(1)} collective-permute-done((bf16[448,128]{1,0:T(8,128)(2,1)S(1)}, bf16[448,128]{1,0:T(8,128)(2,1)S(1)}, u32[]{:S(2)}, u32[]{:S(2)}) %collective-permute-start.3) | collective-permute-done | bytes 114720 | tf_op jit(solution)/shard_map/ppermute | solution.py:544
  34.2 1.0 collective-permute-done.5.refs_5_
  35.1 0.7 collective-permute-done.6.refs_6_
  35.8 2.8 %shard_map.220 = bf16[8,144,128]{2,1,0:T(8,128)(2,1)S(1)} custom-call(s32[4]{0:T(128)S(1)} %pad_add_fusion.me_ref, bf16[448,128]{1,0:T(8,128)(2,1)S(1)} %collective-permute-done.refs_0_, bf16[448,128]{1,0:T(8,128)(2,1)S(1)} %collective-permute-done.1.refs_1_, bf16[448,128]{1,0:T(8,128)(2,1)S(1)} %collective-permute-done.2.refs_2_, ...), custom_call_target="tpu_custom_call" | custom-call | flops 411041792 | bytes 917520 | tf_op jit(solution)/shard_map/pallas_call | solution.py:481
  38.6 12.3 %all_to_all.15.att_ref = bf16[8,144,128]{2,1,0:T(8,128)(2,1)S(1)} all-to-all(bf16[8,144,128]{2,1,0:T(8,128)(2,1)S(1)} %shard_map.220), channel_id=1, replica_groups=mesh['dp'=4,'ctx'=8] {'ctx'}, dimensions={0} | all-to-all | bytes 589824 | tf_op jit(solution)/shard_map/all_to_all | solution.py:506
  51.0 2.7 %shard_map.221 = (bf16[8,216,128]{2,1,0:T(8,128)(2,1)S(1)}, bf16[288,512]{1,0:T(8,128)(2,1)S(1)}, bf16[288,1024]{1,0:T(8,128)(2,1)S(1)}, f32[288,128]{1,0:T(8,128)S(1)}) custom-call(bf16[8,144,128]{2,1,0:T(8,128)(2,1)S(1)} %all_to_all.15.att_ref, bf16[288,1024]{1,0:T(8,128)(2,1)S(1)} %get-tuple-element.63.tok_ref, bf16[512,1024]{1,0:T(8,128)(2,1)S(1)} %copy-done.2, ...), custom_call_target="tpu_custom_call" | custom-call | flops 603979776 | bytes 4659456 | tf_op jit(solution)/shard_map/pallas_call | solution.py:481
  53.6 12.2 %all_to_all.16.q_ref.kv_ref = bf16[8,216,128]{2,1,0:T(8,128)(2,1)S(1)} all-to-all(bf16[8,216,128]{2,1,0:T(8,128)(2,1)S(1)} %get-tuple-element.64), channel_id=1, replica_groups=mesh['dp'=4,'ctx'=8] {'ctx'}, dimensions={0} | all-to-all | bytes 884736 | tf_op jit(solution)/shard_map/all_to_all | solution.py:506
  65.9 7.7 %shard_map.222 = bf16[8,72,128]{2,1,0:T(8,128)(2,1)S(1)} custom-call(bf16[8,216,128]{2,1,0:T(8,128)(2,1)S(1)} %all_to_all.16.q_ref.kv_ref, bf16[8,216,128]{2,1,0:T(8,128)(2,1)S(1)} %all_to_all.16.q_ref.kv_ref), custom_call_target="tpu_custom_call" | custom-call | flops 2717908992 | bytes 884736 | tf_op jit(solution)/shard_map/pallas_call | solution.py:481
  73.7 10.5 %all_to_all.17.att_ref = bf16[8,72,128]{2,1,0:T(8,128)(2,1)S(1)} all-to-all(bf16[8,72,128]{2,1,0:T(8,128)(2,1)S(1)} %shard_map.222), channel_id=1, replica_groups=mesh['dp'=4,'ctx'=8] {'ctx'}, dimensions={0} | all-to-all | bytes 294912 | tf_op jit(solution)/shard_map/all_to_all | solution.py:506
  84.2 5.0 %shard_map.223 = (bf16[288,256]{1,0:T(8,128)(2,1)S(1)}, f32[288,512]{1,0:T(8,128)S(1)}, bf16[288,2048]{1,0:T(8,128)(2,1)S(1)}, f32[288,512]{1,0:T(8,128)S(1)}, b...) custom-call(s32[4]{0:T(128)S(1)} %pad_add_fusion.me_ref, ...), custom_call_target="tpu_custom_call" | custom-call | flops 1811939328 | bytes 6686736 | tf_op jit(solution)/shard_map/pallas_call | solution.py:481
  89.5 0.6 shard_map.224.dz_ref
  90.1 2.7 %shard_map.225 = (bf16[4,4,16,384]{3,2,1,0:T(8,128)(2,1)S(1)}, bf16[4,4,16,384]{3,2,1,0:T(8,128)(2,1)S(1)}) custom-call(s32[4]{0:T(128)S(1)} %pad_add_fusion.me_ref, bf16[288,256]{1,0:T(8,128)(2,1)S(1)} %get-tuple-element.69.dec_att_ref, f32[288,512]{1,0:T(8,128)S(1)} %get-tuple-element.70.mid_ref, bf16[288,2048]{1,0:T(8,128)(2,1)S(1)} %get-tuple-element.71.slope_ref, ...), custom_call_target="tpu_custom_call" | custom-call | flops 12079595520 | bytes 6411280 | tf_op jit(solution)/shard_map/pallas_call | solution.py:481
  92.8 1.8 %collective-permute-done.8.other_ref.refs_1_ = bf16[4,36,512]{2,1,0:T(8,128)(2,1)S(1)} collective-permute-done((bf16[4,36,512]{2,1,0:T(8,128)(2,1)S(1)}, bf16[4,36,512]{2,1,0:T(8,128)(2,1)S(1)}, u32[]{:S(2)}, u32[]{:S(2)}) %collective-permute-start.8) | collective-permute-done | bytes 147488 | tf_op jit(solution)/shard_map/ppermute | solution.py:544
  94.7 1.4 %collective-permute-done.9.out_got_ref = bf16[4,4,16,384]{3,2,1,0:T(8,128)(2,1)S(1)} collective-permute-done((bf16[4,4,16,384]{3,2,1,0:T(8,128)(2,1)S(1)}, bf16[4,4,16,384]{3,2,1,0:T(8,128)(2,1)S(1)}, u32[]{:S(2)}, u32[]{:S(2)}) %collective-permute-start.9) | collective-permute-done | bytes 196640 | tf_op jit(solution)/shard_map/ppermute | solution.py:544
  96.3 1.3 collective-permute-start.10
  97.6 1.7 %collective-permute-start.11 = (bf16[4,16,1408]{2,1,0:T(8,128)(2,1)S(1)}, bf16[4,16,1408]{2,1,0:T(8,128)(2,1)S(1)}, u32[]{:S(2)}, u32[]{:S(2)}) collective-permute-start(bf16[4,16,1408]{2,1,0:T(8,128)(2,1)S(1)} %get-tuple-element.84), channel_id=1, source_target_pairs={{0,1},{1,0},{2,3},{3,2},{4,5},{5,4},{6,7},{7,6},{8,9},{9,8},{10,11... | collective-permute-start | bytes 540680 | tf_op jit(solution)/shard_map/ppermute | solution.py:544
  99.3 0.5 collective-permute-start.12
  99.8 0.4 collective-permute-start.13
  100.2 1.9 %collective-permute-start.14 = (bf16[2,36,512]{2,1,0:T(8,128)(2,1)S(1)}, bf16[2,36,512]{2,1,0:T(8,128)(2,1)S(1)}, u32[]{:S(2)}, u32[]{:S(2)}) collective-permute-start(bf16[2,36,512]{2,1,0:T(8,128)(2,1)S(1)} %get-tuple-element.88), channel_id=1, source_target_pairs={{0,6},{1,7},{2,4},{3,5},{4,2},{5,3},{6,0},{7,1},{8,14},{9,15},{10,... | collective-permute-start | bytes 221192 | tf_op jit(solution)/shard_map/ppermute | solution.py:544
  102.1 6.0 %collective-permute-done.13.refs_3_ = bf16[2,36,512]{2,1,0:T(8,128)(2,1)S(1)} collective-permute-done((bf16[2,36,512]{2,1,0:T(8,128)(2,1)S(1)}, bf16[2,36,512]{2,1,0:T(8,128)(2,1)S(1)}, u32[]{:S(2)}, u32[]{:S(2)}) %collective-permute-start.13) | collective-permute-done | bytes 73760 | tf_op jit(solution)/shard_map/ppermute | solution.py:544
  108.2 1.1 collective-permute-start.15
  109.3 2.5 %collective-permute-start.16 = (bf16[16,1408]{1,0:T(8,128)(2,1)S(1)}, bf16[16,1408]{1,0:T(8,128)(2,1)S(1)}, u32[]{:S(2)}, u32[]{:S(2)}) collective-permute-start(bf16[16,1408]{1,0:T(8,128)(2,1)S(1)} %get-tuple-element.91), channel_id=1, source_target_pairs={{0,4},{1,5},{2,6},{3,7},{4,0},{5,1},{6,2},{7,3},{8,12},{9,13},{10,... | collective-permute-start | bytes 135176 | tf_op jit(solution)/shard_map/ppermute | solution.py:544
  111.8 0.9 collective-permute-start.17
  112.7 1.7 %collective-permute-done.15.refs_0_ = bf16[16,1408]{1,0:T(8,128)(2,1)S(1)} collective-permute-done((bf16[16,1408]{1,0:T(8,128)(2,1)S(1)}, bf16[16,1408]{1,0:T(8,128)(2,1)S(1)}, u32[]{:S(2)}, u32[]{:S(2)}) %collective-permute-start.15) | collective-permute-done | bytes 45088 | tf_op jit(solution)/shard_map/ppermute | solution.py:544
  114.4 0.9 collective-permute-done.16.refs_1_
  115.2 0.6 collective-permute-done.17.refs_2_
  115.8 1.5 %collective-permute-start.20 = (bf16[16,1408]{1,0:T(8,128)(2,1)S(1)}, bf16[16,1408]{1,0:T(8,128)(2,1)S(1)}, u32[]{:S(2)}, u32[]{:S(2)}) collective-permute-start(bf16[16,1408]{1,0:T(8,128)(2,1)S(1)} %shard_map.228.refs_0_), channel_id=1, source_target_pairs={{0,6},{1,7},{2,4},{3,5},{4,2},{5,3},{6,0},{7,1},{8,14},{9,15},{10,... | collective-permute-start | bytes 135176 | tf_op jit(solution)/shard_map/ppermute | solution.py:544
  117.4 0.9 collective-permute-start.19
  118.3 2.0 %collective-permute-start.18 = (bf16[16,1408]{1,0:T(8,128)(2,1)S(1)}, bf16[16,1408]{1,0:T(8,128)(2,1)S(1)}, u32[]{:S(2)}, u32[]{:S(2)}) collective-permute-start(bf16[16,1408]{1,0:T(8,128)(2,1)S(1)} %shard_map.228.refs_0_), channel_id=1, source_target_pairs={{0,2},{1,3},{2,0},{3,1},{4,6},{5,7},{6,4},{7,5},{8,10},{9,11},{10,... | collective-permute-start | bytes 135176 | tf_op jit(solution)/shard_map/ppermute | solution.py:544
  120.3 1.9 %shard_map.230 = bf16[288,1024]{1,0:T(8,128)(2,1)} custom-call(s32[4]{0:T(128)S(1)} %pad_add_fusion.me_ref, bf16[512,1024]{1,0:T(8,128)(2,1)S(1)} %copy-done, bf16[4,36,512]{2,1,0:T(8,128)(2,1)S(1)} %get-tuple-element.81.mine_ref.refs_0_, bf16[4,36,512]{2,1,0:T(8,128)(2,1)S(1)} %collective-permute-done.8.other_ref.refs_1_, ...), custom_call_target="tpu_custom_call" | custom-call | flops 301989888 | bytes 1564688 | tf_op jit(solution)/shard_map/pallas_call | solution.py:481
  122.2 0.6 collective-permute-done.19.refs_2_
  122.8 2.0 %collective-permute-start.24 = (bf16[4,16,1408]{2,1,0:T(8,128)(2,1)S(1)}, bf16[4,16,1408]{2,1,0:T(8,128)(2,1)S(1)}, u32[]{:S(2)}, u32[]{:S(2)}) collective-permute-start(bf16[4,16,1408]{2,1,0:T(8,128)(2,1)S(1)} %shard_map.229.refs_0_), channel_id=1, source_target_pairs={{0,17},{1,16},{2,19},{3,18},{4,21},{5,20},{6,23},{7,22},{8,25},{9,... | collective-permute-start | bytes 540680 | tf_op jit(solution)/shard_map/ppermute | solution.py:544
  124.9 1.0 collective-permute-start.23
  125.8 0.5 collective-permute-start.22
  126.4 3.8 %collective-permute-done.24.refs_3_ = bf16[4,16,1408]{2,1,0:T(8,128)(2,1)S(1)} collective-permute-done((bf16[4,16,1408]{2,1,0:T(8,128)(2,1)S(1)}, bf16[4,16,1408]{2,1,0:T(8,128)(2,1)S(1)}, u32[]{:S(2)}, u32[]{:S(2)}) %collective-permute-start.24) | collective-permute-done | bytes 180256 | tf_op jit(solution)/shard_map/ppermute | solution.py:544
  130.1 1.6 %collective-permute-done.23.refs_2_ = bf16[4,16,1408]{2,1,0:T(8,128)(2,1)S(1)} collective-permute-done((bf16[4,16,1408]{2,1,0:T(8,128)(2,1)S(1)}, bf16[4,16,1408]{2,1,0:T(8,128)(2,1)S(1)}, u32[]{:S(2)}, u32[]{:S(2)}) %collective-permute-start.23) | collective-permute-done | bytes 180256 | tf_op jit(solution)/shard_map/ppermute | solution.py:544
  131.8 0.5 collective-permute-start.26
  132.3 0.9 collective-permute-done.27.refs_6_
  133.2 0.3 collective-permute-done.26.refs_5_
  133.4 2.2 %shard_map.231 = (f32[512,1024]{1,0:T(8,128)}, f32[256,512]{1,0:T(8,128)}, f32[1,1]{1,0:T(1,128)}) custom-call(s32[4]{0:T(128)S(1)} %pad_add_fusion.me_ref, bf16[4,16,1408]{2,1,0:T(8,128)(2,1)S(1)} %shard_map.229.refs_0_, bf16[4,16,1408]{2,1,0:T(8,128)(2,1)S(1)} %collective-permute-done.22.refs_1_, bf16[4,16,1408]{2,1,0:T(8,128)(2,1)S(1)} %collective-permute-done.23.refs_2_, ...), custom_call_target="tpu_custom_call" | custom-call | bytes 1441808 | tf_op jit(solution)/shard_map/pallas_call | solution.py:481
  (59 shorter events, 0.8 us)
Async XLA Ops:
  0.8 50.1 %copy-start.3 = (bf16[1024,512]{1,0:T(8,128)(2,1)S(1)}, bf16[1024,512]{1,0:T(8,128)(2,1)}, u32[]{:S(2)}) copy-start(bf16[1024,512]{1,0:T(8,128)(2,1)} %w_dec_ref.1) | copy-start | bytes 3145732
  0.8 50.1 %copy-start.4 = (bf16[512,768]{1,0:T(8,128)(2,1)S(1)}, bf16[512,768]{1,0:T(8,128)(2,1)}, u32[]{:S(2)}) copy-start(bf16[512,768]{1,0:T(8,128)(2,1)} %w_qkv_ref.1) | copy-start | bytes 2359300
  8.3 42.6 %copy-start.1 = (bf16[1,288,1024]{2,1,0:T(8,128)(2,1)S(1)}, bf16[1,288,1024]{2,1,0:T(8,128)(2,1)}, u32[]{:S(2)}) copy-start(bf16[1,288,1024]{2,1,0:T(8,128)(2,1)} %param.21) | copy-start | bytes 1769476
  8.3 42.6 %copy-start.2 = (bf16[512,1024]{1,0:T(8,128)(2,1)S(1)}, bf16[512,1024]{1,0:T(8,128)(2,1)}, u32[]{:S(2)}) copy-start(bf16[512,1024]{1,0:T(8,128)(2,1)} %w_out_ref.2) | copy-start | bytes 3145732
  8.3 42.6 %copy-start.5 = (bf16[288,512]{1,0:T(8,128)(2,1)S(1)}, bf16[288,512]{1,0:T(8,128)(2,1)}, u32[]{:S(2)}) copy-start(bf16[288,512]{1,0:T(8,128)(2,1)} %pos_ref.1) | copy-start | bytes 884740
  8.3 42.6 %copy-start.6 = (s32[1,288]{1,0:T(1,128)S(1)}, s32[1,288]{1,0:T(1,128)}, u32[]{:S(2)}) copy-start(s32[1,288]{1,0:T(1,128)} %slots_ref.3) | copy-start | bytes 3460
  8.3 42.6 %copy-start.7 = (bf16[1024]{0:T(1024)(128)(2,1)S(1)}, bf16[1024]{0:T(1024)(128)(2,1)}, u32[]{:S(2)}) copy-start(bf16[1024]{0:T(1024)(128)(2,1)} %out_gain_ref.1) | copy-start | bytes 6148
  8.3 42.6 %copy-start.8 = (s32[1,288]{1,0:T(1,128)S(1)}, s32[1,288]{1,0:T(1,128)}, u32[]{:S(2)}) copy-start(s32[1,288]{1,0:T(1,128)} %owner_ref.1) | copy-start | bytes 3460
  8.4 42.6 %copy-start.10 = (bf16[512]{0:T(512)(128)(2,1)S(1)}, bf16[512]{0:T(512)(128)(2,1)}, u32[]{:S(2)}) copy-start(bf16[512]{0:T(512)(128)(2,1)} %mask_ref.1) | copy-start | bytes 3076
  8.4 42.6 %copy-start.11 = (bf16[512]{0:T(512)(128)(2,1)S(1)}, bf16[512]{0:T(512)(128)(2,1)}, u32[]{:S(2)}) copy-start(bf16[512]{0:T(512)(128)(2,1)} %gain_ref.3) | copy-start | bytes 3076
  8.4 10.5 %collective-permute-start = (bf16[448,128]{1,0:T(8,128)(2,1)S(1)}, bf16[448,128]{1,0:T(8,128)(2,1)S(1)}, u32[]{:S(2)}, u32[]{:S(2)}) collective-permute-start(bf16[448,128]{1,0:T(8,128)(2,1)S(1)} %get-tuple-element.55), channel_id=1, source_target_pairs={{0,6},{1,7},{2,4},{3,5},{4,2},{5,3},{6,0},{7,1},{8,14},{9,15},{10,... | collective-permute-start | bytes 344072 | tf_op jit(solution)/shard_map/ppermute | solution.py:544
  13.5 14.6 %collective-permute-start.1 = (bf16[448,128]{1,0:T(8,128)(2,1)S(1)}, bf16[448,128]{1,0:T(8,128)(2,1)S(1)}, u32[]{:S(2)}, u32[]{:S(2)}) collective-permute-start(bf16[448,128]{1,0:T(8,128)(2,1)S(1)} %get-tuple-element.56), channel_id=1, source_target_pairs={{0,7},{1,6},{2,5},{3,4},{4,3},{5,2},{6,1},{7,0},{8,15},{9,14},{10,... | collective-permute-start | bytes 344072 | tf_op jit(solution)/shard_map/ppermute | solution.py:544
  14.7 16.9 %collective-permute-start.2 = (bf16[448,128]{1,0:T(8,128)(2,1)S(1)}, bf16[448,128]{1,0:T(8,128)(2,1)S(1)}, u32[]{:S(2)}, u32[]{:S(2)}) collective-permute-start(bf16[448,128]{1,0:T(8,128)(2,1)S(1)} %get-tuple-element.57), channel_id=1, source_target_pairs={{0,4},{1,5},{2,6},{3,7},{4,0},{5,1},{6,2},{7,3},{8,12},{9,13},{10,... | collective-permute-start | bytes 344072 | tf_op jit(solution)/shard_map/ppermute | solution.py:544
  15.5 18.7 %collective-permute-start.3 = (bf16[448,128]{1,0:T(8,128)(2,1)S(1)}, bf16[448,128]{1,0:T(8,128)(2,1)S(1)}, u32[]{:S(2)}, u32[]{:S(2)}) collective-permute-start(bf16[448,128]{1,0:T(8,128)(2,1)S(1)} %get-tuple-element.58), channel_id=1, source_target_pairs={{0,5},{1,4},{2,7},{3,6},{4,1},{5,0},{6,3},{7,2},{8,13},{9,12},{10,... | collective-permute-start | bytes 344072 | tf_op jit(solution)/shard_map/ppermute | solution.py:544
  17.4 16.8 %collective-permute-start.4 = (bf16[448,128]{1,0:T(8,128)(2,1)S(1)}, bf16[448,128]{1,0:T(8,128)(2,1)S(1)}, u32[]{:S(2)}, u32[]{:S(2)}) collective-permute-start(bf16[448,128]{1,0:T(8,128)(2,1)S(1)} %get-tuple-element.59), channel_id=1, source_target_pairs={{0,2},{1,3},{2,0},{3,1},{4,6},{5,7},{6,4},{7,5},{8,10},{9,11},{10,... | collective-permute-start | bytes 344072 | tf_op jit(solution)/shard_map/ppermute | solution.py:544
  18.8 16.3 %collective-permute-start.5 = (bf16[448,128]{1,0:T(8,128)(2,1)S(1)}, bf16[448,128]{1,0:T(8,128)(2,1)S(1)}, u32[]{:S(2)}, u32[]{:S(2)}) collective-permute-start(bf16[448,128]{1,0:T(8,128)(2,1)S(1)} %get-tuple-element.60), channel_id=1, source_target_pairs={{0,3},{1,2},{2,1},{3,0},{4,7},{5,6},{6,5},{7,4},{8,11},{9,10},{10,... | collective-permute-start | bytes 344072 | tf_op jit(solution)/shard_map/ppermute | solution.py:544
  28.1 7.7 %collective-permute-start.6 = (bf16[448,128]{1,0:T(8,128)(2,1)S(1)}, bf16[448,128]{1,0:T(8,128)(2,1)S(1)}, u32[]{:S(2)}, u32[]{:S(2)}) collective-permute-start(bf16[448,128]{1,0:T(8,128)(2,1)S(1)} %get-tuple-element.61), channel_id=1, source_target_pairs={{0,1},{1,0},{2,3},{3,2},{4,5},{5,4},{6,7},{7,6},{8,9},{9,8},{10,11... | collective-permute-start | bytes 344072 | tf_op jit(solution)/shard_map/ppermute | solution.py:544
  65.9 18.3 %copy-start = (bf16[512,1024]{1,0:T(8,128)(2,1)S(1)}, bf16[512,1024]{1,0:T(8,128)(2,1)}, u32[]{:S(2)}) copy-start(bf16[512,1024]{1,0:T(8,128)(2,1)} %w_head_ref.5) | copy-start | bytes 3145732
  65.9 18.3 %copy-start.9 = (bf16[512]{0:T(512)(128)(2,1)S(1)}, bf16[512]{0:T(512)(128)(2,1)}, u32[]{:S(2)}) copy-start(bf16[512]{0:T(512)(128)(2,1)} %head_gain_ref.3) | copy-start | bytes 3076
  65.9 18.3 %copy-start.12 = (bf16[512,2048]{1,0:T(8,128)(2,1)S(1)}, bf16[512,2048]{1,0:T(8,128)(2,1)}, u32[]{:S(2)}) copy-start(bf16[512,2048]{1,0:T(8,128)(2,1)} %w_up_ref.3) | copy-start | bytes 6291460
  65.9 18.3 %copy-start.13 = (bf16[2048,512]{1,0:T(8,128)(2,1)S(1)}, bf16[2048,512]{1,0:T(8,128)(2,1)}, u32[]{:S(2)}) copy-start(bf16[2048,512]{1,0:T(8,128)(2,1)} %w_down_ref.3) | copy-start | bytes 6291460
  65.9 18.3 %copy-start.14 = (bf16[256,512]{1,0:T(8,128)(2,1)S(1)}, bf16[256,512]{1,0:T(8,128)(2,1)}, u32[]{:S(2)}) copy-start(bf16[256,512]{1,0:T(8,128)(2,1)} %w_out_ref.3) | copy-start | bytes 786436
  65.9 18.3 %copy-start.15 = (bf16[512]{0:T(512)(128)(2,1)S(1)}, bf16[512]{0:T(512)(128)(2,1)}, u32[]{:S(2)}) copy-start(bf16[512]{0:T(512)(128)(2,1)} %feed_gain_ref.3) | copy-start | bytes 3076
  89.3 5.4 %collective-permute-start.8 = (bf16[4,36,512]{2,1,0:T(8,128)(2,1)S(1)}, bf16[4,36,512]{2,1,0:T(8,128)(2,1)S(1)}, u32[]{:S(2)}, u32[]{:S(2)}) collective-permute-start(bf16[4,36,512]{2,1,0:T(8,128)(2,1)S(1)} %get-tuple-element.77), channel_id=1, source_target_pairs={{0,1},{1,0},{2,3},{3,2},{4,5},{5,4},{6,7},{7,6},{8,9},{9,8},{10,11... | collective-permute-start | bytes 442376 | tf_op jit(solution)/shard_map/ppermute | solution.py:544
  89.5 5.2 %collective-permute-start.7 = (bf16[4,4,16,1024]{3,2,1,0:T(8,128)(2,1)S(1)}, bf16[4,4,16,1024]{3,2,1,0:T(8,128)(2,1)S(1)}, u32[]{:S(2)}, u32[]{:S(2)}) collective-permute-start(bf16[4,4,16,1024]{3,2,1,0:T(8,128)(2,1)S(1)} %get-tuple-element.76), channel_id=1, source_target_pairs={{0,8},{1,9},{2,10},{3,11},{4,12},{5,13},{6,14},{7,15},{8,0},{9,1},... | collective-permute-start | bytes 1572872 | tf_op jit(solution)/shard_map/ppermute | solution.py:544
  94.7 1.4 %collective-permute-start.9 = (bf16[4,4,16,384]{3,2,1,0:T(8,128)(2,1)S(1)}, bf16[4,4,16,384]{3,2,1,0:T(8,128)(2,1)S(1)}, u32[]{:S(2)}, u32[]{:S(2)}) collective-permute-start(bf16[4,4,16,384]{3,2,1,0:T(8,128)(2,1)S(1)} %get-tuple-element.80), channel_id=1, source_target_pairs={{0,8},{1,9},{2,10},{3,11},{4,12},{5,13},{6,14},{7,15},{8,0},{9,1},... | collective-permute-start | bytes 589832 | tf_op jit(solution)/shard_map/ppermute | solution.py:544
  96.3 11.8 %collective-permute-start.10 = (bf16[4,16,1408]{2,1,0:T(8,128)(2,1)S(1)}, bf16[4,16,1408]{2,1,0:T(8,128)(2,1)S(1)}, u32[]{:S(2)}, u32[]{:S(2)}) collective-permute-start(bf16[4,16,1408]{2,1,0:T(8,128)(2,1)S(1)} %get-tuple-element.83), channel_id=1, source_target_pairs={{0,17},{1,16},{2,19},{3,18},{4,21},{5,20},{6,23},{7,22},{8,25},{9,... | collective-permute-start | bytes 540680 | tf_op jit(solution)/shard_map/ppermute | solution.py:544
  97.6 10.5 %collective-permute-start.11 = (bf16[4,16,1408]{2,1,0:T(8,128)(2,1)S(1)}, bf16[4,16,1408]{2,1,0:T(8,128)(2,1)S(1)}, u32[]{:S(2)}, u32[]{:S(2)}) collective-permute-start(bf16[4,16,1408]{2,1,0:T(8,128)(2,1)S(1)} %get-tuple-element.84), channel_id=1, source_target_pairs={{0,1},{1,0},{2,3},{3,2},{4,5},{5,4},{6,7},{7,6},{8,9},{9,8},{10,11... | collective-permute-start | bytes 540680 | tf_op jit(solution)/shard_map/ppermute | solution.py:544
  99.3 8.8 %collective-permute-start.12 = (bf16[4,16,1408]{2,1,0:T(8,128)(2,1)S(1)}, bf16[4,16,1408]{2,1,0:T(8,128)(2,1)S(1)}, u32[]{:S(2)}, u32[]{:S(2)}) collective-permute-start(bf16[4,16,1408]{2,1,0:T(8,128)(2,1)S(1)} %get-tuple-element.85), channel_id=1, source_target_pairs={{0,16},{1,17},{2,18},{3,19},{4,20},{5,21},{6,22},{7,23},{8,24},{9,... | collective-permute-start | bytes 540680 | tf_op jit(solution)/shard_map/ppermute | solution.py:544
  99.8 8.3 %collective-permute-start.13 = (bf16[2,36,512]{2,1,0:T(8,128)(2,1)S(1)}, bf16[2,36,512]{2,1,0:T(8,128)(2,1)S(1)}, u32[]{:S(2)}, u32[]{:S(2)}) collective-permute-start(bf16[2,36,512]{2,1,0:T(8,128)(2,1)S(1)} %get-tuple-element.87), channel_id=1, source_target_pairs={{0,4},{1,5},{2,6},{3,7},{4,0},{5,1},{6,2},{7,3},{8,12},{9,13},{10,... | collective-permute-start | bytes 221192 | tf_op jit(solution)/shard_map/ppermute | solution.py:544
  100.2 7.9 %collective-permute-start.14 = (bf16[2,36,512]{2,1,0:T(8,128)(2,1)S(1)}, bf16[2,36,512]{2,1,0:T(8,128)(2,1)S(1)}, u32[]{:S(2)}, u32[]{:S(2)}) collective-permute-start(bf16[2,36,512]{2,1,0:T(8,128)(2,1)S(1)} %get-tuple-element.88), channel_id=1, source_target_pairs={{0,6},{1,7},{2,4},{3,5},{4,2},{5,3},{6,0},{7,1},{8,14},{9,15},{10,... | collective-permute-start | bytes 221192 | tf_op jit(solution)/shard_map/ppermute | solution.py:544
  108.1 12.2 %collective-permute-start.21 = (bf16[2,36,512]{2,1,0:T(8,128)(2,1)S(1)}, bf16[2,36,512]{2,1,0:T(8,128)(2,1)S(1)}, u32[]{:S(2)}, u32[]{:S(2)}) collective-permute-start(bf16[2,36,512]{2,1,0:T(8,128)(2,1)S(1)} %get-tuple-element.94), channel_id=1, source_target_pairs={{0,2},{1,3},{2,0},{3,1},{4,6},{5,7},{6,4},{7,5},{8,10},{9,11},{10,... | collective-permute-start | bytes 221192 | tf_op jit(solution)/shard_map/ppermute | solution.py:544
  108.2 6.2 %collective-permute-start.15 = (bf16[16,1408]{1,0:T(8,128)(2,1)S(1)}, bf16[16,1408]{1,0:T(8,128)(2,1)S(1)}, u32[]{:S(2)}, u32[]{:S(2)}) collective-permute-start(bf16[16,1408]{1,0:T(8,128)(2,1)S(1)} %get-tuple-element.90), channel_id=1, source_target_pairs={{0,6},{1,7},{2,4},{3,5},{4,2},{5,3},{6,0},{7,1},{8,14},{9,15},{10,... | collective-permute-start | bytes 135176 | tf_op jit(solution)/shard_map/ppermute | solution.py:544
  109.3 6.0 %collective-permute-start.16 = (bf16[16,1408]{1,0:T(8,128)(2,1)S(1)}, bf16[16,1408]{1,0:T(8,128)(2,1)S(1)}, u32[]{:S(2)}, u32[]{:S(2)}) collective-permute-start(bf16[16,1408]{1,0:T(8,128)(2,1)S(1)} %get-tuple-element.91), channel_id=1, source_target_pairs={{0,4},{1,5},{2,6},{3,7},{4,0},{5,1},{6,2},{7,3},{8,12},{9,13},{10,... | collective-permute-start | bytes 135176 | tf_op jit(solution)/shard_map/ppermute | solution.py:544
  111.8 4.0 %collective-permute-start.17 = (bf16[16,1408]{1,0:T(8,128)(2,1)S(1)}, bf16[16,1408]{1,0:T(8,128)(2,1)S(1)}, u32[]{:S(2)}, u32[]{:S(2)}) collective-permute-start(bf16[16,1408]{1,0:T(8,128)(2,1)S(1)} %get-tuple-element.92), channel_id=1, source_target_pairs={{0,2},{1,3},{2,0},{3,1},{4,6},{5,7},{6,4},{7,5},{8,10},{9,11},{10,... | collective-permute-start | bytes 135176 | tf_op jit(solution)/shard_map/ppermute | solution.py:544
  115.8 6.3 %collective-permute-start.20 = (bf16[16,1408]{1,0:T(8,128)(2,1)S(1)}, bf16[16,1408]{1,0:T(8,128)(2,1)S(1)}, u32[]{:S(2)}, u32[]{:S(2)}) collective-permute-start(bf16[16,1408]{1,0:T(8,128)(2,1)S(1)} %shard_map.228.refs_0_), channel_id=1, source_target_pairs={{0,6},{1,7},{2,4},{3,5},{4,2},{5,3},{6,0},{7,1},{8,14},{9,15},{10,... | collective-permute-start | bytes 135176 | tf_op jit(solution)/shard_map/ppermute | solution.py:544
  117.4 5.4 %collective-permute-start.19 = (bf16[16,1408]{1,0:T(8,128)(2,1)S(1)}, bf16[16,1408]{1,0:T(8,128)(2,1)S(1)}, u32[]{:S(2)}, u32[]{:S(2)}) collective-permute-start(bf16[16,1408]{1,0:T(8,128)(2,1)S(1)} %shard_map.228.refs_0_), channel_id=1, source_target_pairs={{0,4},{1,5},{2,6},{3,7},{4,0},{5,1},{6,2},{7,3},{8,12},{9,13},{10,... | collective-permute-start | bytes 135176 | tf_op jit(solution)/shard_map/ppermute | solution.py:544
  118.3 4.5 %collective-permute-start.18 = (bf16[16,1408]{1,0:T(8,128)(2,1)S(1)}, bf16[16,1408]{1,0:T(8,128)(2,1)S(1)}, u32[]{:S(2)}, u32[]{:S(2)}) collective-permute-start(bf16[16,1408]{1,0:T(8,128)(2,1)S(1)} %shard_map.228.refs_0_), channel_id=1, source_target_pairs={{0,2},{1,3},{2,0},{3,1},{4,6},{5,7},{6,4},{7,5},{8,10},{9,11},{10,... | collective-permute-start | bytes 135176 | tf_op jit(solution)/shard_map/ppermute | solution.py:544
  122.8 7.3 %collective-permute-start.24 = (bf16[4,16,1408]{2,1,0:T(8,128)(2,1)S(1)}, bf16[4,16,1408]{2,1,0:T(8,128)(2,1)S(1)}, u32[]{:S(2)}, u32[]{:S(2)}) collective-permute-start(bf16[4,16,1408]{2,1,0:T(8,128)(2,1)S(1)} %shard_map.229.refs_0_), channel_id=1, source_target_pairs={{0,17},{1,16},{2,19},{3,18},{4,21},{5,20},{6,23},{7,22},{8,25},{9,... | collective-permute-start | bytes 540680 | tf_op jit(solution)/shard_map/ppermute | solution.py:544
  124.9 6.9 %collective-permute-start.23 = (bf16[4,16,1408]{2,1,0:T(8,128)(2,1)S(1)}, bf16[4,16,1408]{2,1,0:T(8,128)(2,1)S(1)}, u32[]{:S(2)}, u32[]{:S(2)}) collective-permute-start(bf16[4,16,1408]{2,1,0:T(8,128)(2,1)S(1)} %shard_map.229.refs_0_), channel_id=1, source_target_pairs={{0,1},{1,0},{2,3},{3,2},{4,5},{5,4},{6,7},{7,6},{8,9},{9,8},{10,11... | collective-permute-start | bytes 540680 | tf_op jit(solution)/shard_map/ppermute | solution.py:544
  125.8 5.9 %collective-permute-start.22 = (bf16[4,16,1408]{2,1,0:T(8,128)(2,1)S(1)}, bf16[4,16,1408]{2,1,0:T(8,128)(2,1)S(1)}, u32[]{:S(2)}, u32[]{:S(2)}) collective-permute-start(bf16[4,16,1408]{2,1,0:T(8,128)(2,1)S(1)} %shard_map.229.refs_0_), channel_id=1, source_target_pairs={{0,16},{1,17},{2,18},{3,19},{4,20},{5,21},{6,22},{7,23},{8,24},{9,... | collective-permute-start | bytes 540680 | tf_op jit(solution)/shard_map/ppermute | solution.py:544
  126.4 5.9 %collective-permute-start.25 = (bf16[4,16,1408]{2,1,0:T(8,128)(2,1)S(1)}, bf16[4,16,1408]{2,1,0:T(8,128)(2,1)S(1)}, u32[]{:S(2)}, u32[]{:S(2)}) collective-permute-start(bf16[4,16,1408]{2,1,0:T(8,128)(2,1)S(1)} %shard_map.229.refs_0_), channel_id=1, source_target_pairs={{0,8},{1,9},{2,10},{3,11},{4,12},{5,13},{6,14},{7,15},{8,0},{9,1},... | collective-permute-start | bytes 540680 | tf_op jit(solution)/shard_map/ppermute | solution.py:544
  130.1 2.1 %collective-permute-start.28 = (bf16[4,16,1408]{2,1,0:T(8,128)(2,1)S(1)}, bf16[4,16,1408]{2,1,0:T(8,128)(2,1)S(1)}, u32[]{:S(2)}, u32[]{:S(2)}) collective-permute-start(bf16[4,16,1408]{2,1,0:T(8,128)(2,1)S(1)} %collective-permute-done.24.refs_3_), channel_id=1, source_target_pairs={{0,8},{1,9},{2,10},{3,11},{4,12},{5,13},{6,14},{7,15},{8,0},{9,1},... | collective-permute-start | bytes 540680 | tf_op jit(solution)/shard_map/ppermute | solution.py:544
  131.8 1.4 %collective-permute-start.27 = (bf16[4,16,1408]{2,1,0:T(8,128)(2,1)S(1)}, bf16[4,16,1408]{2,1,0:T(8,128)(2,1)S(1)}, u32[]{:S(2)}, u32[]{:S(2)}) collective-permute-start(bf16[4,16,1408]{2,1,0:T(8,128)(2,1)S(1)} %collective-permute-done.23.refs_2_), channel_id=1, source_target_pairs={{0,8},{1,9},{2,10},{3,11},{4,12},{5,13},{6,14},{7,15},{8,0},{9,1},... | collective-permute-start | bytes 540680 | tf_op jit(solution)/shard_map/ppermute | solution.py:544
  131.8 1.7 %collective-permute-start.26 = (bf16[4,16,1408]{2,1,0:T(8,128)(2,1)S(1)}, bf16[4,16,1408]{2,1,0:T(8,128)(2,1)S(1)}, u32[]{:S(2)}, u32[]{:S(2)}) collective-permute-start(bf16[4,16,1408]{2,1,0:T(8,128)(2,1)S(1)} %collective-permute-done.22.refs_1_), channel_id=1, source_target_pairs={{0,8},{1,9},{2,10},{3,11},{4,12},{5,13},{6,14},{7,15},{8,0},{9,1},... | collective-permute-start | bytes 540680 | tf_op jit(solution)/shard_map/ppermute | solution.py:544

commit v9 on v8

--- a/solution.py
+++ b/solution.py
@@ -379,18 +379,15 @@
         out_ref[:, cols] = dot(zn_buf[...], w_head_ref[:, cols]).astype(BF)
 
 
-def head_back_kernel(dpred_ref, z_ref, head_gain_ref, w_head_ref, dz_ref):
-    dz_ref[...] = norm_backward(
-        z_ref[...], head_gain_ref[...], dot_t(dpred_ref[...], w_head_ref[...])
-    ).astype(BF)
-
-
 def backward_kernel(
-    me_ref, dec_att_ref, mid_ref, slope_ref, dz_ref, loss_ref, feed_gain_ref, w_up_ref, w_down_ref,
+    me_ref, dec_att_ref, mid_ref, slope_ref, dpred_ref, z_ref, loss_ref, head_gain_ref, w_head_ref,
+    feed_gain_ref, w_up_ref, w_down_ref,
     keep_ref, send_ref, back_buf, out_buf,
 ):
     hidden = w_up_ref.shape[1]
-    dz = dz_ref[...]
+    dz = norm_backward(
+        z_ref[...], head_gain_ref[...], dot_t(dpred_ref[...], w_head_ref[...])
+    ).astype(BF)
     tile = 512
     for at in range(0, hidden, tile):
         cols = slice(at, at + tile)
@@ -548,11 +545,11 @@
 COLUMN = ((0, 2), (0, 4), (0, 6))
 
 
-def sum_by_permutes(head_keep, head_send, zn_keep, zn_send, head_back, backward, rebuild):
+def sum_by_permutes(head_keep, head_send, zn_keep, zn_send, backward, rebuild):
     shape = jax.ShapeDtypeStruct
     head_got = across(head_send, 1, 0)
     zn_got = across(zn_send, 0, 1)
-    out_keep, out_send = backward(head_back())
+    out_keep, out_send = backward()
     out_send, head_got, zn_got = lax.optimization_barrier((out_send, head_got, zn_got))
     out_got = across(out_send, 1, 0)
     block = shape((head_keep.shape[2], head_keep.shape[3] + out_keep.shape[3]), BF)
@@ -761,16 +758,7 @@
         flops=2 * rows * dec_width * (2 * hidden + 2 * pixels),
     )
 
-    def head_back():
-        return vmem_call(
-            head_back_kernel,
-            [shape((rows, dec_width), BF)],
-            [],
-            [dpred, z, head_gain, w_head],
-            flops=2 * rows * dec_width * pixels,
-        )[0]
-
-    def backward(dz):
+    def backward():
         return vmem_call(
             backward_kernel,
             [shape((4, 4, tall, dec_width // 2 + 128), BF)] * 2,
@@ -778,7 +766,10 @@
                 pltpu.VMEM((rows, dec_width), F32),
                 pltpu.VMEM((w_dec_out.shape[0], dec_width), F32),
             ],
-            [me, dec_att, y_mid, slope, dz, loss_part, decoder_feed_gain, w_up, w_down],
+            [
+                me, dec_att, y_mid, slope, dpred, z, loss_part, head_gain, w_head,
+                decoder_feed_gain, w_up, w_down,
+            ],
             smem=(0,),
             flops=40 * rows * dec_width * hidden,
         )
@@ -797,10 +788,10 @@
 
     if repeat == 1:
         ours, theirs, reconstruction = sum_by_permutes(
-            head_keep, head_send, *zn, head_back, backward, rebuild
+            head_keep, head_send, *zn, backward, rebuild
         )
     else:
-        out_keep, out_send = backward(head_back())
+        out_keep, out_send = backward()
         ours, theirs = sum_by_blocks(
             jnp.concatenate([head_keep, out_keep], axis=3),
             jnp.concatenate([head_send, out_send], axis=3),

time: 136 us -> 136 us (level)
    pallas_call x13 -> x12, Pallas kernels: 33.4 us -> 33.3 us  [vmem_call(): pl.pallas_call(kernel, out_shape=outs, in_specs=space, out_specs=[pl.Bloc...]
where the time goes in v9:
time: 136 us
  starting transfers between devices  38.7 us (28%)
  blocking collectives  35.1 us (26%)
  Pallas kernels  33.3 us (24%)
  waiting for transfers between devices  27.2 us (20%)
    ppermute x29, starting transfers between devices, across(): return lax.ppermute(x, ('dp', 'ctx'), pairs)  38.7 us
    all_to_all x3, blocking collectives, swap(): lax.all_to_all(x, axis, split_axis=0, concat_axis=0, tiled=True, axis_ind...  35.1 us
    pallas_call x12, Pallas kernels, vmem_call(): pl.pallas_call(kernel, out_shape=outs, in_specs=space, out_specs=[pl.Bloc...  33.3 us
    ppermute x29, waiting for transfers between devices, across(): return lax.ppermute(x, ('dp', 'ctx'), pairs)  27.2 us
  transfers between devices with their start and end apart: 29, of which 15 were waited for; matrix products, arithmetic and copies ran while one was open for 0% of the time, Pallas kernels for 4%

profile of v9, /device:TPU:0, one launch (start us, length us, event | category | flops | bytes accessed | tf_op | source)
XLA Modules:
  0.0 135.6 jit_solution(8424673671449916927)
XLA Ops:
  0.8 7.5 %shard_map.219 = (bf16[288,1024]{1,0:T(8,128)(2,1)S(1)}, bf16[448,128]{1,0:T(8,128)(2,1)S(1)}, bf16[448,128]{1,0:T(8,128)(2,1)S(1)}, bf16[448,128]{1,0:T(8,128)(...) custom-call(s32[4]{0:T(128)S(1)} %pad_add_fusion.me_ref, ...), custom_call_target="tpu_custom_call" | custom-call | flops 1509949440 | bytes 6425744 | tf_op jit(solution)/shard_map/pallas_call | solution.py:478
  8.4 5.1 %collective-permute-start = (bf16[448,128]{1,0:T(8,128)(2,1)S(1)}, bf16[448,128]{1,0:T(8,128)(2,1)S(1)}, u32[]{:S(2)}, u32[]{:S(2)}) collective-permute-start(bf16[448,128]{1,0:T(8,128)(2,1)S(1)} %get-tuple-element.55), channel_id=1, source_target_pairs={{0,6},{1,7},{2,4},{3,5},{4,2},{5,3},{6,0},{7,1},{8,14},{9,15},{10,... | collective-permute-start | bytes 344072 | tf_op jit(solution)/shard_map/ppermute | solution.py:541
  13.5 1.2 collective-permute-start.1
  14.7 0.8 collective-permute-start.2
  15.5 1.9 %collective-permute-start.3 = (bf16[448,128]{1,0:T(8,128)(2,1)S(1)}, bf16[448,128]{1,0:T(8,128)(2,1)S(1)}, u32[]{:S(2)}, u32[]{:S(2)}) collective-permute-start(bf16[448,128]{1,0:T(8,128)(2,1)S(1)} %get-tuple-element.58), channel_id=1, source_target_pairs={{0,5},{1,4},{2,7},{3,6},{4,1},{5,0},{6,3},{7,2},{8,13},{9,12},{10,... | collective-permute-start | bytes 344072 | tf_op jit(solution)/shard_map/ppermute | solution.py:541
  17.4 1.4 %collective-permute-start.4 = (bf16[448,128]{1,0:T(8,128)(2,1)S(1)}, bf16[448,128]{1,0:T(8,128)(2,1)S(1)}, u32[]{:S(2)}, u32[]{:S(2)}) collective-permute-start(bf16[448,128]{1,0:T(8,128)(2,1)S(1)} %get-tuple-element.59), channel_id=1, source_target_pairs={{0,2},{1,3},{2,0},{3,1},{4,6},{5,7},{6,4},{7,5},{8,10},{9,11},{10,... | collective-permute-start | bytes 344072 | tf_op jit(solution)/shard_map/ppermute | solution.py:541
  18.8 9.3 %collective-permute-start.5 = (bf16[448,128]{1,0:T(8,128)(2,1)S(1)}, bf16[448,128]{1,0:T(8,128)(2,1)S(1)}, u32[]{:S(2)}, u32[]{:S(2)}) collective-permute-start(bf16[448,128]{1,0:T(8,128)(2,1)S(1)} %get-tuple-element.60), channel_id=1, source_target_pairs={{0,3},{1,2},{2,1},{3,0},{4,7},{5,6},{6,5},{7,4},{8,11},{9,10},{10,... | collective-permute-start | bytes 344072 | tf_op jit(solution)/shard_map/ppermute | solution.py:541
  28.1 3.5 %collective-permute-done.2.refs_2_ = bf16[448,128]{1,0:T(8,128)(2,1)S(1)} collective-permute-done((bf16[448,128]{1,0:T(8,128)(2,1)S(1)}, bf16[448,128]{1,0:T(8,128)(2,1)S(1)}, u32[]{:S(2)}, u32[]{:S(2)}) %collective-permute-start.2) | collective-permute-done | bytes 114720 | tf_op jit(solution)/shard_map/ppermute | solution.py:541
  31.6 2.5 %collective-permute-done.3.refs_3_ = bf16[448,128]{1,0:T(8,128)(2,1)S(1)} collective-permute-done((bf16[448,128]{1,0:T(8,128)(2,1)S(1)}, bf16[448,128]{1,0:T(8,128)(2,1)S(1)}, u32[]{:S(2)}, u32[]{:S(2)}) %collective-permute-start.3) | collective-permute-done | bytes 114720 | tf_op jit(solution)/shard_map/ppermute | solution.py:541
  34.2 1.0 collective-permute-done.5.refs_5_
  35.1 0.7 collective-permute-done.6.refs_6_
  35.8 2.8 %shard_map.220 = bf16[8,144,128]{2,1,0:T(8,128)(2,1)S(1)} custom-call(s32[4]{0:T(128)S(1)} %pad_add_fusion.me_ref, bf16[448,128]{1,0:T(8,128)(2,1)S(1)} %collective-permute-done.refs_0_, bf16[448,128]{1,0:T(8,128)(2,1)S(1)} %collective-permute-done.1.refs_1_, bf16[448,128]{1,0:T(8,128)(2,1)S(1)} %collective-permute-done.2.refs_2_, ...), custom_call_target="tpu_custom_call" | custom-call | flops 411041792 | bytes 917520 | tf_op jit(solution)/shard_map/pallas_call | solution.py:478
  38.6 12.3 %all_to_all.15.att_ref = bf16[8,144,128]{2,1,0:T(8,128)(2,1)S(1)} all-to-all(bf16[8,144,128]{2,1,0:T(8,128)(2,1)S(1)} %shard_map.220), channel_id=1, replica_groups=mesh['dp'=4,'ctx'=8] {'ctx'}, dimensions={0} | all-to-all | bytes 589824 | tf_op jit(solution)/shard_map/all_to_all | solution.py:503
  51.0 2.7 %shard_map.221 = (bf16[8,216,128]{2,1,0:T(8,128)(2,1)S(1)}, bf16[288,512]{1,0:T(8,128)(2,1)S(1)}, bf16[288,1024]{1,0:T(8,128)(2,1)S(1)}, f32[288,128]{1,0:T(8,128)S(1)}) custom-call(bf16[8,144,128]{2,1,0:T(8,128)(2,1)S(1)} %all_to_all.15.att_ref, bf16[288,1024]{1,0:T(8,128)(2,1)S(1)} %get-tuple-element.63.tok_ref, bf16[512,1024]{1,0:T(8,128)(2,1)S(1)} %copy-done.2, ...), custom_call_target="tpu_custom_call" | custom-call | flops 603979776 | bytes 4659456 | tf_op jit(solution)/shard_map/pallas_call | solution.py:478
  53.6 12.3 %all_to_all.16.q_ref.kv_ref = bf16[8,216,128]{2,1,0:T(8,128)(2,1)S(1)} all-to-all(bf16[8,216,128]{2,1,0:T(8,128)(2,1)S(1)} %get-tuple-element.64), channel_id=1, replica_groups=mesh['dp'=4,'ctx'=8] {'ctx'}, dimensions={0} | all-to-all | bytes 884736 | tf_op jit(solution)/shard_map/all_to_all | solution.py:503
  65.9 7.7 %shard_map.222 = bf16[8,72,128]{2,1,0:T(8,128)(2,1)S(1)} custom-call(bf16[8,216,128]{2,1,0:T(8,128)(2,1)S(1)} %all_to_all.16.q_ref.kv_ref, bf16[8,216,128]{2,1,0:T(8,128)(2,1)S(1)} %all_to_all.16.q_ref.kv_ref), custom_call_target="tpu_custom_call" | custom-call | flops 2717908992 | bytes 884736 | tf_op jit(solution)/shard_map/pallas_call | solution.py:478
  73.7 10.5 %all_to_all.17.att_ref = bf16[8,72,128]{2,1,0:T(8,128)(2,1)S(1)} all-to-all(bf16[8,72,128]{2,1,0:T(8,128)(2,1)S(1)} %shard_map.222), channel_id=1, replica_groups=mesh['dp'=4,'ctx'=8] {'ctx'}, dimensions={0} | all-to-all | bytes 294912 | tf_op jit(solution)/shard_map/all_to_all | solution.py:503
  84.2 5.0 %shard_map.223 = (bf16[288,256]{1,0:T(8,128)(2,1)S(1)}, f32[288,512]{1,0:T(8,128)S(1)}, bf16[288,2048]{1,0:T(8,128)(2,1)S(1)}, f32[288,512]{1,0:T(8,128)S(1)}, b...) custom-call(s32[4]{0:T(128)S(1)} %pad_add_fusion.me_ref, ...), custom_call_target="tpu_custom_call" | custom-call | flops 1811939328 | bytes 6686736 | tf_op jit(solution)/shard_map/pallas_call | solution.py:478
  89.3 0.2 collective-permute-start.8
  89.5 3.2 %shard_map.224 = (bf16[4,4,16,384]{3,2,1,0:T(8,128)(2,1)S(1)}, bf16[4,4,16,384]{3,2,1,0:T(8,128)(2,1)S(1)}) custom-call(s32[4]{0:T(128)S(1)} %pad_add_fusion.me_ref, bf16[288,256]{1,0:T(8,128)(2,1)S(1)} %get-tuple-element.69.dec_att_ref, f32[288,512]{1,0:T(8,128)S(1)} %get-tuple-element.70.mid_ref, bf16[288,2048]{1,0:T(8,128)(2,1)S(1)} %get-tuple-element.71.slope_ref, ...), custom_call_target="tpu_custom_call" | custom-call | flops 12079595520 | bytes 8345616 | tf_op jit(solution)/shard_map/pallas_call | solution.py:478
  92.7 2.0 %collective-permute-done.8.other_ref.refs_1_ = bf16[4,36,512]{2,1,0:T(8,128)(2,1)S(1)} collective-permute-done((bf16[4,36,512]{2,1,0:T(8,128)(2,1)S(1)}, bf16[4,36,512]{2,1,0:T(8,128)(2,1)S(1)}, u32[]{:S(2)}, u32[]{:S(2)}) %collective-permute-start.8) | collective-permute-done | bytes 147488 | tf_op jit(solution)/shard_map/ppermute | solution.py:541
  94.6 1.4 %collective-permute-done.9.out_got_ref = bf16[4,4,16,384]{3,2,1,0:T(8,128)(2,1)S(1)} collective-permute-done((bf16[4,4,16,384]{3,2,1,0:T(8,128)(2,1)S(1)}, bf16[4,4,16,384]{3,2,1,0:T(8,128)(2,1)S(1)}, u32[]{:S(2)}, u32[]{:S(2)}) %collective-permute-start.9) | collective-permute-done | bytes 196640 | tf_op jit(solution)/shard_map/ppermute | solution.py:541
  96.3 1.2 collective-permute-start.10
  97.4 1.9 %collective-permute-start.11 = (bf16[4,16,1408]{2,1,0:T(8,128)(2,1)S(1)}, bf16[4,16,1408]{2,1,0:T(8,128)(2,1)S(1)}, u32[]{:S(2)}, u32[]{:S(2)}) collective-permute-start(bf16[4,16,1408]{2,1,0:T(8,128)(2,1)S(1)} %get-tuple-element.84), channel_id=1, source_target_pairs={{0,1},{1,0},{2,3},{3,2},{4,5},{5,4},{6,7},{7,6},{8,9},{9,8},{10,11... | collective-permute-start | bytes 540680 | tf_op jit(solution)/shard_map/ppermute | solution.py:541
  99.3 0.5 collective-permute-start.12
  99.8 0.4 collective-permute-start.13
  100.2 1.9 %collective-permute-start.14 = (bf16[2,36,512]{2,1,0:T(8,128)(2,1)S(1)}, bf16[2,36,512]{2,1,0:T(8,128)(2,1)S(1)}, u32[]{:S(2)}, u32[]{:S(2)}) collective-permute-start(bf16[2,36,512]{2,1,0:T(8,128)(2,1)S(1)} %get-tuple-element.88), channel_id=1, source_target_pairs={{0,6},{1,7},{2,4},{3,5},{4,2},{5,3},{6,0},{7,1},{8,14},{9,15},{10,... | collective-permute-start | bytes 221192 | tf_op jit(solution)/shard_map/ppermute | solution.py:541
  102.0 6.0 %collective-permute-done.13.refs_3_ = bf16[2,36,512]{2,1,0:T(8,128)(2,1)S(1)} collective-permute-done((bf16[2,36,512]{2,1,0:T(8,128)(2,1)S(1)}, bf16[2,36,512]{2,1,0:T(8,128)(2,1)S(1)}, u32[]{:S(2)}, u32[]{:S(2)}) %collective-permute-start.13) | collective-permute-done | bytes 73760 | tf_op jit(solution)/shard_map/ppermute | solution.py:541
  108.2 1.1 collective-permute-start.15
  109.3 2.5 %collective-permute-start.16 = (bf16[16,1408]{1,0:T(8,128)(2,1)S(1)}, bf16[16,1408]{1,0:T(8,128)(2,1)S(1)}, u32[]{:S(2)}, u32[]{:S(2)}) collective-permute-start(bf16[16,1408]{1,0:T(8,128)(2,1)S(1)} %get-tuple-element.91), channel_id=1, source_target_pairs={{0,4},{1,5},{2,6},{3,7},{4,0},{5,1},{6,2},{7,3},{8,12},{9,13},{10,... | collective-permute-start | bytes 135176 | tf_op jit(solution)/shard_map/ppermute | solution.py:541
  111.7 0.9 collective-permute-start.17
  112.6 1.7 %collective-permute-done.15.refs_0_ = bf16[16,1408]{1,0:T(8,128)(2,1)S(1)} collective-permute-done((bf16[16,1408]{1,0:T(8,128)(2,1)S(1)}, bf16[16,1408]{1,0:T(8,128)(2,1)S(1)}, u32[]{:S(2)}, u32[]{:S(2)}) %collective-permute-start.15) | collective-permute-done | bytes 45088 | tf_op jit(solution)/shard_map/ppermute | solution.py:541
  114.4 0.8 collective-permute-done.16.refs_1_
  115.2 0.6 collective-permute-done.17.refs_2_
  115.8 1.5 %collective-permute-start.20 = (bf16[16,1408]{1,0:T(8,128)(2,1)S(1)}, bf16[16,1408]{1,0:T(8,128)(2,1)S(1)}, u32[]{:S(2)}, u32[]{:S(2)}) collective-permute-start(bf16[16,1408]{1,0:T(8,128)(2,1)S(1)} %shard_map.227.refs_0_), channel_id=1, source_target_pairs={{0,6},{1,7},{2,4},{3,5},{4,2},{5,3},{6,0},{7,1},{8,14},{9,15},{10,... | collective-permute-start | bytes 135176 | tf_op jit(solution)/shard_map/ppermute | solution.py:541
  117.3 0.9 collective-permute-start.19
  118.3 2.0 %collective-permute-start.18 = (bf16[16,1408]{1,0:T(8,128)(2,1)S(1)}, bf16[16,1408]{1,0:T(8,128)(2,1)S(1)}, u32[]{:S(2)}, u32[]{:S(2)}) collective-permute-start(bf16[16,1408]{1,0:T(8,128)(2,1)S(1)} %shard_map.227.refs_0_), channel_id=1, source_target_pairs={{0,2},{1,3},{2,0},{3,1},{4,6},{5,7},{6,4},{7,5},{8,10},{9,11},{10,... | collective-permute-start | bytes 135176 | tf_op jit(solution)/shard_map/ppermute | solution.py:541
  120.3 1.9 %shard_map.229 = bf16[288,1024]{1,0:T(8,128)(2,1)} custom-call(s32[4]{0:T(128)S(1)} %pad_add_fusion.me_ref, bf16[512,1024]{1,0:T(8,128)(2,1)S(1)} %copy-done.1, bf16[4,36,512]{2,1,0:T(8,128)(2,1)S(1)} %get-tuple-element.81.mine_ref.refs_0_, bf16[4,36,512]{2,1,0:T(8,128)(2,1)S(1)} %collective-permute-done.8.other_ref.refs_1_, ...), custom_call_target="tpu_custom_call" | custom-call | flops 301989888 | bytes 1564688 | tf_op jit(solution)/shard_map/pallas_call | solution.py:478
  122.1 0.6 collective-permute-done.19.refs_2_
  122.8 1.8 %collective-permute-start.24 = (bf16[4,16,1408]{2,1,0:T(8,128)(2,1)S(1)}, bf16[4,16,1408]{2,1,0:T(8,128)(2,1)S(1)}, u32[]{:S(2)}, u32[]{:S(2)}) collective-permute-start(bf16[4,16,1408]{2,1,0:T(8,128)(2,1)S(1)} %shard_map.228.refs_0_), channel_id=1, source_target_pairs={{0,17},{1,16},{2,19},{3,18},{4,21},{5,20},{6,23},{7,22},{8,25},{9,... | collective-permute-start | bytes 540680 | tf_op jit(solution)/shard_map/ppermute | solution.py:541
  124.6 1.2 collective-permute-start.23
  125.8 0.5 collective-permute-start.22
  126.4 3.3 %collective-permute-done.24.refs_3_ = bf16[4,16,1408]{2,1,0:T(8,128)(2,1)S(1)} collective-permute-done((bf16[4,16,1408]{2,1,0:T(8,128)(2,1)S(1)}, bf16[4,16,1408]{2,1,0:T(8,128)(2,1)S(1)}, u32[]{:S(2)}, u32[]{:S(2)}) %collective-permute-start.24) | collective-permute-done | bytes 180256 | tf_op jit(solution)/shard_map/ppermute | solution.py:541
  129.7 1.8 %collective-permute-done.23.refs_2_ = bf16[4,16,1408]{2,1,0:T(8,128)(2,1)S(1)} collective-permute-done((bf16[4,16,1408]{2,1,0:T(8,128)(2,1)S(1)}, bf16[4,16,1408]{2,1,0:T(8,128)(2,1)S(1)}, u32[]{:S(2)}, u32[]{:S(2)}) %collective-permute-start.23) | collective-permute-done | bytes 180256 | tf_op jit(solution)/shard_map/ppermute | solution.py:541
  131.5 0.5 collective-permute-start.26
  132.0 0.9 collective-permute-done.27.refs_6_
  132.9 0.3 collective-permute-done.26.refs_5_
  133.2 2.2 %shard_map.230 = (f32[512,1024]{1,0:T(8,128)}, f32[256,512]{1,0:T(8,128)}, f32[1,1]{1,0:T(1,128)}) custom-call(s32[4]{0:T(128)S(1)} %pad_add_fusion.me_ref, bf16[4,16,1408]{2,1,0:T(8,128)(2,1)S(1)} %shard_map.228.refs_0_, bf16[4,16,1408]{2,1,0:T(8,128)(2,1)S(1)} %collective-permute-done.22.refs_1_, bf16[4,16,1408]{2,1,0:T(8,128)(2,1)S(1)} %collective-permute-done.23.refs_2_, ...), custom_call_target="tpu_custom_call" | custom-call | bytes 1441808 | tf_op jit(solution)/shard_map/pallas_call | solution.py:478
  (58 shorter events, 0.5 us)
Async XLA Ops:
  0.8 50.1 %copy-start.3 = (bf16[1024,512]{1,0:T(8,128)(2,1)S(1)}, bf16[1024,512]{1,0:T(8,128)(2,1)}, u32[]{:S(2)}) copy-start(bf16[1024,512]{1,0:T(8,128)(2,1)} %w_dec_ref.1) | copy-start | bytes 3145732
  0.8 50.1 %copy-start.4 = (bf16[512,768]{1,0:T(8,128)(2,1)S(1)}, bf16[512,768]{1,0:T(8,128)(2,1)}, u32[]{:S(2)}) copy-start(bf16[512,768]{1,0:T(8,128)(2,1)} %w_qkv_ref.1) | copy-start | bytes 2359300
  8.3 42.6 %copy-start = (bf16[1,288,1024]{2,1,0:T(8,128)(2,1)S(1)}, bf16[1,288,1024]{2,1,0:T(8,128)(2,1)}, u32[]{:S(2)}) copy-start(bf16[1,288,1024]{2,1,0:T(8,128)(2,1)} %param.21) | copy-start | bytes 1769476
  8.3 42.6 %copy-start.2 = (bf16[512,1024]{1,0:T(8,128)(2,1)S(1)}, bf16[512,1024]{1,0:T(8,128)(2,1)}, u32[]{:S(2)}) copy-start(bf16[512,1024]{1,0:T(8,128)(2,1)} %w_out_ref.2) | copy-start | bytes 3145732
  8.3 42.6 %copy-start.5 = (bf16[288,512]{1,0:T(8,128)(2,1)S(1)}, bf16[288,512]{1,0:T(8,128)(2,1)}, u32[]{:S(2)}) copy-start(bf16[288,512]{1,0:T(8,128)(2,1)} %pos_ref.1) | copy-start | bytes 884740
  8.3 42.6 %copy-start.6 = (s32[1,288]{1,0:T(1,128)S(1)}, s32[1,288]{1,0:T(1,128)}, u32[]{:S(2)}) copy-start(s32[1,288]{1,0:T(1,128)} %slots_ref.3) | copy-start | bytes 3460
  8.3 42.6 %copy-start.7 = (bf16[1024]{0:T(1024)(128)(2,1)S(1)}, bf16[1024]{0:T(1024)(128)(2,1)}, u32[]{:S(2)}) copy-start(bf16[1024]{0:T(1024)(128)(2,1)} %out_gain_ref.1) | copy-start | bytes 6148
  8.3 42.6 %copy-start.8 = (s32[1,288]{1,0:T(1,128)S(1)}, s32[1,288]{1,0:T(1,128)}, u32[]{:S(2)}) copy-start(s32[1,288]{1,0:T(1,128)} %owner_ref.1) | copy-start | bytes 3460
  8.4 42.6 %copy-start.9 = (bf16[512]{0:T(512)(128)(2,1)S(1)}, bf16[512]{0:T(512)(128)(2,1)}, u32[]{:S(2)}) copy-start(bf16[512]{0:T(512)(128)(2,1)} %mask_ref.1) | copy-start | bytes 3076
  8.4 42.6 %copy-start.10 = (bf16[512]{0:T(512)(128)(2,1)S(1)}, bf16[512]{0:T(512)(128)(2,1)}, u32[]{:S(2)}) copy-start(bf16[512]{0:T(512)(128)(2,1)} %gain_ref.3) | copy-start | bytes 3076
  8.4 10.5 %collective-permute-start = (bf16[448,128]{1,0:T(8,128)(2,1)S(1)}, bf16[448,128]{1,0:T(8,128)(2,1)S(1)}, u32[]{:S(2)}, u32[]{:S(2)}) collective-permute-start(bf16[448,128]{1,0:T(8,128)(2,1)S(1)} %get-tuple-element.55), channel_id=1, source_target_pairs={{0,6},{1,7},{2,4},{3,5},{4,2},{5,3},{6,0},{7,1},{8,14},{9,15},{10,... | collective-permute-start | bytes 344072 | tf_op jit(solution)/shard_map/ppermute | solution.py:541
  13.5 14.6 %collective-permute-start.1 = (bf16[448,128]{1,0:T(8,128)(2,1)S(1)}, bf16[448,128]{1,0:T(8,128)(2,1)S(1)}, u32[]{:S(2)}, u32[]{:S(2)}) collective-permute-start(bf16[448,128]{1,0:T(8,128)(2,1)S(1)} %get-tuple-element.56), channel_id=1, source_target_pairs={{0,7},{1,6},{2,5},{3,4},{4,3},{5,2},{6,1},{7,0},{8,15},{9,14},{10,... | collective-permute-start | bytes 344072 | tf_op jit(solution)/shard_map/ppermute | solution.py:541
  14.7 16.9 %collective-permute-start.2 = (bf16[448,128]{1,0:T(8,128)(2,1)S(1)}, bf16[448,128]{1,0:T(8,128)(2,1)S(1)}, u32[]{:S(2)}, u32[]{:S(2)}) collective-permute-start(bf16[448,128]{1,0:T(8,128)(2,1)S(1)} %get-tuple-element.57), channel_id=1, source_target_pairs={{0,4},{1,5},{2,6},{3,7},{4,0},{5,1},{6,2},{7,3},{8,12},{9,13},{10,... | collective-permute-start | bytes 344072 | tf_op jit(solution)/shard_map/ppermute | solution.py:541
  15.5 18.7 %collective-permute-start.3 = (bf16[448,128]{1,0:T(8,128)(2,1)S(1)}, bf16[448,128]{1,0:T(8,128)(2,1)S(1)}, u32[]{:S(2)}, u32[]{:S(2)}) collective-permute-start(bf16[448,128]{1,0:T(8,128)(2,1)S(1)} %get-tuple-element.58), channel_id=1, source_target_pairs={{0,5},{1,4},{2,7},{3,6},{4,1},{5,0},{6,3},{7,2},{8,13},{9,12},{10,... | collective-permute-start | bytes 344072 | tf_op jit(solution)/shard_map/ppermute | solution.py:541
  17.4 16.8 %collective-permute-start.4 = (bf16[448,128]{1,0:T(8,128)(2,1)S(1)}, bf16[448,128]{1,0:T(8,128)(2,1)S(1)}, u32[]{:S(2)}, u32[]{:S(2)}) collective-permute-start(bf16[448,128]{1,0:T(8,128)(2,1)S(1)} %get-tuple-element.59), channel_id=1, source_target_pairs={{0,2},{1,3},{2,0},{3,1},{4,6},{5,7},{6,4},{7,5},{8,10},{9,11},{10,... | collective-permute-start | bytes 344072 | tf_op jit(solution)/shard_map/ppermute | solution.py:541
  18.8 16.3 %collective-permute-start.5 = (bf16[448,128]{1,0:T(8,128)(2,1)S(1)}, bf16[448,128]{1,0:T(8,128)(2,1)S(1)}, u32[]{:S(2)}, u32[]{:S(2)}) collective-permute-start(bf16[448,128]{1,0:T(8,128)(2,1)S(1)} %get-tuple-element.60), channel_id=1, source_target_pairs={{0,3},{1,2},{2,1},{3,0},{4,7},{5,6},{6,5},{7,4},{8,11},{9,10},{10,... | collective-permute-start | bytes 344072 | tf_op jit(solution)/shard_map/ppermute | solution.py:541
  28.1 7.7 %collective-permute-start.6 = (bf16[448,128]{1,0:T(8,128)(2,1)S(1)}, bf16[448,128]{1,0:T(8,128)(2,1)S(1)}, u32[]{:S(2)}, u32[]{:S(2)}) collective-permute-start(bf16[448,128]{1,0:T(8,128)(2,1)S(1)} %get-tuple-element.61), channel_id=1, source_target_pairs={{0,1},{1,0},{2,3},{3,2},{4,5},{5,4},{6,7},{7,6},{8,9},{9,8},{10,11... | collective-permute-start | bytes 344072 | tf_op jit(solution)/shard_map/ppermute | solution.py:541
  65.9 18.3 %copy-start.1 = (bf16[512,1024]{1,0:T(8,128)(2,1)S(1)}, bf16[512,1024]{1,0:T(8,128)(2,1)}, u32[]{:S(2)}) copy-start(bf16[512,1024]{1,0:T(8,128)(2,1)} %w_head_ref.5) | copy-start | bytes 3145732
  65.9 18.3 %copy-start.11 = (bf16[512,2048]{1,0:T(8,128)(2,1)S(1)}, bf16[512,2048]{1,0:T(8,128)(2,1)}, u32[]{:S(2)}) copy-start(bf16[512,2048]{1,0:T(8,128)(2,1)} %w_up_ref.3) | copy-start | bytes 6291460
  65.9 18.3 %copy-start.12 = (bf16[2048,512]{1,0:T(8,128)(2,1)S(1)}, bf16[2048,512]{1,0:T(8,128)(2,1)}, u32[]{:S(2)}) copy-start(bf16[2048,512]{1,0:T(8,128)(2,1)} %w_down_ref.3) | copy-start | bytes 6291460
  65.9 18.3 %copy-start.13 = (bf16[256,512]{1,0:T(8,128)(2,1)S(1)}, bf16[256,512]{1,0:T(8,128)(2,1)}, u32[]{:S(2)}) copy-start(bf16[256,512]{1,0:T(8,128)(2,1)} %w_out_ref.3) | copy-start | bytes 786436
  65.9 18.3 %copy-start.14 = (bf16[512]{0:T(512)(128)(2,1)S(1)}, bf16[512]{0:T(512)(128)(2,1)}, u32[]{:S(2)}) copy-start(bf16[512]{0:T(512)(128)(2,1)} %feed_gain_ref.3) | copy-start | bytes 3076
  65.9 18.3 %copy-start.15 = (bf16[512]{0:T(512)(128)(2,1)S(1)}, bf16[512]{0:T(512)(128)(2,1)}, u32[]{:S(2)}) copy-start(bf16[512]{0:T(512)(128)(2,1)} %head_gain_ref.3) | copy-start | bytes 3076
  89.3 5.4 %collective-permute-start.8 = (bf16[4,36,512]{2,1,0:T(8,128)(2,1)S(1)}, bf16[4,36,512]{2,1,0:T(8,128)(2,1)S(1)}, u32[]{:S(2)}, u32[]{:S(2)}) collective-permute-start(bf16[4,36,512]{2,1,0:T(8,128)(2,1)S(1)} %get-tuple-element.77), channel_id=1, source_target_pairs={{0,1},{1,0},{2,3},{3,2},{4,5},{5,4},{6,7},{7,6},{8,9},{9,8},{10,11... | collective-permute-start | bytes 442376 | tf_op jit(solution)/shard_map/ppermute | solution.py:541
  89.5 5.2 %collective-permute-start.7 = (bf16[4,4,16,1024]{3,2,1,0:T(8,128)(2,1)S(1)}, bf16[4,4,16,1024]{3,2,1,0:T(8,128)(2,1)S(1)}, u32[]{:S(2)}, u32[]{:S(2)}) collective-permute-start(bf16[4,4,16,1024]{3,2,1,0:T(8,128)(2,1)S(1)} %get-tuple-element.76), channel_id=1, source_target_pairs={{0,8},{1,9},{2,10},{3,11},{4,12},{5,13},{6,14},{7,15},{8,0},{9,1},... | collective-permute-start | bytes 1572872 | tf_op jit(solution)/shard_map/ppermute | solution.py:541
  94.6 1.4 %collective-permute-start.9 = (bf16[4,4,16,384]{3,2,1,0:T(8,128)(2,1)S(1)}, bf16[4,4,16,384]{3,2,1,0:T(8,128)(2,1)S(1)}, u32[]{:S(2)}, u32[]{:S(2)}) collective-permute-start(bf16[4,4,16,384]{3,2,1,0:T(8,128)(2,1)S(1)} %get-tuple-element.80), channel_id=1, source_target_pairs={{0,8},{1,9},{2,10},{3,11},{4,12},{5,13},{6,14},{7,15},{8,0},{9,1},... | collective-permute-start | bytes 589832 | tf_op jit(solution)/shard_map/ppermute | solution.py:541
  96.3 11.8 %collective-permute-start.10 = (bf16[4,16,1408]{2,1,0:T(8,128)(2,1)S(1)}, bf16[4,16,1408]{2,1,0:T(8,128)(2,1)S(1)}, u32[]{:S(2)}, u32[]{:S(2)}) collective-permute-start(bf16[4,16,1408]{2,1,0:T(8,128)(2,1)S(1)} %get-tuple-element.83), channel_id=1, source_target_pairs={{0,17},{1,16},{2,19},{3,18},{4,21},{5,20},{6,23},{7,22},{8,25},{9,... | collective-permute-start | bytes 540680 | tf_op jit(solution)/shard_map/ppermute | solution.py:541
  97.4 10.7 %collective-permute-start.11 = (bf16[4,16,1408]{2,1,0:T(8,128)(2,1)S(1)}, bf16[4,16,1408]{2,1,0:T(8,128)(2,1)S(1)}, u32[]{:S(2)}, u32[]{:S(2)}) collective-permute-start(bf16[4,16,1408]{2,1,0:T(8,128)(2,1)S(1)} %get-tuple-element.84), channel_id=1, source_target_pairs={{0,1},{1,0},{2,3},{3,2},{4,5},{5,4},{6,7},{7,6},{8,9},{9,8},{10,11... | collective-permute-start | bytes 540680 | tf_op jit(solution)/shard_map/ppermute | solution.py:541
  99.3 8.8 %collective-permute-start.12 = (bf16[4,16,1408]{2,1,0:T(8,128)(2,1)S(1)}, bf16[4,16,1408]{2,1,0:T(8,128)(2,1)S(1)}, u32[]{:S(2)}, u32[]{:S(2)}) collective-permute-start(bf16[4,16,1408]{2,1,0:T(8,128)(2,1)S(1)} %get-tuple-element.85), channel_id=1, source_target_pairs={{0,16},{1,17},{2,18},{3,19},{4,20},{5,21},{6,22},{7,23},{8,24},{9,... | collective-permute-start | bytes 540680 | tf_op jit(solution)/shard_map/ppermute | solution.py:541
  99.8 8.2 %collective-permute-start.13 = (bf16[2,36,512]{2,1,0:T(8,128)(2,1)S(1)}, bf16[2,36,512]{2,1,0:T(8,128)(2,1)S(1)}, u32[]{:S(2)}, u32[]{:S(2)}) collective-permute-start(bf16[2,36,512]{2,1,0:T(8,128)(2,1)S(1)} %get-tuple-element.87), channel_id=1, source_target_pairs={{0,4},{1,5},{2,6},{3,7},{4,0},{5,1},{6,2},{7,3},{8,12},{9,13},{10,... | collective-permute-start | bytes 221192 | tf_op jit(solution)/shard_map/ppermute | solution.py:541
  100.2 7.9 %collective-permute-start.14 = (bf16[2,36,512]{2,1,0:T(8,128)(2,1)S(1)}, bf16[2,36,512]{2,1,0:T(8,128)(2,1)S(1)}, u32[]{:S(2)}, u32[]{:S(2)}) collective-permute-start(bf16[2,36,512]{2,1,0:T(8,128)(2,1)S(1)} %get-tuple-element.88), channel_id=1, source_target_pairs={{0,6},{1,7},{2,4},{3,5},{4,2},{5,3},{6,0},{7,1},{8,14},{9,15},{10,... | collective-permute-start | bytes 221192 | tf_op jit(solution)/shard_map/ppermute | solution.py:541
  108.1 12.2 %collective-permute-start.21 = (bf16[2,36,512]{2,1,0:T(8,128)(2,1)S(1)}, bf16[2,36,512]{2,1,0:T(8,128)(2,1)S(1)}, u32[]{:S(2)}, u32[]{:S(2)}) collective-permute-start(bf16[2,36,512]{2,1,0:T(8,128)(2,1)S(1)} %get-tuple-element.94), channel_id=1, source_target_pairs={{0,2},{1,3},{2,0},{3,1},{4,6},{5,7},{6,4},{7,5},{8,10},{9,11},{10,... | collective-permute-start | bytes 221192 | tf_op jit(solution)/shard_map/ppermute | solution.py:541
  108.2 6.2 %collective-permute-start.15 = (bf16[16,1408]{1,0:T(8,128)(2,1)S(1)}, bf16[16,1408]{1,0:T(8,128)(2,1)S(1)}, u32[]{:S(2)}, u32[]{:S(2)}) collective-permute-start(bf16[16,1408]{1,0:T(8,128)(2,1)S(1)} %get-tuple-element.90), channel_id=1, source_target_pairs={{0,6},{1,7},{2,4},{3,5},{4,2},{5,3},{6,0},{7,1},{8,14},{9,15},{10,... | collective-permute-start | bytes 135176 | tf_op jit(solution)/shard_map/ppermute | solution.py:541
  109.3 6.0 %collective-permute-start.16 = (bf16[16,1408]{1,0:T(8,128)(2,1)S(1)}, bf16[16,1408]{1,0:T(8,128)(2,1)S(1)}, u32[]{:S(2)}, u32[]{:S(2)}) collective-permute-start(bf16[16,1408]{1,0:T(8,128)(2,1)S(1)} %get-tuple-element.91), channel_id=1, source_target_pairs={{0,4},{1,5},{2,6},{3,7},{4,0},{5,1},{6,2},{7,3},{8,12},{9,13},{10,... | collective-permute-start | bytes 135176 | tf_op jit(solution)/shard_map/ppermute | solution.py:541
  111.7 4.0 %collective-permute-start.17 = (bf16[16,1408]{1,0:T(8,128)(2,1)S(1)}, bf16[16,1408]{1,0:T(8,128)(2,1)S(1)}, u32[]{:S(2)}, u32[]{:S(2)}) collective-permute-start(bf16[16,1408]{1,0:T(8,128)(2,1)S(1)} %get-tuple-element.92), channel_id=1, source_target_pairs={{0,2},{1,3},{2,0},{3,1},{4,6},{5,7},{6,4},{7,5},{8,10},{9,11},{10,... | collective-permute-start | bytes 135176 | tf_op jit(solution)/shard_map/ppermute | solution.py:541
  115.8 6.3 %collective-permute-start.20 = (bf16[16,1408]{1,0:T(8,128)(2,1)S(1)}, bf16[16,1408]{1,0:T(8,128)(2,1)S(1)}, u32[]{:S(2)}, u32[]{:S(2)}) collective-permute-start(bf16[16,1408]{1,0:T(8,128)(2,1)S(1)} %shard_map.227.refs_0_), channel_id=1, source_target_pairs={{0,6},{1,7},{2,4},{3,5},{4,2},{5,3},{6,0},{7,1},{8,14},{9,15},{10,... | collective-permute-start | bytes 135176 | tf_op jit(solution)/shard_map/ppermute | solution.py:541
  117.3 5.4 %collective-permute-start.19 = (bf16[16,1408]{1,0:T(8,128)(2,1)S(1)}, bf16[16,1408]{1,0:T(8,128)(2,1)S(1)}, u32[]{:S(2)}, u32[]{:S(2)}) collective-permute-start(bf16[16,1408]{1,0:T(8,128)(2,1)S(1)} %shard_map.227.refs_0_), channel_id=1, source_target_pairs={{0,4},{1,5},{2,6},{3,7},{4,0},{5,1},{6,2},{7,3},{8,12},{9,13},{10,... | collective-permute-start | bytes 135176 | tf_op jit(solution)/shard_map/ppermute | solution.py:541
  118.3 4.5 %collective-permute-start.18 = (bf16[16,1408]{1,0:T(8,128)(2,1)S(1)}, bf16[16,1408]{1,0:T(8,128)(2,1)S(1)}, u32[]{:S(2)}, u32[]{:S(2)}) collective-permute-start(bf16[16,1408]{1,0:T(8,128)(2,1)S(1)} %shard_map.227.refs_0_), channel_id=1, source_target_pairs={{0,2},{1,3},{2,0},{3,1},{4,6},{5,7},{6,4},{7,5},{8,10},{9,11},{10,... | collective-permute-start | bytes 135176 | tf_op jit(solution)/shard_map/ppermute | solution.py:541
  122.8 6.9 %collective-permute-start.24 = (bf16[4,16,1408]{2,1,0:T(8,128)(2,1)S(1)}, bf16[4,16,1408]{2,1,0:T(8,128)(2,1)S(1)}, u32[]{:S(2)}, u32[]{:S(2)}) collective-permute-start(bf16[4,16,1408]{2,1,0:T(8,128)(2,1)S(1)} %shard_map.228.refs_0_), channel_id=1, source_target_pairs={{0,17},{1,16},{2,19},{3,18},{4,21},{5,20},{6,23},{7,22},{8,25},{9,... | collective-permute-start | bytes 540680 | tf_op jit(solution)/shard_map/ppermute | solution.py:541
  124.6 6.9 %collective-permute-start.23 = (bf16[4,16,1408]{2,1,0:T(8,128)(2,1)S(1)}, bf16[4,16,1408]{2,1,0:T(8,128)(2,1)S(1)}, u32[]{:S(2)}, u32[]{:S(2)}) collective-permute-start(bf16[4,16,1408]{2,1,0:T(8,128)(2,1)S(1)} %shard_map.228.refs_0_), channel_id=1, source_target_pairs={{0,1},{1,0},{2,3},{3,2},{4,5},{5,4},{6,7},{7,6},{8,9},{9,8},{10,11... | collective-permute-start | bytes 540680 | tf_op jit(solution)/shard_map/ppermute | solution.py:541
  125.8 5.7 %collective-permute-start.22 = (bf16[4,16,1408]{2,1,0:T(8,128)(2,1)S(1)}, bf16[4,16,1408]{2,1,0:T(8,128)(2,1)S(1)}, u32[]{:S(2)}, u32[]{:S(2)}) collective-permute-start(bf16[4,16,1408]{2,1,0:T(8,128)(2,1)S(1)} %shard_map.228.refs_0_), channel_id=1, source_target_pairs={{0,16},{1,17},{2,18},{3,19},{4,20},{5,21},{6,22},{7,23},{8,24},{9,... | collective-permute-start | bytes 540680 | tf_op jit(solution)/shard_map/ppermute | solution.py:541
  126.4 5.7 %collective-permute-start.25 = (bf16[4,16,1408]{2,1,0:T(8,128)(2,1)S(1)}, bf16[4,16,1408]{2,1,0:T(8,128)(2,1)S(1)}, u32[]{:S(2)}, u32[]{:S(2)}) collective-permute-start(bf16[4,16,1408]{2,1,0:T(8,128)(2,1)S(1)} %shard_map.228.refs_0_), channel_id=1, source_target_pairs={{0,8},{1,9},{2,10},{3,11},{4,12},{5,13},{6,14},{7,15},{8,0},{9,1},... | collective-permute-start | bytes 540680 | tf_op jit(solution)/shard_map/ppermute | solution.py:541
  129.7 2.3 %collective-permute-start.28 = (bf16[4,16,1408]{2,1,0:T(8,128)(2,1)S(1)}, bf16[4,16,1408]{2,1,0:T(8,128)(2,1)S(1)}, u32[]{:S(2)}, u32[]{:S(2)}) collective-permute-start(bf16[4,16,1408]{2,1,0:T(8,128)(2,1)S(1)} %collective-permute-done.24.refs_3_), channel_id=1, source_target_pairs={{0,8},{1,9},{2,10},{3,11},{4,12},{5,13},{6,14},{7,15},{8,0},{9,1},... | collective-permute-start | bytes 540680 | tf_op jit(solution)/shard_map/ppermute | solution.py:541
  131.5 1.4 %collective-permute-start.27 = (bf16[4,16,1408]{2,1,0:T(8,128)(2,1)S(1)}, bf16[4,16,1408]{2,1,0:T(8,128)(2,1)S(1)}, u32[]{:S(2)}, u32[]{:S(2)}) collective-permute-start(bf16[4,16,1408]{2,1,0:T(8,128)(2,1)S(1)} %collective-permute-done.23.refs_2_), channel_id=1, source_target_pairs={{0,8},{1,9},{2,10},{3,11},{4,12},{5,13},{6,14},{7,15},{8,0},{9,1},... | collective-permute-start | bytes 540680 | tf_op jit(solution)/shard_map/ppermute | solution.py:541
  131.5 1.7 %collective-permute-start.26 = (bf16[4,16,1408]{2,1,0:T(8,128)(2,1)S(1)}, bf16[4,16,1408]{2,1,0:T(8,128)(2,1)S(1)}, u32[]{:S(2)}, u32[]{:S(2)}) collective-permute-start(bf16[4,16,1408]{2,1,0:T(8,128)(2,1)S(1)} %collective-permute-done.22.refs_1_), channel_id=1, source_target_pairs={{0,8},{1,9},{2,10},{3,11},{4,12},{5,13},{6,14},{7,15},{8,0},{9,1},... | collective-permute-start | bytes 540680 | tf_op jit(solution)/shard_map/ppermute | solution.py:541

commit v10 on v9

--- a/solution.py
+++ b/solution.py
@@ -331,9 +331,10 @@
         square = pre * pre
         t = jnp.tanh(pre * (c + (c * 0.044715) * square))
         gate = 0.5 + 0.5 * t
-        slope = gate + (0.5 * pre) * (1.0 - t * t) * (c + (3 * c * 0.044715) * square)
+        act = pre * gate
+        slope = gate + act * (1.0 - gate) * (2 * c + (6 * c * 0.044715) * square)
         slope_ref[:, cols] = slope.astype(BF)
-        z_ref[...] += dot((pre * gate).astype(BF), w_down_ref[cols, :])
+        z_ref[...] += dot(act.astype(BF), w_down_ref[cols, :])
 
     zn = layer_norm(z_ref[...], head_gain_ref[...])
     zn_buf[...] = zn.astype(BF)

time: 136 us -> 136 us (level)
  no operation moved by 1% of the time
where the time goes in v10:
time: 136 us; the launch traced here: 135 us
  starting transfers between devices  38.7 us (28%)
  blocking collectives  35.1 us (26%)
  Pallas kernels  33.1 us (24%)
  waiting for transfers between devices  27.2 us (20%)
    ppermute x29, starting transfers between devices, across(): return lax.ppermute(x, ('dp', 'ctx'), pairs)  38.7 us
    all_to_all x3, blocking collectives, swap(): lax.all_to_all(x, axis, split_axis=0, concat_axis=0, tiled=True, axis_ind...  35.1 us
    pallas_call x12, Pallas kernels, vmem_call(): pl.pallas_call(kernel, out_shape=outs, in_specs=space, out_specs=[pl.Bloc...  33.1 us
    ppermute x29, waiting for transfers between devices, across(): return lax.ppermute(x, ('dp', 'ctx'), pairs)  27.2 us
  transfers between devices with their start and end apart: 29, of which 15 were waited for; matrix products, arithmetic and copies ran while one was open for 0% of the time, Pallas kernels for 4%

profile of v10, /device:TPU:0, one launch (start us, length us, event | category | flops | bytes accessed | tf_op | source)
XLA Modules:
  0.0 135.4 jit_solution(4962185996636340566)
XLA Ops:
  0.8 7.5 %shard_map.219 = (bf16[288,1024]{1,0:T(8,128)(2,1)S(1)}, bf16[448,128]{1,0:T(8,128)(2,1)S(1)}, bf16[448,128]{1,0:T(8,128)(2,1)S(1)}, bf16[448,128]{1,0:T(8,128)(...) custom-call(s32[4]{0:T(128)S(1)} %pad_add_fusion.me_ref, ...), custom_call_target="tpu_custom_call" | custom-call | flops 1509949440 | bytes 6425744 | tf_op jit(solution)/shard_map/pallas_call | solution.py:479
  8.4 5.1 %collective-permute-start = (bf16[448,128]{1,0:T(8,128)(2,1)S(1)}, bf16[448,128]{1,0:T(8,128)(2,1)S(1)}, u32[]{:S(2)}, u32[]{:S(2)}) collective-permute-start(bf16[448,128]{1,0:T(8,128)(2,1)S(1)} %get-tuple-element.55), channel_id=1, source_target_pairs={{0,6},{1,7},{2,4},{3,5},{4,2},{5,3},{6,0},{7,1},{8,14},{9,15},{10,... | collective-permute-start | bytes 344072 | tf_op jit(solution)/shard_map/ppermute | solution.py:542
  13.5 1.2 collective-permute-start.1
  14.7 0.8 collective-permute-start.2
  15.5 1.9 %collective-permute-start.3 = (bf16[448,128]{1,0:T(8,128)(2,1)S(1)}, bf16[448,128]{1,0:T(8,128)(2,1)S(1)}, u32[]{:S(2)}, u32[]{:S(2)}) collective-permute-start(bf16[448,128]{1,0:T(8,128)(2,1)S(1)} %get-tuple-element.58), channel_id=1, source_target_pairs={{0,5},{1,4},{2,7},{3,6},{4,1},{5,0},{6,3},{7,2},{8,13},{9,12},{10,... | collective-permute-start | bytes 344072 | tf_op jit(solution)/shard_map/ppermute | solution.py:542
  17.4 1.4 %collective-permute-start.4 = (bf16[448,128]{1,0:T(8,128)(2,1)S(1)}, bf16[448,128]{1,0:T(8,128)(2,1)S(1)}, u32[]{:S(2)}, u32[]{:S(2)}) collective-permute-start(bf16[448,128]{1,0:T(8,128)(2,1)S(1)} %get-tuple-element.59), channel_id=1, source_target_pairs={{0,2},{1,3},{2,0},{3,1},{4,6},{5,7},{6,4},{7,5},{8,10},{9,11},{10,... | collective-permute-start | bytes 344072 | tf_op jit(solution)/shard_map/ppermute | solution.py:542
  18.8 9.3 %collective-permute-start.5 = (bf16[448,128]{1,0:T(8,128)(2,1)S(1)}, bf16[448,128]{1,0:T(8,128)(2,1)S(1)}, u32[]{:S(2)}, u32[]{:S(2)}) collective-permute-start(bf16[448,128]{1,0:T(8,128)(2,1)S(1)} %get-tuple-element.60), channel_id=1, source_target_pairs={{0,3},{1,2},{2,1},{3,0},{4,7},{5,6},{6,5},{7,4},{8,11},{9,10},{10,... | collective-permute-start | bytes 344072 | tf_op jit(solution)/shard_map/ppermute | solution.py:542
  28.1 3.5 %collective-permute-done.2.refs_2_ = bf16[448,128]{1,0:T(8,128)(2,1)S(1)} collective-permute-done((bf16[448,128]{1,0:T(8,128)(2,1)S(1)}, bf16[448,128]{1,0:T(8,128)(2,1)S(1)}, u32[]{:S(2)}, u32[]{:S(2)}) %collective-permute-start.2) | collective-permute-done | bytes 114720 | tf_op jit(solution)/shard_map/ppermute | solution.py:542
  31.6 2.5 %collective-permute-done.3.refs_3_ = bf16[448,128]{1,0:T(8,128)(2,1)S(1)} collective-permute-done((bf16[448,128]{1,0:T(8,128)(2,1)S(1)}, bf16[448,128]{1,0:T(8,128)(2,1)S(1)}, u32[]{:S(2)}, u32[]{:S(2)}) %collective-permute-start.3) | collective-permute-done | bytes 114720 | tf_op jit(solution)/shard_map/ppermute | solution.py:542
  34.2 1.0 collective-permute-done.5.refs_5_
  35.1 0.7 collective-permute-done.6.refs_6_
  35.8 2.8 %shard_map.220 = bf16[8,144,128]{2,1,0:T(8,128)(2,1)S(1)} custom-call(s32[4]{0:T(128)S(1)} %pad_add_fusion.me_ref, bf16[448,128]{1,0:T(8,128)(2,1)S(1)} %collective-permute-done.refs_0_, bf16[448,128]{1,0:T(8,128)(2,1)S(1)} %collective-permute-done.1.refs_1_, bf16[448,128]{1,0:T(8,128)(2,1)S(1)} %collective-permute-done.2.refs_2_, ...), custom_call_target="tpu_custom_call" | custom-call | flops 411041792 | bytes 917520 | tf_op jit(solution)/shard_map/pallas_call | solution.py:479
  38.6 12.3 %all_to_all.15.att_ref = bf16[8,144,128]{2,1,0:T(8,128)(2,1)S(1)} all-to-all(bf16[8,144,128]{2,1,0:T(8,128)(2,1)S(1)} %shard_map.220), channel_id=1, replica_groups=mesh['dp'=4,'ctx'=8] {'ctx'}, dimensions={0} | all-to-all | bytes 589824 | tf_op jit(solution)/shard_map/all_to_all | solution.py:504
  51.0 2.7 %shard_map.221 = (bf16[8,216,128]{2,1,0:T(8,128)(2,1)S(1)}, bf16[288,512]{1,0:T(8,128)(2,1)S(1)}, bf16[288,1024]{1,0:T(8,128)(2,1)S(1)}, f32[288,128]{1,0:T(8,128)S(1)}) custom-call(bf16[8,144,128]{2,1,0:T(8,128)(2,1)S(1)} %all_to_all.15.att_ref, bf16[288,1024]{1,0:T(8,128)(2,1)S(1)} %get-tuple-element.63.tok_ref, bf16[512,1024]{1,0:T(8,128)(2,1)S(1)} %copy-done.2, ...), custom_call_target="tpu_custom_call" | custom-call | flops 603979776 | bytes 4659456 | tf_op jit(solution)/shard_map/pallas_call | solution.py:479
  53.6 12.2 %all_to_all.16.q_ref.kv_ref = bf16[8,216,128]{2,1,0:T(8,128)(2,1)S(1)} all-to-all(bf16[8,216,128]{2,1,0:T(8,128)(2,1)S(1)} %get-tuple-element.64), channel_id=1, replica_groups=mesh['dp'=4,'ctx'=8] {'ctx'}, dimensions={0} | all-to-all | bytes 884736 | tf_op jit(solution)/shard_map/all_to_all | solution.py:504
  65.9 7.7 %shard_map.222 = bf16[8,72,128]{2,1,0:T(8,128)(2,1)S(1)} custom-call(bf16[8,216,128]{2,1,0:T(8,128)(2,1)S(1)} %all_to_all.16.q_ref.kv_ref, bf16[8,216,128]{2,1,0:T(8,128)(2,1)S(1)} %all_to_all.16.q_ref.kv_ref), custom_call_target="tpu_custom_call" | custom-call | flops 2717908992 | bytes 884736 | tf_op jit(solution)/shard_map/pallas_call | solution.py:479
  73.7 10.5 %all_to_all.17.att_ref = bf16[8,72,128]{2,1,0:T(8,128)(2,1)S(1)} all-to-all(bf16[8,72,128]{2,1,0:T(8,128)(2,1)S(1)} %shard_map.222), channel_id=1, replica_groups=mesh['dp'=4,'ctx'=8] {'ctx'}, dimensions={0} | all-to-all | bytes 294912 | tf_op jit(solution)/shard_map/all_to_all | solution.py:504
  84.2 4.9 %shard_map.223 = (bf16[288,256]{1,0:T(8,128)(2,1)S(1)}, f32[288,512]{1,0:T(8,128)S(1)}, bf16[288,2048]{1,0:T(8,128)(2,1)S(1)}, f32[288,512]{1,0:T(8,128)S(1)}, b...) custom-call(s32[4]{0:T(128)S(1)} %pad_add_fusion.me_ref, ...), custom_call_target="tpu_custom_call" | custom-call | flops 1811939328 | bytes 6686736 | tf_op jit(solution)/shard_map/pallas_call | solution.py:479
  89.1 0.2 collective-permute-start.8
  89.4 3.2 %shard_map.224 = (bf16[4,4,16,384]{3,2,1,0:T(8,128)(2,1)S(1)}, bf16[4,4,16,384]{3,2,1,0:T(8,128)(2,1)S(1)}) custom-call(s32[4]{0:T(128)S(1)} %pad_add_fusion.me_ref, bf16[288,256]{1,0:T(8,128)(2,1)S(1)} %get-tuple-element.69.dec_att_ref, f32[288,512]{1,0:T(8,128)S(1)} %get-tuple-element.70.mid_ref, bf16[288,2048]{1,0:T(8,128)(2,1)S(1)} %get-tuple-element.71.slope_ref, ...), custom_call_target="tpu_custom_call" | custom-call | flops 12079595520 | bytes 8345616 | tf_op jit(solution)/shard_map/pallas_call | solution.py:479
  92.5 2.0 %collective-permute-done.8.other_ref.refs_1_ = bf16[4,36,512]{2,1,0:T(8,128)(2,1)S(1)} collective-permute-done((bf16[4,36,512]{2,1,0:T(8,128)(2,1)S(1)}, bf16[4,36,512]{2,1,0:T(8,128)(2,1)S(1)}, u32[]{:S(2)}, u32[]{:S(2)}) %collective-permute-start.8) | collective-permute-done | bytes 147488 | tf_op jit(solution)/shard_map/ppermute | solution.py:542
  94.5 1.4 %collective-permute-done.9.out_got_ref = bf16[4,4,16,384]{3,2,1,0:T(8,128)(2,1)S(1)} collective-permute-done((bf16[4,4,16,384]{3,2,1,0:T(8,128)(2,1)S(1)}, bf16[4,4,16,384]{3,2,1,0:T(8,128)(2,1)S(1)}, u32[]{:S(2)}, u32[]{:S(2)}) %collective-permute-start.9) | collective-permute-done | bytes 196640 | tf_op jit(solution)/shard_map/ppermute | solution.py:542
  96.1 1.1 collective-permute-start.10
  97.3 1.9 %collective-permute-start.11 = (bf16[4,16,1408]{2,1,0:T(8,128)(2,1)S(1)}, bf16[4,16,1408]{2,1,0:T(8,128)(2,1)S(1)}, u32[]{:S(2)}, u32[]{:S(2)}) collective-permute-start(bf16[4,16,1408]{2,1,0:T(8,128)(2,1)S(1)} %get-tuple-element.84), channel_id=1, source_target_pairs={{0,1},{1,0},{2,3},{3,2},{4,5},{5,4},{6,7},{7,6},{8,9},{9,8},{10,11... | collective-permute-start | bytes 540680 | tf_op jit(solution)/shard_map/ppermute | solution.py:542
  99.1 0.5 collective-permute-start.12
  99.7 0.4 collective-permute-start.13
  100.0 1.9 %collective-permute-start.14 = (bf16[2,36,512]{2,1,0:T(8,128)(2,1)S(1)}, bf16[2,36,512]{2,1,0:T(8,128)(2,1)S(1)}, u32[]{:S(2)}, u32[]{:S(2)}) collective-permute-start(bf16[2,36,512]{2,1,0:T(8,128)(2,1)S(1)} %get-tuple-element.88), channel_id=1, source_target_pairs={{0,6},{1,7},{2,4},{3,5},{4,2},{5,3},{6,0},{7,1},{8,14},{9,15},{10,... | collective-permute-start | bytes 221192 | tf_op jit(solution)/shard_map/ppermute | solution.py:542
  101.9 6.0 %collective-permute-done.13.refs_3_ = bf16[2,36,512]{2,1,0:T(8,128)(2,1)S(1)} collective-permute-done((bf16[2,36,512]{2,1,0:T(8,128)(2,1)S(1)}, bf16[2,36,512]{2,1,0:T(8,128)(2,1)S(1)}, u32[]{:S(2)}, u32[]{:S(2)}) %collective-permute-start.13) | collective-permute-done | bytes 73760 | tf_op jit(solution)/shard_map/ppermute | solution.py:542
  108.1 1.1 collective-permute-start.15
  109.1 2.5 %collective-permute-start.16 = (bf16[16,1408]{1,0:T(8,128)(2,1)S(1)}, bf16[16,1408]{1,0:T(8,128)(2,1)S(1)}, u32[]{:S(2)}, u32[]{:S(2)}) collective-permute-start(bf16[16,1408]{1,0:T(8,128)(2,1)S(1)} %get-tuple-element.91), channel_id=1, source_target_pairs={{0,4},{1,5},{2,6},{3,7},{4,0},{5,1},{6,2},{7,3},{8,12},{9,13},{10,... | collective-permute-start | bytes 135176 | tf_op jit(solution)/shard_map/ppermute | solution.py:542
  111.6 0.9 collective-permute-start.17
  112.5 1.7 %collective-permute-done.15.refs_0_ = bf16[16,1408]{1,0:T(8,128)(2,1)S(1)} collective-permute-done((bf16[16,1408]{1,0:T(8,128)(2,1)S(1)}, bf16[16,1408]{1,0:T(8,128)(2,1)S(1)}, u32[]{:S(2)}, u32[]{:S(2)}) %collective-permute-start.15) | collective-permute-done | bytes 45088 | tf_op jit(solution)/shard_map/ppermute | solution.py:542
  114.2 0.8 collective-permute-done.16.refs_1_
  115.1 0.6 collective-permute-done.17.refs_2_
  115.7 1.5 %collective-permute-start.20 = (bf16[16,1408]{1,0:T(8,128)(2,1)S(1)}, bf16[16,1408]{1,0:T(8,128)(2,1)S(1)}, u32[]{:S(2)}, u32[]{:S(2)}) collective-permute-start(bf16[16,1408]{1,0:T(8,128)(2,1)S(1)} %shard_map.227.refs_0_), channel_id=1, source_target_pairs={{0,6},{1,7},{2,4},{3,5},{4,2},{5,3},{6,0},{7,1},{8,14},{9,15},{10,... | collective-permute-start | bytes 135176 | tf_op jit(solution)/shard_map/ppermute | solution.py:542
  117.2 0.9 collective-permute-start.19
  118.1 2.0 %collective-permute-start.18 = (bf16[16,1408]{1,0:T(8,128)(2,1)S(1)}, bf16[16,1408]{1,0:T(8,128)(2,1)S(1)}, u32[]{:S(2)}, u32[]{:S(2)}) collective-permute-start(bf16[16,1408]{1,0:T(8,128)(2,1)S(1)} %shard_map.227.refs_0_), channel_id=1, source_target_pairs={{0,2},{1,3},{2,0},{3,1},{4,6},{5,7},{6,4},{7,5},{8,10},{9,11},{10,... | collective-permute-start | bytes 135176 | tf_op jit(solution)/shard_map/ppermute | solution.py:542
  120.1 1.9 %shard_map.229 = bf16[288,1024]{1,0:T(8,128)(2,1)} custom-call(s32[4]{0:T(128)S(1)} %pad_add_fusion.me_ref, bf16[512,1024]{1,0:T(8,128)(2,1)S(1)} %copy-done.1, bf16[4,36,512]{2,1,0:T(8,128)(2,1)S(1)} %get-tuple-element.81.mine_ref.refs_0_, bf16[4,36,512]{2,1,0:T(8,128)(2,1)S(1)} %collective-permute-done.8.other_ref.refs_1_, ...), custom_call_target="tpu_custom_call" | custom-call | flops 301989888 | bytes 1564688 | tf_op jit(solution)/shard_map/pallas_call | solution.py:479
  122.0 0.6 collective-permute-done.19.refs_2_
  122.7 1.8 %collective-permute-start.24 = (bf16[4,16,1408]{2,1,0:T(8,128)(2,1)S(1)}, bf16[4,16,1408]{2,1,0:T(8,128)(2,1)S(1)}, u32[]{:S(2)}, u32[]{:S(2)}) collective-permute-start(bf16[4,16,1408]{2,1,0:T(8,128)(2,1)S(1)} %shard_map.228.refs_0_), channel_id=1, source_target_pairs={{0,17},{1,16},{2,19},{3,18},{4,21},{5,20},{6,23},{7,22},{8,25},{9,... | collective-permute-start | bytes 540680 | tf_op jit(solution)/shard_map/ppermute | solution.py:542
  124.5 1.2 collective-permute-start.23
  125.7 0.6 collective-permute-start.22
  126.2 3.3 %collective-permute-done.24.refs_3_ = bf16[4,16,1408]{2,1,0:T(8,128)(2,1)S(1)} collective-permute-done((bf16[4,16,1408]{2,1,0:T(8,128)(2,1)S(1)}, bf16[4,16,1408]{2,1,0:T(8,128)(2,1)S(1)}, u32[]{:S(2)}, u32[]{:S(2)}) %collective-permute-start.24) | collective-permute-done | bytes 180256 | tf_op jit(solution)/shard_map/ppermute | solution.py:542
  129.5 1.8 %collective-permute-done.23.refs_2_ = bf16[4,16,1408]{2,1,0:T(8,128)(2,1)S(1)} collective-permute-done((bf16[4,16,1408]{2,1,0:T(8,128)(2,1)S(1)}, bf16[4,16,1408]{2,1,0:T(8,128)(2,1)S(1)}, u32[]{:S(2)}, u32[]{:S(2)}) %collective-permute-start.23) | collective-permute-done | bytes 180256 | tf_op jit(solution)/shard_map/ppermute | solution.py:542
  131.4 0.5 collective-permute-start.26
  131.9 0.9 collective-permute-done.27.refs_6_
  132.8 0.3 collective-permute-done.26.refs_5_
  133.0 2.2 %shard_map.230 = (f32[512,1024]{1,0:T(8,128)}, f32[256,512]{1,0:T(8,128)}, f32[1,1]{1,0:T(1,128)}) custom-call(s32[4]{0:T(128)S(1)} %pad_add_fusion.me_ref, bf16[4,16,1408]{2,1,0:T(8,128)(2,1)S(1)} %shard_map.228.refs_0_, bf16[4,16,1408]{2,1,0:T(8,128)(2,1)S(1)} %collective-permute-done.22.refs_1_, bf16[4,16,1408]{2,1,0:T(8,128)(2,1)S(1)} %collective-permute-done.23.refs_2_, ...), custom_call_target="tpu_custom_call" | custom-call | bytes 1441808 | tf_op jit(solution)/shard_map/pallas_call | solution.py:479
  (58 shorter events, 0.5 us)
Async XLA Ops:
  0.8 50.1 %copy-start.3 = (bf16[1024,512]{1,0:T(8,128)(2,1)S(1)}, bf16[1024,512]{1,0:T(8,128)(2,1)}, u32[]{:S(2)}) copy-start(bf16[1024,512]{1,0:T(8,128)(2,1)} %w_dec_ref.1) | copy-start | bytes 3145732
  0.8 50.1 %copy-start.4 = (bf16[512,768]{1,0:T(8,128)(2,1)S(1)}, bf16[512,768]{1,0:T(8,128)(2,1)}, u32[]{:S(2)}) copy-start(bf16[512,768]{1,0:T(8,128)(2,1)} %w_qkv_ref.1) | copy-start | bytes 2359300
  8.3 42.6 %copy-start = (bf16[1,288,1024]{2,1,0:T(8,128)(2,1)S(1)}, bf16[1,288,1024]{2,1,0:T(8,128)(2,1)}, u32[]{:S(2)}) copy-start(bf16[1,288,1024]{2,1,0:T(8,128)(2,1)} %param.21) | copy-start | bytes 1769476
  8.3 42.6 %copy-start.2 = (bf16[512,1024]{1,0:T(8,128)(2,1)S(1)}, bf16[512,1024]{1,0:T(8,128)(2,1)}, u32[]{:S(2)}) copy-start(bf16[512,1024]{1,0:T(8,128)(2,1)} %w_out_ref.2) | copy-start | bytes 3145732
  8.3 42.6 %copy-start.5 = (bf16[288,512]{1,0:T(8,128)(2,1)S(1)}, bf16[288,512]{1,0:T(8,128)(2,1)}, u32[]{:S(2)}) copy-start(bf16[288,512]{1,0:T(8,128)(2,1)} %pos_ref.1) | copy-start | bytes 884740
  8.3 42.6 %copy-start.6 = (s32[1,288]{1,0:T(1,128)S(1)}, s32[1,288]{1,0:T(1,128)}, u32[]{:S(2)}) copy-start(s32[1,288]{1,0:T(1,128)} %slots_ref.3) | copy-start | bytes 3460
  8.3 42.6 %copy-start.7 = (bf16[1024]{0:T(1024)(128)(2,1)S(1)}, bf16[1024]{0:T(1024)(128)(2,1)}, u32[]{:S(2)}) copy-start(bf16[1024]{0:T(1024)(128)(2,1)} %out_gain_ref.1) | copy-start | bytes 6148
  8.3 42.6 %copy-start.8 = (s32[1,288]{1,0:T(1,128)S(1)}, s32[1,288]{1,0:T(1,128)}, u32[]{:S(2)}) copy-start(s32[1,288]{1,0:T(1,128)} %owner_ref.1) | copy-start | bytes 3460
  8.4 42.6 %copy-start.9 = (bf16[512]{0:T(512)(128)(2,1)S(1)}, bf16[512]{0:T(512)(128)(2,1)}, u32[]{:S(2)}) copy-start(bf16[512]{0:T(512)(128)(2,1)} %mask_ref.1) | copy-start | bytes 3076
  8.4 42.6 %copy-start.10 = (bf16[512]{0:T(512)(128)(2,1)S(1)}, bf16[512]{0:T(512)(128)(2,1)}, u32[]{:S(2)}) copy-start(bf16[512]{0:T(512)(128)(2,1)} %gain_ref.3) | copy-start | bytes 3076
  8.4 10.5 %collective-permute-start = (bf16[448,128]{1,0:T(8,128)(2,1)S(1)}, bf16[448,128]{1,0:T(8,128)(2,1)S(1)}, u32[]{:S(2)}, u32[]{:S(2)}) collective-permute-start(bf16[448,128]{1,0:T(8,128)(2,1)S(1)} %get-tuple-element.55), channel_id=1, source_target_pairs={{0,6},{1,7},{2,4},{3,5},{4,2},{5,3},{6,0},{7,1},{8,14},{9,15},{10,... | collective-permute-start | bytes 344072 | tf_op jit(solution)/shard_map/ppermute | solution.py:542
  13.5 14.6 %collective-permute-start.1 = (bf16[448,128]{1,0:T(8,128)(2,1)S(1)}, bf16[448,128]{1,0:T(8,128)(2,1)S(1)}, u32[]{:S(2)}, u32[]{:S(2)}) collective-permute-start(bf16[448,128]{1,0:T(8,128)(2,1)S(1)} %get-tuple-element.56), channel_id=1, source_target_pairs={{0,7},{1,6},{2,5},{3,4},{4,3},{5,2},{6,1},{7,0},{8,15},{9,14},{10,... | collective-permute-start | bytes 344072 | tf_op jit(solution)/shard_map/ppermute | solution.py:542
  14.7 16.9 %collective-permute-start.2 = (bf16[448,128]{1,0:T(8,128)(2,1)S(1)}, bf16[448,128]{1,0:T(8,128)(2,1)S(1)}, u32[]{:S(2)}, u32[]{:S(2)}) collective-permute-start(bf16[448,128]{1,0:T(8,128)(2,1)S(1)} %get-tuple-element.57), channel_id=1, source_target_pairs={{0,4},{1,5},{2,6},{3,7},{4,0},{5,1},{6,2},{7,3},{8,12},{9,13},{10,... | collective-permute-start | bytes 344072 | tf_op jit(solution)/shard_map/ppermute | solution.py:542
  15.5 18.7 %collective-permute-start.3 = (bf16[448,128]{1,0:T(8,128)(2,1)S(1)}, bf16[448,128]{1,0:T(8,128)(2,1)S(1)}, u32[]{:S(2)}, u32[]{:S(2)}) collective-permute-start(bf16[448,128]{1,0:T(8,128)(2,1)S(1)} %get-tuple-element.58), channel_id=1, source_target_pairs={{0,5},{1,4},{2,7},{3,6},{4,1},{5,0},{6,3},{7,2},{8,13},{9,12},{10,... | collective-permute-start | bytes 344072 | tf_op jit(solution)/shard_map/ppermute | solution.py:542
  17.4 16.8 %collective-permute-start.4 = (bf16[448,128]{1,0:T(8,128)(2,1)S(1)}, bf16[448,128]{1,0:T(8,128)(2,1)S(1)}, u32[]{:S(2)}, u32[]{:S(2)}) collective-permute-start(bf16[448,128]{1,0:T(8,128)(2,1)S(1)} %get-tuple-element.59), channel_id=1, source_target_pairs={{0,2},{1,3},{2,0},{3,1},{4,6},{5,7},{6,4},{7,5},{8,10},{9,11},{10,... | collective-permute-start | bytes 344072 | tf_op jit(solution)/shard_map/ppermute | solution.py:542
  18.8 16.3 %collective-permute-start.5 = (bf16[448,128]{1,0:T(8,128)(2,1)S(1)}, bf16[448,128]{1,0:T(8,128)(2,1)S(1)}, u32[]{:S(2)}, u32[]{:S(2)}) collective-permute-start(bf16[448,128]{1,0:T(8,128)(2,1)S(1)} %get-tuple-element.60), channel_id=1, source_target_pairs={{0,3},{1,2},{2,1},{3,0},{4,7},{5,6},{6,5},{7,4},{8,11},{9,10},{10,... | collective-permute-start | bytes 344072 | tf_op jit(solution)/shard_map/ppermute | solution.py:542
  28.1 7.7 %collective-permute-start.6 = (bf16[448,128]{1,0:T(8,128)(2,1)S(1)}, bf16[448,128]{1,0:T(8,128)(2,1)S(1)}, u32[]{:S(2)}, u32[]{:S(2)}) collective-permute-start(bf16[448,128]{1,0:T(8,128)(2,1)S(1)} %get-tuple-element.61), channel_id=1, source_target_pairs={{0,1},{1,0},{2,3},{3,2},{4,5},{5,4},{6,7},{7,6},{8,9},{9,8},{10,11... | collective-permute-start | bytes 344072 | tf_op jit(solution)/shard_map/ppermute | solution.py:542
  65.9 18.3 %copy-start.1 = (bf16[512,1024]{1,0:T(8,128)(2,1)S(1)}, bf16[512,1024]{1,0:T(8,128)(2,1)}, u32[]{:S(2)}) copy-start(bf16[512,1024]{1,0:T(8,128)(2,1)} %w_head_ref.5) | copy-start | bytes 3145732
  65.9 18.3 %copy-start.11 = (bf16[512,2048]{1,0:T(8,128)(2,1)S(1)}, bf16[512,2048]{1,0:T(8,128)(2,1)}, u32[]{:S(2)}) copy-start(bf16[512,2048]{1,0:T(8,128)(2,1)} %w_up_ref.3) | copy-start | bytes 6291460
  65.9 18.3 %copy-start.12 = (bf16[2048,512]{1,0:T(8,128)(2,1)S(1)}, bf16[2048,512]{1,0:T(8,128)(2,1)}, u32[]{:S(2)}) copy-start(bf16[2048,512]{1,0:T(8,128)(2,1)} %w_down_ref.3) | copy-start | bytes 6291460
  65.9 18.3 %copy-start.13 = (bf16[256,512]{1,0:T(8,128)(2,1)S(1)}, bf16[256,512]{1,0:T(8,128)(2,1)}, u32[]{:S(2)}) copy-start(bf16[256,512]{1,0:T(8,128)(2,1)} %w_out_ref.3) | copy-start | bytes 786436
  65.9 18.3 %copy-start.14 = (bf16[512]{0:T(512)(128)(2,1)S(1)}, bf16[512]{0:T(512)(128)(2,1)}, u32[]{:S(2)}) copy-start(bf16[512]{0:T(512)(128)(2,1)} %feed_gain_ref.3) | copy-start | bytes 3076
  65.9 18.3 %copy-start.15 = (bf16[512]{0:T(512)(128)(2,1)S(1)}, bf16[512]{0:T(512)(128)(2,1)}, u32[]{:S(2)}) copy-start(bf16[512]{0:T(512)(128)(2,1)} %head_gain_ref.3) | copy-start | bytes 3076
  89.1 5.4 %collective-permute-start.8 = (bf16[4,36,512]{2,1,0:T(8,128)(2,1)S(1)}, bf16[4,36,512]{2,1,0:T(8,128)(2,1)S(1)}, u32[]{:S(2)}, u32[]{:S(2)}) collective-permute-start(bf16[4,36,512]{2,1,0:T(8,128)(2,1)S(1)} %get-tuple-element.77), channel_id=1, source_target_pairs={{0,1},{1,0},{2,3},{3,2},{4,5},{5,4},{6,7},{7,6},{8,9},{9,8},{10,11... | collective-permute-start | bytes 442376 | tf_op jit(solution)/shard_map/ppermute | solution.py:542
  89.3 5.2 %collective-permute-start.7 = (bf16[4,4,16,1024]{3,2,1,0:T(8,128)(2,1)S(1)}, bf16[4,4,16,1024]{3,2,1,0:T(8,128)(2,1)S(1)}, u32[]{:S(2)}, u32[]{:S(2)}) collective-permute-start(bf16[4,4,16,1024]{3,2,1,0:T(8,128)(2,1)S(1)} %get-tuple-element.76), channel_id=1, source_target_pairs={{0,8},{1,9},{2,10},{3,11},{4,12},{5,13},{6,14},{7,15},{8,0},{9,1},... | collective-permute-start | bytes 1572872 | tf_op jit(solution)/shard_map/ppermute | solution.py:542
  94.5 1.4 %collective-permute-start.9 = (bf16[4,4,16,384]{3,2,1,0:T(8,128)(2,1)S(1)}, bf16[4,4,16,384]{3,2,1,0:T(8,128)(2,1)S(1)}, u32[]{:S(2)}, u32[]{:S(2)}) collective-permute-start(bf16[4,4,16,384]{3,2,1,0:T(8,128)(2,1)S(1)} %get-tuple-element.80), channel_id=1, source_target_pairs={{0,8},{1,9},{2,10},{3,11},{4,12},{5,13},{6,14},{7,15},{8,0},{9,1},... | collective-permute-start | bytes 589832 | tf_op jit(solution)/shard_map/ppermute | solution.py:542
  96.1 11.8 %collective-permute-start.10 = (bf16[4,16,1408]{2,1,0:T(8,128)(2,1)S(1)}, bf16[4,16,1408]{2,1,0:T(8,128)(2,1)S(1)}, u32[]{:S(2)}, u32[]{:S(2)}) collective-permute-start(bf16[4,16,1408]{2,1,0:T(8,128)(2,1)S(1)} %get-tuple-element.83), channel_id=1, source_target_pairs={{0,17},{1,16},{2,19},{3,18},{4,21},{5,20},{6,23},{7,22},{8,25},{9,... | collective-permute-start | bytes 540680 | tf_op jit(solution)/shard_map/ppermute | solution.py:542
  97.3 10.7 %collective-permute-start.11 = (bf16[4,16,1408]{2,1,0:T(8,128)(2,1)S(1)}, bf16[4,16,1408]{2,1,0:T(8,128)(2,1)S(1)}, u32[]{:S(2)}, u32[]{:S(2)}) collective-permute-start(bf16[4,16,1408]{2,1,0:T(8,128)(2,1)S(1)} %get-tuple-element.84), channel_id=1, source_target_pairs={{0,1},{1,0},{2,3},{3,2},{4,5},{5,4},{6,7},{7,6},{8,9},{9,8},{10,11... | collective-permute-start | bytes 540680 | tf_op jit(solution)/shard_map/ppermute | solution.py:542
  99.1 8.8 %collective-permute-start.12 = (bf16[4,16,1408]{2,1,0:T(8,128)(2,1)S(1)}, bf16[4,16,1408]{2,1,0:T(8,128)(2,1)S(1)}, u32[]{:S(2)}, u32[]{:S(2)}) collective-permute-start(bf16[4,16,1408]{2,1,0:T(8,128)(2,1)S(1)} %get-tuple-element.85), channel_id=1, source_target_pairs={{0,16},{1,17},{2,18},{3,19},{4,20},{5,21},{6,22},{7,23},{8,24},{9,... | collective-permute-start | bytes 540680 | tf_op jit(solution)/shard_map/ppermute | solution.py:542
  99.7 8.2 %collective-permute-start.13 = (bf16[2,36,512]{2,1,0:T(8,128)(2,1)S(1)}, bf16[2,36,512]{2,1,0:T(8,128)(2,1)S(1)}, u32[]{:S(2)}, u32[]{:S(2)}) collective-permute-start(bf16[2,36,512]{2,1,0:T(8,128)(2,1)S(1)} %get-tuple-element.87), channel_id=1, source_target_pairs={{0,4},{1,5},{2,6},{3,7},{4,0},{5,1},{6,2},{7,3},{8,12},{9,13},{10,... | collective-permute-start | bytes 221192 | tf_op jit(solution)/shard_map/ppermute | solution.py:542
  100.0 7.9 %collective-permute-start.14 = (bf16[2,36,512]{2,1,0:T(8,128)(2,1)S(1)}, bf16[2,36,512]{2,1,0:T(8,128)(2,1)S(1)}, u32[]{:S(2)}, u32[]{:S(2)}) collective-permute-start(bf16[2,36,512]{2,1,0:T(8,128)(2,1)S(1)} %get-tuple-element.88), channel_id=1, source_target_pairs={{0,6},{1,7},{2,4},{3,5},{4,2},{5,3},{6,0},{7,1},{8,14},{9,15},{10,... | collective-permute-start | bytes 221192 | tf_op jit(solution)/shard_map/ppermute | solution.py:542
  107.9 12.2 %collective-permute-start.21 = (bf16[2,36,512]{2,1,0:T(8,128)(2,1)S(1)}, bf16[2,36,512]{2,1,0:T(8,128)(2,1)S(1)}, u32[]{:S(2)}, u32[]{:S(2)}) collective-permute-start(bf16[2,36,512]{2,1,0:T(8,128)(2,1)S(1)} %get-tuple-element.94), channel_id=1, source_target_pairs={{0,2},{1,3},{2,0},{3,1},{4,6},{5,7},{6,4},{7,5},{8,10},{9,11},{10,... | collective-permute-start | bytes 221192 | tf_op jit(solution)/shard_map/ppermute | solution.py:542
  108.1 6.2 %collective-permute-start.15 = (bf16[16,1408]{1,0:T(8,128)(2,1)S(1)}, bf16[16,1408]{1,0:T(8,128)(2,1)S(1)}, u32[]{:S(2)}, u32[]{:S(2)}) collective-permute-start(bf16[16,1408]{1,0:T(8,128)(2,1)S(1)} %get-tuple-element.90), channel_id=1, source_target_pairs={{0,6},{1,7},{2,4},{3,5},{4,2},{5,3},{6,0},{7,1},{8,14},{9,15},{10,... | collective-permute-start | bytes 135176 | tf_op jit(solution)/shard_map/ppermute | solution.py:542
  109.1 6.0 %collective-permute-start.16 = (bf16[16,1408]{1,0:T(8,128)(2,1)S(1)}, bf16[16,1408]{1,0:T(8,128)(2,1)S(1)}, u32[]{:S(2)}, u32[]{:S(2)}) collective-permute-start(bf16[16,1408]{1,0:T(8,128)(2,1)S(1)} %get-tuple-element.91), channel_id=1, source_target_pairs={{0,4},{1,5},{2,6},{3,7},{4,0},{5,1},{6,2},{7,3},{8,12},{9,13},{10,... | collective-permute-start | bytes 135176 | tf_op jit(solution)/shard_map/ppermute | solution.py:542
  111.6 4.0 %collective-permute-start.17 = (bf16[16,1408]{1,0:T(8,128)(2,1)S(1)}, bf16[16,1408]{1,0:T(8,128)(2,1)S(1)}, u32[]{:S(2)}, u32[]{:S(2)}) collective-permute-start(bf16[16,1408]{1,0:T(8,128)(2,1)S(1)} %get-tuple-element.92), channel_id=1, source_target_pairs={{0,2},{1,3},{2,0},{3,1},{4,6},{5,7},{6,4},{7,5},{8,10},{9,11},{10,... | collective-permute-start | bytes 135176 | tf_op jit(solution)/shard_map/ppermute | solution.py:542
  115.7 6.3 %collective-permute-start.20 = (bf16[16,1408]{1,0:T(8,128)(2,1)S(1)}, bf16[16,1408]{1,0:T(8,128)(2,1)S(1)}, u32[]{:S(2)}, u32[]{:S(2)}) collective-permute-start(bf16[16,1408]{1,0:T(8,128)(2,1)S(1)} %shard_map.227.refs_0_), channel_id=1, source_target_pairs={{0,6},{1,7},{2,4},{3,5},{4,2},{5,3},{6,0},{7,1},{8,14},{9,15},{10,... | collective-permute-start | bytes 135176 | tf_op jit(solution)/shard_map/ppermute | solution.py:542
  117.2 5.4 %collective-permute-start.19 = (bf16[16,1408]{1,0:T(8,128)(2,1)S(1)}, bf16[16,1408]{1,0:T(8,128)(2,1)S(1)}, u32[]{:S(2)}, u32[]{:S(2)}) collective-permute-start(bf16[16,1408]{1,0:T(8,128)(2,1)S(1)} %shard_map.227.refs_0_), channel_id=1, source_target_pairs={{0,4},{1,5},{2,6},{3,7},{4,0},{5,1},{6,2},{7,3},{8,12},{9,13},{10,... | collective-permute-start | bytes 135176 | tf_op jit(solution)/shard_map/ppermute | solution.py:542
  118.1 4.5 %collective-permute-start.18 = (bf16[16,1408]{1,0:T(8,128)(2,1)S(1)}, bf16[16,1408]{1,0:T(8,128)(2,1)S(1)}, u32[]{:S(2)}, u32[]{:S(2)}) collective-permute-start(bf16[16,1408]{1,0:T(8,128)(2,1)S(1)} %shard_map.227.refs_0_), channel_id=1, source_target_pairs={{0,2},{1,3},{2,0},{3,1},{4,6},{5,7},{6,4},{7,5},{8,10},{9,11},{10,... | collective-permute-start | bytes 135176 | tf_op jit(solution)/shard_map/ppermute | solution.py:542
  122.7 6.9 %collective-permute-start.24 = (bf16[4,16,1408]{2,1,0:T(8,128)(2,1)S(1)}, bf16[4,16,1408]{2,1,0:T(8,128)(2,1)S(1)}, u32[]{:S(2)}, u32[]{:S(2)}) collective-permute-start(bf16[4,16,1408]{2,1,0:T(8,128)(2,1)S(1)} %shard_map.228.refs_0_), channel_id=1, source_target_pairs={{0,17},{1,16},{2,19},{3,18},{4,21},{5,20},{6,23},{7,22},{8,25},{9,... | collective-permute-start | bytes 540680 | tf_op jit(solution)/shard_map/ppermute | solution.py:542
  124.5 6.9 %collective-permute-start.23 = (bf16[4,16,1408]{2,1,0:T(8,128)(2,1)S(1)}, bf16[4,16,1408]{2,1,0:T(8,128)(2,1)S(1)}, u32[]{:S(2)}, u32[]{:S(2)}) collective-permute-start(bf16[4,16,1408]{2,1,0:T(8,128)(2,1)S(1)} %shard_map.228.refs_0_), channel_id=1, source_target_pairs={{0,1},{1,0},{2,3},{3,2},{4,5},{5,4},{6,7},{7,6},{8,9},{9,8},{10,11... | collective-permute-start | bytes 540680 | tf_op jit(solution)/shard_map/ppermute | solution.py:542
  125.7 5.7 %collective-permute-start.22 = (bf16[4,16,1408]{2,1,0:T(8,128)(2,1)S(1)}, bf16[4,16,1408]{2,1,0:T(8,128)(2,1)S(1)}, u32[]{:S(2)}, u32[]{:S(2)}) collective-permute-start(bf16[4,16,1408]{2,1,0:T(8,128)(2,1)S(1)} %shard_map.228.refs_0_), channel_id=1, source_target_pairs={{0,16},{1,17},{2,18},{3,19},{4,20},{5,21},{6,22},{7,23},{8,24},{9,... | collective-permute-start | bytes 540680 | tf_op jit(solution)/shard_map/ppermute | solution.py:542
  126.2 5.7 %collective-permute-start.25 = (bf16[4,16,1408]{2,1,0:T(8,128)(2,1)S(1)}, bf16[4,16,1408]{2,1,0:T(8,128)(2,1)S(1)}, u32[]{:S(2)}, u32[]{:S(2)}) collective-permute-start(bf16[4,16,1408]{2,1,0:T(8,128)(2,1)S(1)} %shard_map.228.refs_0_), channel_id=1, source_target_pairs={{0,8},{1,9},{2,10},{3,11},{4,12},{5,13},{6,14},{7,15},{8,0},{9,1},... | collective-permute-start | bytes 540680 | tf_op jit(solution)/shard_map/ppermute | solution.py:542
  129.5 2.3 %collective-permute-start.28 = (bf16[4,16,1408]{2,1,0:T(8,128)(2,1)S(1)}, bf16[4,16,1408]{2,1,0:T(8,128)(2,1)S(1)}, u32[]{:S(2)}, u32[]{:S(2)}) collective-permute-start(bf16[4,16,1408]{2,1,0:T(8,128)(2,1)S(1)} %collective-permute-done.24.refs_3_), channel_id=1, source_target_pairs={{0,8},{1,9},{2,10},{3,11},{4,12},{5,13},{6,14},{7,15},{8,0},{9,1},... | collective-permute-start | bytes 540680 | tf_op jit(solution)/shard_map/ppermute | solution.py:542
  131.4 1.4 %collective-permute-start.27 = (bf16[4,16,1408]{2,1,0:T(8,128)(2,1)S(1)}, bf16[4,16,1408]{2,1,0:T(8,128)(2,1)S(1)}, u32[]{:S(2)}, u32[]{:S(2)}) collective-permute-start(bf16[4,16,1408]{2,1,0:T(8,128)(2,1)S(1)} %collective-permute-done.23.refs_2_), channel_id=1, source_target_pairs={{0,8},{1,9},{2,10},{3,11},{4,12},{5,13},{6,14},{7,15},{8,0},{9,1},... | collective-permute-start | bytes 540680 | tf_op jit(solution)/shard_map/ppermute | solution.py:542
  131.4 1.7 %collective-permute-start.26 = (bf16[4,16,1408]{2,1,0:T(8,128)(2,1)S(1)}, bf16[4,16,1408]{2,1,0:T(8,128)(2,1)S(1)}, u32[]{:S(2)}, u32[]{:S(2)}) collective-permute-start(bf16[4,16,1408]{2,1,0:T(8,128)(2,1)S(1)} %collective-permute-done.22.refs_1_), channel_id=1, source_target_pairs={{0,8},{1,9},{2,10},{3,11},{4,12},{5,13},{6,14},{7,15},{8,0},{9,1},... | collective-permute-start | bytes 540680 | tf_op jit(solution)/shard_map/ppermute | solution.py:542
